TPU v7x, 32 devices: a whole 2x2x4 slice. The times are simulated.
32 devices in a mesh: section: 4 (over y, x), expert: 8 (over z, core).
Axes of the slice: x: 2, y: 2, z: 4, core: 2. Of those that a mesh axis runs over, the one named last changes fastest.
Arguments:
- handoff_forward: bfloat16 [4096, 1024], P(('section', 'expert')), may hold values from -12 to 12
- stashed_input: bfloat16 [4096, 1024], P(('section', 'expert')), may hold values from -12 to 12
- relay_cotangents: bfloat16 [4096, 1024], P(('section', 'expert')), may hold values from -6 to 6
- attention_gain: float32 [4, 1024], P('section'), may hold values from 0.1 to 1.9
- expert_gain: float32 [4, 1024], P('section'), may hold values from 0.1 to 1.9
- w_qkv: bfloat16 [4, 1024, 3072], P('section', 'expert'), may hold values from -0.1875 to 0.1875
- w_out: bfloat16 [4, 1024, 1024], P('section', 'expert'), may hold values from -0.1875 to 0.1875
- w_up: bfloat16 [4, 8, 1024, 704], P('section', 'expert'), may hold values from -0.1875 to 0.1875
- w_down: bfloat16 [4, 8, 704, 1024], P('section', 'expert'), may hold values from -0.21875 to 0.21875
- routes: int32 [2, 4096, 2], P(None, ('section', 'expert')), may hold values from 0 to 7, as said below
- gate_logits: float32 [2, 4096, 2], P(None, ('section', 'expert')), may hold values from -6 to 6
- block_mask: int32 [2, 32, 8, 8], P(None, ('section', 'expert')), may hold values 0 or 1
Outputs:
- layer_output: bfloat16 [4096, 1024], P(('section', 'expert'))
- layer_entry_derivative: bfloat16 [4096, 1024], P(('section', 'expert'))
Inputs may be any that keep to these rules, and one draw needn't show every extreme that they name: `routes`: each row names two different experts; within each aligned block of 128 rows of one micro-batch no expert is named more than 64 times, and one expert, the same for every block of both micro-batches, is named exactly 64 times in every block.
All inputs are finite; a program needn't handle non-finite values. No bound on the sum of `block_mask` on one device may be relied on, other than what follows from the above.
Results may differ from a plain program's by a relative error of at most 0.007.
Values may be sent and summed in bfloat16 or wider, within the bound.
No kernel may reach another device: no remote copies, remote signals or barrier semaphores. Data moves between devices by JAX's collectives and lax.ppermute only.
A program may use at most 128 MiB of HBM per device.

v0:
```python
import functools

import jax
import jax.numpy as jnp
from jax import lax
from jax.experimental import pallas as pl
from jax.experimental.pallas import tpu as pltpu
from jax.sharding import PartitionSpec as P


HEADS = 8
HEAD_DIM = 128
FRAMES = 128
BLOCK = 16
CORES = 2
LANES = 128

EPS = 1e-06
SCORE_SCALE = HEAD_DIM ** (-0.5)
GELU_C = 0.7978845608028654
GELU_A = 0.044715


F32 = jnp.float32
BF16 = jnp.bfloat16
NT = (((1,), (1,)), ((), ()))
TN = (((0,), (0,)), ((), ()))
ANY = pl.BlockSpec(memory_space=pl.ANY)
SMEM = pl.BlockSpec(memory_space=pltpu.SMEM)
VMEM = pl.BlockSpec(memory_space=pltpu.VMEM)
PARAMS = pltpu.CompilerParams(vmem_limit_bytes=56 * 1024 * 1024)


def dot(a, b, dims=(((1,), (0,)), ((), ()))):
    return lax.dot_general(a, b, dims, preferred_element_type=F32)


def mean_last(values):
    return jnp.mean(values, axis=-1, keepdims=True)


def passed_along(value, axis, steps):
    count = lax.axis_size(axis)
    pairs = [(source, (source + steps) % count) for source in range(count)]
    return lax.ppermute(value, axis, pairs)


def line_length():
    return lax.axis_size("expert") // CORES


def chip_pairs(sources, step):
    return [
        (CORES * chip + core, CORES * (chip + step) + core)
        for chip in sources
        for core in range(CORES)
    ]


def swapped(value):
    count = lax.axis_size("expert")
    return lax.ppermute(value, "expert", [(i, i ^ 1) for i in range(count)])


def hop(value, sources, move):
    return lax.ppermute(value, "expert", chip_pairs(sources, move))


def relayed(value):
    length = line_length()
    entries = [value]
    up = down = value
    for step in range(1, length):
        up = hop(up, range(step - 1, length - 1), 1)
        down = hop(down, range(1, length - step + 1), -1)
        entries += [up, down]
    return entries


def with_partner(entries):
    return entries + [swapped(block) for block in entries]


def scattered(blocks):
    length = line_length()
    up = down = None
    for step in range(1, length):
        far = length - step
        send_up, send_down = blocks[far], blocks[length - far]
        if up is not None:
            send_up = send_up + up
            send_down = send_down + down
        up = hop(send_up, range(0, step), 1)
        down = hop(send_down, range(length - step, length), -1)
    return [blocks[0], up, down]


def entry_chips(length, chip):
    listing = [(None, chip)]
    for hop in range(1, length):
        listing.append((chip - hop >= 0, chip - hop))
        listing.append((chip + hop < length, chip + hop))
    return listing


def each_copy(refs, target, sems, rows, chip, core, act):
    count = len(refs) // 2
    listing = entry_chips((count + 1) // 2, chip)
    for side in range(CORES):
        for index, (valid, origin) in enumerate(listing):
            number = side * count + index
            owner = CORES * origin + (core if side == 0 else 1 - core)

            def run(number=number, owner=owner):
                start = pl.multiple_of(owner * rows, rows)
                act(
                    pltpu.make_async_copy(
                        refs[number], target.at[pl.ds(start, rows), :], sems.at[number]
                    )
                )

            if valid is None:
                run()
            else:
                pl.when(valid)(run)


def start_copies(*args):
    each_copy(*args, lambda copy: copy.start())


def wait_copies(*args):
    each_copy(*args, lambda copy: copy.wait())


def head_parts(proj_ref, head):
    def part(index):
        start = (index * HEADS + head) * HEAD_DIM
        return proj_ref[:, start : start + HEAD_DIM]

    query, key, value = part(0), part(1), part(2)
    query_scale = lax.rsqrt(mean_last(query * query) + EPS)
    key_scale = lax.rsqrt(mean_last(key * key) + EPS)
    return query * query_scale, query_scale, key * key_scale, key_scale, value.astype(BF16)


def attn_probs_of(query_bf, key_bf, allowed):
    scores = dot(query_bf, key_bf, NT) * SCORE_SCALE
    expo = jnp.where(allowed, jnp.exp(scores), 0.0)
    return expo / jnp.sum(expo, axis=-1, keepdims=True)


def attend_rows(proj_ref, mask, heads_ref):
    allowed = mask > 0.5
    for head in range(HEADS):
        query_hat, _, key_hat, _, value_bf = head_parts(proj_ref, head)
        probs = attn_probs_of(query_hat.astype(BF16), key_hat.astype(BF16), allowed)
        out = dot(probs.astype(BF16), value_bf)
        heads_ref[:, head * HEAD_DIM : (head + 1) * HEAD_DIM] = out.astype(BF16)


def finish_rows(x, heads, out_w, gain_e, hidden_ref, expert_ref):
    hidden = x.astype(F32) + dot(heads, out_w)
    hidden_ref[...] = hidden
    rms = lax.rsqrt(mean_last(hidden * hidden) + EPS)
    expert_ref[...] = (hidden * rms * gain_e).astype(BF16)


def project_kernel(count, depth, *refs):
    place, xf_ref, xb_ref, gain_a, gain_e, mask_ref = refs[:6]
    mix_refs = refs[6 : 6 + count]
    out_refs = refs[6 + count : 6 + 2 * count]
    projf_ref, projb_ref, hidden_ref, expert_ref = refs[6 + 2 * count : 10 + 2 * count]
    mix_w, out_w, normed, heads, mix_sems, out_sems = refs[10 + 2 * count :]
    chip, core = place[0], place[1]
    start_copies(mix_refs, mix_w, mix_sems, depth, chip, core)
    start_copies(out_refs, out_w, out_sems, depth, chip, core)
    rows = xf_ref.shape[0]
    for index, x_ref in enumerate((xf_ref, xb_ref)):
        x = x_ref[...].astype(F32)
        rms = lax.rsqrt(mean_last(x * x) + EPS)
        normed[index * rows : (index + 1) * rows, :] = (x * rms * gain_a[...]).astype(BF16)
    wait_copies(mix_refs, mix_w, mix_sems, depth, chip, core)
    columns = mix_w.shape[1]
    chunk = 512
    for begin in range(0, columns, chunk):
        piece = dot(normed[...], mix_w[:, begin : begin + chunk])
        projf_ref[:, begin : begin + chunk] = piece[:rows]
        projb_ref[:, begin : begin + chunk] = piece[rows:]
    attend_rows(projb_ref, mask_ref[1], heads)
    wait_copies(out_refs, out_w, out_sems, depth, chip, core)
    finish_rows(xb_ref[...], heads[...], out_w[...], gain_e[...], hidden_ref, expert_ref)


def forward_kernel(count, depth, *refs):
    place, x_ref, proj_ref, gain_e, mask_ref = refs[:5]
    out_refs = refs[5 : 5 + count]
    hidden_ref, expert_ref = refs[5 + count : 7 + count]
    out_w, heads, out_sems = refs[7 + count :]
    chip, core = place[0], place[1]
    start_copies(out_refs, out_w, out_sems, depth, chip, core)
    attend_rows(proj_ref, mask_ref[0], heads)
    wait_copies(out_refs, out_w, out_sems, depth, chip, core)
    finish_rows(x_ref[...], heads[...], out_w[...], gain_e[...], hidden_ref, expert_ref)


def picked_gate(gates, me, expert_count, micro):
    lane = lax.broadcasted_iota(jnp.int32, gates.shape, 1)
    first = 2 * micro * expert_count + me
    hit = (lane == first) | (lane == first + expert_count)
    return jnp.sum(jnp.where(hit, gates, 0.0), axis=-1, keepdims=True)


def cotangent_kernel(count, rows, width, expert_count, *refs):
    place, down_ref = refs[:2]
    cot_refs = refs[2 : 2 + count]
    act_ref, gate_ref = refs[2 + count : 4 + count]
    cot, sems = refs[4 + count :]
    chip, core = place[0], place[1]
    me = CORES * chip + core
    start_copies(cot_refs, cot, sems, rows, chip, core)
    wait_copies(cot_refs, cot, sems, rows, chip, core)
    chunk = 2 * rows

    def step(index, carry):
        start = pl.multiple_of(index * chunk, chunk)
        block = cot[pl.ds(start, chunk), :]
        gates = block[:, width:].astype(F32)
        grad_act = dot(block[:, :width], down_ref[...], NT)
        act_ref[pl.ds(start, chunk), :] = grad_act * picked_gate(gates, me, expert_count, 1)
        gate_ref[pl.ds(start, chunk), :] = jnp.broadcast_to(
            picked_gate(gates, me, expert_count, 0), (chunk, LANES)
        )
        return carry

    lax.fori_loop(0, expert_count * rows // chunk, step, 0)


def give_back(result, mine_ref, other_ref, rows, chip, core):
    length = mine_ref.shape[0]
    for j in range(length):
        origin = lax.rem(chip + j, length)
        for out_ref, side in ((mine_ref, core), (other_ref, 1 - core)):
            start = pl.multiple_of((CORES * origin + side) * rows, rows)
            out_ref[j] = result[pl.ds(start, rows), :]


def expert_backward_kernel(count, rows, *refs):
    place, up_ref, act_ref = refs[:3]
    row_refs = refs[3 : 3 + count]
    mine_ref, other_ref = refs[3 + count : 5 + count]
    tokens, result, sems = refs[5 + count :]
    chip, core = place[0], place[1]
    start_copies(row_refs, tokens, sems, rows, chip, core)
    wait_copies(row_refs, tokens, sems, rows, chip, core)
    chunk = 2 * rows

    def step(index, carry):
        start = pl.multiple_of(index * chunk, chunk)
        pre = dot(tokens[pl.ds(start, chunk), :], up_ref[...])
        square = pre * pre
        bend = jnp.tanh(GELU_C * pre * (1.0 + GELU_A * square))
        slope = 0.5 * (1.0 + bend) + 0.5 * pre * (1.0 - bend * bend) * (
            GELU_C * (1.0 + 3.0 * GELU_A * square)
        )
        grad = (act_ref[pl.ds(start, chunk), :] * slope).astype(BF16)
        result[pl.ds(start, chunk), :] = dot(grad, up_ref[...], NT).astype(BF16)
        return carry

    lax.fori_loop(0, tokens.shape[0] // chunk, step, 0)
    give_back(result, mine_ref, other_ref, rows, chip, core)


def expert_forward_kernel(count, rows, *refs):
    place, up_ref, down_ref, gate_ref = refs[:4]
    row_refs = refs[4 : 4 + count]
    mine_ref, other_ref = refs[4 + count : 6 + count]
    tokens, result, sems = refs[6 + count :]
    chip, core = place[0], place[1]
    start_copies(row_refs, tokens, sems, rows, chip, core)
    wait_copies(row_refs, tokens, sems, rows, chip, core)
    chunk = 2 * rows

    def step(index, carry):
        start = pl.multiple_of(index * chunk, chunk)
        pre = dot(tokens[pl.ds(start, chunk), :], up_ref[...])
        bend = jnp.tanh(GELU_C * pre * (1.0 + GELU_A * (pre * pre)))
        active = (0.5 * pre * (1.0 + bend)).astype(BF16)
        out = dot(active, down_ref[...])
        gate = gate_ref[pl.ds(start, chunk), :][:, :1]
        result[pl.ds(start, chunk), :] = (gate * out).astype(BF16)
        return carry

    lax.fori_loop(0, tokens.shape[0] // chunk, step, 0)
    give_back(result, mine_ref, other_ref, rows, chip, core)


def add_kernel(mine_ref, other_ref, *out_refs):
    for j, out_ref in enumerate(out_refs):
        out_ref[...] = (mine_ref[j].astype(F32) + other_ref[j].astype(F32)).astype(BF16)


def backward_kernel(count, parts, depth, *refs):
    place, x_ref, cot_ref, hidden_ref, proj_ref, gain_a, gain_e, mask_ref = refs[:8]
    part_refs = refs[8 : 8 + parts]
    mix_refs = refs[8 + parts : 8 + parts + count]
    out_refs = refs[8 + parts + count : 8 + parts + 2 * count]
    result_ref = refs[8 + parts + 2 * count]
    mix_w, out_w, mixed, mix_sems, out_sems = refs[9 + parts + 2 * count :]
    chip, core = place[0], place[1]
    start_copies(out_refs, out_w, out_sems, depth, chip, core)
    start_copies(mix_refs, mix_w, mix_sems, depth, chip, core)
    grad_moe = part_refs[0][...].astype(F32)
    for part_ref in part_refs[1:]:
        grad_moe = grad_moe + part_ref[...].astype(F32)
    hidden = hidden_ref[...]
    rms_two = lax.rsqrt(mean_last(hidden * hidden) + EPS)
    normal_two = hidden * rms_two
    grad_two = grad_moe * gain_e[...]
    grad_hidden = cot_ref[...].astype(F32) + rms_two * (
        grad_two - normal_two * mean_last(grad_two * normal_two)
    )
    wait_copies(out_refs, out_w, out_sems, depth, chip, core)
    grad_heads = dot(grad_hidden.astype(BF16), out_w[...], NT).astype(BF16)
    allowed = mask_ref[1] > 0.5
    for head in range(HEADS):
        query_hat, query_scale, key_hat, key_scale, value_bf = head_parts(proj_ref, head)
        query_bf, key_bf = query_hat.astype(BF16), key_hat.astype(BF16)
        probs = attn_probs_of(query_bf, key_bf, allowed)
        grad_out = grad_heads[:, head * HEAD_DIM : (head + 1) * HEAD_DIM]
        grad_probs = dot(grad_out, value_bf, NT)
        grad_value = dot(probs.astype(BF16), grad_out, TN)
        inner = jnp.sum(probs * grad_probs, axis=-1, keepdims=True)
        grad_scores = (probs * (grad_probs - inner) * SCORE_SCALE).astype(BF16)
        grad_qhat = dot(grad_scores, key_bf)
        grad_khat = dot(grad_scores, query_bf, TN)
        grad_query = query_scale * (grad_qhat - query_hat * mean_last(grad_qhat * query_hat))
        grad_key = key_scale * (grad_khat - key_hat * mean_last(grad_khat * key_hat))
        for index, grad in enumerate((grad_query, grad_key, grad_value)):
            start = (index * HEADS + head) * HEAD_DIM
            mixed[:, start : start + HEAD_DIM] = grad.astype(BF16)
    wait_copies(mix_refs, mix_w, mix_sems, depth, chip, core)
    grad_normed = dot(mixed[...], mix_w[...], NT)
    x = x_ref[...].astype(F32)
    rms_one = lax.rsqrt(mean_last(x * x) + EPS)
    normal_one = x * rms_one
    grad_one = grad_normed * gain_a[...]
    result = grad_hidden + rms_one * (grad_one - normal_one * mean_last(grad_one * normal_one))
    result_ref[...] = result.astype(BF16)


def shaped(shape, kind):
    return jax.ShapeDtypeStruct(shape, kind)


def dma(count):
    return pltpu.SemaphoreType.DMA((count,))


def call(kernel, outs, specs, out_specs, scratch, args):
    return pl.pallas_call(
        kernel,
        out_shape=outs,
        in_specs=specs,
        out_specs=out_specs,
        scratch_shapes=scratch,
        compiler_params=PARAMS,
    )(*args)


def dense_gates(routes, logits, expert_count):
    gates = jax.nn.sigmoid(logits)
    hit = routes[..., None] == jnp.arange(expert_count, dtype=jnp.int32)
    return jnp.sum(jnp.where(hit, gates[..., None], 0.0), axis=2)


def gate_columns(routes, logits, expert_count):
    gates = dense_gates(routes, logits, expert_count)
    high = lax.reduce_precision(gates, 8, 7)
    both = jnp.stack([high, gates - high], axis=1).astype(BF16)
    rows = jnp.transpose(both, (2, 0, 1, 3)).reshape(both.shape[2], -1)
    return jnp.pad(rows, ((0, 0), (0, LANES - rows.shape[1])))


def allowed_of(mask_blocks):
    frame_block = jnp.arange(FRAMES, dtype=jnp.int32) // BLOCK
    spread = (frame_block[:, None] == jnp.arange(FRAMES // BLOCK)[None, :]).astype(F32)
    eye = jnp.eye(FRAMES // BLOCK, dtype=F32)
    open_blocks = jnp.maximum((mask_blocks == 1).astype(F32), eye)
    return jnp.einsum("ib,mbc,jc->mij", spread, open_blocks, spread)


def local(
    handoff_forward,
    stashed_input,
    relay_cotangents,
    attention_gain,
    expert_gain,
    w_qkv,
    w_out,
    w_up,
    w_down,
    routes,
    gate_logits,
    block_mask,
):
    length = line_length()
    expert_count = lax.axis_size("expert")
    me = lax.axis_index("expert")
    place = jnp.stack([me // CORES, me % CORES]).astype(jnp.int32)
    tokens, width = handoff_forward.shape
    depth = w_qkv.shape[1]
    total = expert_count * tokens
    columns = w_qkv.shape[2]
    up_weight = w_up[0, 0]
    down_weight = w_down[0, 0]
    hidden_units = up_weight.shape[1]
    count = CORES * (2 * length - 1)

    mixers = with_partner(relayed(w_qkv[0]))
    outers = with_partner(relayed(w_out[0]))
    arriving = passed_along(handoff_forward, "section", 1)
    cotangent = passed_along(relay_cotangents, "section", -1)
    gates = gate_columns(routes, gate_logits, expert_count)
    cots = with_partner(relayed(jnp.concatenate([cotangent, gates], axis=1)))
    mask = allowed_of(block_mask[:, 0])

    proj_fwd, proj_bwd, hidden_bwd, expert_bwd = call(
        functools.partial(project_kernel, count, depth),
        (
            shaped((tokens, columns), F32),
            shaped((tokens, columns), F32),
            shaped((tokens, width), F32),
            shaped((tokens, width), BF16),
        ),
        [SMEM] + [VMEM] * 5 + [ANY] * (2 * count),
        (VMEM,) * 4,
        [
            pltpu.VMEM((width, columns), BF16),
            pltpu.VMEM((width, width), BF16),
            pltpu.VMEM((2 * tokens, width), BF16),
            pltpu.VMEM((tokens, width), BF16),
            dma(count),
            dma(count),
        ],
        [place, arriving, stashed_input, attention_gain, expert_gain, mask] + mixers + outers,
    )
    rows_bwd = with_partner(relayed(expert_bwd))

    hidden_fwd, expert_fwd = call(
        functools.partial(forward_kernel, count, depth),
        (shaped((tokens, width), F32), shaped((tokens, width), BF16)),
        [SMEM] + [VMEM] * 4 + [ANY] * count,
        (VMEM,) * 2,
        [pltpu.VMEM((width, width), BF16), pltpu.VMEM((tokens, width), BF16), dma(count)],
        [place, arriving, proj_fwd, expert_gain, mask] + outers,
    )
    rows_fwd = with_partner(relayed(expert_fwd))

    grad_act, gate_fwd = call(
        functools.partial(cotangent_kernel, count, tokens, width, expert_count),
        (shaped((total, hidden_units), F32), shaped((total, LANES), F32)),
        [SMEM, VMEM] + [ANY] * count,
        (VMEM,) * 2,
        [pltpu.VMEM((total, width + LANES), BF16), dma(count)],
        [place, down_weight] + cots,
    )

    pair = (shaped((length, tokens, width), BF16),) * 2

    def expert_scratch():
        return [pltpu.VMEM((total, width), BF16), pltpu.VMEM((total, width), BF16), dma(count)]

    def combined(mine, other):
        blocks = call(
            add_kernel,
            (shaped((tokens, width), BF16),) * length,
            [VMEM] * 2,
            (VMEM,) * length,
            [],
            [mine, swapped(other)],
        )
        return scattered(blocks)

    mine, other = call(
        functools.partial(expert_backward_kernel, count, tokens),
        pair,
        [SMEM, VMEM, VMEM] + [ANY] * count,
        (VMEM,) * 2,
        expert_scratch(),
        [place, up_weight, grad_act] + rows_bwd,
    )
    grad_parts = combined(mine, other)

    mine, other = call(
        functools.partial(expert_forward_kernel, count, tokens),
        pair,
        [SMEM, VMEM, VMEM, VMEM] + [ANY] * count,
        (VMEM,) * 2,
        expert_scratch(),
        [place, up_weight, down_weight, gate_fwd] + rows_fwd,
    )
    moe_parts = combined(mine, other)

    parts = len(grad_parts)
    derivative = call(
        functools.partial(backward_kernel, count, parts, depth),
        shaped((tokens, width), BF16),
        [SMEM] + [VMEM] * (7 + parts) + [ANY] * (2 * count),
        VMEM,
        [
            pltpu.VMEM((width, columns), BF16),
            pltpu.VMEM((width, width), BF16),
            pltpu.VMEM((tokens, columns), BF16),
            dma(count),
            dma(count),
        ],
        [place, stashed_input, cotangent, hidden_bwd, proj_bwd, attention_gain, expert_gain, mask]
        + grad_parts
        + mixers
        + outers,
    )

    layer_output = hidden_fwd
    for part in moe_parts:
        layer_output = layer_output + part.astype(F32)
    return (layer_output.astype(BF16), derivative)


def solution(mesh):
    placed = (
        P(("section", "expert"), None),
        P(("section", "expert"), None),
        P(("section", "expert"), None),
        P("section", None),
        P("section", None),
        P("section", "expert", None),
        P("section", "expert", None),
        P("section", "expert", None, None),
        P("section", "expert", None, None),
        P(None, ("section", "expert"), None),
        P(None, ("section", "expert"), None),
        P(None, ("section", "expert"), None, None),
    )

    return jax.shard_map(
        local,
        mesh=mesh,
        in_specs=placed,
        out_specs=(P(("section", "expert"), None), P(("section", "expert"), None)),
        check_vma=False,
    )
```

profile of v0, /device:TPU:0, one launch (start us, length us, event | category | flops | bytes accessed | tf_op | source)
XLA Modules:
  0.0 267.7 jit_solution(2672836374376782863)
XLA Ops:
  0.6 5.0 %collective-permute-start.14 = (bf16[128,1024]{1,0:T(8,128)(2,1)}, bf16[128,1024]{1,0:T(8,128)(2,1)S(1)}, u32[]{:S(2)}, u32[]{:S(2)}) collective-permute-start(bf16[128,1024]{1,0:T(8,128)(2,1)} %bitcast.35), channel_id=1, source_target_pairs={{0,2},{1,3},{2,4},{3,5},{4,6},{5,7},{8,10},{9,11},{10,12},{11,13},... | collective-permute-start | bytes 786440 | tf_op jit(solution)/shard_map/ppermute | solution.py:66
  5.6 1.3 collective-permute-start.15
  7.0 2.5 collective-permute-start.27
  11.5 1.4 collective-permute-start.16
  12.9 2.6 collective-permute-done.15.refs_22_.refs_7_.refs_27_
  15.5 1.3 collective-permute-start.17
  16.9 5.2 %collective-permute-start.1 = (bf16[128,3072]{1,0:T(8,128)(2,1)}, bf16[128,3072]{1,0:T(8,128)(2,1)S(1)}, u32[]{:S(2)}, u32[]{:S(2)}) collective-permute-start(bf16[128,3072]{1,0:T(8,128)(2,1)} %bitcast.30), channel_id=1, source_target_pairs={{0,2},{1,3},{2,4},{3,5},{4,6},{5,7},{8,10},{9,11},{10,12},{11,13},... | collective-permute-start | bytes 2359304 | tf_op jit(solution)/shard_map/ppermute | solution.py:66
  22.6 1.3 collective-permute-start.2
  24.5 1.6 collective-permute-done.17.refs_24_.refs_9_.refs_29_
  26.1 3.6 %collective-permute-start.28 = (bf16[128,1152]{1,0:T(8,128)(2,1)S(1)}, bf16[128,1152]{1,0:T(8,128)(2,1)S(1)}, u32[]{:S(2)}, u32[]{:S(2)}) collective-permute-start(bf16[128,1152]{1,0:T(8,128)(2,1)S(1)} %fusion.4.refs_2_), channel_id=1, source_target_pairs={{0,2},{1,3},{2,4},{3,5},{4,6},{5,7},{8,10},{9,11},{10,12},{11,13},... | collective-permute-start | bytes 884744 | tf_op jit(solution)/shard_map/ppermute | solution.py:66
  29.8 1.3 collective-permute-start.29
  31.2 13.9 %collective-permute-done.28.refs_3_ = bf16[128,1152]{1,0:T(8,128)(2,1)S(1)} collective-permute-done((bf16[128,1152]{1,0:T(8,128)(2,1)S(1)}, bf16[128,1152]{1,0:T(8,128)(2,1)S(1)}, u32[]{:S(2)}, u32[]{:S(2)}) %collective-permute-start.28) | collective-permute-done | bytes 294944 | tf_op jit(solution)/shard_map/ppermute | solution.py:66
  45.1 5.8 %collective-permute-done.29.refs_4_ = bf16[128,1152]{1,0:T(8,128)(2,1)S(1)} collective-permute-done((bf16[128,1152]{1,0:T(8,128)(2,1)S(1)}, bf16[128,1152]{1,0:T(8,128)(2,1)S(1)}, u32[]{:S(2)}, u32[]{:S(2)}) %collective-permute-start.29) | collective-permute-done | bytes 294944 | tf_op jit(solution)/shard_map/ppermute | solution.py:66
  51.6 1.3 collective-permute-start.19
  53.7 1.3 collective-permute-start.4
  55.1 7.3 %collective-permute-done.19.refs_26_.refs_11_.refs_31_ = bf16[128,1024]{1,0:T(8,128)(2,1)S(1)} collective-permute-done((bf16[128,1024]{1,0:T(8,128)(2,1)}, bf16[128,1024]{1,0:T(8,128)(2,1)S(1)}, u32[]{:S(2)}, u32[]{:S(2)}) %collective-permute-start.19) | collective-permute-done | bytes 262176 | tf_op jit(solution)/shard_map/ppermute | solution.py:66
  63.2 1.0 collective-permute-done.24.refs_31_.refs_16_.refs_36_
  64.2 1.3 collective-permute-start.31
  66.2 1.6 collective-permute-start.5
  67.7 11.7 %collective-permute-done.4.refs_10_.refs_15_ = bf16[128,3072]{1,0:T(8,128)(2,1)} collective-permute-done((bf16[128,3072]{1,0:T(8,128)(2,1)S(1)}, bf16[128,3072]{1,0:T(8,128)(2,1)}, u32[]{:S(2)}, u32[]{:S(2)}) %collective-permute-start.4) | collective-permute-done | bytes 786464 | tf_op jit(solution)/shard_map/ppermute | solution.py:66
  79.4 1.3 collective-permute-start.6
  80.7 3.4 %collective-permute-done.31.refs_6_ = bf16[128,1152]{1,0:T(8,128)(2,1)S(1)} collective-permute-done((bf16[128,1152]{1,0:T(8,128)(2,1)S(1)}, bf16[128,1152]{1,0:T(8,128)(2,1)S(1)}, u32[]{:S(2)}, u32[]{:S(2)}) %collective-permute-start.31) | collective-permute-done | bytes 294944 | tf_op jit(solution)/shard_map/ppermute | solution.py:66
  86.4 1.3 collective-permute-start.33
  87.9 19.9 %collective-permute-done.33.refs_8_ = bf16[128,1152]{1,0:T(8,128)(2,1)S(1)} collective-permute-done((bf16[128,1152]{1,0:T(8,128)(2,1)S(1)}, bf16[128,1152]{1,0:T(8,128)(2,1)S(1)}, u32[]{:S(2)}, u32[]{:S(2)}) %collective-permute-start.33) | collective-permute-done | bytes 294944 | tf_op jit(solution)/shard_map/ppermute | solution.py:66
  110.3 1.8 fusion.refs_5_.refs_4_.refs_7_
  114.4 10.2 %shard_map.131 = (f32[128,3072]{1,0:T(8,128)}, f32[128,3072]{1,0:T(8,128)}, f32[128,1024]{1,0:T(8,128)}, bf16[128,1024]{1,0:T(8,128)(2,1)}) custom-call(s32[2]{0:T(128)} %pad_add_fusion.refs_0_, bf16[128,1024]{1,0:T(8,128)(2,1)} %collective-permute-done.refs_1_, bf16[128,1024]{1,0:T(8,128)(2,1)} %refs_1_.1, f32[1,1024]{1,0:T(1,128)} %refs_5_.1, ...), custom_call_target="tpu_custom_call" | custom-call | tf_op jit(solution)/shard_map/pallas_call | solution.py:361
  124.6 5.2 %shard_map.132 = (f32[128,1024]{1,0:T(8,128)}, bf16[128,1024]{1,0:T(8,128)(2,1)}) custom-call(s32[2]{0:T(128)} %pad_add_fusion.refs_0_, bf16[128,1024]{1,0:T(8,128)(2,1)} %collective-permute-done.refs_1_, f32[128,3072]{1,0:T(8,128)} %get-tuple-element.22.refs_2_, f32[1,1024]{1,0:T(1,128)} %refs_6_.1, f32[2,128,128]{2,1,0:T(8,128)} %fusion.refs_5_.refs_4_.refs_7_, ...), custom_call_target="tpu_custom_call" | custom-call | tf_op jit(solution)/shard_map/pallas_call | solution.py:361
  129.8 1.5 collective-permute-start.41
  131.3 1.3 collective-permute-start.42
  132.9 8.0 %collective-permute-start.61 = (bf16[128,1024]{1,0:T(8,128)(2,1)S(1)}, bf16[128,1024]{1,0:T(8,128)(2,1)S(1)}, u32[]{:S(2)}, u32[]{:S(2)}) collective-permute-start(bf16[128,1024]{1,0:T(8,128)(2,1)S(1)} %copy-done.42), channel_id=1, source_target_pairs={{0,2},{1,3},{2,4},{3,5},{4,6},{5,7},{8,10},{9,11},{10,12},{11,13},... | collective-permute-start | bytes 786440 | tf_op jit(solution)/shard_map/ppermute | solution.py:66
  140.9 1.3 collective-permute-start.62
  142.5 3.1 %collective-permute-done.42.refs_6_ = bf16[128,1024]{1,0:T(8,128)(2,1)S(1)} collective-permute-done((bf16[128,1024]{1,0:T(8,128)(2,1)}, bf16[128,1024]{1,0:T(8,128)(2,1)S(1)}, u32[]{:S(2)}, u32[]{:S(2)}) %collective-permute-start.42) | collective-permute-done | bytes 262176 | tf_op jit(solution)/shard_map/ppermute | solution.py:66
  146.3 1.3 collective-permute-start.44
  147.7 4.4 %collective-permute-done.62.refs_5_ = bf16[128,1024]{1,0:T(8,128)(2,1)} collective-permute-done((bf16[128,1024]{1,0:T(8,128)(2,1)S(1)}, bf16[128,1024]{1,0:T(8,128)(2,1)}, u32[]{:S(2)}, u32[]{:S(2)}) %collective-permute-start.62) | collective-permute-done | bytes 262176 | tf_op jit(solution)/shard_map/ppermute | solution.py:66
  152.0 1.4 collective-permute-start.63
  153.4 1.3 collective-permute-start.64
  154.7 4.4 %collective-permute-done.44.refs_8_ = bf16[128,1024]{1,0:T(8,128)(2,1)S(1)} collective-permute-done((bf16[128,1024]{1,0:T(8,128)(2,1)S(1)}, bf16[128,1024]{1,0:T(8,128)(2,1)S(1)}, u32[]{:S(2)}, u32[]{:S(2)}) %collective-permute-start.44) | collective-permute-done | bytes 262176 | tf_op jit(solution)/shard_map/ppermute | solution.py:66
  159.8 1.3 collective-permute-start.46
  161.6 6.6 %collective-permute-done.64.refs_7_ = bf16[128,1024]{1,0:T(8,128)(2,1)} collective-permute-done((bf16[128,1024]{1,0:T(8,128)(2,1)}, bf16[128,1024]{1,0:T(8,128)(2,1)}, u32[]{:S(2)}, u32[]{:S(2)}) %collective-permute-start.64) | collective-permute-done | bytes 262176 | tf_op jit(solution)/shard_map/ppermute | solution.py:66
  168.3 1.4 collective-permute-start.65
  169.6 1.5 collective-permute-start.66
  171.1 1.9 collective-permute-done.46.refs_10_
  174.9 1.6 copy.25
  176.5 4.0 %collective-permute-done.66.refs_9_ = bf16[128,1024]{1,0:T(8,128)(2,1)} collective-permute-done((bf16[128,1024]{1,0:T(8,128)(2,1)}, bf16[128,1024]{1,0:T(8,128)(2,1)}, u32[]{:S(2)}, u32[]{:S(2)}) %collective-permute-start.66) | collective-permute-done | bytes 262176 | tf_op jit(solution)/shard_map/ppermute | solution.py:66
  181.1 7.2 %shard_map.133 = (f32[1024,704]{1,0:T(8,128)}, f32[1024,128]{1,0:T(8,128)}) custom-call(s32[2]{0:T(128)} %pad_add_fusion.refs_0_, bf16[704,1024]{1,0:T(8,128)(2,1)} %bitcast.28, bf16[128,1152]{1,0:T(8,128)(2,1)} %copy-done.17, bf16[128,1152]{1,0:T(8,128)(2,1)} %copy-done.22, bf16[128,1152]{1,0:T(8,128)(2,1)} %copy-done.23, bf16[128,1152]{1,0:T(8,128)(2,1)} %copy-done.25, ...), custom_call_target="tpu_custom_call" | custom-call | tf_op jit(solution)/shard_map/pallas_call | solution.py:361
  188.5 10.4 %shard_map.134 = (bf16[4,128,1024]{2,1,0:T(8,128)(2,1)}, bf16[4,128,1024]{2,1,0:T(8,128)(2,1)}) custom-call(s32[2]{0:T(128)} %pad_add_fusion.refs_0_, bf16[1024,704]{1,0:T(8,128)(2,1)} %bitcast.26, bf16[704,1024]{1,0:T(8,128)(2,1)} %bitcast.29, f32[1024,128]{1,0:T(8,128)} %get-tuple-element.24.refs_3_, bf16[128,1024]{1,0:T(8,128)(2,1)} %get-tuple-element.25.refs_4_, ...), custom_call_target="tpu_custom_call" | custom-call | tf_op jit(solution)/shard_map/pallas_call | solution.py:361
  200.4 11.5 %shard_map.136 = (bf16[4,128,1024]{2,1,0:T(8,128)(2,1)}, bf16[4,128,1024]{2,1,0:T(8,128)(2,1)}) custom-call(s32[2]{0:T(128)} %pad_add_fusion.refs_0_, bf16[1024,704]{1,0:T(8,128)(2,1)} %bitcast.27, f32[1024,704]{1,0:T(8,128)} %get-tuple-element.34.refs_2_, bf16[128,1024]{1,0:T(8,128)(2,1)} %get-tuple-element.35.refs_3_, bf16[128,1024]{1,0:T(8,128)(2,1)} %copy-done.43, ...), custom_call_target="tpu_custom_call" | custom-call | tf_op jit(solution)/shard_map/pallas_call | solution.py:361
  212.1 1.0 copy-done.19
  213.1 2.6 shard_map.135
  215.6 1.6 collective-permute-start.55
  218.9 2.6 shard_map.137
  222.3 1.3 collective-permute-start.75
  224.7 4.9 %collective-permute-start.56 = (bf16[128,1024]{1,0:T(8,128)(2,1)S(1)}, bf16[128,1024]{1,0:T(8,128)(2,1)S(1)}, u32[]{:S(2)}, u32[]{:S(2)}) collective-permute-start(bf16[128,1024]{1,0:T(8,128)(2,1)S(1)} %get-tuple-element.44), channel_id=1, source_target_pairs={{0,2},{1,3},{2,4},{3,5},{8,10},{9,11},{10,12},{11,13},{16,18},{17,... | collective-permute-start | bytes 786440 | tf_op jit(solution)/shard_map/ppermute | solution.py:66
  229.6 1.0 collective-permute-done.75
  230.6 1.0 fusion.20
  231.7 4.3 %collective-permute-start.76 = (bf16[128,1024]{1,0:T(8,128)(2,1)S(1)}, bf16[128,1024]{1,0:T(8,128)(2,1)S(1)}, u32[]{:S(2)}, u32[]{:S(2)}) collective-permute-start(bf16[128,1024]{1,0:T(8,128)(2,1)S(1)} %get-tuple-element.43), channel_id=1, source_target_pairs={{0,2},{1,3},{2,4},{3,5},{8,10},{9,11},{10,12},{11,13},{16,18},{17,... | collective-permute-start | bytes 786440 | tf_op jit(solution)/shard_map/ppermute | solution.py:66
  236.9 1.3 collective-permute-start.60
  238.3 4.6 %collective-permute-start.57 = (bf16[128,1024]{1,0:T(8,128)(2,1)S(1)}, bf16[128,1024]{1,0:T(8,128)(2,1)S(1)}, u32[]{:S(2)}, u32[]{:S(2)}) collective-permute-start(bf16[128,1024]{1,0:T(8,128)(2,1)S(1)} %add.52), channel_id=1, source_target_pairs={{0,2},{1,3},{2,4},{3,5},{4,6},{5,7},{8,10},{9,11},{10,12},{11,13},... | collective-permute-start | bytes 786440 | tf_op jit(solution)/shard_map/ppermute | solution.py:66
  243.0 3.2 %collective-permute-start.77 = (bf16[128,1024]{1,0:T(8,128)(2,1)S(1)}, bf16[128,1024]{1,0:T(8,128)(2,1)S(1)}, u32[]{:S(2)}, u32[]{:S(2)}) collective-permute-start(bf16[128,1024]{1,0:T(8,128)(2,1)S(1)} %add.58), channel_id=1, source_target_pairs={{0,2},{1,3},{2,4},{3,5},{4,6},{5,7},{8,10},{9,11},{10,12},{11,13},... | collective-permute-start | bytes 786440 | tf_op jit(solution)/shard_map/ppermute | solution.py:66
  246.2 1.3 collective-permute-start.80
  247.6 2.0 collective-permute-done.57
  250.4 2.5 collective-permute-done.77.refs_9_
  252.9 1.9 collective-permute-done.80.refs_10_
  255.5 12.0 %shard_map.138 = bf16[128,1024]{1,0:T(8,128)(2,1)} custom-call(s32[2]{0:T(128)} %pad_add_fusion.refs_0_, bf16[128,1024]{1,0:T(8,128)(2,1)} %refs_1_.1, bf16[128,1024]{1,0:T(8,128)(2,1)} %copy-done.18, f32[128,1024]{1,0:T(8,128)} %get-tuple-element.32.refs_3_, f32[128,3072]{1,0:T(8,128)} %get-tuple-element.33.refs_4_, f32[1,1024]{1,0:T(1,128)} %refs_5_.1, ...), custom_call_target="tpu_custom_call" | custom-call | tf_op jit(solution)/shard_map/pallas_call | solution.py:361
  (237 shorter events, 26.0 us)
Async XLA Ops:
  0.6 10.8 %collective-permute-start.14 = (bf16[128,1024]{1,0:T(8,128)(2,1)}, bf16[128,1024]{1,0:T(8,128)(2,1)S(1)}, u32[]{:S(2)}, u32[]{:S(2)}) collective-permute-start(bf16[128,1024]{1,0:T(8,128)(2,1)} %bitcast.35), channel_id=1, source_target_pairs={{0,2},{1,3},{2,4},{3,5},{4,6},{5,7},{8,10},{9,11},{10,12},{11,13},... | collective-permute-start | bytes 786440 | tf_op jit(solution)/shard_map/ppermute | solution.py:66
  5.6 9.9 %collective-permute-start.15 = (bf16[128,1024]{1,0:T(8,128)(2,1)}, bf16[128,1024]{1,0:T(8,128)(2,1)S(1)}, u32[]{:S(2)}, u32[]{:S(2)}) collective-permute-start(bf16[128,1024]{1,0:T(8,128)(2,1)} %bitcast.36), channel_id=1, source_target_pairs={{2,0},{3,1},{4,2},{5,3},{6,4},{7,5},{10,8},{11,9},{12,10},{13,11},... | collective-permute-start | bytes 786440 | tf_op jit(solution)/shard_map/ppermute | solution.py:66
  6.9 17.0 %collective-permute-start.20 = (bf16[128,1024]{1,0:T(8,128)(2,1)}, bf16[128,1024]{1,0:T(8,128)(2,1)S(1)}, u32[]{:S(2)}, u32[]{:S(2)}) collective-permute-start(bf16[128,1024]{1,0:T(8,128)(2,1)} %bitcast.37), channel_id=1, source_target_pairs={{0,1},{1,0},{2,3},{3,2},{4,5},{5,4},{6,7},{7,6},{8,9},{9,8},{10,11... | collective-permute-start | bytes 786440 | tf_op jit(solution)/shard_map/ppermute | solution.py:62
  7.0 9.9 %collective-permute-start.27 = (bf16[128,1024]{1,0:T(8,128)(2,1)}, bf16[128,1024]{1,0:T(8,128)(2,1)S(1)}, u32[]{:S(2)}, u32[]{:S(2)}) collective-permute-start(bf16[128,1024]{1,0:T(8,128)(2,1)} %param.14), channel_id=1, source_target_pairs={{0,24},{8,0},{16,8},{24,16},{1,25},{9,1},{17,9},{25,17},{2,26},{10... | collective-permute-start | bytes 786440 | tf_op jit(solution)/shard_map/ppermute | solution.py:45
  9.5 13.1 %collective-permute-start = (bf16[128,1024]{1,0:T(8,128)(2,1)}, bf16[128,1024]{1,0:T(8,128)(2,1)}, u32[]{:S(2)}, u32[]{:S(2)}) collective-permute-start(bf16[128,1024]{1,0:T(8,128)(2,1)} %param.12), channel_id=1, source_target_pairs={{0,8},{8,16},{16,24},{24,0},{1,9},{9,17},{17,25},{25,1},{2,10},{10... | collective-permute-start | bytes 786440 | tf_op jit(solution)/shard_map/ppermute | solution.py:45
  11.5 12.5 %collective-permute-start.16 = (bf16[128,1024]{1,0:T(8,128)(2,1)S(1)}, bf16[128,1024]{1,0:T(8,128)(2,1)}, u32[]{:S(2)}, u32[]{:S(2)}) collective-permute-start(bf16[128,1024]{1,0:T(8,128)(2,1)S(1)} %collective-permute-done.14.refs_21_.refs_6_.refs_26_), channel_id=1, source_target_pairs={{2,4},{3,5},{4,6},{5,7},{10,12},{11,13},{12,14},{13,15},{18,20},{1... | collective-permute-start | bytes 786440 | tf_op jit(solution)/shard_map/ppermute | solution.py:66
  15.5 10.6 %collective-permute-start.17 = (bf16[128,1024]{1,0:T(8,128)(2,1)S(1)}, bf16[128,1024]{1,0:T(8,128)(2,1)}, u32[]{:S(2)}, u32[]{:S(2)}) collective-permute-start(bf16[128,1024]{1,0:T(8,128)(2,1)S(1)} %collective-permute-done.15.refs_22_.refs_7_.refs_27_), channel_id=1, source_target_pairs={{2,0},{3,1},{4,2},{5,3},{10,8},{11,9},{12,10},{13,11},{18,16},{19,... | collective-permute-start | bytes 786440 | tf_op jit(solution)/shard_map/ppermute | solution.py:66
  16.9 36.0 %collective-permute-start.1 = (bf16[128,3072]{1,0:T(8,128)(2,1)}, bf16[128,3072]{1,0:T(8,128)(2,1)S(1)}, u32[]{:S(2)}, u32[]{:S(2)}) collective-permute-start(bf16[128,3072]{1,0:T(8,128)(2,1)} %bitcast.30), channel_id=1, source_target_pairs={{0,2},{1,3},{2,4},{3,5},{4,6},{5,7},{8,10},{9,11},{10,12},{11,13},... | collective-permute-start | bytes 2359304 | tf_op jit(solution)/shard_map/ppermute | solution.py:66
  22.6 31.1 %collective-permute-start.2 = (bf16[128,3072]{1,0:T(8,128)(2,1)}, bf16[128,3072]{1,0:T(8,128)(2,1)S(1)}, u32[]{:S(2)}, u32[]{:S(2)}) collective-permute-start(bf16[128,3072]{1,0:T(8,128)(2,1)} %bitcast.31), channel_id=1, source_target_pairs={{2,0},{3,1},{4,2},{5,3},{6,4},{7,5},{10,8},{11,9},{12,10},{13,11},... | collective-permute-start | bytes 2359304 | tf_op jit(solution)/shard_map/ppermute | solution.py:66
  26.1 19.0 %collective-permute-start.28 = (bf16[128,1152]{1,0:T(8,128)(2,1)S(1)}, bf16[128,1152]{1,0:T(8,128)(2,1)S(1)}, u32[]{:S(2)}, u32[]{:S(2)}) collective-permute-start(bf16[128,1152]{1,0:T(8,128)(2,1)S(1)} %fusion.4.refs_2_), channel_id=1, source_target_pairs={{0,2},{1,3},{2,4},{3,5},{4,6},{5,7},{8,10},{9,11},{10,12},{11,13},... | collective-permute-start | bytes 884744 | tf_op jit(solution)/shard_map/ppermute | solution.py:66
  29.8 21.2 %collective-permute-start.29 = (bf16[128,1152]{1,0:T(8,128)(2,1)S(1)}, bf16[128,1152]{1,0:T(8,128)(2,1)S(1)}, u32[]{:S(2)}, u32[]{:S(2)}) collective-permute-start(bf16[128,1152]{1,0:T(8,128)(2,1)S(1)} %fusion.4.refs_2_), channel_id=1, source_target_pairs={{2,0},{3,1},{4,2},{5,3},{6,4},{7,5},{10,8},{11,9},{12,10},{13,11},... | collective-permute-start | bytes 884744 | tf_op jit(solution)/shard_map/ppermute | solution.py:66
  31.1 20.5 %collective-permute-start.34 = (bf16[128,1152]{1,0:T(8,128)(2,1)S(1)}, bf16[128,1152]{1,0:T(8,128)(2,1)S(1)}, u32[]{:S(2)}, u32[]{:S(2)}) collective-permute-start(bf16[128,1152]{1,0:T(8,128)(2,1)S(1)} %fusion.4.refs_2_), channel_id=1, source_target_pairs={{0,1},{1,0},{2,3},{3,2},{4,5},{5,4},{6,7},{7,6},{8,9},{9,8},{10,11... | collective-permute-start | bytes 884744 | tf_op jit(solution)/shard_map/ppermute | solution.py:62
  45.1 20.4 %collective-permute-start.7 = (bf16[128,3072]{1,0:T(8,128)(2,1)}, bf16[128,3072]{1,0:T(8,128)(2,1)S(1)}, u32[]{:S(2)}, u32[]{:S(2)}) collective-permute-start(bf16[128,3072]{1,0:T(8,128)(2,1)} %bitcast.32), channel_id=1, source_target_pairs={{0,1},{1,0},{2,3},{3,2},{4,5},{5,4},{6,7},{7,6},{8,9},{9,8},{10,11... | collective-permute-start | bytes 2359304 | tf_op jit(solution)/shard_map/ppermute | solution.py:62
  51.6 10.8 %collective-permute-start.19 = (bf16[128,1024]{1,0:T(8,128)(2,1)}, bf16[128,1024]{1,0:T(8,128)(2,1)S(1)}, u32[]{:S(2)}, u32[]{:S(2)}) collective-permute-start(bf16[128,1024]{1,0:T(8,128)(2,1)} %collective-permute-done.17.refs_24_.refs_9_.refs_29_), channel_id=1, source_target_pairs={{2,0},{3,1},{10,8},{11,9},{18,16},{19,17},{26,24},{27,25}} | collective-permute-start | bytes 786440 | tf_op jit(solution)/shard_map/ppermute | solution.py:66
  53.0 13.2 %collective-permute-start.3 = (bf16[128,3072]{1,0:T(8,128)(2,1)S(1)}, bf16[128,3072]{1,0:T(8,128)(2,1)S(1)}, u32[]{:S(2)}, u32[]{:S(2)}) collective-permute-start(bf16[128,3072]{1,0:T(8,128)(2,1)S(1)} %collective-permute-done.1.refs_7_.refs_12_), channel_id=1, source_target_pairs={{2,4},{3,5},{4,6},{5,7},{10,12},{11,13},{12,14},{13,15},{18,20},{1... | collective-permute-start | bytes 2359304 | tf_op jit(solution)/shard_map/ppermute | solution.py:66
  53.7 25.7 %collective-permute-start.4 = (bf16[128,3072]{1,0:T(8,128)(2,1)S(1)}, bf16[128,3072]{1,0:T(8,128)(2,1)}, u32[]{:S(2)}, u32[]{:S(2)}) collective-permute-start(bf16[128,3072]{1,0:T(8,128)(2,1)S(1)} %collective-permute-done.2.refs_8_.refs_13_), channel_id=1, source_target_pairs={{2,0},{3,1},{4,2},{5,3},{10,8},{11,9},{12,10},{13,11},{18,16},{19,... | collective-permute-start | bytes 2359304 | tf_op jit(solution)/shard_map/ppermute | solution.py:66
  64.2 19.9 %collective-permute-start.31 = (bf16[128,1152]{1,0:T(8,128)(2,1)S(1)}, bf16[128,1152]{1,0:T(8,128)(2,1)S(1)}, u32[]{:S(2)}, u32[]{:S(2)}) collective-permute-start(bf16[128,1152]{1,0:T(8,128)(2,1)S(1)} %collective-permute-done.29.refs_4_), channel_id=1, source_target_pairs={{2,0},{3,1},{4,2},{5,3},{10,8},{11,9},{12,10},{13,11},{18,16},{19,... | collective-permute-start | bytes 884744 | tf_op jit(solution)/shard_map/ppermute | solution.py:66
  65.5 18.6 %collective-permute-start.35 = (bf16[128,1152]{1,0:T(8,128)(2,1)S(1)}, bf16[128,1152]{1,0:T(8,128)(2,1)S(1)}, u32[]{:S(2)}, u32[]{:S(2)}) collective-permute-start(bf16[128,1152]{1,0:T(8,128)(2,1)S(1)} %collective-permute-done.28.refs_3_), channel_id=1, source_target_pairs={{0,1},{1,0},{2,3},{3,2},{4,5},{5,4},{6,7},{7,6},{8,9},{9,8},{10,11... | collective-permute-start | bytes 884744 | tf_op jit(solution)/shard_map/ppermute | solution.py:62
  65.7 42.1 %collective-permute-start.8 = (bf16[128,3072]{1,0:T(8,128)(2,1)S(1)}, bf16[128,3072]{1,0:T(8,128)(2,1)S(1)}, u32[]{:S(2)}, u32[]{:S(2)}) collective-permute-start(bf16[128,3072]{1,0:T(8,128)(2,1)S(1)} %collective-permute-done.1.refs_7_.refs_12_), channel_id=1, source_target_pairs={{0,1},{1,0},{2,3},{3,2},{4,5},{5,4},{6,7},{7,6},{8,9},{9,8},{10,11... | collective-permute-start | bytes 2359304 | tf_op jit(solution)/shard_map/ppermute | solution.py:62
  66.2 42.1 %collective-permute-start.5 = (bf16[128,3072]{1,0:T(8,128)(2,1)S(1)}, bf16[128,3072]{1,0:T(8,128)(2,1)}, u32[]{:S(2)}, u32[]{:S(2)}) collective-permute-start(bf16[128,3072]{1,0:T(8,128)(2,1)S(1)} %collective-permute-done.3.refs_9_.refs_14_), channel_id=1, source_target_pairs={{4,6},{5,7},{12,14},{13,15},{20,22},{21,23},{28,30},{29,31}} | collective-permute-start | bytes 2359304 | tf_op jit(solution)/shard_map/ppermute | solution.py:66
  79.4 29.8 %collective-permute-start.6 = (bf16[128,3072]{1,0:T(8,128)(2,1)}, bf16[128,3072]{1,0:T(8,128)(2,1)}, u32[]{:S(2)}, u32[]{:S(2)}) collective-permute-start(bf16[128,3072]{1,0:T(8,128)(2,1)} %collective-permute-done.4.refs_10_.refs_15_), channel_id=1, source_target_pairs={{2,0},{3,1},{10,8},{11,9},{18,16},{19,17},{26,24},{27,25}} | collective-permute-start | bytes 2359304 | tf_op jit(solution)/shard_map/ppermute | solution.py:66
  86.4 21.4 %collective-permute-start.33 = (bf16[128,1152]{1,0:T(8,128)(2,1)S(1)}, bf16[128,1152]{1,0:T(8,128)(2,1)S(1)}, u32[]{:S(2)}, u32[]{:S(2)}) collective-permute-start(bf16[128,1152]{1,0:T(8,128)(2,1)S(1)} %collective-permute-done.31.refs_6_), channel_id=1, source_target_pairs={{2,0},{3,1},{10,8},{11,9},{18,16},{19,17},{26,24},{27,25}} | collective-permute-start | bytes 884744 | tf_op jit(solution)/shard_map/ppermute | solution.py:66
  87.7 21.7 %collective-permute-start.9 = (bf16[128,3072]{1,0:T(8,128)(2,1)S(1)}, bf16[128,3072]{1,0:T(8,128)(2,1)}, u32[]{:S(2)}, u32[]{:S(2)}) collective-permute-start(bf16[128,3072]{1,0:T(8,128)(2,1)S(1)} %collective-permute-done.2.refs_8_.refs_13_), channel_id=1, source_target_pairs={{0,1},{1,0},{2,3},{3,2},{4,5},{5,4},{6,7},{7,6},{8,9},{9,8},{10,11... | collective-permute-start | bytes 2359304 | tf_op jit(solution)/shard_map/ppermute | solution.py:62
  109.4 20.4 %collective-permute-start.36 = (bf16[128,1152]{1,0:T(8,128)(2,1)}, bf16[128,1152]{1,0:T(8,128)(2,1)}, u32[]{:S(2)}, u32[]{:S(2)}) collective-permute-start(bf16[128,1152]{1,0:T(8,128)(2,1)} %copy-done.23), channel_id=1, source_target_pairs={{0,1},{1,0},{2,3},{3,2},{4,5},{5,4},{6,7},{7,6},{8,9},{9,8},{10,11... | collective-permute-start | bytes 884744 | tf_op jit(solution)/shard_map/ppermute | solution.py:62
  110.2 21.1 %collective-permute-start.37 = (bf16[128,1152]{1,0:T(8,128)(2,1)}, bf16[128,1152]{1,0:T(8,128)(2,1)}, u32[]{:S(2)}, u32[]{:S(2)}) collective-permute-start(bf16[128,1152]{1,0:T(8,128)(2,1)} %copy-done.25), channel_id=1, source_target_pairs={{0,1},{1,0},{2,3},{3,2},{4,5},{5,4},{6,7},{7,6},{8,9},{9,8},{10,11... | collective-permute-start | bytes 884744 | tf_op jit(solution)/shard_map/ppermute | solution.py:62
  112.1 20.5 %collective-permute-start.38 = (bf16[128,1152]{1,0:T(8,128)(2,1)}, bf16[128,1152]{1,0:T(8,128)(2,1)}, u32[]{:S(2)}, u32[]{:S(2)}) collective-permute-start(bf16[128,1152]{1,0:T(8,128)(2,1)} %copy-done.26), channel_id=1, source_target_pairs={{0,1},{1,0},{2,3},{3,2},{4,5},{5,4},{6,7},{7,6},{8,9},{9,8},{10,11... | collective-permute-start | bytes 884744 | tf_op jit(solution)/shard_map/ppermute | solution.py:62
  112.5 20.4 %collective-permute-start.39 = (bf16[128,1152]{1,0:T(8,128)(2,1)}, bf16[128,1152]{1,0:T(8,128)(2,1)}, u32[]{:S(2)}, u32[]{:S(2)}) collective-permute-start(bf16[128,1152]{1,0:T(8,128)(2,1)} %copy-done.28), channel_id=1, source_target_pairs={{0,1},{1,0},{2,3},{3,2},{4,5},{5,4},{6,7},{7,6},{8,9},{9,8},{10,11... | collective-permute-start | bytes 884744 | tf_op jit(solution)/shard_map/ppermute | solution.py:62
  113.6 27.4 %collective-permute-start.40 = (bf16[128,1152]{1,0:T(8,128)(2,1)}, bf16[128,1152]{1,0:T(8,128)(2,1)}, u32[]{:S(2)}, u32[]{:S(2)}) collective-permute-start(bf16[128,1152]{1,0:T(8,128)(2,1)} %copy-done.29), channel_id=1, source_target_pairs={{0,1},{1,0},{2,3},{3,2},{4,5},{5,4},{6,7},{7,6},{8,9},{9,8},{10,11... | collective-permute-start | bytes 884744 | tf_op jit(solution)/shard_map/ppermute | solution.py:62
  129.8 12.4 %collective-permute-start.41 = (bf16[128,1024]{1,0:T(8,128)(2,1)}, bf16[128,1024]{1,0:T(8,128)(2,1)S(1)}, u32[]{:S(2)}, u32[]{:S(2)}) collective-permute-start(bf16[128,1024]{1,0:T(8,128)(2,1)} %get-tuple-element.25.refs_4_), channel_id=1, source_target_pairs={{0,2},{1,3},{2,4},{3,5},{4,6},{5,7},{8,10},{9,11},{10,12},{11,13},... | collective-permute-start | bytes 786440 | tf_op jit(solution)/shard_map/ppermute | solution.py:66
  131.3 14.3 %collective-permute-start.42 = (bf16[128,1024]{1,0:T(8,128)(2,1)}, bf16[128,1024]{1,0:T(8,128)(2,1)S(1)}, u32[]{:S(2)}, u32[]{:S(2)}) collective-permute-start(bf16[128,1024]{1,0:T(8,128)(2,1)} %get-tuple-element.25.refs_4_), channel_id=1, source_target_pairs={{2,0},{3,1},{4,2},{5,3},{6,4},{7,5},{10,8},{11,9},{12,10},{13,11},... | collective-permute-start | bytes 786440 | tf_op jit(solution)/shard_map/ppermute | solution.py:66
  132.6 13.6 %collective-permute-start.47 = (bf16[128,1024]{1,0:T(8,128)(2,1)}, bf16[128,1024]{1,0:T(8,128)(2,1)S(1)}, u32[]{:S(2)}, u32[]{:S(2)}) collective-permute-start(bf16[128,1024]{1,0:T(8,128)(2,1)} %get-tuple-element.25.refs_4_), channel_id=1, source_target_pairs={{0,1},{1,0},{2,3},{3,2},{4,5},{5,4},{6,7},{7,6},{8,9},{9,8},{10,11... | collective-permute-start | bytes 786440 | tf_op jit(solution)/shard_map/ppermute | solution.py:62
  132.9 14.7 %collective-permute-start.61 = (bf16[128,1024]{1,0:T(8,128)(2,1)S(1)}, bf16[128,1024]{1,0:T(8,128)(2,1)S(1)}, u32[]{:S(2)}, u32[]{:S(2)}) collective-permute-start(bf16[128,1024]{1,0:T(8,128)(2,1)S(1)} %copy-done.42), channel_id=1, source_target_pairs={{0,2},{1,3},{2,4},{3,5},{4,6},{5,7},{8,10},{9,11},{10,12},{11,13},... | collective-permute-start | bytes 786440 | tf_op jit(solution)/shard_map/ppermute | solution.py:66
  140.9 11.1 %collective-permute-start.62 = (bf16[128,1024]{1,0:T(8,128)(2,1)S(1)}, bf16[128,1024]{1,0:T(8,128)(2,1)}, u32[]{:S(2)}, u32[]{:S(2)}) collective-permute-start(bf16[128,1024]{1,0:T(8,128)(2,1)S(1)} %copy-done.42), channel_id=1, source_target_pairs={{2,0},{3,1},{4,2},{5,3},{6,4},{7,5},{10,8},{11,9},{12,10},{13,11},... | collective-permute-start | bytes 786440 | tf_op jit(solution)/shard_map/ppermute | solution.py:66
  142.3 9.8 %collective-permute-start.67 = (bf16[128,1024]{1,0:T(8,128)(2,1)S(1)}, bf16[128,1024]{1,0:T(8,128)(2,1)S(1)}, u32[]{:S(2)}, u32[]{:S(2)}) collective-permute-start(bf16[128,1024]{1,0:T(8,128)(2,1)S(1)} %copy-done.42), channel_id=1, source_target_pairs={{0,1},{1,0},{2,3},{3,2},{4,5},{5,4},{6,7},{7,6},{8,9},{9,8},{10,11... | collective-permute-start | bytes 786440 | tf_op jit(solution)/shard_map/ppermute | solution.py:62
  145.6 7.8 %collective-permute-start.43 = (bf16[128,1024]{1,0:T(8,128)(2,1)S(1)}, bf16[128,1024]{1,0:T(8,128)(2,1)S(1)}, u32[]{:S(2)}, u32[]{:S(2)}) collective-permute-start(bf16[128,1024]{1,0:T(8,128)(2,1)S(1)} %collective-permute-done.41.refs_5_), channel_id=1, source_target_pairs={{2,4},{3,5},{4,6},{5,7},{10,12},{11,13},{12,14},{13,15},{18,20},{1... | collective-permute-start | bytes 786440 | tf_op jit(solution)/shard_map/ppermute | solution.py:66
  146.3 12.8 %collective-permute-start.44 = (bf16[128,1024]{1,0:T(8,128)(2,1)S(1)}, bf16[128,1024]{1,0:T(8,128)(2,1)S(1)}, u32[]{:S(2)}, u32[]{:S(2)}) collective-permute-start(bf16[128,1024]{1,0:T(8,128)(2,1)S(1)} %collective-permute-done.42.refs_6_), channel_id=1, source_target_pairs={{2,0},{3,1},{4,2},{5,3},{10,8},{11,9},{12,10},{13,11},{18,16},{19,... | collective-permute-start | bytes 786440 | tf_op jit(solution)/shard_map/ppermute | solution.py:66
  147.6 11.5 %collective-permute-start.48 = (bf16[128,1024]{1,0:T(8,128)(2,1)S(1)}, bf16[128,1024]{1,0:T(8,128)(2,1)S(1)}, u32[]{:S(2)}, u32[]{:S(2)}) collective-permute-start(bf16[128,1024]{1,0:T(8,128)(2,1)S(1)} %collective-permute-done.41.refs_5_), channel_id=1, source_target_pairs={{0,1},{1,0},{2,3},{3,2},{4,5},{5,4},{6,7},{7,6},{8,9},{9,8},{10,11... | collective-permute-start | bytes 786440 | tf_op jit(solution)/shard_map/ppermute | solution.py:62
  152.0 7.7 %collective-permute-start.49 = (bf16[128,1024]{1,0:T(8,128)(2,1)S(1)}, bf16[128,1024]{1,0:T(8,128)(2,1)S(1)}, u32[]{:S(2)}, u32[]{:S(2)}) collective-permute-start(bf16[128,1024]{1,0:T(8,128)(2,1)S(1)} %collective-permute-done.42.refs_6_), channel_id=1, source_target_pairs={{0,1},{1,0},{2,3},{3,2},{4,5},{5,4},{6,7},{7,6},{8,9},{9,8},{10,11... | collective-permute-start | bytes 786440 | tf_op jit(solution)/shard_map/ppermute | solution.py:62
  152.0 9.0 %collective-permute-start.63 = (bf16[128,1024]{1,0:T(8,128)(2,1)S(1)}, bf16[128,1024]{1,0:T(8,128)(2,1)}, u32[]{:S(2)}, u32[]{:S(2)}) collective-permute-start(bf16[128,1024]{1,0:T(8,128)(2,1)S(1)} %collective-permute-done.61.refs_4_), channel_id=1, source_target_pairs={{2,4},{3,5},{4,6},{5,7},{10,12},{11,13},{12,14},{13,15},{18,20},{1... | collective-permute-start | bytes 786440 | tf_op jit(solution)/shard_map/ppermute | solution.py:66
  153.4 14.9 %collective-permute-start.64 = (bf16[128,1024]{1,0:T(8,128)(2,1)}, bf16[128,1024]{1,0:T(8,128)(2,1)}, u32[]{:S(2)}, u32[]{:S(2)}) collective-permute-start(bf16[128,1024]{1,0:T(8,128)(2,1)} %collective-permute-done.62.refs_5_), channel_id=1, source_target_pairs={{2,0},{3,1},{4,2},{5,3},{10,8},{11,9},{12,10},{13,11},{18,16},{19,... | collective-permute-start | bytes 786440 | tf_op jit(solution)/shard_map/ppermute | solution.py:66
  159.1 9.2 %collective-permute-start.68 = (bf16[128,1024]{1,0:T(8,128)(2,1)S(1)}, bf16[128,1024]{1,0:T(8,128)(2,1)S(1)}, u32[]{:S(2)}, u32[]{:S(2)}) collective-permute-start(bf16[128,1024]{1,0:T(8,128)(2,1)S(1)} %collective-permute-done.61.refs_4_), channel_id=1, source_target_pairs={{0,1},{1,0},{2,3},{3,2},{4,5},{5,4},{6,7},{7,6},{8,9},{9,8},{10,11... | collective-permute-start | bytes 786440 | tf_op jit(solution)/shard_map/ppermute | solution.py:62
  159.1 10.6 %collective-permute-start.45 = (bf16[128,1024]{1,0:T(8,128)(2,1)S(1)}, bf16[128,1024]{1,0:T(8,128)(2,1)S(1)}, u32[]{:S(2)}, u32[]{:S(2)}) collective-permute-start(bf16[128,1024]{1,0:T(8,128)(2,1)S(1)} %collective-permute-done.43.refs_7_), channel_id=1, source_target_pairs={{4,6},{5,7},{12,14},{13,15},{20,22},{21,23},{28,30},{29,31}} | collective-permute-start | bytes 786440 | tf_op jit(solution)/shard_map/ppermute | solution.py:66
  159.8 13.2 %collective-permute-start.46 = (bf16[128,1024]{1,0:T(8,128)(2,1)S(1)}, bf16[128,1024]{1,0:T(8,128)(2,1)}, u32[]{:S(2)}, u32[]{:S(2)}) collective-permute-start(bf16[128,1024]{1,0:T(8,128)(2,1)S(1)} %collective-permute-done.44.refs_8_), channel_id=1, source_target_pairs={{2,0},{3,1},{10,8},{11,9},{18,16},{19,17},{26,24},{27,25}} | collective-permute-start | bytes 786440 | tf_op jit(solution)/shard_map/ppermute | solution.py:66
  161.1 11.9 %collective-permute-start.50 = (bf16[128,1024]{1,0:T(8,128)(2,1)S(1)}, bf16[128,1024]{1,0:T(8,128)(2,1)S(1)}, u32[]{:S(2)}, u32[]{:S(2)}) collective-permute-start(bf16[128,1024]{1,0:T(8,128)(2,1)S(1)} %collective-permute-done.43.refs_7_), channel_id=1, source_target_pairs={{0,1},{1,0},{2,3},{3,2},{4,5},{5,4},{6,7},{7,6},{8,9},{9,8},{10,11... | collective-permute-start | bytes 786440 | tf_op jit(solution)/shard_map/ppermute | solution.py:62
  168.3 8.2 %collective-permute-start.65 = (bf16[128,1024]{1,0:T(8,128)(2,1)}, bf16[128,1024]{1,0:T(8,128)(2,1)}, u32[]{:S(2)}, u32[]{:S(2)}) collective-permute-start(bf16[128,1024]{1,0:T(8,128)(2,1)} %collective-permute-done.63.refs_6_), channel_id=1, source_target_pairs={{4,6},{5,7},{12,14},{13,15},{20,22},{21,23},{28,30},{29,31}} | collective-permute-start | bytes 786440 | tf_op jit(solution)/shard_map/ppermute | solution.py:66
  169.6 10.9 %collective-permute-start.66 = (bf16[128,1024]{1,0:T(8,128)(2,1)}, bf16[128,1024]{1,0:T(8,128)(2,1)}, u32[]{:S(2)}, u32[]{:S(2)}) collective-permute-start(bf16[128,1024]{1,0:T(8,128)(2,1)} %collective-permute-done.64.refs_7_), channel_id=1, source_target_pairs={{2,0},{3,1},{10,8},{11,9},{18,16},{19,17},{26,24},{27,25}} | collective-permute-start | bytes 786440 | tf_op jit(solution)/shard_map/ppermute | solution.py:66
  173.0 8.1 %collective-permute-start.53 = (bf16[128,1024]{1,0:T(8,128)(2,1)}, bf16[128,1024]{1,0:T(8,128)(2,1)}, u32[]{:S(2)}, u32[]{:S(2)}) collective-permute-start(bf16[128,1024]{1,0:T(8,128)(2,1)} %collective-permute-done.46.refs_10_), channel_id=1, source_target_pairs={{0,1},{1,0},{2,3},{3,2},{4,5},{5,4},{6,7},{7,6},{8,9},{9,8},{10,11... | collective-permute-start | bytes 786440 | tf_op jit(solution)/shard_map/ppermute | solution.py:62
  174.4 24.5 %collective-permute-start.69 = (bf16[128,1024]{1,0:T(8,128)(2,1)}, bf16[128,1024]{1,0:T(8,128)(2,1)}, u32[]{:S(2)}, u32[]{:S(2)}) collective-permute-start(bf16[128,1024]{1,0:T(8,128)(2,1)} %collective-permute-done.62.refs_5_), channel_id=1, source_target_pairs={{0,1},{1,0},{2,3},{3,2},{4,5},{5,4},{6,7},{7,6},{8,9},{9,8},{10,11... | collective-permute-start | bytes 786440 | tf_op jit(solution)/shard_map/ppermute | solution.py:62
  176.5 22.9 %collective-permute-start.70 = (bf16[128,1024]{1,0:T(8,128)(2,1)}, bf16[128,1024]{1,0:T(8,128)(2,1)S(1)}, u32[]{:S(2)}, u32[]{:S(2)}) collective-permute-start(bf16[128,1024]{1,0:T(8,128)(2,1)} %collective-permute-done.63.refs_6_), channel_id=1, source_target_pairs={{0,1},{1,0},{2,3},{3,2},{4,5},{5,4},{6,7},{7,6},{8,9},{9,8},{10,11... | collective-permute-start | bytes 786440 | tf_op jit(solution)/shard_map/ppermute | solution.py:62
  180.5 18.9 %collective-permute-start.71 = (bf16[128,1024]{1,0:T(8,128)(2,1)}, bf16[128,1024]{1,0:T(8,128)(2,1)S(1)}, u32[]{:S(2)}, u32[]{:S(2)}) collective-permute-start(bf16[128,1024]{1,0:T(8,128)(2,1)} %collective-permute-done.64.refs_7_), channel_id=1, source_target_pairs={{0,1},{1,0},{2,3},{3,2},{4,5},{5,4},{6,7},{7,6},{8,9},{9,8},{10,11... | collective-permute-start | bytes 786440 | tf_op jit(solution)/shard_map/ppermute | solution.py:62
  180.6 18.9 %collective-permute-start.72 = (bf16[128,1024]{1,0:T(8,128)(2,1)}, bf16[128,1024]{1,0:T(8,128)(2,1)S(1)}, u32[]{:S(2)}, u32[]{:S(2)}) collective-permute-start(bf16[128,1024]{1,0:T(8,128)(2,1)} %collective-permute-done.65.refs_8_), channel_id=1, source_target_pairs={{0,1},{1,0},{2,3},{3,2},{4,5},{5,4},{6,7},{7,6},{8,9},{9,8},{10,11... | collective-permute-start | bytes 786440 | tf_op jit(solution)/shard_map/ppermute | solution.py:62
  181.1 18.4 %collective-permute-start.73 = (bf16[128,1024]{1,0:T(8,128)(2,1)}, bf16[128,1024]{1,0:T(8,128)(2,1)S(1)}, u32[]{:S(2)}, u32[]{:S(2)}) collective-permute-start(bf16[128,1024]{1,0:T(8,128)(2,1)} %collective-permute-done.66.refs_9_), channel_id=1, source_target_pairs={{0,1},{1,0},{2,3},{3,2},{4,5},{5,4},{6,7},{7,6},{8,9},{9,8},{10,11... | collective-permute-start | bytes 786440 | tf_op jit(solution)/shard_map/ppermute | solution.py:62
  198.9 13.2 %collective-permute-start.54 = (bf16[4,128,1024]{2,1,0:T(8,128)(2,1)}, bf16[4,128,1024]{2,1,0:T(8,128)(2,1)S(1)}, u32[]{:S(2)}, u32[]{:S(2)}) collective-permute-start(bf16[4,128,1024]{2,1,0:T(8,128)(2,1)} %get-tuple-element.27), channel_id=1, source_target_pairs={{0,1},{1,0},{2,3},{3,2},{4,5},{5,4},{6,7},{7,6},{8,9},{9,8},{10,11... | collective-permute-start | bytes 3145736 | tf_op jit(solution)/shard_map/ppermute | solution.py:62
  215.6 8.2 %collective-permute-start.55 = (bf16[128,1024]{1,0:T(8,128)(2,1)}, bf16[128,1024]{1,0:T(8,128)(2,1)S(1)}, u32[]{:S(2)}, u32[]{:S(2)}) collective-permute-start(bf16[128,1024]{1,0:T(8,128)(2,1)} %get-tuple-element.31), channel_id=1, source_target_pairs={{0,2},{1,3},{8,10},{9,11},{16,18},{17,19},{24,26},{25,27}} | collective-permute-start | bytes 786440 | tf_op jit(solution)/shard_map/ppermute | solution.py:66
  221.5 8.1 %collective-permute-start.78 = (bf16[128,1024]{1,0:T(8,128)(2,1)}, bf16[128,1024]{1,0:T(8,128)(2,1)S(1)}, u32[]{:S(2)}, u32[]{:S(2)}) collective-permute-start(bf16[128,1024]{1,0:T(8,128)(2,1)} %get-tuple-element.39), channel_id=1, source_target_pairs={{6,4},{7,5},{14,12},{15,13},{22,20},{23,21},{30,28},{31,29}} | collective-permute-start | bytes 786440 | tf_op jit(solution)/shard_map/ppermute | solution.py:66
  222.3 8.3 %collective-permute-start.75 = (bf16[128,1024]{1,0:T(8,128)(2,1)}, bf16[128,1024]{1,0:T(8,128)(2,1)S(1)}, u32[]{:S(2)}, u32[]{:S(2)}) collective-permute-start(bf16[128,1024]{1,0:T(8,128)(2,1)} %get-tuple-element.41), channel_id=1, source_target_pairs={{0,2},{1,3},{8,10},{9,11},{16,18},{17,19},{24,26},{25,27}} | collective-permute-start | bytes 786440 | tf_op jit(solution)/shard_map/ppermute | solution.py:66
  223.9 13.0 %collective-permute-start.59 = (bf16[128,1024]{1,0:T(8,128)(2,1)S(1)}, bf16[128,1024]{1,0:T(8,128)(2,1)S(1)}, u32[]{:S(2)}, u32[]{:S(2)}) collective-permute-start(bf16[128,1024]{1,0:T(8,128)(2,1)S(1)} %get-tuple-element.45), channel_id=1, source_target_pairs={{4,2},{5,3},{6,4},{7,5},{12,10},{13,11},{14,12},{15,13},{20,18},{2... | collective-permute-start | bytes 786440 | tf_op jit(solution)/shard_map/ppermute | solution.py:66
  224.7 13.5 %collective-permute-start.56 = (bf16[128,1024]{1,0:T(8,128)(2,1)S(1)}, bf16[128,1024]{1,0:T(8,128)(2,1)S(1)}, u32[]{:S(2)}, u32[]{:S(2)}) collective-permute-start(bf16[128,1024]{1,0:T(8,128)(2,1)S(1)} %get-tuple-element.44), channel_id=1, source_target_pairs={{0,2},{1,3},{2,4},{3,5},{8,10},{9,11},{10,12},{11,13},{16,18},{17,... | collective-permute-start | bytes 786440 | tf_op jit(solution)/shard_map/ppermute | solution.py:66
  231.7 11.2 %collective-permute-start.76 = (bf16[128,1024]{1,0:T(8,128)(2,1)S(1)}, bf16[128,1024]{1,0:T(8,128)(2,1)S(1)}, u32[]{:S(2)}, u32[]{:S(2)}) collective-permute-start(bf16[128,1024]{1,0:T(8,128)(2,1)S(1)} %get-tuple-element.43), channel_id=1, source_target_pairs={{0,2},{1,3},{2,4},{3,5},{8,10},{9,11},{10,12},{11,13},{16,18},{17,... | collective-permute-start | bytes 786440 | tf_op jit(solution)/shard_map/ppermute | solution.py:66
  236.0 10.1 %collective-permute-start.79 = (bf16[128,1024]{1,0:T(8,128)(2,1)S(1)}, bf16[128,1024]{1,0:T(8,128)(2,1)S(1)}, u32[]{:S(2)}, u32[]{:S(2)}) collective-permute-start(bf16[128,1024]{1,0:T(8,128)(2,1)S(1)} %get-tuple-element.42), channel_id=1, source_target_pairs={{4,2},{5,3},{6,4},{7,5},{12,10},{13,11},{14,12},{15,13},{20,18},{2... | collective-permute-start | bytes 786440 | tf_op jit(solution)/shard_map/ppermute | solution.py:66
  236.9 10.6 %collective-permute-start.60 = (bf16[128,1024]{1,0:T(8,128)(2,1)S(1)}, bf16[128,1024]{1,0:T(8,128)(2,1)S(1)}, u32[]{:S(2)}, u32[]{:S(2)}) collective-permute-start(bf16[128,1024]{1,0:T(8,128)(2,1)S(1)} %add.55), channel_id=1, source_target_pairs={{2,0},{3,1},{4,2},{5,3},{6,4},{7,5},{10,8},{11,9},{12,10},{13,11},... | collective-permute-start | bytes 786440 | tf_op jit(solution)/shard_map/ppermute | solution.py:66
  238.3 11.2 %collective-permute-start.57 = (bf16[128,1024]{1,0:T(8,128)(2,1)S(1)}, bf16[128,1024]{1,0:T(8,128)(2,1)S(1)}, u32[]{:S(2)}, u32[]{:S(2)}) collective-permute-start(bf16[128,1024]{1,0:T(8,128)(2,1)S(1)} %add.52), channel_id=1, source_target_pairs={{0,2},{1,3},{2,4},{3,5},{4,6},{5,7},{8,10},{9,11},{10,12},{11,13},... | collective-permute-start | bytes 786440 | tf_op jit(solution)/shard_map/ppermute | solution.py:66
  243.0 9.9 %collective-permute-start.77 = (bf16[128,1024]{1,0:T(8,128)(2,1)S(1)}, bf16[128,1024]{1,0:T(8,128)(2,1)S(1)}, u32[]{:S(2)}, u32[]{:S(2)}) collective-permute-start(bf16[128,1024]{1,0:T(8,128)(2,1)S(1)} %add.58), channel_id=1, source_target_pairs={{0,2},{1,3},{2,4},{3,5},{4,6},{5,7},{8,10},{9,11},{10,12},{11,13},... | collective-permute-start | bytes 786440 | tf_op jit(solution)/shard_map/ppermute | solution.py:66
  246.2 8.5 %collective-permute-start.80 = (bf16[128,1024]{1,0:T(8,128)(2,1)S(1)}, bf16[128,1024]{1,0:T(8,128)(2,1)S(1)}, u32[]{:S(2)}, u32[]{:S(2)}) collective-permute-start(bf16[128,1024]{1,0:T(8,128)(2,1)S(1)} %add.60), channel_id=1, source_target_pairs={{2,0},{3,1},{4,2},{5,3},{6,4},{7,5},{10,8},{11,9},{12,10},{13,11},... | collective-permute-start | bytes 786440 | tf_op jit(solution)/shard_map/ppermute | solution.py:66
  (73 other events, 1321.6 us)
where the time goes:
time: 269 us; the launch traced here: 268 us
  waiting for transfers between devices  103 us (38%)
  starting transfers between devices  88.4 us (33%)
  Pallas kernels  61.8 us (23%)
  local copies, waits for them, and re-layouts  6.84 us (3%)
  other arithmetic  4.26 us (2%)
    ppermute x42, waiting for transfers between devices, hop(): return lax.ppermute(value, 'expert', chip_pairs(sources, move))  98.8 us
    ppermute x42, starting transfers between devices, hop(): return lax.ppermute(value, 'expert', chip_pairs(sources, move))  78 us
    pallas_call x8, Pallas kernels, call(): pl.pallas_call(kernel, out_shape=outs, in_specs=specs, out_specs=out_spec...  61.8 us
    ppermute x37, starting transfers between devices, swapped(): return lax.ppermute(value, 'expert', [(i, i ^ 1) for i in range(count)])  7.91 us
    unnamed x113, local copies, waits for them, and re-layouts  6.72 us
  transfers between devices with their start and end apart: 81, of which 25 were waited for; matrix products, arithmetic and copies ran while one was open for 3% of the time, Pallas kernels for 19%

commit v1 on v0

--- a/solution.py
+++ b/solution.py
@@ -95,9 +95,10 @@
     return [blocks[0], up, down]
 
 
-def entry_chips(length, chip):
+def entry_chips(hops, chip):
+    length = line_length()
     listing = [(None, chip)]
-    for hop in range(1, length):
+    for hop in range(1, hops + 1):
         listing.append((chip - hop >= 0, chip - hop))
         listing.append((chip + hop < length, chip + hop))
     return listing
@@ -105,7 +106,7 @@
 
 def each_copy(refs, target, sems, rows, chip, core, act):
     count = len(refs) // 2
-    listing = entry_chips((count + 1) // 2, chip)
+    listing = entry_chips(count // 2, chip)
     for side in range(CORES):
         for index, (valid, origin) in enumerate(listing):
             number = side * count + index
@@ -166,27 +167,74 @@
     expert_ref[...] = (hidden * rms * gain_e).astype(BF16)
 
 
-def project_kernel(count, depth, *refs):
-    place, xf_ref, xb_ref, gain_a, gain_e, mask_ref = refs[:6]
-    mix_refs = refs[6 : 6 + count]
-    out_refs = refs[6 + count : 6 + 2 * count]
-    projf_ref, projb_ref, hidden_ref, expert_ref = refs[6 + 2 * count : 10 + 2 * count]
-    mix_w, out_w, normed, heads, mix_sems, out_sems = refs[10 + 2 * count :]
-    chip, core = place[0], place[1]
+def early_kernel(count, depth, *refs):
+    place, xf_ref, xb_ref, gain_a = refs[:4]
+    mix_refs = refs[4 : 4 + count]
+    sumf_ref, sumb_ref, normed_ref = refs[4 + count : 7 + count]
+    mix_w, mix_sems = refs[7 + count :]
+    chip, core = place[0], place[1]
+    mix_w[...] = jnp.zeros_like(mix_w)
     start_copies(mix_refs, mix_w, mix_sems, depth, chip, core)
-    start_copies(out_refs, out_w, out_sems, depth, chip, core)
     rows = xf_ref.shape[0]
     for index, x_ref in enumerate((xf_ref, xb_ref)):
         x = x_ref[...].astype(F32)
         rms = lax.rsqrt(mean_last(x * x) + EPS)
-        normed[index * rows : (index + 1) * rows, :] = (x * rms * gain_a[...]).astype(BF16)
+        normed_ref[index * rows : (index + 1) * rows, :] = (x * rms * gain_a[...]).astype(BF16)
     wait_copies(mix_refs, mix_w, mix_sems, depth, chip, core)
     columns = mix_w.shape[1]
     chunk = 512
     for begin in range(0, columns, chunk):
-        piece = dot(normed[...], mix_w[:, begin : begin + chunk])
-        projf_ref[:, begin : begin + chunk] = piece[:rows]
-        projb_ref[:, begin : begin + chunk] = piece[rows:]
+        piece = dot(normed_ref[...], mix_w[:, begin : begin + chunk])
+        sumf_ref[:, begin : begin + chunk] = piece[:rows]
+        sumb_ref[:, begin : begin + chunk] = piece[rows:]
+
+
+def last_copies(mix_refs, mix_w, sems, depth, length, chip, core, act):
+    for which, end in ((0, length - 1), (1, 0)):
+
+        @pl.when(chip == end)
+        def _():
+            for side in range(CORES):
+                start = pl.multiple_of((core if side == 0 else 1 - core) * depth, depth)
+                act(
+                    pltpu.make_async_copy(
+                        mix_refs[2 * side + which],
+                        mix_w.at[pl.ds(start, depth), :],
+                        sems.at[2 * side + which],
+                    )
+                )
+
+
+def project_kernel(count, depth, length, *refs):
+    place, sumf_ref, sumb_ref, normed_ref, xb_ref, gain_e, mask_ref = refs[:7]
+    mix_refs = refs[7:11]
+    out_refs = refs[11 : 11 + count]
+    projf_ref, projb_ref, hidden_ref, expert_ref = refs[11 + count : 15 + count]
+    mix_w, out_w, heads, mix_sems, out_sems = refs[15 + count :]
+    chip, core = place[0], place[1]
+    last_copies(mix_refs, mix_w, mix_sems, depth, length, chip, core, lambda copy: copy.start())
+    start_copies(out_refs, out_w, out_sems, depth, chip, core)
+    last_copies(mix_refs, mix_w, mix_sems, depth, length, chip, core, lambda copy: copy.wait())
+    rows = xb_ref.shape[0]
+    columns = mix_w.shape[1]
+    chunk = 512
+    block = CORES * depth
+    for end in (0, length - 1):
+
+        @pl.when(chip == end)
+        def _():
+            far = (length - 1 - end) * block
+            for begin in range(0, columns, chunk):
+                span = slice(begin, begin + chunk)
+                piece = dot(normed_ref[:, far : far + block], mix_w[:, span])
+                projf_ref[:, span] = sumf_ref[:, span] + piece[:rows]
+                projb_ref[:, span] = sumb_ref[:, span] + piece[rows:]
+
+    @pl.when((chip > 0) & (chip < length - 1))
+    def _():
+        projf_ref[...] = sumf_ref[...]
+        projb_ref[...] = sumb_ref[...]
+
     attend_rows(projb_ref, mask_ref[1], heads)
     wait_copies(out_refs, out_w, out_sems, depth, chip, core)
     finish_rows(xb_ref[...], heads[...], out_w[...], gain_e[...], hidden_ref, expert_ref)
@@ -223,7 +271,7 @@
     chunk = 2 * rows
 
     def step(index, carry):
-        start = pl.multiple_of(index * chunk, chunk)
+        start = chunk_start(index, chunk)
         block = cot[pl.ds(start, chunk), :]
         gates = block[:, width:].astype(F32)
         grad_act = dot(block[:, :width], down_ref[...], NT)
@@ -233,7 +281,19 @@
         )
         return carry
 
-    lax.fori_loop(0, expert_count * rows // chunk, step, 0)
+    each_chunk(expert_count * rows // chunk, step)
+
+
+def each_chunk(number, step):
+    if number <= 4:
+        for index in range(number):
+            step(index, 0)
+    else:
+        lax.fori_loop(0, number, step, 0)
+
+
+def chunk_start(index, chunk):
+    return index * chunk if isinstance(index, int) else pl.multiple_of(index * chunk, chunk)
 
 
 def give_back(result, mine_ref, other_ref, rows, chip, core):
@@ -256,7 +316,7 @@
     chunk = 2 * rows
 
     def step(index, carry):
-        start = pl.multiple_of(index * chunk, chunk)
+        start = chunk_start(index, chunk)
         pre = dot(tokens[pl.ds(start, chunk), :], up_ref[...])
         square = pre * pre
         bend = jnp.tanh(GELU_C * pre * (1.0 + GELU_A * square))
@@ -267,7 +327,7 @@
         result[pl.ds(start, chunk), :] = dot(grad, up_ref[...], NT).astype(BF16)
         return carry
 
-    lax.fori_loop(0, tokens.shape[0] // chunk, step, 0)
+    each_chunk(tokens.shape[0] // chunk, step)
     give_back(result, mine_ref, other_ref, rows, chip, core)
 
 
@@ -282,7 +342,7 @@
     chunk = 2 * rows
 
     def step(index, carry):
-        start = pl.multiple_of(index * chunk, chunk)
+        start = chunk_start(index, chunk)
         pre = dot(tokens[pl.ds(start, chunk), :], up_ref[...])
         bend = jnp.tanh(GELU_C * pre * (1.0 + GELU_A * (pre * pre)))
         active = (0.5 * pre * (1.0 + bend)).astype(BF16)
@@ -291,7 +351,7 @@
         result[pl.ds(start, chunk), :] = (gate * out).astype(BF16)
         return carry
 
-    lax.fori_loop(0, tokens.shape[0] // chunk, step, 0)
+    each_chunk(tokens.shape[0] // chunk, step)
     give_back(result, mine_ref, other_ref, rows, chip, core)
 
 
@@ -300,16 +360,14 @@
         out_ref[...] = (mine_ref[j].astype(F32) + other_ref[j].astype(F32)).astype(BF16)
 
 
-def backward_kernel(count, parts, depth, *refs):
-    place, x_ref, cot_ref, hidden_ref, proj_ref, gain_a, gain_e, mask_ref = refs[:8]
-    part_refs = refs[8 : 8 + parts]
-    mix_refs = refs[8 + parts : 8 + parts + count]
-    out_refs = refs[8 + parts + count : 8 + parts + 2 * count]
-    result_ref = refs[8 + parts + 2 * count]
-    mix_w, out_w, mixed, mix_sems, out_sems = refs[9 + parts + 2 * count :]
+def heads_backward_kernel(count, parts, depth, *refs):
+    place, cot_ref, hidden_ref, proj_ref, gain_e, mask_ref = refs[:6]
+    part_refs = refs[6 : 6 + parts]
+    out_refs = refs[6 + parts : 6 + parts + count]
+    mixed_ref, grad_ref = refs[6 + parts + count : 8 + parts + count]
+    out_w, out_sems = refs[8 + parts + count :]
     chip, core = place[0], place[1]
     start_copies(out_refs, out_w, out_sems, depth, chip, core)
-    start_copies(mix_refs, mix_w, mix_sems, depth, chip, core)
     grad_moe = part_refs[0][...].astype(F32)
     for part_ref in part_refs[1:]:
         grad_moe = grad_moe + part_ref[...].astype(F32)
@@ -320,6 +378,7 @@
     grad_hidden = cot_ref[...].astype(F32) + rms_two * (
         grad_two - normal_two * mean_last(grad_two * normal_two)
     )
+    grad_ref[...] = grad_hidden
     wait_copies(out_refs, out_w, out_sems, depth, chip, core)
     grad_heads = dot(grad_hidden.astype(BF16), out_w[...], NT).astype(BF16)
     allowed = mask_ref[1] > 0.5
@@ -338,14 +397,23 @@
         grad_key = key_scale * (grad_khat - key_hat * mean_last(grad_khat * key_hat))
         for index, grad in enumerate((grad_query, grad_key, grad_value)):
             start = (index * HEADS + head) * HEAD_DIM
-            mixed[:, start : start + HEAD_DIM] = grad.astype(BF16)
+            mixed_ref[:, start : start + HEAD_DIM] = grad.astype(BF16)
+
+
+def entry_backward_kernel(count, depth, *refs):
+    place, x_ref, mixed_ref, grad_ref, gain_a = refs[:5]
+    mix_refs = refs[5 : 5 + count]
+    result_ref = refs[5 + count]
+    mix_w, mix_sems = refs[6 + count :]
+    chip, core = place[0], place[1]
+    start_copies(mix_refs, mix_w, mix_sems, depth, chip, core)
     wait_copies(mix_refs, mix_w, mix_sems, depth, chip, core)
-    grad_normed = dot(mixed[...], mix_w[...], NT)
+    grad_normed = dot(mixed_ref[...], mix_w[...], NT)
     x = x_ref[...].astype(F32)
     rms_one = lax.rsqrt(mean_last(x * x) + EPS)
     normal_one = x * rms_one
     grad_one = grad_normed * gain_a[...]
-    result = grad_hidden + rms_one * (grad_one - normal_one * mean_last(grad_one * normal_one))
+    result = grad_ref[...] + rms_one * (grad_one - normal_one * mean_last(grad_one * normal_one))
     result_ref[...] = result.astype(BF16)
 
 
@@ -425,25 +493,40 @@
     cots = with_partner(relayed(jnp.concatenate([cotangent, gates], axis=1)))
     mask = allowed_of(block_mask[:, 0])
 
+    half = count // 2
+    early_mix = mixers[: half - 2] + mixers[half : count - 2]
+    last_mix = mixers[half - 2 : half] + mixers[count - 2 :]
+    early = len(early_mix)
+    sum_fwd, sum_bwd, normed = call(
+        functools.partial(early_kernel, early, depth),
+        (
+            shaped((tokens, columns), F32),
+            shaped((tokens, columns), F32),
+            shaped((2 * tokens, width), BF16),
+        ),
+        [SMEM] + [VMEM] * 3 + [ANY] * early,
+        (VMEM,) * 3,
+        [pltpu.VMEM((width, columns), BF16), dma(early)],
+        [place, arriving, stashed_input, attention_gain] + early_mix,
+    )
     proj_fwd, proj_bwd, hidden_bwd, expert_bwd = call(
-        functools.partial(project_kernel, count, depth),
+        functools.partial(project_kernel, count, depth, length),
         (
             shaped((tokens, columns), F32),
             shaped((tokens, columns), F32),
             shaped((tokens, width), F32),
             shaped((tokens, width), BF16),
         ),
-        [SMEM] + [VMEM] * 5 + [ANY] * (2 * count),
+        [SMEM] + [VMEM] * 6 + [ANY] * (4 + count),
         (VMEM,) * 4,
         [
-            pltpu.VMEM((width, columns), BF16),
+            pltpu.VMEM((CORES * depth, columns), BF16),
             pltpu.VMEM((width, width), BF16),
-            pltpu.VMEM((2 * tokens, width), BF16),
             pltpu.VMEM((tokens, width), BF16),
-            dma(count),
+            dma(4),
             dma(count),
         ],
-        [place, arriving, stashed_input, attention_gain, expert_gain, mask] + mixers + outers,
+        [place, sum_fwd, sum_bwd, normed, stashed_input, expert_gain, mask] + last_mix + outers,
     )
     rows_bwd = with_partner(relayed(expert_bwd))
 
@@ -503,22 +586,21 @@
     moe_parts = combined(mine, other)
 
     parts = len(grad_parts)
+    grad_mixed, grad_hidden = call(
+        functools.partial(heads_backward_kernel, count, parts, depth),
+        (shaped((tokens, columns), BF16), shaped((tokens, width), F32)),
+        [SMEM] + [VMEM] * (5 + parts) + [ANY] * count,
+        (VMEM,) * 2,
+        [pltpu.VMEM((width, width), BF16), dma(count)],
+        [place, cotangent, hidden_bwd, proj_bwd, expert_gain, mask] + grad_parts + outers,
+    )
     derivative = call(
-        functools.partial(backward_kernel, count, parts, depth),
+        functools.partial(entry_backward_kernel, count, depth),
         shaped((tokens, width), BF16),
-        [SMEM] + [VMEM] * (7 + parts) + [ANY] * (2 * count),
+        [SMEM] + [VMEM] * 4 + [ANY] * count,
         VMEM,
-        [
-            pltpu.VMEM((width, columns), BF16),
-            pltpu.VMEM((width, width), BF16),
-            pltpu.VMEM((tokens, columns), BF16),
-            dma(count),
-            dma(count),
-        ],
-        [place, stashed_input, cotangent, hidden_bwd, proj_bwd, attention_gain, expert_gain, mask]
-        + grad_parts
-        + mixers
-        + outers,
+        [pltpu.VMEM((width, columns), BF16), dma(count)],
+        [place, stashed_input, grad_mixed, grad_hidden, attention_gain] + mixers,
     )
 
     layer_output = hidden_fwd

time: 269 us -> 277 us (1.030)
  Pallas kernels: 61.8 us -> 67.5 us
  waiting for transfers between devices: 103 us -> 107 us
    pallas_call x8 -> x10, Pallas kernels: 61.8 us -> 67.5 us  [call(): pl.pallas_call(kernel, out_shape=outs, in_specs=specs, out_specs=out_spec...]
    ppermute x42, waiting for transfers between devices: 98.8 us -> 103 us  [hop(): return lax.ppermute(value, 'expert', chip_pairs(sources, move))]
    unnamed x113 -> x129, local copies, waits for them, and re-layouts: 6.72 us -> 5.37 us
  transfers between devices with their start and end apart: 81 -> 81, of which waited for: 25 -> 23; matrix products, arithmetic and copies ran while one was open for 3% -> 3% of each run, Pallas kernels for 19% -> 24%
where the time goes in v1:
time: 277 us; the launch traced here: 276 us
  waiting for transfers between devices  107 us (39%)
  starting transfers between devices  87.1 us (31%)
  Pallas kernels  67.5 us (24%)
  local copies, waits for them, and re-layouts  5.49 us (2%)
  other arithmetic  4.31 us (2%)
    ppermute x42, waiting for transfers between devices, hop(): return lax.ppermute(value, 'expert', chip_pairs(sources, move))  103 us
    ppermute x42, starting transfers between devices, hop(): return lax.ppermute(value, 'expert', chip_pairs(sources, move))  76.9 us
    pallas_call x10, Pallas kernels, call(): pl.pallas_call(kernel, out_shape=outs, in_specs=specs, out_specs=out_spec...  67.5 us
    ppermute x37, starting transfers between devices, swapped(): return lax.ppermute(value, 'expert', [(i, i ^ 1) for i in range(count)])  7.67 us
  transfers between devices with their start and end apart: 81, of which 23 were waited for; matrix products, arithmetic and copies ran while one was open for 3% of the time, Pallas kernels for 24%

profile of v1, /device:TPU:0, one launch (start us, length us, event | category | flops | bytes accessed | tf_op | source)
XLA Modules:
  0.0 275.7 jit_solution(8000308971209476158)
XLA Ops:
  0.6 5.0 %collective-permute-start.14 = (bf16[128,1024]{1,0:T(8,128)(2,1)}, bf16[128,1024]{1,0:T(8,128)(2,1)S(1)}, u32[]{:S(2)}, u32[]{:S(2)}) collective-permute-start(bf16[128,1024]{1,0:T(8,128)(2,1)} %bitcast.35), channel_id=1, source_target_pairs={{0,2},{1,3},{2,4},{3,5},{4,6},{5,7},{8,10},{9,11},{10,12},{11,13},... | collective-permute-start | bytes 786440 | tf_op jit(solution)/shard_map/ppermute | solution.py:66
  5.6 1.3 collective-permute-start.15
  7.0 2.5 collective-permute-start.27
  12.1 3.3 %collective-permute-done.15.refs_13_.refs_7_.refs_11_ = bf16[128,1024]{1,0:T(8,128)(2,1)S(1)} collective-permute-done((bf16[128,1024]{1,0:T(8,128)(2,1)}, bf16[128,1024]{1,0:T(8,128)(2,1)S(1)}, u32[]{:S(2)}, u32[]{:S(2)}) %collective-permute-start.15) | collective-permute-done | bytes 262176 | tf_op jit(solution)/shard_map/ppermute | solution.py:66
  15.5 1.3 collective-permute-start.17
  16.9 4.6 %collective-permute-start.1 = (bf16[128,3072]{1,0:T(8,128)(2,1)}, bf16[128,3072]{1,0:T(8,128)(2,1)S(1)}, u32[]{:S(2)}, u32[]{:S(2)}) collective-permute-start(bf16[128,3072]{1,0:T(8,128)(2,1)} %bitcast.30), channel_id=1, source_target_pairs={{0,2},{1,3},{2,4},{3,5},{4,6},{5,7},{8,10},{9,11},{10,12},{11,13},... | collective-permute-start | bytes 2359304 | tf_op jit(solution)/shard_map/ppermute | solution.py:66
  21.5 0.9 collective-permute-done.refs_1_
  22.5 1.3 collective-permute-start.2
  24.4 0.9 collective-permute-done.17.refs_15_.refs_9_.refs_13_
  25.3 4.3 %collective-permute-start.28 = (bf16[128,1152]{1,0:T(8,128)(2,1)S(1)}, bf16[128,1152]{1,0:T(8,128)(2,1)S(1)}, u32[]{:S(2)}, u32[]{:S(2)}) collective-permute-start(bf16[128,1152]{1,0:T(8,128)(2,1)S(1)} %fusion.4.refs_2_), channel_id=1, source_target_pairs={{0,2},{1,3},{2,4},{3,5},{4,6},{5,7},{8,10},{9,11},{10,12},{11,13},... | collective-permute-start | bytes 884744 | tf_op jit(solution)/shard_map/ppermute | solution.py:66
  29.7 1.3 collective-permute-start.29
  31.1 13.4 %collective-permute-done.28.refs_3_ = bf16[128,1152]{1,0:T(8,128)(2,1)S(1)} collective-permute-done((bf16[128,1152]{1,0:T(8,128)(2,1)S(1)}, bf16[128,1152]{1,0:T(8,128)(2,1)S(1)}, u32[]{:S(2)}, u32[]{:S(2)}) %collective-permute-start.28) | collective-permute-done | bytes 294944 | tf_op jit(solution)/shard_map/ppermute | solution.py:66
  44.4 6.4 %collective-permute-done.29.refs_4_ = bf16[128,1152]{1,0:T(8,128)(2,1)S(1)} collective-permute-done((bf16[128,1152]{1,0:T(8,128)(2,1)S(1)}, bf16[128,1152]{1,0:T(8,128)(2,1)S(1)}, u32[]{:S(2)}, u32[]{:S(2)}) %collective-permute-start.29) | collective-permute-done | bytes 294944 | tf_op jit(solution)/shard_map/ppermute | solution.py:66
  51.5 1.3 collective-permute-start.19
  52.9 1.6 collective-permute-start.3
  54.4 1.3 collective-permute-start.4
  55.8 5.1 %collective-permute-done.19.refs_17_.refs_11_.refs_15_ = bf16[128,1024]{1,0:T(8,128)(2,1)S(1)} collective-permute-done((bf16[128,1024]{1,0:T(8,128)(2,1)S(1)}, bf16[128,1024]{1,0:T(8,128)(2,1)S(1)}, u32[]{:S(2)}, u32[]{:S(2)}) %collective-permute-start.19) | collective-permute-done | bytes 262176 | tf_op jit(solution)/shard_map/ppermute | solution.py:66
  62.5 1.3 collective-permute-start.31
  65.1 14.6 %collective-permute-done.4.refs_8_.refs_9_ = bf16[128,3072]{1,0:T(8,128)(2,1)} collective-permute-done((bf16[128,3072]{1,0:T(8,128)(2,1)}, bf16[128,3072]{1,0:T(8,128)(2,1)}, u32[]{:S(2)}, u32[]{:S(2)}) %collective-permute-start.4) | collective-permute-done | bytes 786464 | tf_op jit(solution)/shard_map/ppermute | solution.py:66
  79.7 1.3 collective-permute-start.11
  81.0 2.9 %collective-permute-done.31.refs_6_ = bf16[128,1152]{1,0:T(8,128)(2,1)S(1)} collective-permute-done((bf16[128,1152]{1,0:T(8,128)(2,1)S(1)}, bf16[128,1152]{1,0:T(8,128)(2,1)S(1)}, u32[]{:S(2)}, u32[]{:S(2)}) %collective-permute-start.31) | collective-permute-done | bytes 294944 | tf_op jit(solution)/shard_map/ppermute | solution.py:66
  84.5 1.0 collective-permute-done.25.refs_23_.refs_17_.refs_21_
  86.2 1.3 collective-permute-start.33
  87.7 19.3 %collective-permute-done.33.refs_8_ = bf16[128,1152]{1,0:T(8,128)(2,1)S(1)} collective-permute-done((bf16[128,1152]{1,0:T(8,128)(2,1)S(1)}, bf16[128,1152]{1,0:T(8,128)(2,1)S(1)}, u32[]{:S(2)}, u32[]{:S(2)}) %collective-permute-start.33) | collective-permute-done | bytes 294944 | tf_op jit(solution)/shard_map/ppermute | solution.py:66
  108.5 1.1 collective-permute-done.8.refs_12_.refs_15_
  109.8 1.8 fusion.refs_6_.refs_4_.refs_5_
  113.7 7.6 %shard_map.131 = (f32[128,3072]{1,0:T(8,128)}, f32[128,3072]{1,0:T(8,128)}, bf16[256,1024]{1,0:T(8,128)(2,1)}) custom-call(s32[2]{0:T(128)} %pad_add_fusion.refs_0_, bf16[128,1024]{1,0:T(8,128)(2,1)} %copy-done.22, bf16[128,1024]{1,0:T(8,128)(2,1)} %refs_1_.1, f32[1,1024]{1,0:T(1,128)} %refs_4_.5, bf16[128,3072]{1,0:T(8,128)(2,1)} %bitcast.33, ...), custom_call_target="tpu_custom_call" | custom-call | tf_op jit(solution)/shard_map/pallas_call | solution.py:429
  121.3 8.9 %shard_map.132 = (f32[128,3072]{1,0:T(8,128)}, f32[128,3072]{1,0:T(8,128)}, f32[128,1024]{1,0:T(8,128)}, bf16[128,1024]{1,0:T(8,128)(2,1)}) custom-call(s32[2]{0:T(128)} %pad_add_fusion.refs_0_, f32[128,3072]{1,0:T(8,128)} %get-tuple-element.27.refs_1_, f32[128,3072]{1,0:T(8,128)} %get-tuple-element.28.refs_2_, bf16[256,1024]{1,0:T(8,128)(2,1)} %get-tuple-element.29.refs_3_, ...), custom_call_target="tpu_custom_call" | custom-call | tf_op jit(solution)/shard_map/pallas_call | solution.py:429
  130.3 5.3 %shard_map.133 = (f32[128,1024]{1,0:T(8,128)}, bf16[128,1024]{1,0:T(8,128)(2,1)}) custom-call(s32[2]{0:T(128)} %pad_add_fusion.refs_0_, bf16[128,1024]{1,0:T(8,128)(2,1)} %copy-done.22, f32[128,3072]{1,0:T(8,128)} %get-tuple-element.30.refs_2_, f32[1,1024]{1,0:T(1,128)} %refs_4_.4, f32[2,128,128]{2,1,0:T(8,128)} %fusion.refs_6_.refs_4_.refs_5_, ...), custom_call_target="tpu_custom_call" | custom-call | tf_op jit(solution)/shard_map/pallas_call | solution.py:429
  135.6 1.3 collective-permute-start.41
  136.9 1.3 collective-permute-start.42
  138.6 7.0 %collective-permute-start.61 = (bf16[128,1024]{1,0:T(8,128)(2,1)S(1)}, bf16[128,1024]{1,0:T(8,128)(2,1)S(1)}, u32[]{:S(2)}, u32[]{:S(2)}) collective-permute-start(bf16[128,1024]{1,0:T(8,128)(2,1)S(1)} %copy-done.42), channel_id=1, source_target_pairs={{0,2},{1,3},{2,4},{3,5},{4,6},{5,7},{8,10},{9,11},{10,12},{11,13},... | collective-permute-start | bytes 786440 | tf_op jit(solution)/shard_map/ppermute | solution.py:66
  145.6 1.3 collective-permute-start.62
  147.2 3.0 %collective-permute-done.42.refs_6_ = bf16[128,1024]{1,0:T(8,128)(2,1)S(1)} collective-permute-done((bf16[128,1024]{1,0:T(8,128)(2,1)}, bf16[128,1024]{1,0:T(8,128)(2,1)S(1)}, u32[]{:S(2)}, u32[]{:S(2)}) %collective-permute-start.42) | collective-permute-done | bytes 262176 | tf_op jit(solution)/shard_map/ppermute | solution.py:66
  150.9 1.3 collective-permute-start.44
  152.3 6.0 %collective-permute-done.62.refs_5_ = bf16[128,1024]{1,0:T(8,128)(2,1)S(1)} collective-permute-done((bf16[128,1024]{1,0:T(8,128)(2,1)S(1)}, bf16[128,1024]{1,0:T(8,128)(2,1)S(1)}, u32[]{:S(2)}, u32[]{:S(2)}) %collective-permute-start.62) | collective-permute-done | bytes 262176 | tf_op jit(solution)/shard_map/ppermute | solution.py:66
  159.0 1.3 collective-permute-start.64
  160.4 4.9 %collective-permute-done.44.refs_8_ = bf16[128,1024]{1,0:T(8,128)(2,1)S(1)} collective-permute-done((bf16[128,1024]{1,0:T(8,128)(2,1)S(1)}, bf16[128,1024]{1,0:T(8,128)(2,1)S(1)}, u32[]{:S(2)}, u32[]{:S(2)}) %collective-permute-start.44) | collective-permute-done | bytes 262176 | tf_op jit(solution)/shard_map/ppermute | solution.py:66
  166.7 5.9 %collective-permute-done.64.refs_7_ = bf16[128,1024]{1,0:T(8,128)(2,1)S(1)} collective-permute-done((bf16[128,1024]{1,0:T(8,128)(2,1)S(1)}, bf16[128,1024]{1,0:T(8,128)(2,1)S(1)}, u32[]{:S(2)}, u32[]{:S(2)}) %collective-permute-start.64) | collective-permute-done | bytes 262176 | tf_op jit(solution)/shard_map/ppermute | solution.py:66
  172.7 1.5 collective-permute-start.66
  174.2 1.3 collective-permute-start.46
  176.2 7.6 %collective-permute-done.66.refs_9_ = bf16[128,1024]{1,0:T(8,128)(2,1)S(1)} collective-permute-done((bf16[128,1024]{1,0:T(8,128)(2,1)S(1)}, bf16[128,1024]{1,0:T(8,128)(2,1)S(1)}, u32[]{:S(2)}, u32[]{:S(2)}) %collective-permute-start.66) | collective-permute-done | bytes 262176 | tf_op jit(solution)/shard_map/ppermute | solution.py:66
  183.7 4.3 %collective-permute-done.46.refs_10_ = bf16[128,1024]{1,0:T(8,128)(2,1)S(1)} collective-permute-done((bf16[128,1024]{1,0:T(8,128)(2,1)S(1)}, bf16[128,1024]{1,0:T(8,128)(2,1)S(1)}, u32[]{:S(2)}, u32[]{:S(2)}) %collective-permute-start.46) | collective-permute-done | bytes 262176 | tf_op jit(solution)/shard_map/ppermute | solution.py:66
  190.5 1.6 copy.25
  192.0 6.6 %shard_map.134 = (f32[1024,704]{1,0:T(8,128)}, f32[1024,128]{1,0:T(8,128)}) custom-call(s32[2]{0:T(128)} %pad_add_fusion.refs_0_, bf16[704,1024]{1,0:T(8,128)(2,1)} %bitcast.28, bf16[128,1152]{1,0:T(8,128)(2,1)} %copy-done.21, bf16[128,1152]{1,0:T(8,128)(2,1)} %copy-done.27, bf16[128,1152]{1,0:T(8,128)(2,1)} %copy-done.28, bf16[128,1152]{1,0:T(8,128)(2,1)} %copy-done.29, ...), custom_call_target="tpu_custom_call" | custom-call | tf_op jit(solution)/shard_map/pallas_call | solution.py:429
  198.7 9.7 %shard_map.137 = (bf16[4,128,1024]{2,1,0:T(8,128)(2,1)}, bf16[4,128,1024]{2,1,0:T(8,128)(2,1)}) custom-call(s32[2]{0:T(128)} %pad_add_fusion.refs_0_, bf16[1024,704]{1,0:T(8,128)(2,1)} %bitcast.26, f32[1024,704]{1,0:T(8,128)} %get-tuple-element.42.refs_2_, bf16[128,1024]{1,0:T(8,128)(2,1)} %get-tuple-element.43.refs_3_, bf16[128,1024]{1,0:T(8,128)(2,1)} %copy-done.43, ...), custom_call_target="tpu_custom_call" | custom-call | tf_op jit(solution)/shard_map/pallas_call | solution.py:429
  208.6 8.8 %shard_map.135 = (bf16[4,128,1024]{2,1,0:T(8,128)(2,1)}, bf16[4,128,1024]{2,1,0:T(8,128)(2,1)}) custom-call(s32[2]{0:T(128)} %pad_add_fusion.refs_0_, bf16[1024,704]{1,0:T(8,128)(2,1)} %bitcast.27, bf16[704,1024]{1,0:T(8,128)(2,1)} %bitcast.29, f32[1024,128]{1,0:T(8,128)} %get-tuple-element.32.refs_3_, bf16[128,1024]{1,0:T(8,128)(2,1)} %get-tuple-element.33.refs_4_, ...), custom_call_target="tpu_custom_call" | custom-call | tf_op jit(solution)/shard_map/pallas_call | solution.py:429
  218.0 1.0 copy-done.24
  219.0 2.6 shard_map.138
  222.3 1.5 collective-permute-start.75
  223.8 1.0 copy-done.25
  224.8 2.6 shard_map.136
  227.4 1.4 collective-permute-start.55
  229.5 1.2 collective-permute-done.75
  230.7 4.6 %collective-permute-start.76 = (bf16[128,1024]{1,0:T(8,128)(2,1)S(1)}, bf16[128,1024]{1,0:T(8,128)(2,1)S(1)}, u32[]{:S(2)}, u32[]{:S(2)}) collective-permute-start(bf16[128,1024]{1,0:T(8,128)(2,1)S(1)} %get-tuple-element.53), channel_id=1, source_target_pairs={{0,2},{1,3},{2,4},{3,5},{8,10},{9,11},{10,12},{11,13},{16,18},{17,... | collective-permute-start | bytes 786440 | tf_op jit(solution)/shard_map/ppermute | solution.py:66
  236.3 1.0 fusion.21
  238.0 4.9 %collective-permute-start.56 = (bf16[128,1024]{1,0:T(8,128)(2,1)S(1)}, bf16[128,1024]{1,0:T(8,128)(2,1)S(1)}, u32[]{:S(2)}, u32[]{:S(2)}) collective-permute-start(bf16[128,1024]{1,0:T(8,128)(2,1)S(1)} %get-tuple-element.54), channel_id=1, source_target_pairs={{0,2},{1,3},{2,4},{3,5},{8,10},{9,11},{10,12},{11,13},{16,18},{17,... | collective-permute-start | bytes 786440 | tf_op jit(solution)/shard_map/ppermute | solution.py:66
  243.0 4.6 %collective-permute-start.77 = (bf16[128,1024]{1,0:T(8,128)(2,1)S(1)}, bf16[128,1024]{1,0:T(8,128)(2,1)S(1)}, u32[]{:S(2)}, u32[]{:S(2)}) collective-permute-start(bf16[128,1024]{1,0:T(8,128)(2,1)S(1)} %add.58), channel_id=1, source_target_pairs={{0,2},{1,3},{2,4},{3,5},{4,6},{5,7},{8,10},{9,11},{10,12},{11,13},... | collective-permute-start | bytes 786440 | tf_op jit(solution)/shard_map/ppermute | solution.py:66
  247.7 1.3 collective-permute-start.80
  249.1 1.3 collective-permute-start.60
  250.5 5.2 %collective-permute-start.57 = (bf16[128,1024]{1,0:T(8,128)(2,1)S(1)}, bf16[128,1024]{1,0:T(8,128)(2,1)S(1)}, u32[]{:S(2)}, u32[]{:S(2)}) collective-permute-start(bf16[128,1024]{1,0:T(8,128)(2,1)S(1)} %add.52), channel_id=1, source_target_pairs={{0,2},{1,3},{2,4},{3,5},{4,6},{5,7},{8,10},{9,11},{10,12},{11,13},... | collective-permute-start | bytes 786440 | tf_op jit(solution)/shard_map/ppermute | solution.py:66
  255.7 2.9 %collective-permute-done.80.refs_8_ = bf16[128,1024]{1,0:T(8,128)(2,1)S(1)} collective-permute-done((bf16[128,1024]{1,0:T(8,128)(2,1)S(1)}, bf16[128,1024]{1,0:T(8,128)(2,1)S(1)}, u32[]{:S(2)}, u32[]{:S(2)}) %collective-permute-start.80) | collective-permute-done | bytes 262176 | tf_op jit(solution)/shard_map/ppermute | solution.py:66
  259.3 8.1 %shard_map.139 = (bf16[128,3072]{1,0:T(8,128)(2,1)}, f32[128,1024]{1,0:T(8,128)}) custom-call(s32[2]{0:T(128)} %pad_add_fusion.refs_0_, bf16[128,1024]{1,0:T(8,128)(2,1)} %copy-done.23, f32[128,1024]{1,0:T(8,128)} %get-tuple-element.40.refs_2_, f32[128,3072]{1,0:T(8,128)} %get-tuple-element.41.refs_3_, f32[1,1024]{1,0:T(1,128)} %refs_4_.4, ...), custom_call_target="tpu_custom_call" | custom-call | tf_op jit(solution)/shard_map/pallas_call | solution.py:429
  267.4 7.4 %shard_map.140 = bf16[128,1024]{1,0:T(8,128)(2,1)} custom-call(s32[2]{0:T(128)} %pad_add_fusion.refs_0_, bf16[128,1024]{1,0:T(8,128)(2,1)} %refs_1_.1, bf16[128,3072]{1,0:T(8,128)(2,1)} %get-tuple-element.50.refs_2_, f32[128,1024]{1,0:T(8,128)} %get-tuple-element.51.refs_3_, f32[1,1024]{1,0:T(1,128)} %refs_4_.5, bf16[128,3072]{1,0:T(8,128)(2,1)} %bitcast.34, ...), custom_call_target="tpu_custom_call" | custom-call | tf_op jit(solution)/shard_map/pallas_call | solution.py:429
  (255 shorter events, 24.4 us)
Async XLA Ops:
  0.6 10.8 %collective-permute-start.14 = (bf16[128,1024]{1,0:T(8,128)(2,1)}, bf16[128,1024]{1,0:T(8,128)(2,1)S(1)}, u32[]{:S(2)}, u32[]{:S(2)}) collective-permute-start(bf16[128,1024]{1,0:T(8,128)(2,1)} %bitcast.35), channel_id=1, source_target_pairs={{0,2},{1,3},{2,4},{3,5},{4,6},{5,7},{8,10},{9,11},{10,12},{11,13},... | collective-permute-start | bytes 786440 | tf_op jit(solution)/shard_map/ppermute | solution.py:66
  5.6 9.9 %collective-permute-start.15 = (bf16[128,1024]{1,0:T(8,128)(2,1)}, bf16[128,1024]{1,0:T(8,128)(2,1)S(1)}, u32[]{:S(2)}, u32[]{:S(2)}) collective-permute-start(bf16[128,1024]{1,0:T(8,128)(2,1)} %bitcast.36), channel_id=1, source_target_pairs={{2,0},{3,1},{4,2},{5,3},{6,4},{7,5},{10,8},{11,9},{12,10},{13,11},... | collective-permute-start | bytes 786440 | tf_op jit(solution)/shard_map/ppermute | solution.py:66
  6.9 16.9 %collective-permute-start.20 = (bf16[128,1024]{1,0:T(8,128)(2,1)}, bf16[128,1024]{1,0:T(8,128)(2,1)S(1)}, u32[]{:S(2)}, u32[]{:S(2)}) collective-permute-start(bf16[128,1024]{1,0:T(8,128)(2,1)} %bitcast.37), channel_id=1, source_target_pairs={{0,1},{1,0},{2,3},{3,2},{4,5},{5,4},{6,7},{7,6},{8,9},{9,8},{10,11... | collective-permute-start | bytes 786440 | tf_op jit(solution)/shard_map/ppermute | solution.py:62
  7.0 9.9 %collective-permute-start.27 = (bf16[128,1024]{1,0:T(8,128)(2,1)}, bf16[128,1024]{1,0:T(8,128)(2,1)S(1)}, u32[]{:S(2)}, u32[]{:S(2)}) collective-permute-start(bf16[128,1024]{1,0:T(8,128)(2,1)} %param.14), channel_id=1, source_target_pairs={{0,24},{8,0},{16,8},{24,16},{1,25},{9,1},{17,9},{25,17},{2,26},{10... | collective-permute-start | bytes 786440 | tf_op jit(solution)/shard_map/ppermute | solution.py:45
  9.5 13.0 %collective-permute-start = (bf16[128,1024]{1,0:T(8,128)(2,1)}, bf16[128,1024]{1,0:T(8,128)(2,1)S(1)}, u32[]{:S(2)}, u32[]{:S(2)}) collective-permute-start(bf16[128,1024]{1,0:T(8,128)(2,1)} %param.12), channel_id=1, source_target_pairs={{0,8},{8,16},{16,24},{24,0},{1,9},{9,17},{17,25},{25,1},{2,10},{10... | collective-permute-start | bytes 786440 | tf_op jit(solution)/shard_map/ppermute | solution.py:45
  11.5 12.4 %collective-permute-start.16 = (bf16[128,1024]{1,0:T(8,128)(2,1)S(1)}, bf16[128,1024]{1,0:T(8,128)(2,1)S(1)}, u32[]{:S(2)}, u32[]{:S(2)}) collective-permute-start(bf16[128,1024]{1,0:T(8,128)(2,1)S(1)} %collective-permute-done.14.refs_12_.refs_6_.refs_10_), channel_id=1, source_target_pairs={{2,4},{3,5},{4,6},{5,7},{10,12},{11,13},{12,14},{13,15},{18,20},{1... | collective-permute-start | bytes 786440 | tf_op jit(solution)/shard_map/ppermute | solution.py:66
  15.5 9.8 %collective-permute-start.17 = (bf16[128,1024]{1,0:T(8,128)(2,1)S(1)}, bf16[128,1024]{1,0:T(8,128)(2,1)S(1)}, u32[]{:S(2)}, u32[]{:S(2)}) collective-permute-start(bf16[128,1024]{1,0:T(8,128)(2,1)S(1)} %collective-permute-done.15.refs_13_.refs_7_.refs_11_), channel_id=1, source_target_pairs={{2,0},{3,1},{4,2},{5,3},{10,8},{11,9},{12,10},{13,11},{18,16},{19,... | collective-permute-start | bytes 786440 | tf_op jit(solution)/shard_map/ppermute | solution.py:66
  16.9 35.9 %collective-permute-start.1 = (bf16[128,3072]{1,0:T(8,128)(2,1)}, bf16[128,3072]{1,0:T(8,128)(2,1)S(1)}, u32[]{:S(2)}, u32[]{:S(2)}) collective-permute-start(bf16[128,3072]{1,0:T(8,128)(2,1)} %bitcast.30), channel_id=1, source_target_pairs={{0,2},{1,3},{2,4},{3,5},{4,6},{5,7},{8,10},{9,11},{10,12},{11,13},... | collective-permute-start | bytes 2359304 | tf_op jit(solution)/shard_map/ppermute | solution.py:66
  22.5 31.9 %collective-permute-start.2 = (bf16[128,3072]{1,0:T(8,128)(2,1)}, bf16[128,3072]{1,0:T(8,128)(2,1)}, u32[]{:S(2)}, u32[]{:S(2)}) collective-permute-start(bf16[128,3072]{1,0:T(8,128)(2,1)} %bitcast.31), channel_id=1, source_target_pairs={{2,0},{3,1},{4,2},{5,3},{6,4},{7,5},{10,8},{11,9},{12,10},{13,11},... | collective-permute-start | bytes 2359304 | tf_op jit(solution)/shard_map/ppermute | solution.py:66
  25.3 19.1 %collective-permute-start.28 = (bf16[128,1152]{1,0:T(8,128)(2,1)S(1)}, bf16[128,1152]{1,0:T(8,128)(2,1)S(1)}, u32[]{:S(2)}, u32[]{:S(2)}) collective-permute-start(bf16[128,1152]{1,0:T(8,128)(2,1)S(1)} %fusion.4.refs_2_), channel_id=1, source_target_pairs={{0,2},{1,3},{2,4},{3,5},{4,6},{5,7},{8,10},{9,11},{10,12},{11,13},... | collective-permute-start | bytes 884744 | tf_op jit(solution)/shard_map/ppermute | solution.py:66
  29.7 21.2 %collective-permute-start.29 = (bf16[128,1152]{1,0:T(8,128)(2,1)S(1)}, bf16[128,1152]{1,0:T(8,128)(2,1)S(1)}, u32[]{:S(2)}, u32[]{:S(2)}) collective-permute-start(bf16[128,1152]{1,0:T(8,128)(2,1)S(1)} %fusion.4.refs_2_), channel_id=1, source_target_pairs={{2,0},{3,1},{4,2},{5,3},{6,4},{7,5},{10,8},{11,9},{12,10},{13,11},... | collective-permute-start | bytes 884744 | tf_op jit(solution)/shard_map/ppermute | solution.py:66
  31.0 20.5 %collective-permute-start.34 = (bf16[128,1152]{1,0:T(8,128)(2,1)S(1)}, bf16[128,1152]{1,0:T(8,128)(2,1)}, u32[]{:S(2)}, u32[]{:S(2)}) collective-permute-start(bf16[128,1152]{1,0:T(8,128)(2,1)S(1)} %fusion.4.refs_2_), channel_id=1, source_target_pairs={{0,1},{1,0},{2,3},{3,2},{4,5},{5,4},{6,7},{7,6},{8,9},{9,8},{10,11... | collective-permute-start | bytes 884744 | tf_op jit(solution)/shard_map/ppermute | solution.py:62
  44.4 19.3 %collective-permute-start.5 = (bf16[128,3072]{1,0:T(8,128)(2,1)}, bf16[128,3072]{1,0:T(8,128)(2,1)S(1)}, u32[]{:S(2)}, u32[]{:S(2)}) collective-permute-start(bf16[128,3072]{1,0:T(8,128)(2,1)} %bitcast.32), channel_id=1, source_target_pairs={{0,1},{1,0},{2,3},{3,2},{4,5},{5,4},{6,7},{7,6},{8,9},{9,8},{10,11... | collective-permute-start | bytes 2359304 | tf_op jit(solution)/shard_map/ppermute | solution.py:62
  51.5 9.4 %collective-permute-start.19 = (bf16[128,1024]{1,0:T(8,128)(2,1)S(1)}, bf16[128,1024]{1,0:T(8,128)(2,1)S(1)}, u32[]{:S(2)}, u32[]{:S(2)}) collective-permute-start(bf16[128,1024]{1,0:T(8,128)(2,1)S(1)} %collective-permute-done.17.refs_15_.refs_9_.refs_13_), channel_id=1, source_target_pairs={{2,0},{3,1},{10,8},{11,9},{18,16},{19,17},{26,24},{27,25}} | collective-permute-start | bytes 786440 | tf_op jit(solution)/shard_map/ppermute | solution.py:66
  52.9 11.5 %collective-permute-start.3 = (bf16[128,3072]{1,0:T(8,128)(2,1)S(1)}, bf16[128,3072]{1,0:T(8,128)(2,1)}, u32[]{:S(2)}, u32[]{:S(2)}) collective-permute-start(bf16[128,3072]{1,0:T(8,128)(2,1)S(1)} %collective-permute-done.1.refs_5_.refs_6_), channel_id=1, source_target_pairs={{2,4},{3,5},{4,6},{5,7},{10,12},{11,13},{12,14},{13,15},{18,20},{1... | collective-permute-start | bytes 2359304 | tf_op jit(solution)/shard_map/ppermute | solution.py:66
  54.4 25.3 %collective-permute-start.4 = (bf16[128,3072]{1,0:T(8,128)(2,1)}, bf16[128,3072]{1,0:T(8,128)(2,1)}, u32[]{:S(2)}, u32[]{:S(2)}) collective-permute-start(bf16[128,3072]{1,0:T(8,128)(2,1)} %collective-permute-done.2.refs_6_.refs_7_), channel_id=1, source_target_pairs={{2,0},{3,1},{4,2},{5,3},{10,8},{11,9},{12,10},{13,11},{18,16},{19,... | collective-permute-start | bytes 2359304 | tf_op jit(solution)/shard_map/ppermute | solution.py:66
  62.5 21.5 %collective-permute-start.31 = (bf16[128,1152]{1,0:T(8,128)(2,1)S(1)}, bf16[128,1152]{1,0:T(8,128)(2,1)S(1)}, u32[]{:S(2)}, u32[]{:S(2)}) collective-permute-start(bf16[128,1152]{1,0:T(8,128)(2,1)S(1)} %collective-permute-done.29.refs_4_), channel_id=1, source_target_pairs={{2,0},{3,1},{4,2},{5,3},{10,8},{11,9},{12,10},{13,11},{18,16},{19,... | collective-permute-start | bytes 884744 | tf_op jit(solution)/shard_map/ppermute | solution.py:66
  63.8 20.2 %collective-permute-start.35 = (bf16[128,1152]{1,0:T(8,128)(2,1)S(1)}, bf16[128,1152]{1,0:T(8,128)(2,1)S(1)}, u32[]{:S(2)}, u32[]{:S(2)}) collective-permute-start(bf16[128,1152]{1,0:T(8,128)(2,1)S(1)} %collective-permute-done.28.refs_3_), channel_id=1, source_target_pairs={{0,1},{1,0},{2,3},{3,2},{4,5},{5,4},{6,7},{7,6},{8,9},{9,8},{10,11... | collective-permute-start | bytes 884744 | tf_op jit(solution)/shard_map/ppermute | solution.py:62
  64.0 43.0 %collective-permute-start.6 = (bf16[128,3072]{1,0:T(8,128)(2,1)S(1)}, bf16[128,3072]{1,0:T(8,128)(2,1)S(1)}, u32[]{:S(2)}, u32[]{:S(2)}) collective-permute-start(bf16[128,3072]{1,0:T(8,128)(2,1)S(1)} %collective-permute-done.1.refs_5_.refs_6_), channel_id=1, source_target_pairs={{0,1},{1,0},{2,3},{3,2},{4,5},{5,4},{6,7},{7,6},{8,9},{9,8},{10,11... | collective-permute-start | bytes 2359304 | tf_op jit(solution)/shard_map/ppermute | solution.py:62
  64.4 43.2 %collective-permute-start.10 = (bf16[128,3072]{1,0:T(8,128)(2,1)}, bf16[128,3072]{1,0:T(8,128)(2,1)S(1)}, u32[]{:S(2)}, u32[]{:S(2)}) collective-permute-start(bf16[128,3072]{1,0:T(8,128)(2,1)} %collective-permute-done.3.refs_7_.refs_8_), channel_id=1, source_target_pairs={{4,6},{5,7},{12,14},{13,15},{20,22},{21,23},{28,30},{29,31}} | collective-permute-start | bytes 2359304 | tf_op jit(solution)/shard_map/ppermute | solution.py:66
  79.7 28.0 %collective-permute-start.11 = (bf16[128,3072]{1,0:T(8,128)(2,1)}, bf16[128,3072]{1,0:T(8,128)(2,1)S(1)}, u32[]{:S(2)}, u32[]{:S(2)}) collective-permute-start(bf16[128,3072]{1,0:T(8,128)(2,1)} %collective-permute-done.4.refs_8_.refs_9_), channel_id=1, source_target_pairs={{2,0},{3,1},{10,8},{11,9},{18,16},{19,17},{26,24},{27,25}} | collective-permute-start | bytes 2359304 | tf_op jit(solution)/shard_map/ppermute | solution.py:66
  86.2 20.8 %collective-permute-start.33 = (bf16[128,1152]{1,0:T(8,128)(2,1)S(1)}, bf16[128,1152]{1,0:T(8,128)(2,1)S(1)}, u32[]{:S(2)}, u32[]{:S(2)}) collective-permute-start(bf16[128,1152]{1,0:T(8,128)(2,1)S(1)} %collective-permute-done.31.refs_6_), channel_id=1, source_target_pairs={{2,0},{3,1},{10,8},{11,9},{18,16},{19,17},{26,24},{27,25}} | collective-permute-start | bytes 884744 | tf_op jit(solution)/shard_map/ppermute | solution.py:66
  87.5 20.8 %collective-permute-start.7 = (bf16[128,3072]{1,0:T(8,128)(2,1)}, bf16[128,3072]{1,0:T(8,128)(2,1)}, u32[]{:S(2)}, u32[]{:S(2)}) collective-permute-start(bf16[128,3072]{1,0:T(8,128)(2,1)} %collective-permute-done.2.refs_6_.refs_7_), channel_id=1, source_target_pairs={{0,1},{1,0},{2,3},{3,2},{4,5},{5,4},{6,7},{7,6},{8,9},{9,8},{10,11... | collective-permute-start | bytes 2359304 | tf_op jit(solution)/shard_map/ppermute | solution.py:62
  108.3 27.2 %collective-permute-start.36 = (bf16[128,1152]{1,0:T(8,128)(2,1)}, bf16[128,1152]{1,0:T(8,128)(2,1)}, u32[]{:S(2)}, u32[]{:S(2)}) collective-permute-start(bf16[128,1152]{1,0:T(8,128)(2,1)} %copy-done.28), channel_id=1, source_target_pairs={{0,1},{1,0},{2,3},{3,2},{4,5},{5,4},{6,7},{7,6},{8,9},{9,8},{10,11... | collective-permute-start | bytes 884744 | tf_op jit(solution)/shard_map/ppermute | solution.py:62
  109.6 27.2 %collective-permute-start.37 = (bf16[128,1152]{1,0:T(8,128)(2,1)}, bf16[128,1152]{1,0:T(8,128)(2,1)}, u32[]{:S(2)}, u32[]{:S(2)}) collective-permute-start(bf16[128,1152]{1,0:T(8,128)(2,1)} %copy-done.29), channel_id=1, source_target_pairs={{0,1},{1,0},{2,3},{3,2},{4,5},{5,4},{6,7},{7,6},{8,9},{9,8},{10,11... | collective-permute-start | bytes 884744 | tf_op jit(solution)/shard_map/ppermute | solution.py:62
  111.5 26.7 %collective-permute-start.38 = (bf16[128,1152]{1,0:T(8,128)(2,1)}, bf16[128,1152]{1,0:T(8,128)(2,1)}, u32[]{:S(2)}, u32[]{:S(2)}) collective-permute-start(bf16[128,1152]{1,0:T(8,128)(2,1)} %copy-done.30), channel_id=1, source_target_pairs={{0,1},{1,0},{2,3},{3,2},{4,5},{5,4},{6,7},{7,6},{8,9},{9,8},{10,11... | collective-permute-start | bytes 884744 | tf_op jit(solution)/shard_map/ppermute | solution.py:62
  111.9 26.7 %collective-permute-start.39 = (bf16[128,1152]{1,0:T(8,128)(2,1)}, bf16[128,1152]{1,0:T(8,128)(2,1)}, u32[]{:S(2)}, u32[]{:S(2)}) collective-permute-start(bf16[128,1152]{1,0:T(8,128)(2,1)} %copy-done.32), channel_id=1, source_target_pairs={{0,1},{1,0},{2,3},{3,2},{4,5},{5,4},{6,7},{7,6},{8,9},{9,8},{10,11... | collective-permute-start | bytes 884744 | tf_op jit(solution)/shard_map/ppermute | solution.py:62
  112.9 32.7 %collective-permute-start.40 = (bf16[128,1152]{1,0:T(8,128)(2,1)}, bf16[128,1152]{1,0:T(8,128)(2,1)}, u32[]{:S(2)}, u32[]{:S(2)}) collective-permute-start(bf16[128,1152]{1,0:T(8,128)(2,1)} %copy-done.33), channel_id=1, source_target_pairs={{0,1},{1,0},{2,3},{3,2},{4,5},{5,4},{6,7},{7,6},{8,9},{9,8},{10,11... | collective-permute-start | bytes 884744 | tf_op jit(solution)/shard_map/ppermute | solution.py:62
  135.6 11.3 %collective-permute-start.41 = (bf16[128,1024]{1,0:T(8,128)(2,1)}, bf16[128,1024]{1,0:T(8,128)(2,1)S(1)}, u32[]{:S(2)}, u32[]{:S(2)}) collective-permute-start(bf16[128,1024]{1,0:T(8,128)(2,1)} %get-tuple-element.33.refs_4_), channel_id=1, source_target_pairs={{0,2},{1,3},{2,4},{3,5},{4,6},{5,7},{8,10},{9,11},{10,12},{11,13},... | collective-permute-start | bytes 786440 | tf_op jit(solution)/shard_map/ppermute | solution.py:66
  136.9 13.3 %collective-permute-start.42 = (bf16[128,1024]{1,0:T(8,128)(2,1)}, bf16[128,1024]{1,0:T(8,128)(2,1)S(1)}, u32[]{:S(2)}, u32[]{:S(2)}) collective-permute-start(bf16[128,1024]{1,0:T(8,128)(2,1)} %get-tuple-element.33.refs_4_), channel_id=1, source_target_pairs={{2,0},{3,1},{4,2},{5,3},{6,4},{7,5},{10,8},{11,9},{12,10},{13,11},... | collective-permute-start | bytes 786440 | tf_op jit(solution)/shard_map/ppermute | solution.py:66
  138.2 12.7 %collective-permute-start.47 = (bf16[128,1024]{1,0:T(8,128)(2,1)}, bf16[128,1024]{1,0:T(8,128)(2,1)S(1)}, u32[]{:S(2)}, u32[]{:S(2)}) collective-permute-start(bf16[128,1024]{1,0:T(8,128)(2,1)} %get-tuple-element.33.refs_4_), channel_id=1, source_target_pairs={{0,1},{1,0},{2,3},{3,2},{4,5},{5,4},{6,7},{7,6},{8,9},{9,8},{10,11... | collective-permute-start | bytes 786440 | tf_op jit(solution)/shard_map/ppermute | solution.py:62
  138.6 13.6 %collective-permute-start.61 = (bf16[128,1024]{1,0:T(8,128)(2,1)S(1)}, bf16[128,1024]{1,0:T(8,128)(2,1)S(1)}, u32[]{:S(2)}, u32[]{:S(2)}) collective-permute-start(bf16[128,1024]{1,0:T(8,128)(2,1)S(1)} %copy-done.42), channel_id=1, source_target_pairs={{0,2},{1,3},{2,4},{3,5},{4,6},{5,7},{8,10},{9,11},{10,12},{11,13},... | collective-permute-start | bytes 786440 | tf_op jit(solution)/shard_map/ppermute | solution.py:66
  145.6 12.7 %collective-permute-start.62 = (bf16[128,1024]{1,0:T(8,128)(2,1)S(1)}, bf16[128,1024]{1,0:T(8,128)(2,1)S(1)}, u32[]{:S(2)}, u32[]{:S(2)}) collective-permute-start(bf16[128,1024]{1,0:T(8,128)(2,1)S(1)} %copy-done.42), channel_id=1, source_target_pairs={{2,0},{3,1},{4,2},{5,3},{6,4},{7,5},{10,8},{11,9},{12,10},{13,11},... | collective-permute-start | bytes 786440 | tf_op jit(solution)/shard_map/ppermute | solution.py:66
  146.9 12.1 %collective-permute-start.67 = (bf16[128,1024]{1,0:T(8,128)(2,1)S(1)}, bf16[128,1024]{1,0:T(8,128)(2,1)S(1)}, u32[]{:S(2)}, u32[]{:S(2)}) collective-permute-start(bf16[128,1024]{1,0:T(8,128)(2,1)S(1)} %copy-done.42), channel_id=1, source_target_pairs={{0,1},{1,0},{2,3},{3,2},{4,5},{5,4},{6,7},{7,6},{8,9},{9,8},{10,11... | collective-permute-start | bytes 786440 | tf_op jit(solution)/shard_map/ppermute | solution.py:62
  150.2 10.1 %collective-permute-start.43 = (bf16[128,1024]{1,0:T(8,128)(2,1)S(1)}, bf16[128,1024]{1,0:T(8,128)(2,1)S(1)}, u32[]{:S(2)}, u32[]{:S(2)}) collective-permute-start(bf16[128,1024]{1,0:T(8,128)(2,1)S(1)} %collective-permute-done.41.refs_5_), channel_id=1, source_target_pairs={{2,4},{3,5},{4,6},{5,7},{10,12},{11,13},{12,14},{13,15},{18,20},{1... | collective-permute-start | bytes 786440 | tf_op jit(solution)/shard_map/ppermute | solution.py:66
  150.9 14.4 %collective-permute-start.44 = (bf16[128,1024]{1,0:T(8,128)(2,1)S(1)}, bf16[128,1024]{1,0:T(8,128)(2,1)S(1)}, u32[]{:S(2)}, u32[]{:S(2)}) collective-permute-start(bf16[128,1024]{1,0:T(8,128)(2,1)S(1)} %collective-permute-done.42.refs_6_), channel_id=1, source_target_pairs={{2,0},{3,1},{4,2},{5,3},{10,8},{11,9},{12,10},{13,11},{18,16},{19,... | collective-permute-start | bytes 786440 | tf_op jit(solution)/shard_map/ppermute | solution.py:66
  152.2 13.1 %collective-permute-start.48 = (bf16[128,1024]{1,0:T(8,128)(2,1)S(1)}, bf16[128,1024]{1,0:T(8,128)(2,1)S(1)}, u32[]{:S(2)}, u32[]{:S(2)}) collective-permute-start(bf16[128,1024]{1,0:T(8,128)(2,1)S(1)} %collective-permute-done.41.refs_5_), channel_id=1, source_target_pairs={{0,1},{1,0},{2,3},{3,2},{4,5},{5,4},{6,7},{7,6},{8,9},{9,8},{10,11... | collective-permute-start | bytes 786440 | tf_op jit(solution)/shard_map/ppermute | solution.py:62
  159.0 13.6 %collective-permute-start.64 = (bf16[128,1024]{1,0:T(8,128)(2,1)S(1)}, bf16[128,1024]{1,0:T(8,128)(2,1)S(1)}, u32[]{:S(2)}, u32[]{:S(2)}) collective-permute-start(bf16[128,1024]{1,0:T(8,128)(2,1)S(1)} %collective-permute-done.62.refs_5_), channel_id=1, source_target_pairs={{2,0},{3,1},{4,2},{5,3},{10,8},{11,9},{12,10},{13,11},{18,16},{19,... | collective-permute-start | bytes 786440 | tf_op jit(solution)/shard_map/ppermute | solution.py:66
  160.3 13.8 %collective-permute-start.68 = (bf16[128,1024]{1,0:T(8,128)(2,1)S(1)}, bf16[128,1024]{1,0:T(8,128)(2,1)S(1)}, u32[]{:S(2)}, u32[]{:S(2)}) collective-permute-start(bf16[128,1024]{1,0:T(8,128)(2,1)S(1)} %collective-permute-done.61.refs_4_), channel_id=1, source_target_pairs={{0,1},{1,0},{2,3},{3,2},{4,5},{5,4},{6,7},{7,6},{8,9},{9,8},{10,11... | collective-permute-start | bytes 786440 | tf_op jit(solution)/shard_map/ppermute | solution.py:62
  165.3 10.1 %collective-permute-start.69 = (bf16[128,1024]{1,0:T(8,128)(2,1)S(1)}, bf16[128,1024]{1,0:T(8,128)(2,1)S(1)}, u32[]{:S(2)}, u32[]{:S(2)}) collective-permute-start(bf16[128,1024]{1,0:T(8,128)(2,1)S(1)} %collective-permute-done.62.refs_5_), channel_id=1, source_target_pairs={{0,1},{1,0},{2,3},{3,2},{4,5},{5,4},{6,7},{7,6},{8,9},{9,8},{10,11... | collective-permute-start | bytes 786440 | tf_op jit(solution)/shard_map/ppermute | solution.py:62
  165.4 10.2 %collective-permute-start.45 = (bf16[128,1024]{1,0:T(8,128)(2,1)S(1)}, bf16[128,1024]{1,0:T(8,128)(2,1)S(1)}, u32[]{:S(2)}, u32[]{:S(2)}) collective-permute-start(bf16[128,1024]{1,0:T(8,128)(2,1)S(1)} %collective-permute-done.43.refs_7_), channel_id=1, source_target_pairs={{4,6},{5,7},{12,14},{13,15},{20,22},{21,23},{28,30},{29,31}} | collective-permute-start | bytes 786440 | tf_op jit(solution)/shard_map/ppermute | solution.py:66
  166.1 10.0 %collective-permute-start.65 = (bf16[128,1024]{1,0:T(8,128)(2,1)S(1)}, bf16[128,1024]{1,0:T(8,128)(2,1)S(1)}, u32[]{:S(2)}, u32[]{:S(2)}) collective-permute-start(bf16[128,1024]{1,0:T(8,128)(2,1)S(1)} %collective-permute-done.63.refs_6_), channel_id=1, source_target_pairs={{4,6},{5,7},{12,14},{13,15},{20,22},{21,23},{28,30},{29,31}} | collective-permute-start | bytes 786440 | tf_op jit(solution)/shard_map/ppermute | solution.py:66
  172.7 11.1 %collective-permute-start.66 = (bf16[128,1024]{1,0:T(8,128)(2,1)S(1)}, bf16[128,1024]{1,0:T(8,128)(2,1)S(1)}, u32[]{:S(2)}, u32[]{:S(2)}) collective-permute-start(bf16[128,1024]{1,0:T(8,128)(2,1)S(1)} %collective-permute-done.64.refs_7_), channel_id=1, source_target_pairs={{2,0},{3,1},{10,8},{11,9},{18,16},{19,17},{26,24},{27,25}} | collective-permute-start | bytes 786440 | tf_op jit(solution)/shard_map/ppermute | solution.py:66
  174.2 13.8 %collective-permute-start.46 = (bf16[128,1024]{1,0:T(8,128)(2,1)S(1)}, bf16[128,1024]{1,0:T(8,128)(2,1)S(1)}, u32[]{:S(2)}, u32[]{:S(2)}) collective-permute-start(bf16[128,1024]{1,0:T(8,128)(2,1)S(1)} %collective-permute-done.44.refs_8_), channel_id=1, source_target_pairs={{2,0},{3,1},{10,8},{11,9},{18,16},{19,17},{26,24},{27,25}} | collective-permute-start | bytes 786440 | tf_op jit(solution)/shard_map/ppermute | solution.py:66
  175.5 12.5 %collective-permute-start.70 = (bf16[128,1024]{1,0:T(8,128)(2,1)S(1)}, bf16[128,1024]{1,0:T(8,128)(2,1)S(1)}, u32[]{:S(2)}, u32[]{:S(2)}) collective-permute-start(bf16[128,1024]{1,0:T(8,128)(2,1)S(1)} %collective-permute-done.63.refs_6_), channel_id=1, source_target_pairs={{0,1},{1,0},{2,3},{3,2},{4,5},{5,4},{6,7},{7,6},{8,9},{9,8},{10,11... | collective-permute-start | bytes 786440 | tf_op jit(solution)/shard_map/ppermute | solution.py:62
  175.6 12.9 %collective-permute-start.71 = (bf16[128,1024]{1,0:T(8,128)(2,1)S(1)}, bf16[128,1024]{1,0:T(8,128)(2,1)S(1)}, u32[]{:S(2)}, u32[]{:S(2)}) collective-permute-start(bf16[128,1024]{1,0:T(8,128)(2,1)S(1)} %collective-permute-done.64.refs_7_), channel_id=1, source_target_pairs={{0,1},{1,0},{2,3},{3,2},{4,5},{5,4},{6,7},{7,6},{8,9},{9,8},{10,11... | collective-permute-start | bytes 786440 | tf_op jit(solution)/shard_map/ppermute | solution.py:62
  176.1 12.5 %collective-permute-start.72 = (bf16[128,1024]{1,0:T(8,128)(2,1)S(1)}, bf16[128,1024]{1,0:T(8,128)(2,1)S(1)}, u32[]{:S(2)}, u32[]{:S(2)}) collective-permute-start(bf16[128,1024]{1,0:T(8,128)(2,1)S(1)} %collective-permute-done.65.refs_8_), channel_id=1, source_target_pairs={{0,1},{1,0},{2,3},{3,2},{4,5},{5,4},{6,7},{7,6},{8,9},{9,8},{10,11... | collective-permute-start | bytes 786440 | tf_op jit(solution)/shard_map/ppermute | solution.py:62
  188.0 20.5 %collective-permute-start.49 = (bf16[128,1024]{1,0:T(8,128)(2,1)S(1)}, bf16[128,1024]{1,0:T(8,128)(2,1)}, u32[]{:S(2)}, u32[]{:S(2)}) collective-permute-start(bf16[128,1024]{1,0:T(8,128)(2,1)S(1)} %collective-permute-done.42.refs_6_), channel_id=1, source_target_pairs={{0,1},{1,0},{2,3},{3,2},{4,5},{5,4},{6,7},{7,6},{8,9},{9,8},{10,11... | collective-permute-start | bytes 786440 | tf_op jit(solution)/shard_map/ppermute | solution.py:62
  188.0 20.6 %collective-permute-start.50 = (bf16[128,1024]{1,0:T(8,128)(2,1)S(1)}, bf16[128,1024]{1,0:T(8,128)(2,1)}, u32[]{:S(2)}, u32[]{:S(2)}) collective-permute-start(bf16[128,1024]{1,0:T(8,128)(2,1)S(1)} %collective-permute-done.43.refs_7_), channel_id=1, source_target_pairs={{0,1},{1,0},{2,3},{3,2},{4,5},{5,4},{6,7},{7,6},{8,9},{9,8},{10,11... | collective-permute-start | bytes 786440 | tf_op jit(solution)/shard_map/ppermute | solution.py:62
  188.5 20.1 %collective-permute-start.51 = (bf16[128,1024]{1,0:T(8,128)(2,1)S(1)}, bf16[128,1024]{1,0:T(8,128)(2,1)}, u32[]{:S(2)}, u32[]{:S(2)}) collective-permute-start(bf16[128,1024]{1,0:T(8,128)(2,1)S(1)} %collective-permute-done.44.refs_8_), channel_id=1, source_target_pairs={{0,1},{1,0},{2,3},{3,2},{4,5},{5,4},{6,7},{7,6},{8,9},{9,8},{10,11... | collective-permute-start | bytes 786440 | tf_op jit(solution)/shard_map/ppermute | solution.py:62
  188.6 20.0 %collective-permute-start.52 = (bf16[128,1024]{1,0:T(8,128)(2,1)S(1)}, bf16[128,1024]{1,0:T(8,128)(2,1)}, u32[]{:S(2)}, u32[]{:S(2)}) collective-permute-start(bf16[128,1024]{1,0:T(8,128)(2,1)S(1)} %collective-permute-done.45.refs_9_), channel_id=1, source_target_pairs={{0,1},{1,0},{2,3},{3,2},{4,5},{5,4},{6,7},{7,6},{8,9},{9,8},{10,11... | collective-permute-start | bytes 786440 | tf_op jit(solution)/shard_map/ppermute | solution.py:62
  190.0 18.6 %collective-permute-start.53 = (bf16[128,1024]{1,0:T(8,128)(2,1)S(1)}, bf16[128,1024]{1,0:T(8,128)(2,1)}, u32[]{:S(2)}, u32[]{:S(2)}) collective-permute-start(bf16[128,1024]{1,0:T(8,128)(2,1)S(1)} %collective-permute-done.46.refs_10_), channel_id=1, source_target_pairs={{0,1},{1,0},{2,3},{3,2},{4,5},{5,4},{6,7},{7,6},{8,9},{9,8},{10,11... | collective-permute-start | bytes 786440 | tf_op jit(solution)/shard_map/ppermute | solution.py:62
  208.5 9.5 %collective-permute-start.74 = (bf16[4,128,1024]{2,1,0:T(8,128)(2,1)}, bf16[4,128,1024]{2,1,0:T(8,128)(2,1)S(1)}, u32[]{:S(2)}, u32[]{:S(2)}) collective-permute-start(bf16[4,128,1024]{2,1,0:T(8,128)(2,1)} %get-tuple-element.45), channel_id=1, source_target_pairs={{0,1},{1,0},{2,3},{3,2},{4,5},{5,4},{6,7},{7,6},{8,9},{9,8},{10,11... | collective-permute-start | bytes 3145736 | tf_op jit(solution)/shard_map/ppermute | solution.py:62
  221.5 8.0 %collective-permute-start.78 = (bf16[128,1024]{1,0:T(8,128)(2,1)}, bf16[128,1024]{1,0:T(8,128)(2,1)S(1)}, u32[]{:S(2)}, u32[]{:S(2)}) collective-permute-start(bf16[128,1024]{1,0:T(8,128)(2,1)} %get-tuple-element.47), channel_id=1, source_target_pairs={{6,4},{7,5},{14,12},{15,13},{22,20},{23,21},{30,28},{31,29}} | collective-permute-start | bytes 786440 | tf_op jit(solution)/shard_map/ppermute | solution.py:66
  222.3 8.3 %collective-permute-start.75 = (bf16[128,1024]{1,0:T(8,128)(2,1)}, bf16[128,1024]{1,0:T(8,128)(2,1)S(1)}, u32[]{:S(2)}, u32[]{:S(2)}) collective-permute-start(bf16[128,1024]{1,0:T(8,128)(2,1)} %get-tuple-element.49), channel_id=1, source_target_pairs={{0,2},{1,3},{8,10},{9,11},{16,18},{17,19},{24,26},{25,27}} | collective-permute-start | bytes 786440 | tf_op jit(solution)/shard_map/ppermute | solution.py:66
  227.4 8.9 %collective-permute-start.55 = (bf16[128,1024]{1,0:T(8,128)(2,1)}, bf16[128,1024]{1,0:T(8,128)(2,1)S(1)}, u32[]{:S(2)}, u32[]{:S(2)}) collective-permute-start(bf16[128,1024]{1,0:T(8,128)(2,1)} %get-tuple-element.39), channel_id=1, source_target_pairs={{0,2},{1,3},{8,10},{9,11},{16,18},{17,19},{24,26},{25,27}} | collective-permute-start | bytes 786440 | tf_op jit(solution)/shard_map/ppermute | solution.py:66
  230.7 12.2 %collective-permute-start.76 = (bf16[128,1024]{1,0:T(8,128)(2,1)S(1)}, bf16[128,1024]{1,0:T(8,128)(2,1)S(1)}, u32[]{:S(2)}, u32[]{:S(2)}) collective-permute-start(bf16[128,1024]{1,0:T(8,128)(2,1)S(1)} %get-tuple-element.53), channel_id=1, source_target_pairs={{0,2},{1,3},{2,4},{3,5},{8,10},{9,11},{10,12},{11,13},{16,18},{17,... | collective-permute-start | bytes 786440 | tf_op jit(solution)/shard_map/ppermute | solution.py:66
  235.4 12.2 %collective-permute-start.79 = (bf16[128,1024]{1,0:T(8,128)(2,1)S(1)}, bf16[128,1024]{1,0:T(8,128)(2,1)S(1)}, u32[]{:S(2)}, u32[]{:S(2)}) collective-permute-start(bf16[128,1024]{1,0:T(8,128)(2,1)S(1)} %get-tuple-element.52), channel_id=1, source_target_pairs={{4,2},{5,3},{6,4},{7,5},{12,10},{13,11},{14,12},{15,13},{20,18},{2... | collective-permute-start | bytes 786440 | tf_op jit(solution)/shard_map/ppermute | solution.py:66
  237.3 11.7 %collective-permute-start.59 = (bf16[128,1024]{1,0:T(8,128)(2,1)S(1)}, bf16[128,1024]{1,0:T(8,128)(2,1)S(1)}, u32[]{:S(2)}, u32[]{:S(2)}) collective-permute-start(bf16[128,1024]{1,0:T(8,128)(2,1)S(1)} %get-tuple-element.55), channel_id=1, source_target_pairs={{4,2},{5,3},{6,4},{7,5},{12,10},{13,11},{14,12},{15,13},{20,18},{2... | collective-permute-start | bytes 786440 | tf_op jit(solution)/shard_map/ppermute | solution.py:66
  238.0 12.4 %collective-permute-start.56 = (bf16[128,1024]{1,0:T(8,128)(2,1)S(1)}, bf16[128,1024]{1,0:T(8,128)(2,1)S(1)}, u32[]{:S(2)}, u32[]{:S(2)}) collective-permute-start(bf16[128,1024]{1,0:T(8,128)(2,1)S(1)} %get-tuple-element.54), channel_id=1, source_target_pairs={{0,2},{1,3},{2,4},{3,5},{8,10},{9,11},{10,12},{11,13},{16,18},{17,... | collective-permute-start | bytes 786440 | tf_op jit(solution)/shard_map/ppermute | solution.py:66
  243.0 12.6 %collective-permute-start.77 = (bf16[128,1024]{1,0:T(8,128)(2,1)S(1)}, bf16[128,1024]{1,0:T(8,128)(2,1)S(1)}, u32[]{:S(2)}, u32[]{:S(2)}) collective-permute-start(bf16[128,1024]{1,0:T(8,128)(2,1)S(1)} %add.58), channel_id=1, source_target_pairs={{0,2},{1,3},{2,4},{3,5},{4,6},{5,7},{8,10},{9,11},{10,12},{11,13},... | collective-permute-start | bytes 786440 | tf_op jit(solution)/shard_map/ppermute | solution.py:66
  247.7 10.9 %collective-permute-start.80 = (bf16[128,1024]{1,0:T(8,128)(2,1)S(1)}, bf16[128,1024]{1,0:T(8,128)(2,1)S(1)}, u32[]{:S(2)}, u32[]{:S(2)}) collective-permute-start(bf16[128,1024]{1,0:T(8,128)(2,1)S(1)} %add.60), channel_id=1, source_target_pairs={{2,0},{3,1},{4,2},{5,3},{6,4},{7,5},{10,8},{11,9},{12,10},{13,11},... | collective-permute-start | bytes 786440 | tf_op jit(solution)/shard_map/ppermute | solution.py:66
  249.1 25.7 %collective-permute-start.60 = (bf16[128,1024]{1,0:T(8,128)(2,1)S(1)}, bf16[128,1024]{1,0:T(8,128)(2,1)S(1)}, u32[]{:S(2)}, u32[]{:S(2)}) collective-permute-start(bf16[128,1024]{1,0:T(8,128)(2,1)S(1)} %add.55), channel_id=1, source_target_pairs={{2,0},{3,1},{4,2},{5,3},{6,4},{7,5},{10,8},{11,9},{12,10},{13,11},... | collective-permute-start | bytes 786440 | tf_op jit(solution)/shard_map/ppermute | solution.py:66
  250.5 24.3 %collective-permute-start.57 = (bf16[128,1024]{1,0:T(8,128)(2,1)S(1)}, bf16[128,1024]{1,0:T(8,128)(2,1)S(1)}, u32[]{:S(2)}, u32[]{:S(2)}) collective-permute-start(bf16[128,1024]{1,0:T(8,128)(2,1)S(1)} %add.52), channel_id=1, source_target_pairs={{0,2},{1,3},{2,4},{3,5},{4,6},{5,7},{8,10},{9,11},{10,12},{11,13},... | collective-permute-start | bytes 786440 | tf_op jit(solution)/shard_map/ppermute | solution.py:66
  (81 other events, 1707.3 us)

commit v2 on v1

--- a/solution.py
+++ b/solution.py
@@ -95,6 +95,20 @@
     return [blocks[0], up, down]
 
 
+def across(blocks):
+    length = line_length()
+    groups = [[CORES * chip + core for chip in range(length)] for core in range(CORES)]
+    return lax.all_to_all(
+        blocks, "expert", split_axis=0, concat_axis=0, axis_index_groups=groups, tiled=True
+    )
+
+
+def spread(value):
+    copies = jnp.broadcast_to(value[None], (line_length(),) + value.shape)
+    mine = across(copies)
+    return [mine, swapped(mine)]
+
+
 def entry_chips(hops, chip):
     length = line_length()
     listing = [(None, chip)]
@@ -124,6 +138,23 @@
                 run()
             else:
                 pl.when(valid)(run)
+
+
+def line_copies(refs, target, sems, rows, chip, core, act):
+    for side, ref in enumerate(refs):
+        for origin in range(ref.shape[0]):
+            owner = CORES * origin + (core if side == 0 else 1 - core)
+            start = pl.multiple_of(owner * rows, rows)
+            act(
+                pltpu.make_async_copy(
+                    ref.at[origin], target.at[pl.ds(start, rows), :], sems.at[side, origin]
+                )
+            )
+
+
+def fetch_line(*args):
+    line_copies(*args, lambda copy: copy.start())
+    line_copies(*args, lambda copy: copy.wait())
 
 
 def start_copies(*args):
@@ -259,15 +290,11 @@
     return jnp.sum(jnp.where(hit, gates, 0.0), axis=-1, keepdims=True)
 
 
-def cotangent_kernel(count, rows, width, expert_count, *refs):
-    place, down_ref = refs[:2]
-    cot_refs = refs[2 : 2 + count]
-    act_ref, gate_ref = refs[2 + count : 4 + count]
-    cot, sems = refs[4 + count :]
+def cotangent_kernel(rows, width, expert_count, *refs):
+    place, down_ref, mine, other, act_ref, gate_ref, cot, sems = refs
     chip, core = place[0], place[1]
     me = CORES * chip + core
-    start_copies(cot_refs, cot, sems, rows, chip, core)
-    wait_copies(cot_refs, cot, sems, rows, chip, core)
+    fetch_line((mine, other), cot, sems, rows, chip, core)
     chunk = 2 * rows
 
     def step(index, carry):
@@ -296,23 +323,19 @@
     return index * chunk if isinstance(index, int) else pl.multiple_of(index * chunk, chunk)
 
 
-def give_back(result, mine_ref, other_ref, rows, chip, core):
-    length = mine_ref.shape[0]
-    for j in range(length):
-        origin = lax.rem(chip + j, length)
+def give_back(result, mine_ref, other_ref, rows, core):
+    for owner in range(mine_ref.shape[0]):
         for out_ref, side in ((mine_ref, core), (other_ref, 1 - core)):
-            start = pl.multiple_of((CORES * origin + side) * rows, rows)
-            out_ref[j] = result[pl.ds(start, rows), :]
-
-
-def expert_backward_kernel(count, rows, *refs):
+            start = pl.multiple_of((CORES * owner + side) * rows, rows)
+            out_ref[owner] = result[pl.ds(start, rows), :]
+
+
+def expert_backward_kernel(rows, *refs):
     place, up_ref, act_ref = refs[:3]
-    row_refs = refs[3 : 3 + count]
-    mine_ref, other_ref = refs[3 + count : 5 + count]
-    tokens, result, sems = refs[5 + count :]
-    chip, core = place[0], place[1]
-    start_copies(row_refs, tokens, sems, rows, chip, core)
-    wait_copies(row_refs, tokens, sems, rows, chip, core)
+    row_refs = refs[3:5]
+    mine_ref, other_ref, tokens, result, sems = refs[5:]
+    chip, core = place[0], place[1]
+    fetch_line(row_refs, tokens, sems, rows, chip, core)
     chunk = 2 * rows
 
     def step(index, carry):
@@ -328,14 +351,13 @@
         return carry
 
     each_chunk(tokens.shape[0] // chunk, step)
-    give_back(result, mine_ref, other_ref, rows, chip, core)
+    give_back(result, mine_ref, other_ref, rows, core)
 
 
 def expert_forward_kernel(count, rows, *refs):
     place, up_ref, down_ref, gate_ref = refs[:4]
     row_refs = refs[4 : 4 + count]
-    mine_ref, other_ref = refs[4 + count : 6 + count]
-    tokens, result, sems = refs[6 + count :]
+    mine_ref, other_ref, tokens, result, sems = refs[4 + count :]
     chip, core = place[0], place[1]
     start_copies(row_refs, tokens, sems, rows, chip, core)
     wait_copies(row_refs, tokens, sems, rows, chip, core)
@@ -352,25 +374,28 @@
         return carry
 
     each_chunk(tokens.shape[0] // chunk, step)
-    give_back(result, mine_ref, other_ref, rows, chip, core)
-
-
-def add_kernel(mine_ref, other_ref, *out_refs):
+    give_back(result, mine_ref, other_ref, rows, core)
+
+
+def add_kernel(mine_ref, other_ref, out_ref):
+    out_ref[...] = (mine_ref[...].astype(F32) + other_ref[...].astype(F32)).astype(BF16)
+
+
+def add_apart_kernel(place, mine_ref, other_ref, *out_refs):
     for j, out_ref in enumerate(out_refs):
-        out_ref[...] = (mine_ref[j].astype(F32) + other_ref[j].astype(F32)).astype(BF16)
-
-
-def heads_backward_kernel(count, parts, depth, *refs):
-    place, cot_ref, hidden_ref, proj_ref, gain_e, mask_ref = refs[:6]
-    part_refs = refs[6 : 6 + parts]
-    out_refs = refs[6 + parts : 6 + parts + count]
-    mixed_ref, grad_ref = refs[6 + parts + count : 8 + parts + count]
-    out_w, out_sems = refs[8 + parts + count :]
+        owner = lax.rem(place[0] + j, len(out_refs))
+        out_ref[...] = (mine_ref[owner].astype(F32) + other_ref[owner].astype(F32)).astype(BF16)
+
+
+def heads_backward_kernel(count, depth, *refs):
+    place, cot_ref, hidden_ref, proj_ref, gain_e, mask_ref, part_ref = refs[:7]
+    out_refs = refs[7 : 7 + count]
+    mixed_ref, grad_ref, out_w, out_sems = refs[7 + count :]
     chip, core = place[0], place[1]
     start_copies(out_refs, out_w, out_sems, depth, chip, core)
-    grad_moe = part_refs[0][...].astype(F32)
-    for part_ref in part_refs[1:]:
-        grad_moe = grad_moe + part_ref[...].astype(F32)
+    grad_moe = part_ref[0].astype(F32)
+    for index in range(1, part_ref.shape[0]):
+        grad_moe = grad_moe + part_ref[index].astype(F32)
     hidden = hidden_ref[...]
     rms_two = lax.rsqrt(mean_last(hidden * hidden) + EPS)
     normal_two = hidden * rms_two
@@ -422,7 +447,7 @@
 
 
 def dma(count):
-    return pltpu.SemaphoreType.DMA((count,))
+    return pltpu.SemaphoreType.DMA(count if isinstance(count, tuple) else (count,))
 
 
 def call(kernel, outs, specs, out_specs, scratch, args):
@@ -490,7 +515,7 @@
     arriving = passed_along(handoff_forward, "section", 1)
     cotangent = passed_along(relay_cotangents, "section", -1)
     gates = gate_columns(routes, gate_logits, expert_count)
-    cots = with_partner(relayed(jnp.concatenate([cotangent, gates], axis=1)))
+    cots = spread(jnp.concatenate([cotangent, gates], axis=1))
     mask = allowed_of(block_mask[:, 0])
 
     half = count // 2
@@ -528,7 +553,7 @@
         ],
         [place, sum_fwd, sum_bwd, normed, stashed_input, expert_gain, mask] + last_mix + outers,
     )
-    rows_bwd = with_partner(relayed(expert_bwd))
+    rows_bwd = spread(expert_bwd)
 
     hidden_fwd, expert_fwd = call(
         functools.partial(forward_kernel, count, depth),
@@ -541,58 +566,56 @@
     rows_fwd = with_partner(relayed(expert_fwd))
 
     grad_act, gate_fwd = call(
-        functools.partial(cotangent_kernel, count, tokens, width, expert_count),
+        functools.partial(cotangent_kernel, tokens, width, expert_count),
         (shaped((total, hidden_units), F32), shaped((total, LANES), F32)),
-        [SMEM, VMEM] + [ANY] * count,
+        [SMEM, VMEM] + [ANY] * 2,
         (VMEM,) * 2,
-        [pltpu.VMEM((total, width + LANES), BF16), dma(count)],
+        [pltpu.VMEM((total, width + LANES), BF16), dma((CORES, length))],
         [place, down_weight] + cots,
     )
 
     pair = (shaped((length, tokens, width), BF16),) * 2
 
-    def expert_scratch():
-        return [pltpu.VMEM((total, width), BF16), pltpu.VMEM((total, width), BF16), dma(count)]
-
-    def combined(mine, other):
-        blocks = call(
-            add_kernel,
-            (shaped((tokens, width), BF16),) * length,
-            [VMEM] * 2,
-            (VMEM,) * length,
-            [],
-            [mine, swapped(other)],
-        )
-        return scattered(blocks)
+    def expert_scratch(sems):
+        return [pltpu.VMEM((total, width), BF16), pltpu.VMEM((total, width), BF16), dma(sems)]
 
     mine, other = call(
-        functools.partial(expert_backward_kernel, count, tokens),
+        functools.partial(expert_backward_kernel, tokens),
         pair,
-        [SMEM, VMEM, VMEM] + [ANY] * count,
+        [SMEM, VMEM, VMEM] + [ANY] * 2,
         (VMEM,) * 2,
-        expert_scratch(),
+        expert_scratch((CORES, length)),
         [place, up_weight, grad_act] + rows_bwd,
     )
-    grad_parts = combined(mine, other)
+    grad_parts = across(call(add_kernel, pair[0], [VMEM] * 2, VMEM, [], [mine, swapped(other)]))
 
     mine, other = call(
         functools.partial(expert_forward_kernel, count, tokens),
         pair,
         [SMEM, VMEM, VMEM, VMEM] + [ANY] * count,
         (VMEM,) * 2,
-        expert_scratch(),
+        expert_scratch(count),
         [place, up_weight, down_weight, gate_fwd] + rows_fwd,
     )
-    moe_parts = combined(mine, other)
-
-    parts = len(grad_parts)
+    moe_parts = scattered(
+        call(
+            add_apart_kernel,
+            (shaped((tokens, width), BF16),) * length,
+            [SMEM] + [VMEM] * 2,
+            (VMEM,) * length,
+            [],
+            [place, mine, swapped(other)],
+        ),
+    )
+
     grad_mixed, grad_hidden = call(
-        functools.partial(heads_backward_kernel, count, parts, depth),
+        functools.partial(heads_backward_kernel, count, depth),
         (shaped((tokens, columns), BF16), shaped((tokens, width), F32)),
-        [SMEM] + [VMEM] * (5 + parts) + [ANY] * count,
+        [SMEM] + [VMEM] * 6 + [ANY] * count,
         (VMEM,) * 2,
         [pltpu.VMEM((width, width), BF16), dma(count)],
-        [place, cotangent, hidden_bwd, proj_bwd, expert_gain, mask] + grad_parts + outers,
+        [place, cotangent, hidden_bwd, proj_bwd, expert_gain, mask, grad_parts]
+        + outers,
     )
     derivative = call(
         functools.partial(entry_backward_kernel, count, depth),

time: 277 us -> 305 us (1.10)
  waiting for transfers between devices: 107 us -> 152 us
  starting transfers between devices: 87.1 us -> 64.8 us
  local copies, waits for them, and re-layouts: 5.49 us -> 11.7 us
    ppermute x42 -> x24, starting transfers between devices: 76.9 us -> 44.3 us  [hop(): return lax.ppermute(value, 'expert', chip_pairs(sources, move))]
    all_to_all x0 -> x3, waiting for transfers between devices: none -> 26.1 us  [across(): lax.all_to_all(blocks, 'expert', split_axis=0, concat_axis=0, axis_index_...]
    ppermute x42 -> x24, waiting for transfers between devices: 103 us -> 119 us  [hop(): return lax.ppermute(value, 'expert', chip_pairs(sources, move))]
    all_to_all x0 -> x3, starting transfers between devices: none -> 11 us  [across(): lax.all_to_all(blocks, 'expert', split_axis=0, concat_axis=0, axis_index_...]
    broadcast_in_dim x0 -> x2, local copies, waits for them, and re-layouts: none -> 3.45 us  [spread(): copies = jnp.broadcast_to(value[None], (line_length(),) + value.shape)]
    unnamed x129 -> x81, local copies, waits for them, and re-layouts: 5.37 us -> 8.08 us
    ppermute x37 -> x25, starting transfers between devices: 7.67 us -> 5.51 us  [swapped(): return lax.ppermute(value, 'expert', [(i, i ^ 1) for i in range(count)])]
  transfers between devices with their start and end apart: 81 -> 54, of which waited for: 23 -> 19; matrix products, arithmetic and copies ran while one was open for 3% -> 3% of each run, Pallas kernels for 24% -> 17%
where the time goes in v2:
time: 305 us; the launch traced here: 304 us
  waiting for transfers between devices  152 us (50%)
  Pallas kernels  68 us (22%)
  starting transfers between devices  64.8 us (21%)
  local copies, waits for them, and re-layouts  11.7 us (4%)
  other arithmetic  5.03 us (2%)
    ppermute x24, waiting for transfers between devices, hop(): return lax.ppermute(value, 'expert', chip_pairs(sources, move))  119 us
    pallas_call x10, Pallas kernels, call(): pl.pallas_call(kernel, out_shape=outs, in_specs=specs, out_specs=out_spec...  68 us
    ppermute x24, starting transfers between devices, hop(): return lax.ppermute(value, 'expert', chip_pairs(sources, move))  44.3 us
    all_to_all x3, waiting for transfers between devices, across(): lax.all_to_all(blocks, 'expert', split_axis=0, concat_axis=0, axis_index_...  26.1 us
    all_to_all x3, starting transfers between devices, across(): lax.all_to_all(blocks, 'expert', split_axis=0, concat_axis=0, axis_index_...  11 us
    unnamed x81, local copies, waits for them, and re-layouts  8.08 us
  transfers between devices with their start and end apart: 54, of which 19 were waited for; matrix products, arithmetic and copies ran while one was open for 3% of the time, Pallas kernels for 17%

profile of v2, /device:TPU:0, one launch (start us, length us, event | category | flops | bytes accessed | tf_op | source)
XLA Modules:
  0.0 304.0 jit_solution(16403940510644558849)
XLA Ops:
  0.6 5.9 %collective-permute-start.1 = (bf16[128,3072]{1,0:T(8,128)(2,1)}, bf16[128,3072]{1,0:T(8,128)(2,1)}, u32[]{:S(2)}, u32[]{:S(2)}) collective-permute-start(bf16[128,3072]{1,0:T(8,128)(2,1)} %bitcast.30), channel_id=1, source_target_pairs={{0,2},{1,3},{2,4},{3,5},{4,6},{5,7},{8,10},{9,11},{10,12},{11,13},... | collective-permute-start | bytes 2359304 | tf_op jit(solution)/shard_map/ppermute | solution.py:66
  6.5 1.3 collective-permute-start.2
  7.8 1.5 collective-permute-start
  9.3 4.6 %collective-permute-start.14 = (bf16[128,1024]{1,0:T(8,128)(2,1)}, bf16[128,1024]{1,0:T(8,128)(2,1)S(1)}, u32[]{:S(2)}, u32[]{:S(2)}) collective-permute-start(bf16[128,1024]{1,0:T(8,128)(2,1)} %bitcast.35), channel_id=1, source_target_pairs={{0,2},{1,3},{2,4},{3,5},{4,6},{5,7},{8,10},{9,11},{10,12},{11,13},... | collective-permute-start | bytes 786440 | tf_op jit(solution)/shard_map/ppermute | solution.py:66
  13.9 1.3 collective-permute-start.15
  15.2 1.5 collective-permute-done.refs_1_
  16.7 11.6 %collective-permute-done.14.refs_12_.refs_6_.refs_8_ = bf16[128,1024]{1,0:T(8,128)(2,1)S(1)} collective-permute-done((bf16[128,1024]{1,0:T(8,128)(2,1)}, bf16[128,1024]{1,0:T(8,128)(2,1)S(1)}, u32[]{:S(2)}, u32[]{:S(2)}) %collective-permute-start.14) | collective-permute-done | bytes 262176 | tf_op jit(solution)/shard_map/ppermute | solution.py:66
  28.3 2.4 collective-permute-start.27
  30.8 2.5 collective-permute-done.15.refs_13_.refs_7_.refs_9_
  33.9 0.7 add_divide_fusion
  34.6 1.6 collective-permute-start.3
  36.2 1.3 collective-permute-start.4
  37.5 0.7 select_reduce_fusion
  38.3 1.3 collective-permute-start.17
  40.3 24.9 %collective-permute-done.17.refs_15_.refs_9_.refs_11_ = bf16[128,1024]{1,0:T(8,128)(2,1)} collective-permute-done((bf16[128,1024]{1,0:T(8,128)(2,1)S(1)}, bf16[128,1024]{1,0:T(8,128)(2,1)}, u32[]{:S(2)}, u32[]{:S(2)}) %collective-permute-start.17) | collective-permute-done | bytes 262176 | tf_op jit(solution)/shard_map/ppermute | solution.py:66
  65.2 0.7 collective-permute-start.18
  66.5 1.2 broadcast_in_dim.18
  67.7 3.5 %all-to-all-start = ((bf16[4,128,1152]{2,1,0:T(8,128)(2,1)}), bf16[4,128,1152]{2,1,0:T(8,128)(2,1)S(1)}, u32[]{:S(2)}, u32[]{:S(2)}) async-start(bf16[4,128,1152]{2,1,0:T(8,128)(2,1)} %broadcast_in_dim.18), calls=%async_computation | async-start | bytes 2359296 | tf_op jit(solution)/shard_map/all_to_all | solution.py:101
  71.3 1.3 collective-permute-start.19
  72.6 0.7 collective-permute-start.10
  73.4 1.3 collective-permute-start.11
  74.7 19.7 %collective-permute-done.19.refs_17_.refs_11_.refs_13_ = bf16[128,1024]{1,0:T(8,128)(2,1)S(1)} collective-permute-done((bf16[128,1024]{1,0:T(8,128)(2,1)}, bf16[128,1024]{1,0:T(8,128)(2,1)S(1)}, u32[]{:S(2)}, u32[]{:S(2)}) %collective-permute-start.19) | collective-permute-done | bytes 262176 | tf_op jit(solution)/shard_map/ppermute | solution.py:66
  94.3 1.7 collective-permute-done.23.refs_21_.refs_15_.refs_17_
  97.1 18.4 %collective-permute-done.11.refs_8_.refs_11_ = bf16[128,3072]{1,0:T(8,128)(2,1)S(1)} collective-permute-done((bf16[128,3072]{1,0:T(8,128)(2,1)}, bf16[128,3072]{1,0:T(8,128)(2,1)S(1)}, u32[]{:S(2)}, u32[]{:S(2)}) %collective-permute-start.11) | collective-permute-done | bytes 786464 | tf_op jit(solution)/shard_map/ppermute | solution.py:66
  117.3 1.1 fusion.refs_6_.refs_4_.refs_5_
  118.3 7.6 %shard_map.131 = (f32[128,3072]{1,0:T(8,128)}, f32[128,3072]{1,0:T(8,128)}, bf16[256,1024]{1,0:T(8,128)(2,1)}) custom-call(s32[2]{0:T(128)} %pad_add_fusion.refs_0_.place, bf16[128,1024]{1,0:T(8,128)(2,1)} %copy-done.19, bf16[128,1024]{1,0:T(8,128)(2,1)} %refs_1_.1, f32[1,1024]{1,0:T(1,128)} %refs_4_.5, bf16[128,3072]{1,0:T(8,128)(2,1)} %bitcast.33, ...), custom_call_target="tpu_custom_call" | custom-call | tf_op jit(solution)/shard_map/pallas_call | solution.py:454
  126.9 8.9 %shard_map.132 = (f32[128,3072]{1,0:T(8,128)}, f32[128,3072]{1,0:T(8,128)}, f32[128,1024]{1,0:T(8,128)}, bf16[128,1024]{1,0:T(8,128)(2,1)}) custom-call(s32[2]{0:T(128)} %pad_add_fusion.refs_0_.place, f32[128,3072]{1,0:T(8,128)} %get-tuple-element.23.refs_1_, f32[128,3072]{1,0:T(8,128)} %get-tuple-element.24.refs_2_, ...), custom_call_target="tpu_custom_call" | custom-call | tf_op jit(solution)/shard_map/pallas_call | solution.py:454
  135.8 2.3 broadcast_in_dim.19
  138.1 3.5 %all-to-all-start.1 = ((bf16[4,128,1024]{2,1,0:T(8,128)(2,1)}), bf16[4,128,1024]{2,1,0:T(8,128)(2,1)S(1)}, u32[]{:S(2)}, u32[]{:S(2)}) async-start(bf16[4,128,1024]{2,1,0:T(8,128)(2,1)} %broadcast_in_dim.19), calls=%async_computation.1 | async-start | bytes 2097152 | tf_op jit(solution)/shard_map/all_to_all | solution.py:101
  141.8 26.1 %all-to-all-done.1.refs_3_ = bf16[4,128,1024]{2,1,0:T(8,128)(2,1)S(1)} async-done(((bf16[4,128,1024]{2,1,0:T(8,128)(2,1)}), bf16[4,128,1024]{2,1,0:T(8,128)(2,1)S(1)}, u32[]{:S(2)}, u32[]{:S(2)}) %all-to-all-start.1) | async-done | bytes 1048608 | tf_op jit(solution)/shard_map/all_to_all | solution.py:101
  167.8 5.5 %shard_map.133 = (f32[128,1024]{1,0:T(8,128)}, bf16[128,1024]{1,0:T(8,128)(2,1)}) custom-call(s32[2]{0:T(128)} %pad_add_fusion.refs_0_.place, bf16[128,1024]{1,0:T(8,128)(2,1)} %copy-done.19, f32[128,3072]{1,0:T(8,128)} %get-tuple-element.26.refs_2_, f32[1,1024]{1,0:T(1,128)} %refs_4_.4, f32[2,128,128]{2,1,0:T(8,128)} %fusion.refs_6_.refs_4_.refs_5_, ...), custom_call_target="tpu_custom_call" | custom-call | tf_op jit(solution)/shard_map/pallas_call | solution.py:454
  173.3 1.3 collective-permute-start.29
  174.6 1.3 collective-permute-start.30
  175.9 5.1 %collective-permute-done.29.refs_5_ = bf16[128,1024]{1,0:T(8,128)(2,1)S(1)} collective-permute-done((bf16[128,1024]{1,0:T(8,128)(2,1)}, bf16[128,1024]{1,0:T(8,128)(2,1)S(1)}, u32[]{:S(2)}, u32[]{:S(2)}) %collective-permute-start.29) | collective-permute-done | bytes 262176 | tf_op jit(solution)/shard_map/ppermute | solution.py:66
  181.7 3.3 %collective-permute-done.30.refs_6_ = bf16[128,1024]{1,0:T(8,128)(2,1)S(1)} collective-permute-done((bf16[128,1024]{1,0:T(8,128)(2,1)}, bf16[128,1024]{1,0:T(8,128)(2,1)S(1)}, u32[]{:S(2)}, u32[]{:S(2)}) %collective-permute-start.30) | collective-permute-done | bytes 262176 | tf_op jit(solution)/shard_map/ppermute | solution.py:66
  185.1 1.3 collective-permute-start.32
  187.0 7.4 %collective-permute-done.32.refs_8_ = bf16[128,1024]{1,0:T(8,128)(2,1)S(1)} collective-permute-done((bf16[128,1024]{1,0:T(8,128)(2,1)S(1)}, bf16[128,1024]{1,0:T(8,128)(2,1)S(1)}, u32[]{:S(2)}, u32[]{:S(2)}) %collective-permute-start.32) | collective-permute-done | bytes 262176 | tf_op jit(solution)/shard_map/ppermute | solution.py:66
  195.1 1.0 copy-done.22
  196.1 1.5 collective-permute-start.34
  197.6 2.6 copy.25
  200.1 6.6 %shard_map.134 = (f32[1024,704]{1,0:T(8,128)}, f32[1024,128]{1,0:T(8,128)}) custom-call(s32[2]{0:T(128)} %pad_add_fusion.refs_0_.place, bf16[704,1024]{1,0:T(8,128)(2,1)} %bitcast.28, bf16[4,128,1152]{2,1,0:T(8,128)(2,1)} %copy-done, bf16[4,128,1152]{2,1,0:T(8,128)(2,1)} %collective-permute-done.28.refs_3_), custom_call_target="tpu_custom_call" | custom-call | tf_op jit(solution)/shard_map/pallas_call | solution.py:454
  206.7 9.7 %shard_map.137 = (bf16[4,128,1024]{2,1,0:T(8,128)(2,1)}, bf16[4,128,1024]{2,1,0:T(8,128)(2,1)}) custom-call(s32[2]{0:T(128)} %pad_add_fusion.refs_0_.place, bf16[1024,704]{1,0:T(8,128)(2,1)} %bitcast.26, f32[1024,704]{1,0:T(8,128)} %get-tuple-element.38.refs_2_, bf16[4,128,1024]{2,1,0:T(8,128)(2,1)} %copy-done.2, bf16[4,128,1024]{2,1,0:T(8,128)(2,1)} %copy-done.22), custom_call_target="tpu_custom_call" | custom-call | tf_op jit(solution)/shard_map/pallas_call | solution.py:454
  217.8 2.0 collective-permute-done.38.refs_14_
  221.6 8.7 %shard_map.135 = (bf16[4,128,1024]{2,1,0:T(8,128)(2,1)}, bf16[4,128,1024]{2,1,0:T(8,128)(2,1)}) custom-call(s32[2]{0:T(128)} %pad_add_fusion.refs_0_.place, bf16[1024,704]{1,0:T(8,128)(2,1)} %bitcast.27, bf16[704,1024]{1,0:T(8,128)(2,1)} %bitcast.29, f32[1024,128]{1,0:T(8,128)} %get-tuple-element.28.refs_3_, bf16[128,1024]{1,0:T(8,128)(2,1)} %get-tuple-element.29.refs_4_, ...), custom_call_target="tpu_custom_call" | custom-call | tf_op jit(solution)/shard_map/pallas_call | solution.py:454
  230.5 1.0 copy-done.18
  231.5 2.8 shard_map.138
  234.3 3.9 %all-to-all-start.2 = ((bf16[4,128,1024]{2,1,0:T(8,128)(2,1)}), bf16[4,128,1024]{2,1,0:T(8,128)(2,1)S(1)}, u32[]{:S(2)}, u32[]{:S(2)}) async-start(bf16[4,128,1024]{2,1,0:T(8,128)(2,1)} %shard_map.138), calls=%async_computation.2 | async-start | bytes 2097152 | tf_op jit(solution)/shard_map/all_to_all | solution.py:101
  238.3 1.0 copy-done.20
  239.2 2.7 shard_map.136
  242.0 4.3 %collective-permute-start.43 = (bf16[128,1024]{1,0:T(8,128)(2,1)}, bf16[128,1024]{1,0:T(8,128)(2,1)S(1)}, u32[]{:S(2)}, u32[]{:S(2)}) collective-permute-start(bf16[128,1024]{1,0:T(8,128)(2,1)} %get-tuple-element.35), channel_id=1, source_target_pairs={{0,2},{1,3},{8,10},{9,11},{16,18},{17,19},{24,26},{25,27}} | collective-permute-start | bytes 786440 | tf_op jit(solution)/shard_map/ppermute | solution.py:66
  247.0 14.6 %collective-permute-done.43 = bf16[128,1024]{1,0:T(8,128)(2,1)S(1)} collective-permute-done((bf16[128,1024]{1,0:T(8,128)(2,1)}, bf16[128,1024]{1,0:T(8,128)(2,1)S(1)}, u32[]{:S(2)}, u32[]{:S(2)}) %collective-permute-start.43) | collective-permute-done | bytes 262176 | tf_op jit(solution)/shard_map/ppermute | solution.py:66
  261.6 1.0 fusion.20
  262.6 4.3 %collective-permute-start.44 = (bf16[128,1024]{1,0:T(8,128)(2,1)S(1)}, bf16[128,1024]{1,0:T(8,128)(2,1)S(1)}, u32[]{:S(2)}, u32[]{:S(2)}) collective-permute-start(bf16[128,1024]{1,0:T(8,128)(2,1)S(1)} %get-tuple-element.44), channel_id=1, source_target_pairs={{0,2},{1,3},{2,4},{3,5},{8,10},{9,11},{10,12},{11,13},{16,18},{17,... | collective-permute-start | bytes 786440 | tf_op jit(solution)/shard_map/ppermute | solution.py:66
  266.9 0.7 collective-permute-start.47
  267.6 4.5 %collective-permute-done.44 = bf16[128,1024]{1,0:T(8,128)(2,1)S(1)} collective-permute-done((bf16[128,1024]{1,0:T(8,128)(2,1)S(1)}, bf16[128,1024]{1,0:T(8,128)(2,1)S(1)}, u32[]{:S(2)}, u32[]{:S(2)}) %collective-permute-start.44) | collective-permute-done | bytes 262176 | tf_op jit(solution)/shard_map/ppermute | solution.py:66
  272.1 1.0 add.40
  273.1 4.4 %collective-permute-start.45 = (bf16[128,1024]{1,0:T(8,128)(2,1)S(1)}, bf16[128,1024]{1,0:T(8,128)(2,1)S(1)}, u32[]{:S(2)}, u32[]{:S(2)}) collective-permute-start(bf16[128,1024]{1,0:T(8,128)(2,1)S(1)} %add.40), channel_id=1, source_target_pairs={{0,2},{1,3},{2,4},{3,5},{4,6},{5,7},{8,10},{9,11},{10,12},{11,13},... | collective-permute-start | bytes 786440 | tf_op jit(solution)/shard_map/ppermute | solution.py:66
  277.6 1.5 collective-permute-start.48
  279.1 2.7 collective-permute-done.45
  281.9 4.6 %collective-permute-done.48 = bf16[128,1024]{1,0:T(8,128)(2,1)S(1)} collective-permute-done((bf16[128,1024]{1,0:T(8,128)(2,1)S(1)}, bf16[128,1024]{1,0:T(8,128)(2,1)S(1)}, u32[]{:S(2)}, u32[]{:S(2)}) %collective-permute-start.48) | collective-permute-done | bytes 262176 | tf_op jit(solution)/shard_map/ppermute | solution.py:66
  286.5 0.8 add_convert_fusion
  287.3 1.0 copy-done.1
  288.3 8.2 %shard_map.139 = (bf16[128,3072]{1,0:T(8,128)(2,1)}, f32[128,1024]{1,0:T(8,128)}) custom-call(s32[2]{0:T(128)} %pad_add_fusion.refs_0_.place, bf16[128,1024]{1,0:T(8,128)(2,1)} %copy-done.21, f32[128,1024]{1,0:T(8,128)} %get-tuple-element.36.refs_2_, f32[128,3072]{1,0:T(8,128)} %get-tuple-element.37.refs_3_, f32[1,1024]{1,0:T(1,128)} %refs_4_.4, ...), custom_call_target="tpu_custom_call" | custom-call | tf_op jit(solution)/shard_map/pallas_call | solution.py:454
  296.5 7.3 %shard_map.140 = bf16[128,1024]{1,0:T(8,128)(2,1)} custom-call(s32[2]{0:T(128)} %pad_add_fusion.refs_0_.place, bf16[128,1024]{1,0:T(8,128)(2,1)} %refs_1_.1, bf16[128,3072]{1,0:T(8,128)(2,1)} %get-tuple-element.42.refs_2_, f32[128,1024]{1,0:T(8,128)} %get-tuple-element.43.refs_3_, f32[1,1024]{1,0:T(1,128)} %refs_4_.5, bf16[128,3072]{1,0:T(8,128)(2,1)} %bitcast.34, ...), custom_call_target="tpu_custom_call" | custom-call | tf_op jit(solution)/shard_map/pallas_call | solution.py:454
  (152 shorter events, 11.9 us)
Async XLA Ops:
  0.6 34.0 %collective-permute-start.1 = (bf16[128,3072]{1,0:T(8,128)(2,1)}, bf16[128,3072]{1,0:T(8,128)(2,1)}, u32[]{:S(2)}, u32[]{:S(2)}) collective-permute-start(bf16[128,3072]{1,0:T(8,128)(2,1)} %bitcast.30), channel_id=1, source_target_pairs={{0,2},{1,3},{2,4},{3,5},{4,6},{5,7},{8,10},{9,11},{10,12},{11,13},... | collective-permute-start | bytes 2359304 | tf_op jit(solution)/shard_map/ppermute | solution.py:66
  6.5 29.7 %collective-permute-start.2 = (bf16[128,3072]{1,0:T(8,128)(2,1)}, bf16[128,3072]{1,0:T(8,128)(2,1)S(1)}, u32[]{:S(2)}, u32[]{:S(2)}) collective-permute-start(bf16[128,3072]{1,0:T(8,128)(2,1)} %bitcast.31), channel_id=1, source_target_pairs={{2,0},{3,1},{4,2},{5,3},{6,4},{7,5},{10,8},{11,9},{12,10},{13,11},... | collective-permute-start | bytes 2359304 | tf_op jit(solution)/shard_map/ppermute | solution.py:66
  7.8 8.9 %collective-permute-start = (bf16[128,1024]{1,0:T(8,128)(2,1)}, bf16[128,1024]{1,0:T(8,128)(2,1)S(1)}, u32[]{:S(2)}, u32[]{:S(2)}) collective-permute-start(bf16[128,1024]{1,0:T(8,128)(2,1)} %param.12), channel_id=1, source_target_pairs={{0,8},{8,16},{16,24},{24,0},{1,9},{9,17},{17,25},{25,1},{2,10},{10... | collective-permute-start | bytes 786440 | tf_op jit(solution)/shard_map/ppermute | solution.py:45
  9.3 19.0 %collective-permute-start.14 = (bf16[128,1024]{1,0:T(8,128)(2,1)}, bf16[128,1024]{1,0:T(8,128)(2,1)S(1)}, u32[]{:S(2)}, u32[]{:S(2)}) collective-permute-start(bf16[128,1024]{1,0:T(8,128)(2,1)} %bitcast.35), channel_id=1, source_target_pairs={{0,2},{1,3},{2,4},{3,5},{4,6},{5,7},{8,10},{9,11},{10,12},{11,13},... | collective-permute-start | bytes 786440 | tf_op jit(solution)/shard_map/ppermute | solution.py:66
  13.9 19.3 %collective-permute-start.15 = (bf16[128,1024]{1,0:T(8,128)(2,1)}, bf16[128,1024]{1,0:T(8,128)(2,1)S(1)}, u32[]{:S(2)}, u32[]{:S(2)}) collective-permute-start(bf16[128,1024]{1,0:T(8,128)(2,1)} %bitcast.36), channel_id=1, source_target_pairs={{2,0},{3,1},{4,2},{5,3},{6,4},{7,5},{10,8},{11,9},{12,10},{13,11},... | collective-permute-start | bytes 786440 | tf_op jit(solution)/shard_map/ppermute | solution.py:66
  16.7 21.4 %collective-permute-start.20 = (bf16[128,1024]{1,0:T(8,128)(2,1)}, bf16[128,1024]{1,0:T(8,128)(2,1)S(1)}, u32[]{:S(2)}, u32[]{:S(2)}) collective-permute-start(bf16[128,1024]{1,0:T(8,128)(2,1)} %bitcast.37), channel_id=1, source_target_pairs={{0,1},{1,0},{2,3},{3,2},{4,5},{5,4},{6,7},{7,6},{8,9},{9,8},{10,11... | collective-permute-start | bytes 786440 | tf_op jit(solution)/shard_map/ppermute | solution.py:62
  28.3 39.4 %copy-start.6 = (bf16[128,1024]{1,0:T(8,128)(2,1)}, bf16[128,1024]{1,0:T(8,128)(2,1)S(1)}, u32[]{:S(2)}) copy-start(bf16[128,1024]{1,0:T(8,128)(2,1)S(1)} %collective-permute-done.14.refs_12_.refs_6_.refs_8_) | copy-start | bytes 786436
  28.3 9.9 %collective-permute-start.27 = (bf16[128,1024]{1,0:T(8,128)(2,1)}, bf16[128,1024]{1,0:T(8,128)(2,1)S(1)}, u32[]{:S(2)}, u32[]{:S(2)}) collective-permute-start(bf16[128,1024]{1,0:T(8,128)(2,1)} %param.14), channel_id=1, source_target_pairs={{0,24},{8,0},{16,8},{24,16},{1,25},{9,1},{17,9},{25,17},{2,26},{10... | collective-permute-start | bytes 786440 | tf_op jit(solution)/shard_map/ppermute | solution.py:45
  33.2 34.5 %copy-start.7 = (bf16[128,1024]{1,0:T(8,128)(2,1)}, bf16[128,1024]{1,0:T(8,128)(2,1)S(1)}, u32[]{:S(2)}) copy-start(bf16[128,1024]{1,0:T(8,128)(2,1)S(1)} %collective-permute-done.15.refs_13_.refs_7_.refs_9_) | copy-start | bytes 786436
  33.2 6.3 %collective-permute-start.16 = (bf16[128,1024]{1,0:T(8,128)(2,1)S(1)}, bf16[128,1024]{1,0:T(8,128)(2,1)S(1)}, u32[]{:S(2)}, u32[]{:S(2)}) collective-permute-start(bf16[128,1024]{1,0:T(8,128)(2,1)S(1)} %collective-permute-done.14.refs_12_.refs_6_.refs_8_), channel_id=1, source_target_pairs={{2,4},{3,5},{4,6},{5,7},{10,12},{11,13},{12,14},{13,15},{18,20},{1... | collective-permute-start | bytes 786440 | tf_op jit(solution)/shard_map/ppermute | solution.py:66
  34.6 38.0 %collective-permute-start.3 = (bf16[128,3072]{1,0:T(8,128)(2,1)}, bf16[128,3072]{1,0:T(8,128)(2,1)}, u32[]{:S(2)}, u32[]{:S(2)}) collective-permute-start(bf16[128,3072]{1,0:T(8,128)(2,1)} %collective-permute-done.1.refs_5_.refs_6_), channel_id=1, source_target_pairs={{2,4},{3,5},{4,6},{5,7},{10,12},{11,13},{12,14},{13,15},{18,20},{1... | collective-permute-start | bytes 2359304 | tf_op jit(solution)/shard_map/ppermute | solution.py:66
  36.2 59.9 %copy-start.5 = (bf16[128,3072]{1,0:T(8,128)(2,1)}, bf16[128,3072]{1,0:T(8,128)(2,1)S(1)}, u32[]{:S(2)}) copy-start(bf16[128,3072]{1,0:T(8,128)(2,1)S(1)} %collective-permute-done.2.refs_6_.refs_7_) | copy-start | bytes 2359300
  36.2 37.2 %collective-permute-start.4 = (bf16[128,3072]{1,0:T(8,128)(2,1)S(1)}, bf16[128,3072]{1,0:T(8,128)(2,1)}, u32[]{:S(2)}, u32[]{:S(2)}) collective-permute-start(bf16[128,3072]{1,0:T(8,128)(2,1)S(1)} %collective-permute-done.2.refs_6_.refs_7_), channel_id=1, source_target_pairs={{2,0},{3,1},{4,2},{5,3},{10,8},{11,9},{12,10},{13,11},{18,16},{19,... | collective-permute-start | bytes 2359304 | tf_op jit(solution)/shard_map/ppermute | solution.py:66
  38.2 27.0 %collective-permute-start.21 = (bf16[128,1024]{1,0:T(8,128)(2,1)S(1)}, bf16[128,1024]{1,0:T(8,128)(2,1)S(1)}, u32[]{:S(2)}, u32[]{:S(2)}) collective-permute-start(bf16[128,1024]{1,0:T(8,128)(2,1)S(1)} %collective-permute-done.14.refs_12_.refs_6_.refs_8_), channel_id=1, source_target_pairs={{0,1},{1,0},{2,3},{3,2},{4,5},{5,4},{6,7},{7,6},{8,9},{9,8},{10,11... | collective-permute-start | bytes 786440 | tf_op jit(solution)/shard_map/ppermute | solution.py:62
  38.3 35.1 %copy-start.21 = (bf16[128,1024]{1,0:T(8,128)(2,1)}, bf16[128,1024]{1,0:T(8,128)(2,1)S(1)}, u32[]{:S(2)}) copy-start(bf16[128,1024]{1,0:T(8,128)(2,1)S(1)} %collective-permute-done.27.refs_1_) | copy-start | bytes 786436
  38.3 26.9 %collective-permute-start.17 = (bf16[128,1024]{1,0:T(8,128)(2,1)S(1)}, bf16[128,1024]{1,0:T(8,128)(2,1)}, u32[]{:S(2)}, u32[]{:S(2)}) collective-permute-start(bf16[128,1024]{1,0:T(8,128)(2,1)S(1)} %collective-permute-done.15.refs_13_.refs_7_.refs_9_), channel_id=1, source_target_pairs={{2,0},{3,1},{4,2},{5,3},{10,8},{11,9},{12,10},{13,11},{18,16},{19,... | collective-permute-start | bytes 786440 | tf_op jit(solution)/shard_map/ppermute | solution.py:66
  39.6 26.3 %collective-permute-start.22 = (bf16[128,1024]{1,0:T(8,128)(2,1)S(1)}, bf16[128,1024]{1,0:T(8,128)(2,1)S(1)}, u32[]{:S(2)}, u32[]{:S(2)}) collective-permute-start(bf16[128,1024]{1,0:T(8,128)(2,1)S(1)} %collective-permute-done.15.refs_13_.refs_7_.refs_9_), channel_id=1, source_target_pairs={{0,1},{1,0},{2,3},{3,2},{4,5},{5,4},{6,7},{7,6},{8,9},{9,8},{10,11... | collective-permute-start | bytes 786440 | tf_op jit(solution)/shard_map/ppermute | solution.py:62
  65.2 31.0 %collective-permute-start.5 = (bf16[128,3072]{1,0:T(8,128)(2,1)}, bf16[128,3072]{1,0:T(8,128)(2,1)}, u32[]{:S(2)}, u32[]{:S(2)}) collective-permute-start(bf16[128,3072]{1,0:T(8,128)(2,1)} %bitcast.32), channel_id=1, source_target_pairs={{0,1},{1,0},{2,3},{3,2},{4,5},{5,4},{6,7},{7,6},{8,9},{9,8},{10,11... | collective-permute-start | bytes 2359304 | tf_op jit(solution)/shard_map/ppermute | solution.py:62
  65.2 6.1 %collective-permute-start.18 = (bf16[128,1024]{1,0:T(8,128)(2,1)S(1)}, bf16[128,1024]{1,0:T(8,128)(2,1)S(1)}, u32[]{:S(2)}, u32[]{:S(2)}) collective-permute-start(bf16[128,1024]{1,0:T(8,128)(2,1)S(1)} %collective-permute-done.16.refs_14_.refs_8_.refs_10_), channel_id=1, source_target_pairs={{4,6},{5,7},{12,14},{13,15},{20,22},{21,23},{28,30},{29,31}} | collective-permute-start | bytes 786440 | tf_op jit(solution)/shard_map/ppermute | solution.py:66
  65.9 30.7 %collective-permute-start.6 = (bf16[128,3072]{1,0:T(8,128)(2,1)}, bf16[128,3072]{1,0:T(8,128)(2,1)}, u32[]{:S(2)}, u32[]{:S(2)}) collective-permute-start(bf16[128,3072]{1,0:T(8,128)(2,1)} %collective-permute-done.1.refs_5_.refs_6_), channel_id=1, source_target_pairs={{0,1},{1,0},{2,3},{3,2},{4,5},{5,4},{6,7},{7,6},{8,9},{9,8},{10,11... | collective-permute-start | bytes 2359304 | tf_op jit(solution)/shard_map/ppermute | solution.py:62
  67.7 49.6 %copy-start.39 = (s32[2,1,8,8]{3,2,1,0:T(8,128)S(1)}, s32[2,1,8,8]{3,2,1,0:T(8,128)}, u32[]{:S(2)}) copy-start(s32[2,1,8,8]{3,2,1,0:T(8,128)} %param.23) | copy-start | bytes 1540
  67.7 68.1 %all-to-all-start = ((bf16[4,128,1152]{2,1,0:T(8,128)(2,1)}), bf16[4,128,1152]{2,1,0:T(8,128)(2,1)S(1)}, u32[]{:S(2)}, u32[]{:S(2)}) async-start(bf16[4,128,1152]{2,1,0:T(8,128)(2,1)} %broadcast_in_dim.18), calls=%async_computation | async-start | bytes 2359296 | tf_op jit(solution)/shard_map/all_to_all | solution.py:101
  71.3 23.0 %collective-permute-start.19 = (bf16[128,1024]{1,0:T(8,128)(2,1)}, bf16[128,1024]{1,0:T(8,128)(2,1)S(1)}, u32[]{:S(2)}, u32[]{:S(2)}) collective-permute-start(bf16[128,1024]{1,0:T(8,128)(2,1)} %collective-permute-done.17.refs_15_.refs_9_.refs_11_), channel_id=1, source_target_pairs={{2,0},{3,1},{10,8},{11,9},{18,16},{19,17},{26,24},{27,25}} | collective-permute-start | bytes 786440 | tf_op jit(solution)/shard_map/ppermute | solution.py:66
  72.6 24.1 %collective-permute-start.10 = (bf16[128,3072]{1,0:T(8,128)(2,1)}, bf16[128,3072]{1,0:T(8,128)(2,1)S(1)}, u32[]{:S(2)}, u32[]{:S(2)}) collective-permute-start(bf16[128,3072]{1,0:T(8,128)(2,1)} %collective-permute-done.3.refs_7_.refs_8_), channel_id=1, source_target_pairs={{4,6},{5,7},{12,14},{13,15},{20,22},{21,23},{28,30},{29,31}} | collective-permute-start | bytes 2359304 | tf_op jit(solution)/shard_map/ppermute | solution.py:66
  73.4 42.1 %collective-permute-start.11 = (bf16[128,3072]{1,0:T(8,128)(2,1)}, bf16[128,3072]{1,0:T(8,128)(2,1)S(1)}, u32[]{:S(2)}, u32[]{:S(2)}) collective-permute-start(bf16[128,3072]{1,0:T(8,128)(2,1)} %collective-permute-done.4.refs_8_.refs_9_), channel_id=1, source_target_pairs={{2,0},{3,1},{10,8},{11,9},{18,16},{19,17},{26,24},{27,25}} | collective-permute-start | bytes 2359304 | tf_op jit(solution)/shard_map/ppermute | solution.py:66
  94.3 1.7 collective-permute-start.23
  96.1 19.5 %collective-permute-start.7 = (bf16[128,3072]{1,0:T(8,128)(2,1)S(1)}, bf16[128,3072]{1,0:T(8,128)(2,1)}, u32[]{:S(2)}, u32[]{:S(2)}) collective-permute-start(bf16[128,3072]{1,0:T(8,128)(2,1)S(1)} %collective-permute-done.2.refs_6_.refs_7_), channel_id=1, source_target_pairs={{0,1},{1,0},{2,3},{3,2},{4,5},{5,4},{6,7},{7,6},{8,9},{9,8},{10,11... | collective-permute-start | bytes 2359304 | tf_op jit(solution)/shard_map/ppermute | solution.py:62
  96.2 19.9 %collective-permute-start.8 = (bf16[128,3072]{1,0:T(8,128)(2,1)}, bf16[128,3072]{1,0:T(8,128)(2,1)}, u32[]{:S(2)}, u32[]{:S(2)}) collective-permute-start(bf16[128,3072]{1,0:T(8,128)(2,1)} %collective-permute-done.3.refs_7_.refs_8_), channel_id=1, source_target_pairs={{0,1},{1,0},{2,3},{3,2},{4,5},{5,4},{6,7},{7,6},{8,9},{9,8},{10,11... | collective-permute-start | bytes 2359304 | tf_op jit(solution)/shard_map/ppermute | solution.py:62
  96.6 19.6 %collective-permute-start.9 = (bf16[128,3072]{1,0:T(8,128)(2,1)}, bf16[128,3072]{1,0:T(8,128)(2,1)}, u32[]{:S(2)}, u32[]{:S(2)}) collective-permute-start(bf16[128,3072]{1,0:T(8,128)(2,1)} %collective-permute-done.4.refs_8_.refs_9_), channel_id=1, source_target_pairs={{0,1},{1,0},{2,3},{3,2},{4,5},{5,4},{6,7},{7,6},{8,9},{9,8},{10,11... | collective-permute-start | bytes 2359304 | tf_op jit(solution)/shard_map/ppermute | solution.py:62
  96.7 29.3 %collective-permute-start.12 = (bf16[128,3072]{1,0:T(8,128)(2,1)S(1)}, bf16[128,3072]{1,0:T(8,128)(2,1)}, u32[]{:S(2)}, u32[]{:S(2)}) collective-permute-start(bf16[128,3072]{1,0:T(8,128)(2,1)S(1)} %collective-permute-done.10.refs_7_.refs_10_), channel_id=1, source_target_pairs={{0,1},{1,0},{2,3},{3,2},{4,5},{5,4},{6,7},{7,6},{8,9},{9,8},{10,11... | collective-permute-start | bytes 2359304 | tf_op jit(solution)/shard_map/ppermute | solution.py:62
  115.5 10.6 %collective-permute-start.13 = (bf16[128,3072]{1,0:T(8,128)(2,1)S(1)}, bf16[128,3072]{1,0:T(8,128)(2,1)}, u32[]{:S(2)}, u32[]{:S(2)}) collective-permute-start(bf16[128,3072]{1,0:T(8,128)(2,1)S(1)} %collective-permute-done.11.refs_8_.refs_11_), channel_id=1, source_target_pairs={{0,1},{1,0},{2,3},{3,2},{4,5},{5,4},{6,7},{7,6},{8,9},{9,8},{10,11... | collective-permute-start | bytes 2359304 | tf_op jit(solution)/shard_map/ppermute | solution.py:62
  115.6 10.4 %collective-permute-start.24 = (bf16[128,1024]{1,0:T(8,128)(2,1)}, bf16[128,1024]{1,0:T(8,128)(2,1)S(1)}, u32[]{:S(2)}, u32[]{:S(2)}) collective-permute-start(bf16[128,1024]{1,0:T(8,128)(2,1)} %collective-permute-done.17.refs_15_.refs_9_.refs_11_), channel_id=1, source_target_pairs={{0,1},{1,0},{2,3},{3,2},{4,5},{5,4},{6,7},{7,6},{8,9},{9,8},{10,11... | collective-permute-start | bytes 786440 | tf_op jit(solution)/shard_map/ppermute | solution.py:62
  116.1 9.9 %collective-permute-start.25 = (bf16[128,1024]{1,0:T(8,128)(2,1)}, bf16[128,1024]{1,0:T(8,128)(2,1)S(1)}, u32[]{:S(2)}, u32[]{:S(2)}) collective-permute-start(bf16[128,1024]{1,0:T(8,128)(2,1)} %copy-done.12), channel_id=1, source_target_pairs={{0,1},{1,0},{2,3},{3,2},{4,5},{5,4},{6,7},{7,6},{8,9},{9,8},{10,11... | collective-permute-start | bytes 786440 | tf_op jit(solution)/shard_map/ppermute | solution.py:62
  116.2 9.8 %collective-permute-start.26 = (bf16[128,1024]{1,0:T(8,128)(2,1)}, bf16[128,1024]{1,0:T(8,128)(2,1)S(1)}, u32[]{:S(2)}, u32[]{:S(2)}) collective-permute-start(bf16[128,1024]{1,0:T(8,128)(2,1)} %copy-done.13), channel_id=1, source_target_pairs={{0,1},{1,0},{2,3},{3,2},{4,5},{5,4},{6,7},{7,6},{8,9},{9,8},{10,11... | collective-permute-start | bytes 786440 | tf_op jit(solution)/shard_map/ppermute | solution.py:62
  138.1 29.7 %all-to-all-start.1 = ((bf16[4,128,1024]{2,1,0:T(8,128)(2,1)}), bf16[4,128,1024]{2,1,0:T(8,128)(2,1)S(1)}, u32[]{:S(2)}, u32[]{:S(2)}) async-start(bf16[4,128,1024]{2,1,0:T(8,128)(2,1)} %broadcast_in_dim.19), calls=%async_computation.1 | async-start | bytes 2097152 | tf_op jit(solution)/shard_map/all_to_all | solution.py:101
  141.6 44.8 %collective-permute-start.28 = (bf16[4,128,1152]{2,1,0:T(8,128)(2,1)S(1)}, bf16[4,128,1152]{2,1,0:T(8,128)(2,1)}, u32[]{:S(2)}, u32[]{:S(2)}) collective-permute-start(bf16[4,128,1152]{2,1,0:T(8,128)(2,1)S(1)} %all-to-all-done.refs_2_), channel_id=1, source_target_pairs={{0,1},{1,0},{2,3},{3,2},{4,5},{5,4},{6,7},{7,6},{8,9},{9,8},{10,11... | collective-permute-start | bytes 3538952 | tf_op jit(solution)/shard_map/ppermute | solution.py:62
  167.8 27.3 %collective-permute-start.49 = (bf16[4,128,1024]{2,1,0:T(8,128)(2,1)S(1)}, bf16[4,128,1024]{2,1,0:T(8,128)(2,1)S(1)}, u32[]{:S(2)}, u32[]{:S(2)}) collective-permute-start(bf16[4,128,1024]{2,1,0:T(8,128)(2,1)S(1)} %all-to-all-done.1.refs_3_), channel_id=1, source_target_pairs={{0,1},{1,0},{2,3},{3,2},{4,5},{5,4},{6,7},{7,6},{8,9},{9,8},{10,11... | collective-permute-start | bytes 3145736 | tf_op jit(solution)/shard_map/ppermute | solution.py:62
  173.3 7.7 %collective-permute-start.29 = (bf16[128,1024]{1,0:T(8,128)(2,1)}, bf16[128,1024]{1,0:T(8,128)(2,1)S(1)}, u32[]{:S(2)}, u32[]{:S(2)}) collective-permute-start(bf16[128,1024]{1,0:T(8,128)(2,1)} %get-tuple-element.29.refs_4_), channel_id=1, source_target_pairs={{0,2},{1,3},{2,4},{3,5},{4,6},{5,7},{8,10},{9,11},{10,12},{11,13},... | collective-permute-start | bytes 786440 | tf_op jit(solution)/shard_map/ppermute | solution.py:66
  174.6 10.4 %collective-permute-start.30 = (bf16[128,1024]{1,0:T(8,128)(2,1)}, bf16[128,1024]{1,0:T(8,128)(2,1)S(1)}, u32[]{:S(2)}, u32[]{:S(2)}) collective-permute-start(bf16[128,1024]{1,0:T(8,128)(2,1)} %get-tuple-element.29.refs_4_), channel_id=1, source_target_pairs={{2,0},{3,1},{4,2},{5,3},{6,4},{7,5},{10,8},{11,9},{12,10},{13,11},... | collective-permute-start | bytes 786440 | tf_op jit(solution)/shard_map/ppermute | solution.py:66
  181.0 35.4 %copy-start.24 = (bf16[128,1024]{1,0:T(8,128)(2,1)}, bf16[128,1024]{1,0:T(8,128)(2,1)S(1)}, u32[]{:S(2)}) copy-start(bf16[128,1024]{1,0:T(8,128)(2,1)S(1)} %collective-permute-done.29.refs_5_) | copy-start | bytes 786436
  181.1 5.9 %collective-permute-start.31 = (bf16[128,1024]{1,0:T(8,128)(2,1)S(1)}, bf16[128,1024]{1,0:T(8,128)(2,1)S(1)}, u32[]{:S(2)}, u32[]{:S(2)}) collective-permute-start(bf16[128,1024]{1,0:T(8,128)(2,1)S(1)} %collective-permute-done.29.refs_5_), channel_id=1, source_target_pairs={{2,4},{3,5},{4,6},{5,7},{10,12},{11,13},{12,14},{13,15},{18,20},{1... | collective-permute-start | bytes 786440 | tf_op jit(solution)/shard_map/ppermute | solution.py:66
  185.1 31.4 %copy-start.25 = (bf16[128,1024]{1,0:T(8,128)(2,1)}, bf16[128,1024]{1,0:T(8,128)(2,1)S(1)}, u32[]{:S(2)}) copy-start(bf16[128,1024]{1,0:T(8,128)(2,1)S(1)} %collective-permute-done.30.refs_6_) | copy-start | bytes 786436
  185.1 9.4 %collective-permute-start.32 = (bf16[128,1024]{1,0:T(8,128)(2,1)S(1)}, bf16[128,1024]{1,0:T(8,128)(2,1)S(1)}, u32[]{:S(2)}, u32[]{:S(2)}) collective-permute-start(bf16[128,1024]{1,0:T(8,128)(2,1)S(1)} %collective-permute-done.30.refs_6_), channel_id=1, source_target_pairs={{2,0},{3,1},{4,2},{5,3},{10,8},{11,9},{12,10},{13,11},{18,16},{19,... | collective-permute-start | bytes 786440 | tf_op jit(solution)/shard_map/ppermute | solution.py:66
  186.4 30.1 %collective-permute-start.35 = (bf16[128,1024]{1,0:T(8,128)(2,1)}, bf16[128,1024]{1,0:T(8,128)(2,1)S(1)}, u32[]{:S(2)}, u32[]{:S(2)}) collective-permute-start(bf16[128,1024]{1,0:T(8,128)(2,1)} %get-tuple-element.29.refs_4_), channel_id=1, source_target_pairs={{0,1},{1,0},{2,3},{3,2},{4,5},{5,4},{6,7},{7,6},{8,9},{9,8},{10,11... | collective-permute-start | bytes 786440 | tf_op jit(solution)/shard_map/ppermute | solution.py:62
  186.5 30.1 %collective-permute-start.36 = (bf16[128,1024]{1,0:T(8,128)(2,1)S(1)}, bf16[128,1024]{1,0:T(8,128)(2,1)S(1)}, u32[]{:S(2)}, u32[]{:S(2)}) collective-permute-start(bf16[128,1024]{1,0:T(8,128)(2,1)S(1)} %collective-permute-done.29.refs_5_), channel_id=1, source_target_pairs={{0,1},{1,0},{2,3},{3,2},{4,5},{5,4},{6,7},{7,6},{8,9},{9,8},{10,11... | collective-permute-start | bytes 786440 | tf_op jit(solution)/shard_map/ppermute | solution.py:62
  186.9 30.2 %collective-permute-start.37 = (bf16[128,1024]{1,0:T(8,128)(2,1)S(1)}, bf16[128,1024]{1,0:T(8,128)(2,1)S(1)}, u32[]{:S(2)}, u32[]{:S(2)}) collective-permute-start(bf16[128,1024]{1,0:T(8,128)(2,1)S(1)} %collective-permute-done.30.refs_6_), channel_id=1, source_target_pairs={{0,1},{1,0},{2,3},{3,2},{4,5},{5,4},{6,7},{7,6},{8,9},{9,8},{10,11... | collective-permute-start | bytes 786440 | tf_op jit(solution)/shard_map/ppermute | solution.py:62
  194.4 22.8 %collective-permute-start.33 = (bf16[128,1024]{1,0:T(8,128)(2,1)S(1)}, bf16[128,1024]{1,0:T(8,128)(2,1)S(1)}, u32[]{:S(2)}, u32[]{:S(2)}) collective-permute-start(bf16[128,1024]{1,0:T(8,128)(2,1)S(1)} %collective-permute-done.31.refs_7_), channel_id=1, source_target_pairs={{4,6},{5,7},{12,14},{13,15},{20,22},{21,23},{28,30},{29,31}} | collective-permute-start | bytes 786440 | tf_op jit(solution)/shard_map/ppermute | solution.py:66
  196.1 21.6 %collective-permute-start.34 = (bf16[128,1024]{1,0:T(8,128)(2,1)S(1)}, bf16[128,1024]{1,0:T(8,128)(2,1)S(1)}, u32[]{:S(2)}, u32[]{:S(2)}) collective-permute-start(bf16[128,1024]{1,0:T(8,128)(2,1)S(1)} %collective-permute-done.32.refs_8_), channel_id=1, source_target_pairs={{2,0},{3,1},{10,8},{11,9},{18,16},{19,17},{26,24},{27,25}} | collective-permute-start | bytes 786440 | tf_op jit(solution)/shard_map/ppermute | solution.py:66
  216.5 14.1 %collective-permute-start.50 = (bf16[4,128,1024]{2,1,0:T(8,128)(2,1)}, bf16[4,128,1024]{2,1,0:T(8,128)(2,1)S(1)}, u32[]{:S(2)}, u32[]{:S(2)}) collective-permute-start(bf16[4,128,1024]{2,1,0:T(8,128)(2,1)} %get-tuple-element.41), channel_id=1, source_target_pairs={{0,1},{1,0},{2,3},{3,2},{4,5},{5,4},{6,7},{7,6},{8,9},{9,8},{10,11... | collective-permute-start | bytes 3145736 | tf_op jit(solution)/shard_map/ppermute | solution.py:62
  216.6 3.2 %collective-permute-start.38 = (bf16[128,1024]{1,0:T(8,128)(2,1)S(1)}, bf16[128,1024]{1,0:T(8,128)(2,1)S(1)}, u32[]{:S(2)}, u32[]{:S(2)}) collective-permute-start(bf16[128,1024]{1,0:T(8,128)(2,1)S(1)} %collective-permute-done.31.refs_7_), channel_id=1, source_target_pairs={{0,1},{1,0},{2,3},{3,2},{4,5},{5,4},{6,7},{7,6},{8,9},{9,8},{10,11... | collective-permute-start | bytes 786440 | tf_op jit(solution)/shard_map/ppermute | solution.py:62
  217.1 3.0 collective-permute-start.39
  217.2 3.3 %collective-permute-start.40 = (bf16[128,1024]{1,0:T(8,128)(2,1)S(1)}, bf16[128,1024]{1,0:T(8,128)(2,1)S(1)}, u32[]{:S(2)}, u32[]{:S(2)}) collective-permute-start(bf16[128,1024]{1,0:T(8,128)(2,1)S(1)} %collective-permute-done.33.refs_9_), channel_id=1, source_target_pairs={{0,1},{1,0},{2,3},{3,2},{4,5},{5,4},{6,7},{7,6},{8,9},{9,8},{10,11... | collective-permute-start | bytes 786440 | tf_op jit(solution)/shard_map/ppermute | solution.py:62
  217.7 3.2 %collective-permute-start.41 = (bf16[128,1024]{1,0:T(8,128)(2,1)S(1)}, bf16[128,1024]{1,0:T(8,128)(2,1)S(1)}, u32[]{:S(2)}, u32[]{:S(2)}) collective-permute-start(bf16[128,1024]{1,0:T(8,128)(2,1)S(1)} %collective-permute-done.34.refs_10_), channel_id=1, source_target_pairs={{0,1},{1,0},{2,3},{3,2},{4,5},{5,4},{6,7},{7,6},{8,9},{9,8},{10,11... | collective-permute-start | bytes 786440 | tf_op jit(solution)/shard_map/ppermute | solution.py:62
  230.3 7.9 %collective-permute-start.42 = (bf16[4,128,1024]{2,1,0:T(8,128)(2,1)}, bf16[4,128,1024]{2,1,0:T(8,128)(2,1)S(1)}, u32[]{:S(2)}, u32[]{:S(2)}) collective-permute-start(bf16[4,128,1024]{2,1,0:T(8,128)(2,1)} %get-tuple-element.31), channel_id=1, source_target_pairs={{0,1},{1,0},{2,3},{3,2},{4,5},{5,4},{6,7},{7,6},{8,9},{9,8},{10,11... | collective-permute-start | bytes 3145736 | tf_op jit(solution)/shard_map/ppermute | solution.py:62
  234.3 53.0 %all-to-all-start.2 = ((bf16[4,128,1024]{2,1,0:T(8,128)(2,1)}), bf16[4,128,1024]{2,1,0:T(8,128)(2,1)S(1)}, u32[]{:S(2)}, u32[]{:S(2)}) async-start(bf16[4,128,1024]{2,1,0:T(8,128)(2,1)} %shard_map.138), calls=%async_computation.2 | async-start | bytes 2097152 | tf_op jit(solution)/shard_map/all_to_all | solution.py:101
  241.9 35.6 %copy-start.37 = (bf16[128,1024]{1,0:T(8,128)(2,1)S(1)}, bf16[128,1024]{1,0:T(8,128)(2,1)}, u32[]{:S(2)}) copy-start(bf16[128,1024]{1,0:T(8,128)(2,1)} %get-tuple-element.35) | copy-start | bytes 786436
  242.0 44.5 %copy-start.23 = (f32[128,1024]{1,0:T(8,128)S(1)}, f32[128,1024]{1,0:T(8,128)}, u32[]{:S(2)}) copy-start(f32[128,1024]{1,0:T(8,128)} %get-tuple-element.27) | copy-start | bytes 1572868
  242.0 44.5 %copy-start.38 = (bf16[128,1024]{1,0:T(8,128)(2,1)S(1)}, bf16[128,1024]{1,0:T(8,128)(2,1)}, u32[]{:S(2)}) copy-start(bf16[128,1024]{1,0:T(8,128)(2,1)} %get-tuple-element.32) | copy-start | bytes 786436
  242.0 19.6 %collective-permute-start.43 = (bf16[128,1024]{1,0:T(8,128)(2,1)}, bf16[128,1024]{1,0:T(8,128)(2,1)S(1)}, u32[]{:S(2)}, u32[]{:S(2)}) collective-permute-start(bf16[128,1024]{1,0:T(8,128)(2,1)} %get-tuple-element.35), channel_id=1, source_target_pairs={{0,2},{1,3},{8,10},{9,11},{16,18},{17,19},{24,26},{25,27}} | collective-permute-start | bytes 786440 | tf_op jit(solution)/shard_map/ppermute | solution.py:66
  246.3 15.3 %collective-permute-start.46 = (bf16[128,1024]{1,0:T(8,128)(2,1)}, bf16[128,1024]{1,0:T(8,128)(2,1)S(1)}, u32[]{:S(2)}, u32[]{:S(2)}) collective-permute-start(bf16[128,1024]{1,0:T(8,128)(2,1)} %get-tuple-element.33), channel_id=1, source_target_pairs={{6,4},{7,5},{14,12},{15,13},{22,20},{23,21},{30,28},{31,29}} | collective-permute-start | bytes 786440 | tf_op jit(solution)/shard_map/ppermute | solution.py:66
  262.6 9.5 %collective-permute-start.44 = (bf16[128,1024]{1,0:T(8,128)(2,1)S(1)}, bf16[128,1024]{1,0:T(8,128)(2,1)S(1)}, u32[]{:S(2)}, u32[]{:S(2)}) collective-permute-start(bf16[128,1024]{1,0:T(8,128)(2,1)S(1)} %get-tuple-element.44), channel_id=1, source_target_pairs={{0,2},{1,3},{2,4},{3,5},{8,10},{9,11},{10,12},{11,13},{16,18},{17,... | collective-permute-start | bytes 786440 | tf_op jit(solution)/shard_map/ppermute | solution.py:66
  266.9 10.6 %collective-permute-start.47 = (bf16[128,1024]{1,0:T(8,128)(2,1)S(1)}, bf16[128,1024]{1,0:T(8,128)(2,1)S(1)}, u32[]{:S(2)}, u32[]{:S(2)}) collective-permute-start(bf16[128,1024]{1,0:T(8,128)(2,1)S(1)} %get-tuple-element.45), channel_id=1, source_target_pairs={{4,2},{5,3},{6,4},{7,5},{12,10},{13,11},{14,12},{15,13},{20,18},{2... | collective-permute-start | bytes 786440 | tf_op jit(solution)/shard_map/ppermute | solution.py:66
  273.1 8.8 %collective-permute-start.45 = (bf16[128,1024]{1,0:T(8,128)(2,1)S(1)}, bf16[128,1024]{1,0:T(8,128)(2,1)S(1)}, u32[]{:S(2)}, u32[]{:S(2)}) collective-permute-start(bf16[128,1024]{1,0:T(8,128)(2,1)S(1)} %add.40), channel_id=1, source_target_pairs={{0,2},{1,3},{2,4},{3,5},{4,6},{5,7},{8,10},{9,11},{10,12},{11,13},... | collective-permute-start | bytes 786440 | tf_op jit(solution)/shard_map/ppermute | solution.py:66
  277.6 8.9 %collective-permute-start.48 = (bf16[128,1024]{1,0:T(8,128)(2,1)S(1)}, bf16[128,1024]{1,0:T(8,128)(2,1)S(1)}, u32[]{:S(2)}, u32[]{:S(2)}) collective-permute-start(bf16[128,1024]{1,0:T(8,128)(2,1)S(1)} %add.43), channel_id=1, source_target_pairs={{2,0},{3,1},{4,2},{5,3},{6,4},{7,5},{10,8},{11,9},{12,10},{13,11},... | collective-permute-start | bytes 786440 | tf_op jit(solution)/shard_map/ppermute | solution.py:66
  (30 other events, 252.9 us)

commit v3 on v2

--- a/solution.py
+++ b/solution.py
@@ -103,8 +103,7 @@
     )
 
 
-def spread(value):
-    copies = jnp.broadcast_to(value[None], (line_length(),) + value.shape)
+def spread(copies):
     mine = across(copies)
     return [mine, swapped(mine)]
 
@@ -195,7 +194,7 @@
     hidden = x.astype(F32) + dot(heads, out_w)
     hidden_ref[...] = hidden
     rms = lax.rsqrt(mean_last(hidden * hidden) + EPS)
-    expert_ref[...] = (hidden * rms * gain_e).astype(BF16)
+    expert_ref[...] = jnp.broadcast_to((hidden * rms * gain_e).astype(BF16), expert_ref.shape)
 
 
 def early_kernel(count, depth, *refs):
@@ -375,10 +374,6 @@
 
     each_chunk(tokens.shape[0] // chunk, step)
     give_back(result, mine_ref, other_ref, rows, core)
-
-
-def add_kernel(mine_ref, other_ref, out_ref):
-    out_ref[...] = (mine_ref[...].astype(F32) + other_ref[...].astype(F32)).astype(BF16)
 
 
 def add_apart_kernel(place, mine_ref, other_ref, *out_refs):
@@ -515,7 +510,8 @@
     arriving = passed_along(handoff_forward, "section", 1)
     cotangent = passed_along(relay_cotangents, "section", -1)
     gates = gate_columns(routes, gate_logits, expert_count)
-    cots = spread(jnp.concatenate([cotangent, gates], axis=1))
+    cot_block = jnp.concatenate([cotangent, gates], axis=1)
+    cots = spread(jnp.broadcast_to(cot_block[None], (length,) + cot_block.shape))
     mask = allowed_of(block_mask[:, 0])
 
     half = count // 2
@@ -540,7 +536,7 @@
             shaped((tokens, columns), F32),
             shaped((tokens, columns), F32),
             shaped((tokens, width), F32),
-            shaped((tokens, width), BF16),
+            shaped((length, tokens, width), BF16),
         ),
         [SMEM] + [VMEM] * 6 + [ANY] * (4 + count),
         (VMEM,) * 4,
@@ -587,7 +583,7 @@
         expert_scratch((CORES, length)),
         [place, up_weight, grad_act] + rows_bwd,
     )
-    grad_parts = across(call(add_kernel, pair[0], [VMEM] * 2, VMEM, [], [mine, swapped(other)]))
+    grad_parts = across(mine + swapped(other))
 
     mine, other = call(
         functools.partial(expert_forward_kernel, count, tokens),

time: 305 us -> 301 us (0.987)
  local copies, waits for them, and re-layouts: 11.7 us -> 8.42 us
    pallas_call x10 -> x9, Pallas kernels: 68 us -> 65.5 us  [call(): pl.pallas_call(kernel, out_shape=outs, in_specs=specs, out_specs=out_spec...]
  transfers between devices with their start and end apart: 54 -> 54, of which waited for: 19 -> 19; matrix products, arithmetic and copies ran while one was open for 3% -> 4% of each run, Pallas kernels for 17% -> 17%
where the time goes in v3:
time: 301 us; the launch traced here: 300 us
  waiting for transfers between devices  152 us (50%)
  Pallas kernels  65.5 us (22%)
  starting transfers between devices  64.8 us (22%)
  local copies, waits for them, and re-layouts  8.42 us (3%)
  other arithmetic  6.45 us (2%)
    ppermute x24, waiting for transfers between devices, hop(): return lax.ppermute(value, 'expert', chip_pairs(sources, move))  119 us
    pallas_call x9, Pallas kernels, call(): pl.pallas_call(kernel, out_shape=outs, in_specs=specs, out_specs=out_spec...  65.5 us
    ppermute x24, starting transfers between devices, hop(): return lax.ppermute(value, 'expert', chip_pairs(sources, move))  44.3 us
    all_to_all x3, waiting for transfers between devices, across(): lax.all_to_all(blocks, 'expert', split_axis=0, concat_axis=0, axis_index_...  26.1 us
    all_to_all x3, starting transfers between devices, across(): lax.all_to_all(blocks, 'expert', split_axis=0, concat_axis=0, axis_index_...  11 us
    unnamed x81, local copies, waits for them, and re-layouts  7.09 us
  transfers between devices with their start and end apart: 54, of which 19 were waited for; matrix products, arithmetic and copies ran while one was open for 4% of the time, Pallas kernels for 17%

profile of v3, /device:TPU:0, one launch (start us, length us, event | category | flops | bytes accessed | tf_op | source)
XLA Modules:
  0.0 299.8 jit_solution(6300767412409503902)
XLA Ops:
  0.6 5.9 %collective-permute-start.1 = (bf16[128,3072]{1,0:T(8,128)(2,1)}, bf16[128,3072]{1,0:T(8,128)(2,1)}, u32[]{:S(2)}, u32[]{:S(2)}) collective-permute-start(bf16[128,3072]{1,0:T(8,128)(2,1)} %bitcast.30), channel_id=1, source_target_pairs={{0,2},{1,3},{2,4},{3,5},{4,6},{5,7},{8,10},{9,11},{10,12},{11,13},... | collective-permute-start | bytes 2359304 | tf_op jit(solution)/shard_map/ppermute | solution.py:66
  6.5 1.3 collective-permute-start.2
  7.8 1.5 collective-permute-start
  9.3 4.6 %collective-permute-start.14 = (bf16[128,1024]{1,0:T(8,128)(2,1)}, bf16[128,1024]{1,0:T(8,128)(2,1)S(1)}, u32[]{:S(2)}, u32[]{:S(2)}) collective-permute-start(bf16[128,1024]{1,0:T(8,128)(2,1)} %bitcast.35), channel_id=1, source_target_pairs={{0,2},{1,3},{2,4},{3,5},{4,6},{5,7},{8,10},{9,11},{10,12},{11,13},... | collective-permute-start | bytes 786440 | tf_op jit(solution)/shard_map/ppermute | solution.py:66
  13.9 1.3 collective-permute-start.15
  15.2 1.5 collective-permute-done.refs_1_
  16.7 11.6 %collective-permute-done.14.refs_12_.refs_6_.refs_8_ = bf16[128,1024]{1,0:T(8,128)(2,1)S(1)} collective-permute-done((bf16[128,1024]{1,0:T(8,128)(2,1)}, bf16[128,1024]{1,0:T(8,128)(2,1)S(1)}, u32[]{:S(2)}, u32[]{:S(2)}) %collective-permute-start.14) | collective-permute-done | bytes 262176 | tf_op jit(solution)/shard_map/ppermute | solution.py:66
  28.3 2.4 collective-permute-start.27
  30.8 2.5 collective-permute-done.15.refs_13_.refs_7_.refs_9_
  33.2 0.7 collective-permute-start.16
  33.9 0.7 add_divide_fusion
  34.6 1.6 collective-permute-start.3
  36.2 1.3 collective-permute-start.4
  37.5 0.7 select_reduce_fusion
  38.3 1.3 collective-permute-start.17
  40.3 24.9 %collective-permute-done.17.refs_15_.refs_9_.refs_11_ = bf16[128,1024]{1,0:T(8,128)(2,1)} collective-permute-done((bf16[128,1024]{1,0:T(8,128)(2,1)S(1)}, bf16[128,1024]{1,0:T(8,128)(2,1)}, u32[]{:S(2)}, u32[]{:S(2)}) %collective-permute-start.17) | collective-permute-done | bytes 262176 | tf_op jit(solution)/shard_map/ppermute | solution.py:66
  65.2 0.7 collective-permute-start.18
  66.5 1.2 broadcast_in_dim.16
  67.7 3.5 %all-to-all-start = ((bf16[4,128,1152]{2,1,0:T(8,128)(2,1)}), bf16[4,128,1152]{2,1,0:T(8,128)(2,1)S(1)}, u32[]{:S(2)}, u32[]{:S(2)}) async-start(bf16[4,128,1152]{2,1,0:T(8,128)(2,1)} %broadcast_in_dim.16), calls=%async_computation | async-start | bytes 2359296 | tf_op jit(solution)/shard_map/all_to_all | solution.py:101
  71.3 1.3 collective-permute-start.19
  72.6 0.7 collective-permute-start.10
  73.4 1.3 collective-permute-start.11
  74.7 19.7 %collective-permute-done.19.refs_17_.refs_11_.refs_13_ = bf16[128,1024]{1,0:T(8,128)(2,1)S(1)} collective-permute-done((bf16[128,1024]{1,0:T(8,128)(2,1)}, bf16[128,1024]{1,0:T(8,128)(2,1)S(1)}, u32[]{:S(2)}, u32[]{:S(2)}) %collective-permute-start.19) | collective-permute-done | bytes 262176 | tf_op jit(solution)/shard_map/ppermute | solution.py:66
  94.3 1.7 collective-permute-done.23.refs_21_.refs_15_.refs_17_
  97.1 18.4 %collective-permute-done.11.refs_8_.refs_11_ = bf16[128,3072]{1,0:T(8,128)(2,1)S(1)} collective-permute-done((bf16[128,3072]{1,0:T(8,128)(2,1)}, bf16[128,3072]{1,0:T(8,128)(2,1)S(1)}, u32[]{:S(2)}, u32[]{:S(2)}) %collective-permute-start.11) | collective-permute-done | bytes 786464 | tf_op jit(solution)/shard_map/ppermute | solution.py:66
  117.3 1.1 fusion.refs_6_.refs_4_.refs_5_
  118.3 7.6 %shard_map.131 = (f32[128,3072]{1,0:T(8,128)}, f32[128,3072]{1,0:T(8,128)}, bf16[256,1024]{1,0:T(8,128)(2,1)}) custom-call(s32[2]{0:T(128)} %pad_add_fusion.refs_0_.place, bf16[128,1024]{1,0:T(8,128)(2,1)} %copy-done.19, bf16[128,1024]{1,0:T(8,128)(2,1)} %refs_1_.1, f32[1,1024]{1,0:T(1,128)} %refs_4_.5, bf16[128,3072]{1,0:T(8,128)(2,1)} %bitcast.33, ...), custom_call_target="tpu_custom_call" | custom-call | tf_op jit(solution)/shard_map/pallas_call | solution.py:449
  126.9 9.1 %shard_map.132 = (f32[128,3072]{1,0:T(8,128)}, f32[128,3072]{1,0:T(8,128)}, f32[128,1024]{1,0:T(8,128)}, bf16[4,128,1024]{2,1,0:T(8,128)(2,1)}) custom-call(s32[2]{0:T(128)} %pad_add_fusion.refs_0_.place, f32[128,3072]{1,0:T(8,128)} %get-tuple-element.23.refs_1_, f32[128,3072]{1,0:T(8,128)} %get-tuple-element.24.refs_2_, ...), custom_call_target="tpu_custom_call" | custom-call | tf_op jit(solution)/shard_map/pallas_call | solution.py:449
  136.1 3.5 %all-to-all-start.1 = ((bf16[4,128,1024]{2,1,0:T(8,128)(2,1)}), bf16[4,128,1024]{2,1,0:T(8,128)(2,1)S(1)}, u32[]{:S(2)}, u32[]{:S(2)}) async-start(bf16[4,128,1024]{2,1,0:T(8,128)(2,1)} %get-tuple-element.39), calls=%async_computation.1 | async-start | bytes 2097152 | tf_op jit(solution)/shard_map/all_to_all | solution.py:101
  139.7 26.1 %all-to-all-done.1.refs_3_ = bf16[4,128,1024]{2,1,0:T(8,128)(2,1)S(1)} async-done(((bf16[4,128,1024]{2,1,0:T(8,128)(2,1)}), bf16[4,128,1024]{2,1,0:T(8,128)(2,1)S(1)}, u32[]{:S(2)}, u32[]{:S(2)}) %all-to-all-start.1) | async-done | bytes 1048608 | tf_op jit(solution)/shard_map/all_to_all | solution.py:101
  165.8 5.5 %shard_map.133 = (f32[128,1024]{1,0:T(8,128)}, bf16[128,1024]{1,0:T(8,128)(2,1)}) custom-call(s32[2]{0:T(128)} %pad_add_fusion.refs_0_.place, bf16[128,1024]{1,0:T(8,128)(2,1)} %copy-done.19, f32[128,3072]{1,0:T(8,128)} %get-tuple-element.26.refs_2_, f32[1,1024]{1,0:T(1,128)} %refs_4_.4, f32[2,128,128]{2,1,0:T(8,128)} %fusion.refs_6_.refs_4_.refs_5_, ...), custom_call_target="tpu_custom_call" | custom-call | tf_op jit(solution)/shard_map/pallas_call | solution.py:449
  171.3 1.3 collective-permute-start.29
  172.6 1.3 collective-permute-start.30
  173.9 5.1 %collective-permute-done.29.refs_5_ = bf16[128,1024]{1,0:T(8,128)(2,1)S(1)} collective-permute-done((bf16[128,1024]{1,0:T(8,128)(2,1)}, bf16[128,1024]{1,0:T(8,128)(2,1)S(1)}, u32[]{:S(2)}, u32[]{:S(2)}) %collective-permute-start.29) | collective-permute-done | bytes 262176 | tf_op jit(solution)/shard_map/ppermute | solution.py:66
  179.7 3.3 %collective-permute-done.30.refs_6_ = bf16[128,1024]{1,0:T(8,128)(2,1)S(1)} collective-permute-done((bf16[128,1024]{1,0:T(8,128)(2,1)}, bf16[128,1024]{1,0:T(8,128)(2,1)S(1)}, u32[]{:S(2)}, u32[]{:S(2)}) %collective-permute-start.30) | collective-permute-done | bytes 262176 | tf_op jit(solution)/shard_map/ppermute | solution.py:66
  183.1 1.3 collective-permute-start.32
  185.0 7.4 %collective-permute-done.32.refs_8_ = bf16[128,1024]{1,0:T(8,128)(2,1)S(1)} collective-permute-done((bf16[128,1024]{1,0:T(8,128)(2,1)S(1)}, bf16[128,1024]{1,0:T(8,128)(2,1)S(1)}, u32[]{:S(2)}, u32[]{:S(2)}) %collective-permute-start.32) | collective-permute-done | bytes 262176 | tf_op jit(solution)/shard_map/ppermute | solution.py:66
  193.1 1.0 copy-done.22
  194.1 1.5 collective-permute-start.34
  195.6 2.6 copy.25
  198.1 6.6 %shard_map.134 = (f32[1024,704]{1,0:T(8,128)}, f32[1024,128]{1,0:T(8,128)}) custom-call(s32[2]{0:T(128)} %pad_add_fusion.refs_0_.place, bf16[704,1024]{1,0:T(8,128)(2,1)} %bitcast.28, bf16[4,128,1152]{2,1,0:T(8,128)(2,1)} %copy-done, bf16[4,128,1152]{2,1,0:T(8,128)(2,1)} %collective-permute-done.28.refs_3_), custom_call_target="tpu_custom_call" | custom-call | tf_op jit(solution)/shard_map/pallas_call | solution.py:449
  204.7 9.7 %shard_map.137 = (bf16[4,128,1024]{2,1,0:T(8,128)(2,1)}, bf16[4,128,1024]{2,1,0:T(8,128)(2,1)}) custom-call(s32[2]{0:T(128)} %pad_add_fusion.refs_0_.place, bf16[1024,704]{1,0:T(8,128)(2,1)} %bitcast.26, f32[1024,704]{1,0:T(8,128)} %get-tuple-element.38.refs_2_, bf16[4,128,1024]{2,1,0:T(8,128)(2,1)} %copy-done.2, bf16[4,128,1024]{2,1,0:T(8,128)(2,1)} %copy-done.22), custom_call_target="tpu_custom_call" | custom-call | tf_op jit(solution)/shard_map/pallas_call | solution.py:449
  215.8 2.0 collective-permute-done.38.refs_14_
  219.6 8.8 %shard_map.135 = (bf16[4,128,1024]{2,1,0:T(8,128)(2,1)}, bf16[4,128,1024]{2,1,0:T(8,128)(2,1)}) custom-call(s32[2]{0:T(128)} %pad_add_fusion.refs_0_.place, bf16[1024,704]{1,0:T(8,128)(2,1)} %bitcast.27, bf16[704,1024]{1,0:T(8,128)(2,1)} %bitcast.29, f32[1024,128]{1,0:T(8,128)} %get-tuple-element.28.refs_3_, bf16[128,1024]{1,0:T(8,128)(2,1)} %get-tuple-element.29.refs_4_, ...), custom_call_target="tpu_custom_call" | custom-call | tf_op jit(solution)/shard_map/pallas_call | solution.py:449
  228.6 1.4 add.48
  230.1 3.9 %all-to-all-start.2 = ((bf16[4,128,1024]{2,1,0:T(8,128)(2,1)}), bf16[4,128,1024]{2,1,0:T(8,128)(2,1)S(1)}, u32[]{:S(2)}, u32[]{:S(2)}) async-start(bf16[4,128,1024]{2,1,0:T(8,128)(2,1)} %add.48), calls=%async_computation.2 | async-start | bytes 2097152 | tf_op jit(solution)/shard_map/all_to_all | solution.py:101
  234.0 1.0 copy-done.20
  235.0 2.7 shard_map.136
  237.7 4.3 %collective-permute-start.43 = (bf16[128,1024]{1,0:T(8,128)(2,1)}, bf16[128,1024]{1,0:T(8,128)(2,1)S(1)}, u32[]{:S(2)}, u32[]{:S(2)}) collective-permute-start(bf16[128,1024]{1,0:T(8,128)(2,1)} %get-tuple-element.35), channel_id=1, source_target_pairs={{0,2},{1,3},{8,10},{9,11},{16,18},{17,19},{24,26},{25,27}} | collective-permute-start | bytes 786440 | tf_op jit(solution)/shard_map/ppermute | solution.py:66
  242.0 0.7 collective-permute-start.46
  242.7 14.6 %collective-permute-done.43 = bf16[128,1024]{1,0:T(8,128)(2,1)S(1)} collective-permute-done((bf16[128,1024]{1,0:T(8,128)(2,1)}, bf16[128,1024]{1,0:T(8,128)(2,1)S(1)}, u32[]{:S(2)}, u32[]{:S(2)}) %collective-permute-start.43) | collective-permute-done | bytes 262176 | tf_op jit(solution)/shard_map/ppermute | solution.py:66
  257.3 1.0 fusion.20
  258.3 4.3 %collective-permute-start.44 = (bf16[128,1024]{1,0:T(8,128)(2,1)S(1)}, bf16[128,1024]{1,0:T(8,128)(2,1)S(1)}, u32[]{:S(2)}, u32[]{:S(2)}) collective-permute-start(bf16[128,1024]{1,0:T(8,128)(2,1)S(1)} %get-tuple-element.44), channel_id=1, source_target_pairs={{0,2},{1,3},{2,4},{3,5},{8,10},{9,11},{10,12},{11,13},{16,18},{17,... | collective-permute-start | bytes 786440 | tf_op jit(solution)/shard_map/ppermute | solution.py:66
  262.6 0.7 collective-permute-start.47
  263.3 4.5 %collective-permute-done.44 = bf16[128,1024]{1,0:T(8,128)(2,1)S(1)} collective-permute-done((bf16[128,1024]{1,0:T(8,128)(2,1)S(1)}, bf16[128,1024]{1,0:T(8,128)(2,1)S(1)}, u32[]{:S(2)}, u32[]{:S(2)}) %collective-permute-start.44) | collective-permute-done | bytes 262176 | tf_op jit(solution)/shard_map/ppermute | solution.py:66
  267.8 1.0 add.43
  268.9 4.4 %collective-permute-start.45 = (bf16[128,1024]{1,0:T(8,128)(2,1)S(1)}, bf16[128,1024]{1,0:T(8,128)(2,1)S(1)}, u32[]{:S(2)}, u32[]{:S(2)}) collective-permute-start(bf16[128,1024]{1,0:T(8,128)(2,1)S(1)} %add.43), channel_id=1, source_target_pairs={{0,2},{1,3},{2,4},{3,5},{4,6},{5,7},{8,10},{9,11},{10,12},{11,13},... | collective-permute-start | bytes 786440 | tf_op jit(solution)/shard_map/ppermute | solution.py:66
  273.4 1.5 collective-permute-start.48
  274.9 2.7 collective-permute-done.45
  277.6 4.6 %collective-permute-done.48 = bf16[128,1024]{1,0:T(8,128)(2,1)S(1)} collective-permute-done((bf16[128,1024]{1,0:T(8,128)(2,1)S(1)}, bf16[128,1024]{1,0:T(8,128)(2,1)S(1)}, u32[]{:S(2)}, u32[]{:S(2)}) %collective-permute-start.48) | collective-permute-done | bytes 262176 | tf_op jit(solution)/shard_map/ppermute | solution.py:66
  282.2 0.8 add_convert_fusion
  283.1 1.0 copy-done.1
  284.1 8.2 %shard_map.138 = (bf16[128,3072]{1,0:T(8,128)(2,1)}, f32[128,1024]{1,0:T(8,128)}) custom-call(s32[2]{0:T(128)} %pad_add_fusion.refs_0_.place, bf16[128,1024]{1,0:T(8,128)(2,1)} %copy-done.21, f32[128,1024]{1,0:T(8,128)} %get-tuple-element.36.refs_2_, f32[128,3072]{1,0:T(8,128)} %get-tuple-element.37.refs_3_, f32[1,1024]{1,0:T(1,128)} %refs_4_.4, ...), custom_call_target="tpu_custom_call" | custom-call | tf_op jit(solution)/shard_map/pallas_call | solution.py:449
  292.3 7.3 %shard_map.139 = bf16[128,1024]{1,0:T(8,128)(2,1)} custom-call(s32[2]{0:T(128)} %pad_add_fusion.refs_0_.place, bf16[128,1024]{1,0:T(8,128)(2,1)} %refs_1_.1, bf16[128,3072]{1,0:T(8,128)(2,1)} %get-tuple-element.42.refs_2_, f32[128,1024]{1,0:T(8,128)} %get-tuple-element.43.refs_3_, f32[1,1024]{1,0:T(1,128)} %refs_4_.5, bf16[128,3072]{1,0:T(8,128)(2,1)} %bitcast.34, ...), custom_call_target="tpu_custom_call" | custom-call | tf_op jit(solution)/shard_map/pallas_call | solution.py:449
  (151 shorter events, 10.6 us)
Async XLA Ops:
  0.6 34.0 %collective-permute-start.1 = (bf16[128,3072]{1,0:T(8,128)(2,1)}, bf16[128,3072]{1,0:T(8,128)(2,1)}, u32[]{:S(2)}, u32[]{:S(2)}) collective-permute-start(bf16[128,3072]{1,0:T(8,128)(2,1)} %bitcast.30), channel_id=1, source_target_pairs={{0,2},{1,3},{2,4},{3,5},{4,6},{5,7},{8,10},{9,11},{10,12},{11,13},... | collective-permute-start | bytes 2359304 | tf_op jit(solution)/shard_map/ppermute | solution.py:66
  6.5 29.7 %collective-permute-start.2 = (bf16[128,3072]{1,0:T(8,128)(2,1)}, bf16[128,3072]{1,0:T(8,128)(2,1)S(1)}, u32[]{:S(2)}, u32[]{:S(2)}) collective-permute-start(bf16[128,3072]{1,0:T(8,128)(2,1)} %bitcast.31), channel_id=1, source_target_pairs={{2,0},{3,1},{4,2},{5,3},{6,4},{7,5},{10,8},{11,9},{12,10},{13,11},... | collective-permute-start | bytes 2359304 | tf_op jit(solution)/shard_map/ppermute | solution.py:66
  7.8 8.9 %collective-permute-start = (bf16[128,1024]{1,0:T(8,128)(2,1)}, bf16[128,1024]{1,0:T(8,128)(2,1)S(1)}, u32[]{:S(2)}, u32[]{:S(2)}) collective-permute-start(bf16[128,1024]{1,0:T(8,128)(2,1)} %param.12), channel_id=1, source_target_pairs={{0,8},{8,16},{16,24},{24,0},{1,9},{9,17},{17,25},{25,1},{2,10},{10... | collective-permute-start | bytes 786440 | tf_op jit(solution)/shard_map/ppermute | solution.py:45
  9.3 19.0 %collective-permute-start.14 = (bf16[128,1024]{1,0:T(8,128)(2,1)}, bf16[128,1024]{1,0:T(8,128)(2,1)S(1)}, u32[]{:S(2)}, u32[]{:S(2)}) collective-permute-start(bf16[128,1024]{1,0:T(8,128)(2,1)} %bitcast.35), channel_id=1, source_target_pairs={{0,2},{1,3},{2,4},{3,5},{4,6},{5,7},{8,10},{9,11},{10,12},{11,13},... | collective-permute-start | bytes 786440 | tf_op jit(solution)/shard_map/ppermute | solution.py:66
  13.9 19.3 %collective-permute-start.15 = (bf16[128,1024]{1,0:T(8,128)(2,1)}, bf16[128,1024]{1,0:T(8,128)(2,1)S(1)}, u32[]{:S(2)}, u32[]{:S(2)}) collective-permute-start(bf16[128,1024]{1,0:T(8,128)(2,1)} %bitcast.36), channel_id=1, source_target_pairs={{2,0},{3,1},{4,2},{5,3},{6,4},{7,5},{10,8},{11,9},{12,10},{13,11},... | collective-permute-start | bytes 786440 | tf_op jit(solution)/shard_map/ppermute | solution.py:66
  16.7 21.4 %collective-permute-start.20 = (bf16[128,1024]{1,0:T(8,128)(2,1)}, bf16[128,1024]{1,0:T(8,128)(2,1)S(1)}, u32[]{:S(2)}, u32[]{:S(2)}) collective-permute-start(bf16[128,1024]{1,0:T(8,128)(2,1)} %bitcast.37), channel_id=1, source_target_pairs={{0,1},{1,0},{2,3},{3,2},{4,5},{5,4},{6,7},{7,6},{8,9},{9,8},{10,11... | collective-permute-start | bytes 786440 | tf_op jit(solution)/shard_map/ppermute | solution.py:62
  28.3 39.4 %copy-start.6 = (bf16[128,1024]{1,0:T(8,128)(2,1)}, bf16[128,1024]{1,0:T(8,128)(2,1)S(1)}, u32[]{:S(2)}) copy-start(bf16[128,1024]{1,0:T(8,128)(2,1)S(1)} %collective-permute-done.14.refs_12_.refs_6_.refs_8_) | copy-start | bytes 786436
  28.3 9.9 %collective-permute-start.27 = (bf16[128,1024]{1,0:T(8,128)(2,1)}, bf16[128,1024]{1,0:T(8,128)(2,1)S(1)}, u32[]{:S(2)}, u32[]{:S(2)}) collective-permute-start(bf16[128,1024]{1,0:T(8,128)(2,1)} %param.14), channel_id=1, source_target_pairs={{0,24},{8,0},{16,8},{24,16},{1,25},{9,1},{17,9},{25,17},{2,26},{10... | collective-permute-start | bytes 786440 | tf_op jit(solution)/shard_map/ppermute | solution.py:45
  33.2 34.5 %copy-start.7 = (bf16[128,1024]{1,0:T(8,128)(2,1)}, bf16[128,1024]{1,0:T(8,128)(2,1)S(1)}, u32[]{:S(2)}) copy-start(bf16[128,1024]{1,0:T(8,128)(2,1)S(1)} %collective-permute-done.15.refs_13_.refs_7_.refs_9_) | copy-start | bytes 786436
  33.2 6.3 %collective-permute-start.16 = (bf16[128,1024]{1,0:T(8,128)(2,1)S(1)}, bf16[128,1024]{1,0:T(8,128)(2,1)S(1)}, u32[]{:S(2)}, u32[]{:S(2)}) collective-permute-start(bf16[128,1024]{1,0:T(8,128)(2,1)S(1)} %collective-permute-done.14.refs_12_.refs_6_.refs_8_), channel_id=1, source_target_pairs={{2,4},{3,5},{4,6},{5,7},{10,12},{11,13},{12,14},{13,15},{18,20},{1... | collective-permute-start | bytes 786440 | tf_op jit(solution)/shard_map/ppermute | solution.py:66
  34.6 38.0 %collective-permute-start.3 = (bf16[128,3072]{1,0:T(8,128)(2,1)}, bf16[128,3072]{1,0:T(8,128)(2,1)}, u32[]{:S(2)}, u32[]{:S(2)}) collective-permute-start(bf16[128,3072]{1,0:T(8,128)(2,1)} %collective-permute-done.1.refs_5_.refs_6_), channel_id=1, source_target_pairs={{2,4},{3,5},{4,6},{5,7},{10,12},{11,13},{12,14},{13,15},{18,20},{1... | collective-permute-start | bytes 2359304 | tf_op jit(solution)/shard_map/ppermute | solution.py:66
  36.2 59.9 %copy-start.5 = (bf16[128,3072]{1,0:T(8,128)(2,1)}, bf16[128,3072]{1,0:T(8,128)(2,1)S(1)}, u32[]{:S(2)}) copy-start(bf16[128,3072]{1,0:T(8,128)(2,1)S(1)} %collective-permute-done.2.refs_6_.refs_7_) | copy-start | bytes 2359300
  36.2 37.2 %collective-permute-start.4 = (bf16[128,3072]{1,0:T(8,128)(2,1)S(1)}, bf16[128,3072]{1,0:T(8,128)(2,1)}, u32[]{:S(2)}, u32[]{:S(2)}) collective-permute-start(bf16[128,3072]{1,0:T(8,128)(2,1)S(1)} %collective-permute-done.2.refs_6_.refs_7_), channel_id=1, source_target_pairs={{2,0},{3,1},{4,2},{5,3},{10,8},{11,9},{12,10},{13,11},{18,16},{19,... | collective-permute-start | bytes 2359304 | tf_op jit(solution)/shard_map/ppermute | solution.py:66
  38.2 27.0 %collective-permute-start.21 = (bf16[128,1024]{1,0:T(8,128)(2,1)S(1)}, bf16[128,1024]{1,0:T(8,128)(2,1)S(1)}, u32[]{:S(2)}, u32[]{:S(2)}) collective-permute-start(bf16[128,1024]{1,0:T(8,128)(2,1)S(1)} %collective-permute-done.14.refs_12_.refs_6_.refs_8_), channel_id=1, source_target_pairs={{0,1},{1,0},{2,3},{3,2},{4,5},{5,4},{6,7},{7,6},{8,9},{9,8},{10,11... | collective-permute-start | bytes 786440 | tf_op jit(solution)/shard_map/ppermute | solution.py:62
  38.3 35.1 %copy-start.21 = (bf16[128,1024]{1,0:T(8,128)(2,1)}, bf16[128,1024]{1,0:T(8,128)(2,1)S(1)}, u32[]{:S(2)}) copy-start(bf16[128,1024]{1,0:T(8,128)(2,1)S(1)} %collective-permute-done.27.refs_1_) | copy-start | bytes 786436
  38.3 26.9 %collective-permute-start.17 = (bf16[128,1024]{1,0:T(8,128)(2,1)S(1)}, bf16[128,1024]{1,0:T(8,128)(2,1)}, u32[]{:S(2)}, u32[]{:S(2)}) collective-permute-start(bf16[128,1024]{1,0:T(8,128)(2,1)S(1)} %collective-permute-done.15.refs_13_.refs_7_.refs_9_), channel_id=1, source_target_pairs={{2,0},{3,1},{4,2},{5,3},{10,8},{11,9},{12,10},{13,11},{18,16},{19,... | collective-permute-start | bytes 786440 | tf_op jit(solution)/shard_map/ppermute | solution.py:66
  39.6 26.3 %collective-permute-start.22 = (bf16[128,1024]{1,0:T(8,128)(2,1)S(1)}, bf16[128,1024]{1,0:T(8,128)(2,1)S(1)}, u32[]{:S(2)}, u32[]{:S(2)}) collective-permute-start(bf16[128,1024]{1,0:T(8,128)(2,1)S(1)} %collective-permute-done.15.refs_13_.refs_7_.refs_9_), channel_id=1, source_target_pairs={{0,1},{1,0},{2,3},{3,2},{4,5},{5,4},{6,7},{7,6},{8,9},{9,8},{10,11... | collective-permute-start | bytes 786440 | tf_op jit(solution)/shard_map/ppermute | solution.py:62
  65.2 31.0 %collective-permute-start.5 = (bf16[128,3072]{1,0:T(8,128)(2,1)}, bf16[128,3072]{1,0:T(8,128)(2,1)}, u32[]{:S(2)}, u32[]{:S(2)}) collective-permute-start(bf16[128,3072]{1,0:T(8,128)(2,1)} %bitcast.32), channel_id=1, source_target_pairs={{0,1},{1,0},{2,3},{3,2},{4,5},{5,4},{6,7},{7,6},{8,9},{9,8},{10,11... | collective-permute-start | bytes 2359304 | tf_op jit(solution)/shard_map/ppermute | solution.py:62
  65.2 6.1 %collective-permute-start.18 = (bf16[128,1024]{1,0:T(8,128)(2,1)S(1)}, bf16[128,1024]{1,0:T(8,128)(2,1)S(1)}, u32[]{:S(2)}, u32[]{:S(2)}) collective-permute-start(bf16[128,1024]{1,0:T(8,128)(2,1)S(1)} %collective-permute-done.16.refs_14_.refs_8_.refs_10_), channel_id=1, source_target_pairs={{4,6},{5,7},{12,14},{13,15},{20,22},{21,23},{28,30},{29,31}} | collective-permute-start | bytes 786440 | tf_op jit(solution)/shard_map/ppermute | solution.py:66
  65.9 30.7 %collective-permute-start.6 = (bf16[128,3072]{1,0:T(8,128)(2,1)}, bf16[128,3072]{1,0:T(8,128)(2,1)}, u32[]{:S(2)}, u32[]{:S(2)}) collective-permute-start(bf16[128,3072]{1,0:T(8,128)(2,1)} %collective-permute-done.1.refs_5_.refs_6_), channel_id=1, source_target_pairs={{0,1},{1,0},{2,3},{3,2},{4,5},{5,4},{6,7},{7,6},{8,9},{9,8},{10,11... | collective-permute-start | bytes 2359304 | tf_op jit(solution)/shard_map/ppermute | solution.py:62
  67.7 49.6 %copy-start.39 = (s32[2,1,8,8]{3,2,1,0:T(8,128)S(1)}, s32[2,1,8,8]{3,2,1,0:T(8,128)}, u32[]{:S(2)}) copy-start(s32[2,1,8,8]{3,2,1,0:T(8,128)} %param.23) | copy-start | bytes 1540
  67.7 68.3 %all-to-all-start = ((bf16[4,128,1152]{2,1,0:T(8,128)(2,1)}), bf16[4,128,1152]{2,1,0:T(8,128)(2,1)S(1)}, u32[]{:S(2)}, u32[]{:S(2)}) async-start(bf16[4,128,1152]{2,1,0:T(8,128)(2,1)} %broadcast_in_dim.16), calls=%async_computation | async-start | bytes 2359296 | tf_op jit(solution)/shard_map/all_to_all | solution.py:101
  71.3 23.0 %collective-permute-start.19 = (bf16[128,1024]{1,0:T(8,128)(2,1)}, bf16[128,1024]{1,0:T(8,128)(2,1)S(1)}, u32[]{:S(2)}, u32[]{:S(2)}) collective-permute-start(bf16[128,1024]{1,0:T(8,128)(2,1)} %collective-permute-done.17.refs_15_.refs_9_.refs_11_), channel_id=1, source_target_pairs={{2,0},{3,1},{10,8},{11,9},{18,16},{19,17},{26,24},{27,25}} | collective-permute-start | bytes 786440 | tf_op jit(solution)/shard_map/ppermute | solution.py:66
  72.6 24.1 %collective-permute-start.10 = (bf16[128,3072]{1,0:T(8,128)(2,1)}, bf16[128,3072]{1,0:T(8,128)(2,1)S(1)}, u32[]{:S(2)}, u32[]{:S(2)}) collective-permute-start(bf16[128,3072]{1,0:T(8,128)(2,1)} %collective-permute-done.3.refs_7_.refs_8_), channel_id=1, source_target_pairs={{4,6},{5,7},{12,14},{13,15},{20,22},{21,23},{28,30},{29,31}} | collective-permute-start | bytes 2359304 | tf_op jit(solution)/shard_map/ppermute | solution.py:66
  73.4 42.1 %collective-permute-start.11 = (bf16[128,3072]{1,0:T(8,128)(2,1)}, bf16[128,3072]{1,0:T(8,128)(2,1)S(1)}, u32[]{:S(2)}, u32[]{:S(2)}) collective-permute-start(bf16[128,3072]{1,0:T(8,128)(2,1)} %collective-permute-done.4.refs_8_.refs_9_), channel_id=1, source_target_pairs={{2,0},{3,1},{10,8},{11,9},{18,16},{19,17},{26,24},{27,25}} | collective-permute-start | bytes 2359304 | tf_op jit(solution)/shard_map/ppermute | solution.py:66
  94.3 1.7 collective-permute-start.23
  96.1 19.5 %collective-permute-start.7 = (bf16[128,3072]{1,0:T(8,128)(2,1)S(1)}, bf16[128,3072]{1,0:T(8,128)(2,1)}, u32[]{:S(2)}, u32[]{:S(2)}) collective-permute-start(bf16[128,3072]{1,0:T(8,128)(2,1)S(1)} %collective-permute-done.2.refs_6_.refs_7_), channel_id=1, source_target_pairs={{0,1},{1,0},{2,3},{3,2},{4,5},{5,4},{6,7},{7,6},{8,9},{9,8},{10,11... | collective-permute-start | bytes 2359304 | tf_op jit(solution)/shard_map/ppermute | solution.py:62
  96.2 19.9 %collective-permute-start.8 = (bf16[128,3072]{1,0:T(8,128)(2,1)}, bf16[128,3072]{1,0:T(8,128)(2,1)}, u32[]{:S(2)}, u32[]{:S(2)}) collective-permute-start(bf16[128,3072]{1,0:T(8,128)(2,1)} %collective-permute-done.3.refs_7_.refs_8_), channel_id=1, source_target_pairs={{0,1},{1,0},{2,3},{3,2},{4,5},{5,4},{6,7},{7,6},{8,9},{9,8},{10,11... | collective-permute-start | bytes 2359304 | tf_op jit(solution)/shard_map/ppermute | solution.py:62
  96.6 19.6 %collective-permute-start.9 = (bf16[128,3072]{1,0:T(8,128)(2,1)}, bf16[128,3072]{1,0:T(8,128)(2,1)}, u32[]{:S(2)}, u32[]{:S(2)}) collective-permute-start(bf16[128,3072]{1,0:T(8,128)(2,1)} %collective-permute-done.4.refs_8_.refs_9_), channel_id=1, source_target_pairs={{0,1},{1,0},{2,3},{3,2},{4,5},{5,4},{6,7},{7,6},{8,9},{9,8},{10,11... | collective-permute-start | bytes 2359304 | tf_op jit(solution)/shard_map/ppermute | solution.py:62
  96.7 29.3 %collective-permute-start.12 = (bf16[128,3072]{1,0:T(8,128)(2,1)S(1)}, bf16[128,3072]{1,0:T(8,128)(2,1)}, u32[]{:S(2)}, u32[]{:S(2)}) collective-permute-start(bf16[128,3072]{1,0:T(8,128)(2,1)S(1)} %collective-permute-done.10.refs_7_.refs_10_), channel_id=1, source_target_pairs={{0,1},{1,0},{2,3},{3,2},{4,5},{5,4},{6,7},{7,6},{8,9},{9,8},{10,11... | collective-permute-start | bytes 2359304 | tf_op jit(solution)/shard_map/ppermute | solution.py:62
  115.5 10.5 %collective-permute-start.13 = (bf16[128,3072]{1,0:T(8,128)(2,1)S(1)}, bf16[128,3072]{1,0:T(8,128)(2,1)}, u32[]{:S(2)}, u32[]{:S(2)}) collective-permute-start(bf16[128,3072]{1,0:T(8,128)(2,1)S(1)} %collective-permute-done.11.refs_8_.refs_11_), channel_id=1, source_target_pairs={{0,1},{1,0},{2,3},{3,2},{4,5},{5,4},{6,7},{7,6},{8,9},{9,8},{10,11... | collective-permute-start | bytes 2359304 | tf_op jit(solution)/shard_map/ppermute | solution.py:62
  115.6 10.4 %collective-permute-start.24 = (bf16[128,1024]{1,0:T(8,128)(2,1)}, bf16[128,1024]{1,0:T(8,128)(2,1)S(1)}, u32[]{:S(2)}, u32[]{:S(2)}) collective-permute-start(bf16[128,1024]{1,0:T(8,128)(2,1)} %collective-permute-done.17.refs_15_.refs_9_.refs_11_), channel_id=1, source_target_pairs={{0,1},{1,0},{2,3},{3,2},{4,5},{5,4},{6,7},{7,6},{8,9},{9,8},{10,11... | collective-permute-start | bytes 786440 | tf_op jit(solution)/shard_map/ppermute | solution.py:62
  116.1 9.9 %collective-permute-start.25 = (bf16[128,1024]{1,0:T(8,128)(2,1)}, bf16[128,1024]{1,0:T(8,128)(2,1)S(1)}, u32[]{:S(2)}, u32[]{:S(2)}) collective-permute-start(bf16[128,1024]{1,0:T(8,128)(2,1)} %copy-done.12), channel_id=1, source_target_pairs={{0,1},{1,0},{2,3},{3,2},{4,5},{5,4},{6,7},{7,6},{8,9},{9,8},{10,11... | collective-permute-start | bytes 786440 | tf_op jit(solution)/shard_map/ppermute | solution.py:62
  116.2 9.8 %collective-permute-start.26 = (bf16[128,1024]{1,0:T(8,128)(2,1)}, bf16[128,1024]{1,0:T(8,128)(2,1)S(1)}, u32[]{:S(2)}, u32[]{:S(2)}) collective-permute-start(bf16[128,1024]{1,0:T(8,128)(2,1)} %copy-done.13), channel_id=1, source_target_pairs={{0,1},{1,0},{2,3},{3,2},{4,5},{5,4},{6,7},{7,6},{8,9},{9,8},{10,11... | collective-permute-start | bytes 786440 | tf_op jit(solution)/shard_map/ppermute | solution.py:62
  136.0 35.3 %copy-start = (bf16[4,128,1152]{2,1,0:T(8,128)(2,1)}, bf16[4,128,1152]{2,1,0:T(8,128)(2,1)S(1)}, u32[]{:S(2)}) copy-start(bf16[4,128,1152]{2,1,0:T(8,128)(2,1)S(1)} %all-to-all-done.refs_2_) | copy-start | bytes 3538948
  136.1 29.8 %all-to-all-start.1 = ((bf16[4,128,1024]{2,1,0:T(8,128)(2,1)}), bf16[4,128,1024]{2,1,0:T(8,128)(2,1)S(1)}, u32[]{:S(2)}, u32[]{:S(2)}) async-start(bf16[4,128,1024]{2,1,0:T(8,128)(2,1)} %get-tuple-element.39), calls=%async_computation.1 | async-start | bytes 2097152 | tf_op jit(solution)/shard_map/all_to_all | solution.py:101
  139.6 44.9 %collective-permute-start.28 = (bf16[4,128,1152]{2,1,0:T(8,128)(2,1)S(1)}, bf16[4,128,1152]{2,1,0:T(8,128)(2,1)}, u32[]{:S(2)}, u32[]{:S(2)}) collective-permute-start(bf16[4,128,1152]{2,1,0:T(8,128)(2,1)S(1)} %all-to-all-done.refs_2_), channel_id=1, source_target_pairs={{0,1},{1,0},{2,3},{3,2},{4,5},{5,4},{6,7},{7,6},{8,9},{9,8},{10,11... | collective-permute-start | bytes 3538952 | tf_op jit(solution)/shard_map/ppermute | solution.py:62
  165.8 27.3 %collective-permute-start.49 = (bf16[4,128,1024]{2,1,0:T(8,128)(2,1)S(1)}, bf16[4,128,1024]{2,1,0:T(8,128)(2,1)S(1)}, u32[]{:S(2)}, u32[]{:S(2)}) collective-permute-start(bf16[4,128,1024]{2,1,0:T(8,128)(2,1)S(1)} %all-to-all-done.1.refs_3_), channel_id=1, source_target_pairs={{0,1},{1,0},{2,3},{3,2},{4,5},{5,4},{6,7},{7,6},{8,9},{9,8},{10,11... | collective-permute-start | bytes 3145736 | tf_op jit(solution)/shard_map/ppermute | solution.py:62
  171.3 7.7 %collective-permute-start.29 = (bf16[128,1024]{1,0:T(8,128)(2,1)}, bf16[128,1024]{1,0:T(8,128)(2,1)S(1)}, u32[]{:S(2)}, u32[]{:S(2)}) collective-permute-start(bf16[128,1024]{1,0:T(8,128)(2,1)} %get-tuple-element.29.refs_4_), channel_id=1, source_target_pairs={{0,2},{1,3},{2,4},{3,5},{4,6},{5,7},{8,10},{9,11},{10,12},{11,13},... | collective-permute-start | bytes 786440 | tf_op jit(solution)/shard_map/ppermute | solution.py:66
  172.6 10.4 %collective-permute-start.30 = (bf16[128,1024]{1,0:T(8,128)(2,1)}, bf16[128,1024]{1,0:T(8,128)(2,1)S(1)}, u32[]{:S(2)}, u32[]{:S(2)}) collective-permute-start(bf16[128,1024]{1,0:T(8,128)(2,1)} %get-tuple-element.29.refs_4_), channel_id=1, source_target_pairs={{2,0},{3,1},{4,2},{5,3},{6,4},{7,5},{10,8},{11,9},{12,10},{13,11},... | collective-permute-start | bytes 786440 | tf_op jit(solution)/shard_map/ppermute | solution.py:66
  179.1 35.4 %copy-start.24 = (bf16[128,1024]{1,0:T(8,128)(2,1)}, bf16[128,1024]{1,0:T(8,128)(2,1)S(1)}, u32[]{:S(2)}) copy-start(bf16[128,1024]{1,0:T(8,128)(2,1)S(1)} %collective-permute-done.29.refs_5_) | copy-start | bytes 786436
  179.1 5.9 %collective-permute-start.31 = (bf16[128,1024]{1,0:T(8,128)(2,1)S(1)}, bf16[128,1024]{1,0:T(8,128)(2,1)S(1)}, u32[]{:S(2)}, u32[]{:S(2)}) collective-permute-start(bf16[128,1024]{1,0:T(8,128)(2,1)S(1)} %collective-permute-done.29.refs_5_), channel_id=1, source_target_pairs={{2,4},{3,5},{4,6},{5,7},{10,12},{11,13},{12,14},{13,15},{18,20},{1... | collective-permute-start | bytes 786440 | tf_op jit(solution)/shard_map/ppermute | solution.py:66
  183.1 9.4 %collective-permute-start.32 = (bf16[128,1024]{1,0:T(8,128)(2,1)S(1)}, bf16[128,1024]{1,0:T(8,128)(2,1)S(1)}, u32[]{:S(2)}, u32[]{:S(2)}) collective-permute-start(bf16[128,1024]{1,0:T(8,128)(2,1)S(1)} %collective-permute-done.30.refs_6_), channel_id=1, source_target_pairs={{2,0},{3,1},{4,2},{5,3},{10,8},{11,9},{12,10},{13,11},{18,16},{19,... | collective-permute-start | bytes 786440 | tf_op jit(solution)/shard_map/ppermute | solution.py:66
  184.4 30.1 %collective-permute-start.35 = (bf16[128,1024]{1,0:T(8,128)(2,1)}, bf16[128,1024]{1,0:T(8,128)(2,1)S(1)}, u32[]{:S(2)}, u32[]{:S(2)}) collective-permute-start(bf16[128,1024]{1,0:T(8,128)(2,1)} %get-tuple-element.29.refs_4_), channel_id=1, source_target_pairs={{0,1},{1,0},{2,3},{3,2},{4,5},{5,4},{6,7},{7,6},{8,9},{9,8},{10,11... | collective-permute-start | bytes 786440 | tf_op jit(solution)/shard_map/ppermute | solution.py:62
  184.5 30.1 %collective-permute-start.36 = (bf16[128,1024]{1,0:T(8,128)(2,1)S(1)}, bf16[128,1024]{1,0:T(8,128)(2,1)S(1)}, u32[]{:S(2)}, u32[]{:S(2)}) collective-permute-start(bf16[128,1024]{1,0:T(8,128)(2,1)S(1)} %collective-permute-done.29.refs_5_), channel_id=1, source_target_pairs={{0,1},{1,0},{2,3},{3,2},{4,5},{5,4},{6,7},{7,6},{8,9},{9,8},{10,11... | collective-permute-start | bytes 786440 | tf_op jit(solution)/shard_map/ppermute | solution.py:62
  185.0 30.2 %collective-permute-start.37 = (bf16[128,1024]{1,0:T(8,128)(2,1)S(1)}, bf16[128,1024]{1,0:T(8,128)(2,1)S(1)}, u32[]{:S(2)}, u32[]{:S(2)}) collective-permute-start(bf16[128,1024]{1,0:T(8,128)(2,1)S(1)} %collective-permute-done.30.refs_6_), channel_id=1, source_target_pairs={{0,1},{1,0},{2,3},{3,2},{4,5},{5,4},{6,7},{7,6},{8,9},{9,8},{10,11... | collective-permute-start | bytes 786440 | tf_op jit(solution)/shard_map/ppermute | solution.py:62
  192.4 22.8 %collective-permute-start.33 = (bf16[128,1024]{1,0:T(8,128)(2,1)S(1)}, bf16[128,1024]{1,0:T(8,128)(2,1)S(1)}, u32[]{:S(2)}, u32[]{:S(2)}) collective-permute-start(bf16[128,1024]{1,0:T(8,128)(2,1)S(1)} %collective-permute-done.31.refs_7_), channel_id=1, source_target_pairs={{4,6},{5,7},{12,14},{13,15},{20,22},{21,23},{28,30},{29,31}} | collective-permute-start | bytes 786440 | tf_op jit(solution)/shard_map/ppermute | solution.py:66
  194.1 21.6 %collective-permute-start.34 = (bf16[128,1024]{1,0:T(8,128)(2,1)S(1)}, bf16[128,1024]{1,0:T(8,128)(2,1)S(1)}, u32[]{:S(2)}, u32[]{:S(2)}) collective-permute-start(bf16[128,1024]{1,0:T(8,128)(2,1)S(1)} %collective-permute-done.32.refs_8_), channel_id=1, source_target_pairs={{2,0},{3,1},{10,8},{11,9},{18,16},{19,17},{26,24},{27,25}} | collective-permute-start | bytes 786440 | tf_op jit(solution)/shard_map/ppermute | solution.py:66
  214.5 14.2 %collective-permute-start.50 = (bf16[4,128,1024]{2,1,0:T(8,128)(2,1)}, bf16[4,128,1024]{2,1,0:T(8,128)(2,1)S(1)}, u32[]{:S(2)}, u32[]{:S(2)}) collective-permute-start(bf16[4,128,1024]{2,1,0:T(8,128)(2,1)} %get-tuple-element.41), channel_id=1, source_target_pairs={{0,1},{1,0},{2,3},{3,2},{4,5},{5,4},{6,7},{7,6},{8,9},{9,8},{10,11... | collective-permute-start | bytes 3145736 | tf_op jit(solution)/shard_map/ppermute | solution.py:62
  214.6 3.2 %collective-permute-start.38 = (bf16[128,1024]{1,0:T(8,128)(2,1)S(1)}, bf16[128,1024]{1,0:T(8,128)(2,1)S(1)}, u32[]{:S(2)}, u32[]{:S(2)}) collective-permute-start(bf16[128,1024]{1,0:T(8,128)(2,1)S(1)} %collective-permute-done.31.refs_7_), channel_id=1, source_target_pairs={{0,1},{1,0},{2,3},{3,2},{4,5},{5,4},{6,7},{7,6},{8,9},{9,8},{10,11... | collective-permute-start | bytes 786440 | tf_op jit(solution)/shard_map/ppermute | solution.py:62
  215.1 3.0 %collective-permute-start.39 = (bf16[128,1024]{1,0:T(8,128)(2,1)S(1)}, bf16[128,1024]{1,0:T(8,128)(2,1)S(1)}, u32[]{:S(2)}, u32[]{:S(2)}) collective-permute-start(bf16[128,1024]{1,0:T(8,128)(2,1)S(1)} %collective-permute-done.32.refs_8_), channel_id=1, source_target_pairs={{0,1},{1,0},{2,3},{3,2},{4,5},{5,4},{6,7},{7,6},{8,9},{9,8},{10,11... | collective-permute-start | bytes 786440 | tf_op jit(solution)/shard_map/ppermute | solution.py:62
  215.2 3.3 %collective-permute-start.40 = (bf16[128,1024]{1,0:T(8,128)(2,1)S(1)}, bf16[128,1024]{1,0:T(8,128)(2,1)S(1)}, u32[]{:S(2)}, u32[]{:S(2)}) collective-permute-start(bf16[128,1024]{1,0:T(8,128)(2,1)S(1)} %collective-permute-done.33.refs_9_), channel_id=1, source_target_pairs={{0,1},{1,0},{2,3},{3,2},{4,5},{5,4},{6,7},{7,6},{8,9},{9,8},{10,11... | collective-permute-start | bytes 786440 | tf_op jit(solution)/shard_map/ppermute | solution.py:62
  215.7 3.2 %collective-permute-start.41 = (bf16[128,1024]{1,0:T(8,128)(2,1)S(1)}, bf16[128,1024]{1,0:T(8,128)(2,1)S(1)}, u32[]{:S(2)}, u32[]{:S(2)}) collective-permute-start(bf16[128,1024]{1,0:T(8,128)(2,1)S(1)} %collective-permute-done.34.refs_10_), channel_id=1, source_target_pairs={{0,1},{1,0},{2,3},{3,2},{4,5},{5,4},{6,7},{7,6},{8,9},{9,8},{10,11... | collective-permute-start | bytes 786440 | tf_op jit(solution)/shard_map/ppermute | solution.py:62
  228.4 5.6 %collective-permute-start.42 = (bf16[4,128,1024]{2,1,0:T(8,128)(2,1)}, bf16[4,128,1024]{2,1,0:T(8,128)(2,1)S(1)}, u32[]{:S(2)}, u32[]{:S(2)}) collective-permute-start(bf16[4,128,1024]{2,1,0:T(8,128)(2,1)} %get-tuple-element.31), channel_id=1, source_target_pairs={{0,1},{1,0},{2,3},{3,2},{4,5},{5,4},{6,7},{7,6},{8,9},{9,8},{10,11... | collective-permute-start | bytes 3145736 | tf_op jit(solution)/shard_map/ppermute | solution.py:62
  230.1 53.0 %all-to-all-start.2 = ((bf16[4,128,1024]{2,1,0:T(8,128)(2,1)}), bf16[4,128,1024]{2,1,0:T(8,128)(2,1)S(1)}, u32[]{:S(2)}, u32[]{:S(2)}) async-start(bf16[4,128,1024]{2,1,0:T(8,128)(2,1)} %add.48), calls=%async_computation.2 | async-start | bytes 2097152 | tf_op jit(solution)/shard_map/all_to_all | solution.py:101
  237.7 35.6 %copy-start.37 = (bf16[128,1024]{1,0:T(8,128)(2,1)S(1)}, bf16[128,1024]{1,0:T(8,128)(2,1)}, u32[]{:S(2)}) copy-start(bf16[128,1024]{1,0:T(8,128)(2,1)} %get-tuple-element.35) | copy-start | bytes 786436
  237.7 44.5 %copy-start.23 = (f32[128,1024]{1,0:T(8,128)S(1)}, f32[128,1024]{1,0:T(8,128)}, u32[]{:S(2)}) copy-start(f32[128,1024]{1,0:T(8,128)} %get-tuple-element.27) | copy-start | bytes 1572868
  237.7 44.5 %copy-start.38 = (bf16[128,1024]{1,0:T(8,128)(2,1)S(1)}, bf16[128,1024]{1,0:T(8,128)(2,1)}, u32[]{:S(2)}) copy-start(bf16[128,1024]{1,0:T(8,128)(2,1)} %get-tuple-element.32) | copy-start | bytes 786436
  237.7 19.6 %collective-permute-start.43 = (bf16[128,1024]{1,0:T(8,128)(2,1)}, bf16[128,1024]{1,0:T(8,128)(2,1)S(1)}, u32[]{:S(2)}, u32[]{:S(2)}) collective-permute-start(bf16[128,1024]{1,0:T(8,128)(2,1)} %get-tuple-element.35), channel_id=1, source_target_pairs={{0,2},{1,3},{8,10},{9,11},{16,18},{17,19},{24,26},{25,27}} | collective-permute-start | bytes 786440 | tf_op jit(solution)/shard_map/ppermute | solution.py:66
  242.0 15.3 %collective-permute-start.46 = (bf16[128,1024]{1,0:T(8,128)(2,1)}, bf16[128,1024]{1,0:T(8,128)(2,1)S(1)}, u32[]{:S(2)}, u32[]{:S(2)}) collective-permute-start(bf16[128,1024]{1,0:T(8,128)(2,1)} %get-tuple-element.33), channel_id=1, source_target_pairs={{6,4},{7,5},{14,12},{15,13},{22,20},{23,21},{30,28},{31,29}} | collective-permute-start | bytes 786440 | tf_op jit(solution)/shard_map/ppermute | solution.py:66
  258.3 9.5 %collective-permute-start.44 = (bf16[128,1024]{1,0:T(8,128)(2,1)S(1)}, bf16[128,1024]{1,0:T(8,128)(2,1)S(1)}, u32[]{:S(2)}, u32[]{:S(2)}) collective-permute-start(bf16[128,1024]{1,0:T(8,128)(2,1)S(1)} %get-tuple-element.44), channel_id=1, source_target_pairs={{0,2},{1,3},{2,4},{3,5},{8,10},{9,11},{10,12},{11,13},{16,18},{17,... | collective-permute-start | bytes 786440 | tf_op jit(solution)/shard_map/ppermute | solution.py:66
  262.6 10.6 %collective-permute-start.47 = (bf16[128,1024]{1,0:T(8,128)(2,1)S(1)}, bf16[128,1024]{1,0:T(8,128)(2,1)S(1)}, u32[]{:S(2)}, u32[]{:S(2)}) collective-permute-start(bf16[128,1024]{1,0:T(8,128)(2,1)S(1)} %get-tuple-element.45), channel_id=1, source_target_pairs={{4,2},{5,3},{6,4},{7,5},{12,10},{13,11},{14,12},{15,13},{20,18},{2... | collective-permute-start | bytes 786440 | tf_op jit(solution)/shard_map/ppermute | solution.py:66
  268.9 8.8 %collective-permute-start.45 = (bf16[128,1024]{1,0:T(8,128)(2,1)S(1)}, bf16[128,1024]{1,0:T(8,128)(2,1)S(1)}, u32[]{:S(2)}, u32[]{:S(2)}) collective-permute-start(bf16[128,1024]{1,0:T(8,128)(2,1)S(1)} %add.43), channel_id=1, source_target_pairs={{0,2},{1,3},{2,4},{3,5},{4,6},{5,7},{8,10},{9,11},{10,12},{11,13},... | collective-permute-start | bytes 786440 | tf_op jit(solution)/shard_map/ppermute | solution.py:66
  273.4 8.9 %collective-permute-start.48 = (bf16[128,1024]{1,0:T(8,128)(2,1)S(1)}, bf16[128,1024]{1,0:T(8,128)(2,1)S(1)}, u32[]{:S(2)}, u32[]{:S(2)}) collective-permute-start(bf16[128,1024]{1,0:T(8,128)(2,1)S(1)} %add.46), channel_id=1, source_target_pairs={{2,0},{3,1},{4,2},{5,3},{6,4},{7,5},{10,8},{11,9},{12,10},{13,11},... | collective-permute-start | bytes 786440 | tf_op jit(solution)/shard_map/ppermute | solution.py:66
  (30 other events, 286.5 us)

commit v4 on v3

--- a/solution.py
+++ b/solution.py
@@ -129,7 +129,7 @@
                 start = pl.multiple_of(owner * rows, rows)
                 act(
                     pltpu.make_async_copy(
-                        refs[number], target.at[pl.ds(start, rows), :], sems.at[number]
+                        refs[number], target.at[pl.ds(start, rows), :], sems.at[owner]
                     )
                 )
 
@@ -164,6 +164,13 @@
     each_copy(*args, lambda copy: copy.wait())
 
 
+def wait_chip(ref, target, sems, rows, chip):
+    for owner in range(CORES * chip, CORES * (chip + 1)):
+        pltpu.make_async_copy(
+            ref, target.at[owner * rows : (owner + 1) * rows, :], sems.at[owner]
+        ).wait()
+
+
 def head_parts(proj_ref, head):
     def part(index):
         start = (index * HEADS + head) * HEAD_DIM
@@ -194,14 +201,15 @@
     hidden = x.astype(F32) + dot(heads, out_w)
     hidden_ref[...] = hidden
     rms = lax.rsqrt(mean_last(hidden * hidden) + EPS)
-    expert_ref[...] = jnp.broadcast_to((hidden * rms * gain_e).astype(BF16), expert_ref.shape)
+    expert_ref[...] = (hidden * rms * gain_e).astype(BF16)
 
 
 def early_kernel(count, depth, *refs):
-    place, xf_ref, xb_ref, gain_a = refs[:4]
-    mix_refs = refs[4 : 4 + count]
-    sumf_ref, sumb_ref, normed_ref = refs[4 + count : 7 + count]
-    mix_w, mix_sems = refs[7 + count :]
+    place, xf_ref, xb_ref, gain_a, mask_ref = refs[:5]
+    mix_refs = refs[5 : 5 + count]
+    sumf_ref, sumb_ref, normed_ref, allowed_ref = refs[5 + count : 9 + count]
+    mix_w, mix_sems = refs[9 + count :]
+    allowed_ref[...] = mask_ref[...]
     chip, core = place[0], place[1]
     mix_w[...] = jnp.zeros_like(mix_w)
     start_copies(mix_refs, mix_w, mix_sems, depth, chip, core)
@@ -329,24 +337,25 @@
             out_ref[owner] = result[pl.ds(start, rows), :]
 
 
-def expert_backward_kernel(rows, *refs):
+def expert_backward_kernel(count, rows, *refs):
     place, up_ref, act_ref = refs[:3]
-    row_refs = refs[3:5]
-    mine_ref, other_ref, tokens, result, sems = refs[5:]
-    chip, core = place[0], place[1]
-    fetch_line(row_refs, tokens, sems, rows, chip, core)
+    row_refs = refs[3 : 3 + count]
+    mine_ref, other_ref, tokens, result, sems = refs[3 + count :]
+    chip, core = place[0], place[1]
+    start_copies(row_refs, tokens, sems, rows, chip, core)
+    wait_copies(row_refs, tokens, sems, rows, chip, core)
     chunk = 2 * rows
 
     def step(index, carry):
         start = chunk_start(index, chunk)
-        pre = dot(tokens[pl.ds(start, chunk), :], up_ref[...])
+        pre = dot(tokens[pl.ds(start, chunk), :], up_ref[...], NT)
         square = pre * pre
         bend = jnp.tanh(GELU_C * pre * (1.0 + GELU_A * square))
         slope = 0.5 * (1.0 + bend) + 0.5 * pre * (1.0 - bend * bend) * (
             GELU_C * (1.0 + 3.0 * GELU_A * square)
         )
         grad = (act_ref[pl.ds(start, chunk), :] * slope).astype(BF16)
-        result[pl.ds(start, chunk), :] = dot(grad, up_ref[...], NT).astype(BF16)
+        result[pl.ds(start, chunk), :] = dot(grad, up_ref[...]).astype(BF16)
         return carry
 
     each_chunk(tokens.shape[0] // chunk, step)
@@ -364,7 +373,7 @@
 
     def step(index, carry):
         start = chunk_start(index, chunk)
-        pre = dot(tokens[pl.ds(start, chunk), :], up_ref[...])
+        pre = dot(tokens[pl.ds(start, chunk), :], up_ref[...], NT)
         bend = jnp.tanh(GELU_C * pre * (1.0 + GELU_A * (pre * pre)))
         active = (0.5 * pre * (1.0 + bend)).astype(BF16)
         out = dot(active, down_ref[...])
@@ -424,11 +433,15 @@
     place, x_ref, mixed_ref, grad_ref, gain_a = refs[:5]
     mix_refs = refs[5 : 5 + count]
     result_ref = refs[5 + count]
-    mix_w, mix_sems = refs[6 + count :]
+    mix_w, normed, mix_sems = refs[6 + count :]
     chip, core = place[0], place[1]
     start_copies(mix_refs, mix_w, mix_sems, depth, chip, core)
-    wait_copies(mix_refs, mix_w, mix_sems, depth, chip, core)
-    grad_normed = dot(mixed_ref[...], mix_w[...], NT)
+    block = CORES * depth
+    for origin in range(mix_w.shape[0] // block):
+        wait_chip(mix_refs[0], mix_w, mix_sems, depth, origin)
+        span = slice(origin * block, (origin + 1) * block)
+        normed[:, span] = dot(mixed_ref[...], mix_w[span, :], NT)
+    grad_normed = normed[...]
     x = x_ref[...].astype(F32)
     rms_one = lax.rsqrt(mean_last(x * x) + EPS)
     normal_one = x * rms_one
@@ -500,9 +513,9 @@
     depth = w_qkv.shape[1]
     total = expert_count * tokens
     columns = w_qkv.shape[2]
-    up_weight = w_up[0, 0]
+    up_weight = jnp.swapaxes(w_up[0, 0], 0, 1)
     down_weight = w_down[0, 0]
-    hidden_units = up_weight.shape[1]
+    hidden_units = up_weight.shape[0]
     count = CORES * (2 * length - 1)
 
     mixers = with_partner(relayed(w_qkv[0]))
@@ -518,17 +531,18 @@
     early_mix = mixers[: half - 2] + mixers[half : count - 2]
     last_mix = mixers[half - 2 : half] + mixers[count - 2 :]
     early = len(early_mix)
-    sum_fwd, sum_bwd, normed = call(
+    sum_fwd, sum_bwd, normed, mask = call(
         functools.partial(early_kernel, early, depth),
         (
             shaped((tokens, columns), F32),
             shaped((tokens, columns), F32),
             shaped((2 * tokens, width), BF16),
+            shaped(mask.shape, F32),
         ),
-        [SMEM] + [VMEM] * 3 + [ANY] * early,
-        (VMEM,) * 3,
-        [pltpu.VMEM((width, columns), BF16), dma(early)],
-        [place, arriving, stashed_input, attention_gain] + early_mix,
+        [SMEM] + [VMEM] * 4 + [ANY] * early,
+        (VMEM,) * 4,
+        [pltpu.VMEM((width, columns), BF16), dma(expert_count)],
+        [place, arriving, stashed_input, attention_gain, mask] + early_mix,
     )
     proj_fwd, proj_bwd, hidden_bwd, expert_bwd = call(
         functools.partial(project_kernel, count, depth, length),
@@ -536,7 +550,7 @@
             shaped((tokens, columns), F32),
             shaped((tokens, columns), F32),
             shaped((tokens, width), F32),
-            shaped((length, tokens, width), BF16),
+            shaped((tokens, width), BF16),
         ),
         [SMEM] + [VMEM] * 6 + [ANY] * (4 + count),
         (VMEM,) * 4,
@@ -545,18 +559,18 @@
             pltpu.VMEM((width, width), BF16),
             pltpu.VMEM((tokens, width), BF16),
             dma(4),
-            dma(count),
+            dma(expert_count),
         ],
         [place, sum_fwd, sum_bwd, normed, stashed_input, expert_gain, mask] + last_mix + outers,
     )
-    rows_bwd = spread(expert_bwd)
+    rows_bwd = with_partner(relayed(expert_bwd))
 
     hidden_fwd, expert_fwd = call(
         functools.partial(forward_kernel, count, depth),
         (shaped((tokens, width), F32), shaped((tokens, width), BF16)),
         [SMEM] + [VMEM] * 4 + [ANY] * count,
         (VMEM,) * 2,
-        [pltpu.VMEM((width, width), BF16), pltpu.VMEM((tokens, width), BF16), dma(count)],
+        [pltpu.VMEM((width, width), BF16), pltpu.VMEM((tokens, width), BF16), dma(expert_count)],
         [place, arriving, proj_fwd, expert_gain, mask] + outers,
     )
     rows_fwd = with_partner(relayed(expert_fwd))
@@ -576,11 +590,11 @@
         return [pltpu.VMEM((total, width), BF16), pltpu.VMEM((total, width), BF16), dma(sems)]
 
     mine, other = call(
-        functools.partial(expert_backward_kernel, tokens),
+        functools.partial(expert_backward_kernel, count, tokens),
         pair,
-        [SMEM, VMEM, VMEM] + [ANY] * 2,
+        [SMEM, VMEM, VMEM] + [ANY] * count,
         (VMEM,) * 2,
-        expert_scratch((CORES, length)),
+        expert_scratch(expert_count),
         [place, up_weight, grad_act] + rows_bwd,
     )
     grad_parts = across(mine + swapped(other))
@@ -590,7 +604,7 @@
         pair,
         [SMEM, VMEM, VMEM, VMEM] + [ANY] * count,
         (VMEM,) * 2,
-        expert_scratch(count),
+        expert_scratch(expert_count),
         [place, up_weight, down_weight, gate_fwd] + rows_fwd,
     )
     moe_parts = scattered(
@@ -609,7 +623,7 @@
         (shaped((tokens, columns), BF16), shaped((tokens, width), F32)),
         [SMEM] + [VMEM] * 6 + [ANY] * count,
         (VMEM,) * 2,
-        [pltpu.VMEM((width, width), BF16), dma(count)],
+        [pltpu.VMEM((width, width), BF16), dma(expert_count)],
         [place, cotangent, hidden_bwd, proj_bwd, expert_gain, mask, grad_parts]
         + outers,
     )
@@ -618,7 +632,11 @@
         shaped((tokens, width), BF16),
         [SMEM] + [VMEM] * 4 + [ANY] * count,
         VMEM,
-        [pltpu.VMEM((width, columns), BF16), dma(count)],
+        [
+            pltpu.VMEM((width, columns), BF16),
+            pltpu.VMEM((tokens, width), F32),
+            dma(expert_count),
+        ],
         [place, stashed_input, grad_mixed, grad_hidden, attention_gain] + mixers,
     )
 

time: 301 us -> 274 us (0.910)
  waiting for transfers between devices: 152 us -> 114 us
  starting transfers between devices: 64.8 us -> 77.8 us
    all_to_all x3 -> x2, waiting for transfers between devices: 26.1 us -> 0.01 us  [across(): lax.all_to_all(blocks, 'expert', split_axis=0, concat_axis=0, axis_index_...]
    ppermute x24 -> x30, waiting for transfers between devices: 119 us -> 105 us  [hop(): return lax.ppermute(value, 'expert', chip_pairs(sources, move))]
    ppermute x24 -> x30, starting transfers between devices: 44.3 us -> 57 us  [hop(): return lax.ppermute(value, 'expert', chip_pairs(sources, move))]
    ppermute x2, waiting for transfers between devices: 1.52 us -> 4.71 us  [passed_along(): return lax.ppermute(value, axis, pairs)]
    unnamed x81 -> x106, local copies, waits for them, and re-layouts: 7.09 us -> 4.77 us
    ppermute x25 -> x31, starting transfers between devices: 5.51 us -> 6.7 us  [swapped(): return lax.ppermute(value, 'expert', [(i, i ^ 1) for i in range(count)])]
    all_to_all x3 -> x2, starting transfers between devices: 11 us -> 11.5 us  [across(): lax.all_to_all(blocks, 'expert', split_axis=0, concat_axis=0, axis_index_...]
  transfers between devices with their start and end apart: 54 -> 65, of which waited for: 19 -> 21; matrix products, arithmetic and copies ran while one was open for 4% -> 3% of each run, Pallas kernels for 17% -> 18%
where the time goes in v4:
time: 274 us; the launch traced here: 273 us
  waiting for transfers between devices  114 us (42%)
  starting transfers between devices  77.8 us (28%)
  Pallas kernels  66 us (24%)
  other arithmetic  6.39 us (2%)
  local copies, waits for them, and re-layouts  5.98 us (2%)
    ppermute x30, waiting for transfers between devices, hop(): return lax.ppermute(value, 'expert', chip_pairs(sources, move))  105 us
    pallas_call x9, Pallas kernels, call(): pl.pallas_call(kernel, out_shape=outs, in_specs=specs, out_specs=out_spec...  66 us
    ppermute x30, starting transfers between devices, hop(): return lax.ppermute(value, 'expert', chip_pairs(sources, move))  57 us
    all_to_all x2, starting transfers between devices, across(): lax.all_to_all(blocks, 'expert', split_axis=0, concat_axis=0, axis_index_...  11.5 us
    ppermute x31, starting transfers between devices, swapped(): return lax.ppermute(value, 'expert', [(i, i ^ 1) for i in range(count)])  6.7 us
  transfers between devices with their start and end apart: 65, of which 21 were waited for; matrix products, arithmetic and copies ran while one was open for 3% of the time, Pallas kernels for 18%

profile of v4, /device:TPU:0, one launch (start us, length us, event | category | flops | bytes accessed | tf_op | source)
XLA Modules:
  0.0 272.7 jit_solution(4482410571092936099)
XLA Ops:
  0.6 5.9 %collective-permute-start.1 = (bf16[128,3072]{1,0:T(8,128)(2,1)}, bf16[128,3072]{1,0:T(8,128)(2,1)}, u32[]{:S(2)}, u32[]{:S(2)}) collective-permute-start(bf16[128,3072]{1,0:T(8,128)(2,1)} %bitcast.32), channel_id=1, source_target_pairs={{0,2},{1,3},{2,4},{3,5},{4,6},{5,7},{8,10},{9,11},{10,12},{11,13},... | collective-permute-start | bytes 2359304 | tf_op jit(solution)/shard_map/ppermute | solution.py:66
  6.5 1.3 collective-permute-start.2
  7.8 2.5 collective-permute-start.27
  10.3 4.6 %collective-permute-start.14 = (bf16[128,1024]{1,0:T(8,128)(2,1)}, bf16[128,1024]{1,0:T(8,128)(2,1)S(1)}, u32[]{:S(2)}, u32[]{:S(2)}) collective-permute-start(bf16[128,1024]{1,0:T(8,128)(2,1)} %bitcast.37), channel_id=1, source_target_pairs={{0,2},{1,3},{2,4},{3,5},{4,6},{5,7},{8,10},{9,11},{10,12},{11,13},... | collective-permute-start | bytes 786440 | tf_op jit(solution)/shard_map/ppermute | solution.py:66
  14.9 0.7 add_divide_fusion
  15.6 0.7 select_reduce_fusion
  16.4 0.9 collective-permute-done.27.refs_1_
  17.3 1.3 collective-permute-start.15
  18.6 3.8 %collective-permute-done.refs_1_ = bf16[128,1024]{1,0:T(8,128)(2,1)S(1)} collective-permute-done((bf16[128,1024]{1,0:T(8,128)(2,1)}, bf16[128,1024]{1,0:T(8,128)(2,1)S(1)}, u32[]{:S(2)}, u32[]{:S(2)}) %collective-permute-start) | collective-permute-done | bytes 262176 | tf_op jit(solution)/shard_map/ppermute | solution.py:45
  22.4 5.9 %collective-permute-done.14.refs_12_.refs_6_.refs_8_ = bf16[128,1024]{1,0:T(8,128)(2,1)S(1)} collective-permute-done((bf16[128,1024]{1,0:T(8,128)(2,1)}, bf16[128,1024]{1,0:T(8,128)(2,1)S(1)}, u32[]{:S(2)}, u32[]{:S(2)}) %collective-permute-start.14) | collective-permute-done | bytes 262176 | tf_op jit(solution)/shard_map/ppermute | solution.py:66
  29.0 1.1 broadcast_in_dim.16
  30.1 7.6 %all-to-all-start = ((bf16[4,128,1152]{2,1,0:T(8,128)(2,1)}), bf16[4,128,1152]{2,1,0:T(8,128)(2,1)S(1)}, u32[]{:S(2)}, u32[]{:S(2)}) async-start(bf16[4,128,1152]{2,1,0:T(8,128)(2,1)} %broadcast_in_dim.16), calls=%async_computation | async-start | bytes 2359296 | tf_op jit(solution)/shard_map/all_to_all | solution.py:101
  37.7 1.3 collective-permute-start.17
  39.7 1.5 collective-permute-start.3
  41.2 1.3 collective-permute-start.4
  42.5 22.2 %collective-permute-done.17.refs_15_.refs_9_.refs_11_ = bf16[128,1024]{1,0:T(8,128)(2,1)S(1)} collective-permute-done((bf16[128,1024]{1,0:T(8,128)(2,1)S(1)}, bf16[128,1024]{1,0:T(8,128)(2,1)S(1)}, u32[]{:S(2)}, u32[]{:S(2)}) %collective-permute-start.17) | collective-permute-done | bytes 262176 | tf_op jit(solution)/shard_map/ppermute | solution.py:66
  65.4 1.3 collective-permute-start.19
  67.5 18.5 %collective-permute-done.19.refs_17_.refs_11_.refs_13_ = bf16[128,1024]{1,0:T(8,128)(2,1)S(1)} collective-permute-done((bf16[128,1024]{1,0:T(8,128)(2,1)S(1)}, bf16[128,1024]{1,0:T(8,128)(2,1)S(1)}, u32[]{:S(2)}, u32[]{:S(2)}) %collective-permute-start.19) | collective-permute-done | bytes 262176 | tf_op jit(solution)/shard_map/ppermute | solution.py:66
  86.7 0.7 collective-permute-start.10
  87.5 1.3 collective-permute-start.11
  91.2 18.2 %collective-permute-done.11.refs_8_.refs_11_ = bf16[128,3072]{1,0:T(8,128)(2,1)S(1)} collective-permute-done((bf16[128,3072]{1,0:T(8,128)(2,1)}, bf16[128,3072]{1,0:T(8,128)(2,1)S(1)}, u32[]{:S(2)}, u32[]{:S(2)}) %collective-permute-start.11) | collective-permute-done | bytes 786464 | tf_op jit(solution)/shard_map/ppermute | solution.py:66
  110.7 1.1 fusion.refs_4_
  111.7 7.6 %shard_map.131 = (f32[128,3072]{1,0:T(8,128)}, f32[128,3072]{1,0:T(8,128)}, bf16[256,1024]{1,0:T(8,128)(2,1)}, f32[2,128,128]{2,1,0:T(8,128)}) custom-call(s32[2]{0:T(128)} %pad_add_fusion.refs_0_.place, bf16[128,1024]{1,0:T(8,128)(2,1)} %copy-done.19, bf16[128,1024]{1,0:T(8,128)(2,1)} %refs_1_.1, f32[1,1024]{1,0:T(1,128)} %refs_4_.5, ...), custom_call_target="tpu_custom_call" | custom-call | tf_op jit(solution)/shard_map/pallas_call | solution.py:462
  119.4 0.9 copy-done.4
  120.3 8.8 %shard_map.132 = (f32[128,3072]{1,0:T(8,128)}, f32[128,3072]{1,0:T(8,128)}, f32[128,1024]{1,0:T(8,128)}, bf16[128,1024]{1,0:T(8,128)(2,1)}) custom-call(s32[2]{0:T(128)} %pad_add_fusion.refs_0_.place, f32[128,3072]{1,0:T(8,128)} %get-tuple-element.24.refs_1_, f32[128,3072]{1,0:T(8,128)} %get-tuple-element.25.refs_2_, ...), custom_call_target="tpu_custom_call" | custom-call | tf_op jit(solution)/shard_map/pallas_call | solution.py:462
  129.1 1.3 collective-permute-start.49
  130.4 1.3 collective-permute-start.50
  131.8 5.1 %shard_map.133 = (f32[128,1024]{1,0:T(8,128)}, bf16[128,1024]{1,0:T(8,128)(2,1)}) custom-call(s32[2]{0:T(128)} %pad_add_fusion.refs_0_.place, bf16[128,1024]{1,0:T(8,128)(2,1)} %copy-done.19, f32[128,3072]{1,0:T(8,128)} %get-tuple-element.28.refs_2_, f32[1,1024]{1,0:T(1,128)} %refs_4_.4, f32[2,128,128]{2,1,0:T(8,128)} %get-tuple-element.27.refs_6_.refs_4_.refs_5_, ...), custom_call_target="tpu_custom_call" | custom-call | tf_op jit(solution)/shard_map/pallas_call | solution.py:462
  136.9 4.6 %collective-permute-start.29 = (bf16[128,1024]{1,0:T(8,128)(2,1)}, bf16[128,1024]{1,0:T(8,128)(2,1)S(1)}, u32[]{:S(2)}, u32[]{:S(2)}) collective-permute-start(bf16[128,1024]{1,0:T(8,128)(2,1)} %get-tuple-element.31.refs_4_), channel_id=1, source_target_pairs={{0,2},{1,3},{2,4},{3,5},{4,6},{5,7},{8,10},{9,11},{10,12},{11,13},... | collective-permute-start | bytes 786440 | tf_op jit(solution)/shard_map/ppermute | solution.py:66
  141.5 1.3 collective-permute-start.30
  142.9 0.7 collective-permute-start.51
  143.6 1.3 collective-permute-start.52
  144.9 2.7 collective-permute-done.29.refs_5_
  148.3 4.5 %collective-permute-done.30.refs_6_ = bf16[128,1024]{1,0:T(8,128)(2,1)S(1)} collective-permute-done((bf16[128,1024]{1,0:T(8,128)(2,1)}, bf16[128,1024]{1,0:T(8,128)(2,1)S(1)}, u32[]{:S(2)}, u32[]{:S(2)}) %collective-permute-start.30) | collective-permute-done | bytes 262176 | tf_op jit(solution)/shard_map/ppermute | solution.py:66
  152.8 1.3 collective-permute-start.32
  154.9 3.5 %collective-permute-done.52.refs_7_ = bf16[128,1024]{1,0:T(8,128)(2,1)S(1)} collective-permute-done((bf16[128,1024]{1,0:T(8,128)(2,1)S(1)}, bf16[128,1024]{1,0:T(8,128)(2,1)S(1)}, u32[]{:S(2)}, u32[]{:S(2)}) %collective-permute-start.52) | collective-permute-done | bytes 262176 | tf_op jit(solution)/shard_map/ppermute | solution.py:66
  158.4 1.3 collective-permute-start.54
  159.8 4.2 %collective-permute-done.32.refs_8_ = bf16[128,1024]{1,0:T(8,128)(2,1)S(1)} collective-permute-done((bf16[128,1024]{1,0:T(8,128)(2,1)S(1)}, bf16[128,1024]{1,0:T(8,128)(2,1)S(1)}, u32[]{:S(2)}, u32[]{:S(2)}) %collective-permute-start.32) | collective-permute-done | bytes 262176 | tf_op jit(solution)/shard_map/ppermute | solution.py:66
  164.6 3.9 %collective-permute-done.54.refs_9_ = bf16[128,1024]{1,0:T(8,128)(2,1)S(1)} collective-permute-done((bf16[128,1024]{1,0:T(8,128)(2,1)S(1)}, bf16[128,1024]{1,0:T(8,128)(2,1)S(1)}, u32[]{:S(2)}, u32[]{:S(2)}) %collective-permute-start.54) | collective-permute-done | bytes 262176 | tf_op jit(solution)/shard_map/ppermute | solution.py:66
  170.2 1.5 collective-permute-start.34
  171.7 6.6 %shard_map.134 = (f32[1024,704]{1,0:T(8,128)}, f32[1024,128]{1,0:T(8,128)}) custom-call(s32[2]{0:T(128)} %pad_add_fusion.refs_0_.place, bf16[704,1024]{1,0:T(8,128)(2,1)} %bitcast.30, bf16[4,128,1152]{2,1,0:T(8,128)(2,1)} %copy-done, bf16[4,128,1152]{2,1,0:T(8,128)(2,1)} %collective-permute-done.28.refs_3_), custom_call_target="tpu_custom_call" | custom-call | tf_op jit(solution)/shard_map/pallas_call | solution.py:462
  178.5 9.8 %shard_map.137 = (bf16[4,128,1024]{2,1,0:T(8,128)(2,1)}, bf16[4,128,1024]{2,1,0:T(8,128)(2,1)}) custom-call(s32[2]{0:T(128)} %pad_add_fusion.refs_0_.place, bf16[704,1024]{1,0:T(8,128)(2,1)} %bitcast.28, f32[1024,704]{1,0:T(8,128)} %get-tuple-element.40.refs_2_, bf16[128,1024]{1,0:T(8,128)(2,1)} %get-tuple-element.41.refs_3_, bf16[128,1024]{1,0:T(8,128)(2,1)} %copy-done.37, ...), custom_call_target="tpu_custom_call" | custom-call | tf_op jit(solution)/shard_map/pallas_call | solution.py:462
  189.7 2.0 collective-permute-done.38.refs_14_
  193.5 8.8 %shard_map.135 = (bf16[4,128,1024]{2,1,0:T(8,128)(2,1)}, bf16[4,128,1024]{2,1,0:T(8,128)(2,1)}) custom-call(s32[2]{0:T(128)} %pad_add_fusion.refs_0_.place, bf16[704,1024]{1,0:T(8,128)(2,1)} %bitcast.29, bf16[704,1024]{1,0:T(8,128)(2,1)} %bitcast.31, f32[1024,128]{1,0:T(8,128)} %get-tuple-element.30.refs_3_, bf16[128,1024]{1,0:T(8,128)(2,1)} %get-tuple-element.31.refs_4_, ...), custom_call_target="tpu_custom_call" | custom-call | tf_op jit(solution)/shard_map/pallas_call | solution.py:462
  202.6 1.4 add.48
  204.0 3.9 %all-to-all-start.1 = ((bf16[4,128,1024]{2,1,0:T(8,128)(2,1)}), bf16[4,128,1024]{2,1,0:T(8,128)(2,1)S(1)}, u32[]{:S(2)}, u32[]{:S(2)}) async-start(bf16[4,128,1024]{2,1,0:T(8,128)(2,1)} %add.48), calls=%async_computation.1 | async-start | bytes 2097152 | tf_op jit(solution)/shard_map/all_to_all | solution.py:101
  207.9 1.0 copy-done.20
  208.9 2.7 shard_map.136
  211.6 4.3 %collective-permute-start.43 = (bf16[128,1024]{1,0:T(8,128)(2,1)}, bf16[128,1024]{1,0:T(8,128)(2,1)S(1)}, u32[]{:S(2)}, u32[]{:S(2)}) collective-permute-start(bf16[128,1024]{1,0:T(8,128)(2,1)} %get-tuple-element.37), channel_id=1, source_target_pairs={{0,2},{1,3},{8,10},{9,11},{16,18},{17,19},{24,26},{25,27}} | collective-permute-start | bytes 786440 | tf_op jit(solution)/shard_map/ppermute | solution.py:66
  215.9 0.7 collective-permute-start.46
  216.6 14.6 %collective-permute-done.43 = bf16[128,1024]{1,0:T(8,128)(2,1)S(1)} collective-permute-done((bf16[128,1024]{1,0:T(8,128)(2,1)}, bf16[128,1024]{1,0:T(8,128)(2,1)S(1)}, u32[]{:S(2)}, u32[]{:S(2)}) %collective-permute-start.43) | collective-permute-done | bytes 262176 | tf_op jit(solution)/shard_map/ppermute | solution.py:66
  231.2 1.0 fusion.20
  232.2 0.7 collective-permute-start.47
  232.9 4.9 %collective-permute-start.44 = (bf16[128,1024]{1,0:T(8,128)(2,1)S(1)}, bf16[128,1024]{1,0:T(8,128)(2,1)S(1)}, u32[]{:S(2)}, u32[]{:S(2)}) collective-permute-start(bf16[128,1024]{1,0:T(8,128)(2,1)S(1)} %get-tuple-element.46), channel_id=1, source_target_pairs={{0,2},{1,3},{2,4},{3,5},{8,10},{9,11},{10,12},{11,13},{16,18},{17,... | collective-permute-start | bytes 786440 | tf_op jit(solution)/shard_map/ppermute | solution.py:66
  237.8 1.0 add.46
  238.9 1.3 collective-permute-start.48
  240.2 2.9 %collective-permute-done.44 = bf16[128,1024]{1,0:T(8,128)(2,1)S(1)} collective-permute-done((bf16[128,1024]{1,0:T(8,128)(2,1)S(1)}, bf16[128,1024]{1,0:T(8,128)(2,1)S(1)}, u32[]{:S(2)}, u32[]{:S(2)}) %collective-permute-start.44) | collective-permute-done | bytes 262176 | tf_op jit(solution)/shard_map/ppermute | solution.py:66
  243.1 7.0 %collective-permute-start.45 = (bf16[128,1024]{1,0:T(8,128)(2,1)S(1)}, bf16[128,1024]{1,0:T(8,128)(2,1)S(1)}, u32[]{:S(2)}, u32[]{:S(2)}) collective-permute-start(bf16[128,1024]{1,0:T(8,128)(2,1)S(1)} %add.43), channel_id=1, source_target_pairs={{0,2},{1,3},{2,4},{3,5},{4,6},{5,7},{8,10},{9,11},{10,12},{11,13},... | collective-permute-start | bytes 786440 | tf_op jit(solution)/shard_map/ppermute | solution.py:66
  250.1 2.9 %collective-permute-done.48 = bf16[128,1024]{1,0:T(8,128)(2,1)S(1)} collective-permute-done((bf16[128,1024]{1,0:T(8,128)(2,1)S(1)}, bf16[128,1024]{1,0:T(8,128)(2,1)S(1)}, u32[]{:S(2)}, u32[]{:S(2)}) %collective-permute-start.48) | collective-permute-done | bytes 262176 | tf_op jit(solution)/shard_map/ppermute | solution.py:66
  252.9 1.3 collective-permute-done.45
  254.2 0.8 add_convert_fusion
  255.1 1.0 copy-done.1
  256.1 8.1 %shard_map.138 = (bf16[128,3072]{1,0:T(8,128)(2,1)}, f32[128,1024]{1,0:T(8,128)}) custom-call(s32[2]{0:T(128)} %pad_add_fusion.refs_0_.place, bf16[128,1024]{1,0:T(8,128)(2,1)} %copy-done.21, f32[128,1024]{1,0:T(8,128)} %get-tuple-element.38.refs_2_, f32[128,3072]{1,0:T(8,128)} %get-tuple-element.39.refs_3_, f32[1,1024]{1,0:T(1,128)} %refs_4_.4, ...), custom_call_target="tpu_custom_call" | custom-call | tf_op jit(solution)/shard_map/pallas_call | solution.py:462
  264.2 8.3 %shard_map.139 = bf16[128,1024]{1,0:T(8,128)(2,1)} custom-call(s32[2]{0:T(128)} %pad_add_fusion.refs_0_.place, bf16[128,1024]{1,0:T(8,128)(2,1)} %refs_1_.1, bf16[128,3072]{1,0:T(8,128)(2,1)} %get-tuple-element.44.refs_2_, f32[128,1024]{1,0:T(8,128)} %get-tuple-element.45.refs_3_, f32[1,1024]{1,0:T(1,128)} %refs_4_.5, bf16[128,3072]{1,0:T(8,128)(2,1)} %bitcast.35, ...), custom_call_target="tpu_custom_call" | custom-call | tf_op jit(solution)/shard_map/pallas_call | solution.py:462
  (198 shorter events, 14.6 us)
Async XLA Ops:
  0.6 39.0 %collective-permute-start.1 = (bf16[128,3072]{1,0:T(8,128)(2,1)}, bf16[128,3072]{1,0:T(8,128)(2,1)}, u32[]{:S(2)}, u32[]{:S(2)}) collective-permute-start(bf16[128,3072]{1,0:T(8,128)(2,1)} %bitcast.32), channel_id=1, source_target_pairs={{0,2},{1,3},{2,4},{3,5},{4,6},{5,7},{8,10},{9,11},{10,12},{11,13},... | collective-permute-start | bytes 2359304 | tf_op jit(solution)/shard_map/ppermute | solution.py:66
  6.5 34.7 %collective-permute-start.2 = (bf16[128,3072]{1,0:T(8,128)(2,1)}, bf16[128,3072]{1,0:T(8,128)(2,1)}, u32[]{:S(2)}, u32[]{:S(2)}) collective-permute-start(bf16[128,3072]{1,0:T(8,128)(2,1)} %bitcast.33), channel_id=1, source_target_pairs={{2,0},{3,1},{4,2},{5,3},{6,4},{7,5},{10,8},{11,9},{12,10},{13,11},... | collective-permute-start | bytes 2359304 | tf_op jit(solution)/shard_map/ppermute | solution.py:66
  7.8 9.5 %collective-permute-start.27 = (bf16[128,1024]{1,0:T(8,128)(2,1)}, bf16[128,1024]{1,0:T(8,128)(2,1)S(1)}, u32[]{:S(2)}, u32[]{:S(2)}) collective-permute-start(bf16[128,1024]{1,0:T(8,128)(2,1)} %param.14), channel_id=1, source_target_pairs={{0,24},{8,0},{16,8},{24,16},{1,25},{9,1},{17,9},{25,17},{2,26},{10... | collective-permute-start | bytes 786440 | tf_op jit(solution)/shard_map/ppermute | solution.py:45
  10.3 12.1 %collective-permute-start = (bf16[128,1024]{1,0:T(8,128)(2,1)}, bf16[128,1024]{1,0:T(8,128)(2,1)S(1)}, u32[]{:S(2)}, u32[]{:S(2)}) collective-permute-start(bf16[128,1024]{1,0:T(8,128)(2,1)} %param.12), channel_id=1, source_target_pairs={{0,8},{8,16},{16,24},{24,0},{1,9},{9,17},{17,25},{25,1},{2,10},{10... | collective-permute-start | bytes 786440 | tf_op jit(solution)/shard_map/ppermute | solution.py:45
  10.3 18.0 %collective-permute-start.14 = (bf16[128,1024]{1,0:T(8,128)(2,1)}, bf16[128,1024]{1,0:T(8,128)(2,1)S(1)}, u32[]{:S(2)}, u32[]{:S(2)}) collective-permute-start(bf16[128,1024]{1,0:T(8,128)(2,1)} %bitcast.37), channel_id=1, source_target_pairs={{0,2},{1,3},{2,4},{3,5},{4,6},{5,7},{8,10},{9,11},{10,12},{11,13},... | collective-permute-start | bytes 786440 | tf_op jit(solution)/shard_map/ppermute | solution.py:66
  17.3 20.4 %collective-permute-start.15 = (bf16[128,1024]{1,0:T(8,128)(2,1)}, bf16[128,1024]{1,0:T(8,128)(2,1)S(1)}, u32[]{:S(2)}, u32[]{:S(2)}) collective-permute-start(bf16[128,1024]{1,0:T(8,128)(2,1)} %bitcast.38), channel_id=1, source_target_pairs={{2,0},{3,1},{4,2},{5,3},{6,4},{7,5},{10,8},{11,9},{12,10},{13,11},... | collective-permute-start | bytes 786440 | tf_op jit(solution)/shard_map/ppermute | solution.py:66
  22.4 16.6 %collective-permute-start.20 = (bf16[128,1024]{1,0:T(8,128)(2,1)}, bf16[128,1024]{1,0:T(8,128)(2,1)S(1)}, u32[]{:S(2)}, u32[]{:S(2)}) collective-permute-start(bf16[128,1024]{1,0:T(8,128)(2,1)} %bitcast.39), channel_id=1, source_target_pairs={{0,1},{1,0},{2,3},{3,2},{4,5},{5,4},{6,7},{7,6},{8,9},{9,8},{10,11... | collective-permute-start | bytes 786440 | tf_op jit(solution)/shard_map/ppermute | solution.py:62
  28.3 10.8 %collective-permute-start.16 = (bf16[128,1024]{1,0:T(8,128)(2,1)S(1)}, bf16[128,1024]{1,0:T(8,128)(2,1)S(1)}, u32[]{:S(2)}, u32[]{:S(2)}) collective-permute-start(bf16[128,1024]{1,0:T(8,128)(2,1)S(1)} %collective-permute-done.14.refs_12_.refs_6_.refs_8_), channel_id=1, source_target_pairs={{2,4},{3,5},{4,6},{5,7},{10,12},{11,13},{12,14},{13,15},{18,20},{1... | collective-permute-start | bytes 786440 | tf_op jit(solution)/shard_map/ppermute | solution.py:66
  30.1 60.5 %all-to-all-start = ((bf16[4,128,1152]{2,1,0:T(8,128)(2,1)}), bf16[4,128,1152]{2,1,0:T(8,128)(2,1)S(1)}, u32[]{:S(2)}, u32[]{:S(2)}) async-start(bf16[4,128,1152]{2,1,0:T(8,128)(2,1)} %broadcast_in_dim.16), calls=%async_computation | async-start | bytes 2359296 | tf_op jit(solution)/shard_map/all_to_all | solution.py:101
  37.7 26.9 %collective-permute-start.17 = (bf16[128,1024]{1,0:T(8,128)(2,1)S(1)}, bf16[128,1024]{1,0:T(8,128)(2,1)S(1)}, u32[]{:S(2)}, u32[]{:S(2)}) collective-permute-start(bf16[128,1024]{1,0:T(8,128)(2,1)S(1)} %collective-permute-done.15.refs_13_.refs_7_.refs_9_), channel_id=1, source_target_pairs={{2,0},{3,1},{4,2},{5,3},{10,8},{11,9},{12,10},{13,11},{18,16},{19,... | collective-permute-start | bytes 786440 | tf_op jit(solution)/shard_map/ppermute | solution.py:66
  39.1 26.3 %collective-permute-start.21 = (bf16[128,1024]{1,0:T(8,128)(2,1)S(1)}, bf16[128,1024]{1,0:T(8,128)(2,1)S(1)}, u32[]{:S(2)}, u32[]{:S(2)}) collective-permute-start(bf16[128,1024]{1,0:T(8,128)(2,1)S(1)} %collective-permute-done.14.refs_12_.refs_6_.refs_8_), channel_id=1, source_target_pairs={{0,1},{1,0},{2,3},{3,2},{4,5},{5,4},{6,7},{7,6},{8,9},{9,8},{10,11... | collective-permute-start | bytes 786440 | tf_op jit(solution)/shard_map/ppermute | solution.py:62
  39.2 27.5 %collective-permute-start.22 = (bf16[128,1024]{1,0:T(8,128)(2,1)S(1)}, bf16[128,1024]{1,0:T(8,128)(2,1)S(1)}, u32[]{:S(2)}, u32[]{:S(2)}) collective-permute-start(bf16[128,1024]{1,0:T(8,128)(2,1)S(1)} %collective-permute-done.15.refs_13_.refs_7_.refs_9_), channel_id=1, source_target_pairs={{0,1},{1,0},{2,3},{3,2},{4,5},{5,4},{6,7},{7,6},{8,9},{9,8},{10,11... | collective-permute-start | bytes 786440 | tf_op jit(solution)/shard_map/ppermute | solution.py:62
  39.7 47.1 %collective-permute-start.3 = (bf16[128,3072]{1,0:T(8,128)(2,1)}, bf16[128,3072]{1,0:T(8,128)(2,1)}, u32[]{:S(2)}, u32[]{:S(2)}) collective-permute-start(bf16[128,3072]{1,0:T(8,128)(2,1)} %collective-permute-done.1.refs_6_), channel_id=1, source_target_pairs={{2,4},{3,5},{4,6},{5,7},{10,12},{11,13},{12,14},{13,15},{18,20},{1... | collective-permute-start | bytes 2359304 | tf_op jit(solution)/shard_map/ppermute | solution.py:66
  41.2 46.3 %collective-permute-start.4 = (bf16[128,3072]{1,0:T(8,128)(2,1)}, bf16[128,3072]{1,0:T(8,128)(2,1)}, u32[]{:S(2)}, u32[]{:S(2)}) collective-permute-start(bf16[128,3072]{1,0:T(8,128)(2,1)} %collective-permute-done.2.refs_7_), channel_id=1, source_target_pairs={{2,0},{3,1},{4,2},{5,3},{10,8},{11,9},{12,10},{13,11},{18,16},{19,... | collective-permute-start | bytes 2359304 | tf_op jit(solution)/shard_map/ppermute | solution.py:66
  64.7 2.1 collective-permute-start.18
  65.4 20.6 %collective-permute-start.19 = (bf16[128,1024]{1,0:T(8,128)(2,1)S(1)}, bf16[128,1024]{1,0:T(8,128)(2,1)S(1)}, u32[]{:S(2)}, u32[]{:S(2)}) collective-permute-start(bf16[128,1024]{1,0:T(8,128)(2,1)S(1)} %collective-permute-done.17.refs_15_.refs_9_.refs_11_), channel_id=1, source_target_pairs={{2,0},{3,1},{10,8},{11,9},{18,16},{19,17},{26,24},{27,25}} | collective-permute-start | bytes 786440 | tf_op jit(solution)/shard_map/ppermute | solution.py:66
  66.7 19.3 %collective-permute-start.23 = (bf16[128,1024]{1,0:T(8,128)(2,1)S(1)}, bf16[128,1024]{1,0:T(8,128)(2,1)}, u32[]{:S(2)}, u32[]{:S(2)}) collective-permute-start(bf16[128,1024]{1,0:T(8,128)(2,1)S(1)} %collective-permute-done.16.refs_14_.refs_8_.refs_10_), channel_id=1, source_target_pairs={{0,1},{1,0},{2,3},{3,2},{4,5},{5,4},{6,7},{7,6},{8,9},{9,8},{10,11... | collective-permute-start | bytes 786440 | tf_op jit(solution)/shard_map/ppermute | solution.py:62
  66.8 19.7 %collective-permute-start.24 = (bf16[128,1024]{1,0:T(8,128)(2,1)S(1)}, bf16[128,1024]{1,0:T(8,128)(2,1)S(1)}, u32[]{:S(2)}, u32[]{:S(2)}) collective-permute-start(bf16[128,1024]{1,0:T(8,128)(2,1)S(1)} %collective-permute-done.17.refs_15_.refs_9_.refs_11_), channel_id=1, source_target_pairs={{0,1},{1,0},{2,3},{3,2},{4,5},{5,4},{6,7},{7,6},{8,9},{9,8},{10,11... | collective-permute-start | bytes 786440 | tf_op jit(solution)/shard_map/ppermute | solution.py:62
  86.0 2.8 %collective-permute-start.5 = (bf16[128,3072]{1,0:T(8,128)(2,1)S(1)}, bf16[128,3072]{1,0:T(8,128)(2,1)S(1)}, u32[]{:S(2)}, u32[]{:S(2)}) collective-permute-start(bf16[128,3072]{1,0:T(8,128)(2,1)S(1)} %bitcast.36), channel_id=1, source_target_pairs={{0,1},{1,0},{2,3},{3,2},{4,5},{5,4},{6,7},{7,6},{8,9},{9,8},{10,11... | collective-permute-start | bytes 2359304 | tf_op jit(solution)/shard_map/ppermute | solution.py:62
  86.0 3.4 %collective-permute-start.6 = (bf16[128,3072]{1,0:T(8,128)(2,1)}, bf16[128,3072]{1,0:T(8,128)(2,1)S(1)}, u32[]{:S(2)}, u32[]{:S(2)}) collective-permute-start(bf16[128,3072]{1,0:T(8,128)(2,1)} %collective-permute-done.1.refs_6_), channel_id=1, source_target_pairs={{0,1},{1,0},{2,3},{3,2},{4,5},{5,4},{6,7},{7,6},{8,9},{9,8},{10,11... | collective-permute-start | bytes 2359304 | tf_op jit(solution)/shard_map/ppermute | solution.py:62
  86.5 4.1 %collective-permute-start.7 = (bf16[128,3072]{1,0:T(8,128)(2,1)}, bf16[128,3072]{1,0:T(8,128)(2,1)}, u32[]{:S(2)}, u32[]{:S(2)}) collective-permute-start(bf16[128,3072]{1,0:T(8,128)(2,1)} %collective-permute-done.2.refs_7_), channel_id=1, source_target_pairs={{0,1},{1,0},{2,3},{3,2},{4,5},{5,4},{6,7},{7,6},{8,9},{9,8},{10,11... | collective-permute-start | bytes 2359304 | tf_op jit(solution)/shard_map/ppermute | solution.py:62
  86.7 4.1 %collective-permute-start.10 = (bf16[128,3072]{1,0:T(8,128)(2,1)}, bf16[128,3072]{1,0:T(8,128)(2,1)S(1)}, u32[]{:S(2)}, u32[]{:S(2)}) collective-permute-start(bf16[128,3072]{1,0:T(8,128)(2,1)} %collective-permute-done.3.refs_8_), channel_id=1, source_target_pairs={{4,6},{5,7},{12,14},{13,15},{20,22},{21,23},{28,30},{29,31}} | collective-permute-start | bytes 2359304 | tf_op jit(solution)/shard_map/ppermute | solution.py:66
  87.5 21.9 %collective-permute-start.11 = (bf16[128,3072]{1,0:T(8,128)(2,1)}, bf16[128,3072]{1,0:T(8,128)(2,1)S(1)}, u32[]{:S(2)}, u32[]{:S(2)}) collective-permute-start(bf16[128,3072]{1,0:T(8,128)(2,1)} %collective-permute-done.4.refs_9_), channel_id=1, source_target_pairs={{2,0},{3,1},{10,8},{11,9},{18,16},{19,17},{26,24},{27,25}} | collective-permute-start | bytes 2359304 | tf_op jit(solution)/shard_map/ppermute | solution.py:66
  88.8 20.6 %collective-permute-start.8 = (bf16[128,3072]{1,0:T(8,128)(2,1)}, bf16[128,3072]{1,0:T(8,128)(2,1)}, u32[]{:S(2)}, u32[]{:S(2)}) collective-permute-start(bf16[128,3072]{1,0:T(8,128)(2,1)} %collective-permute-done.3.refs_8_), channel_id=1, source_target_pairs={{0,1},{1,0},{2,3},{3,2},{4,5},{5,4},{6,7},{7,6},{8,9},{9,8},{10,11... | collective-permute-start | bytes 2359304 | tf_op jit(solution)/shard_map/ppermute | solution.py:62
  89.4 20.5 %collective-permute-start.9 = (bf16[128,3072]{1,0:T(8,128)(2,1)}, bf16[128,3072]{1,0:T(8,128)(2,1)}, u32[]{:S(2)}, u32[]{:S(2)}) collective-permute-start(bf16[128,3072]{1,0:T(8,128)(2,1)} %collective-permute-done.4.refs_9_), channel_id=1, source_target_pairs={{0,1},{1,0},{2,3},{3,2},{4,5},{5,4},{6,7},{7,6},{8,9},{9,8},{10,11... | collective-permute-start | bytes 2359304 | tf_op jit(solution)/shard_map/ppermute | solution.py:62
  90.7 52.1 %collective-permute-start.28 = (bf16[4,128,1152]{2,1,0:T(8,128)(2,1)S(1)}, bf16[4,128,1152]{2,1,0:T(8,128)(2,1)}, u32[]{:S(2)}, u32[]{:S(2)}) collective-permute-start(bf16[4,128,1152]{2,1,0:T(8,128)(2,1)S(1)} %all-to-all-done.refs_2_), channel_id=1, source_target_pairs={{0,1},{1,0},{2,3},{3,2},{4,5},{5,4},{6,7},{7,6},{8,9},{9,8},{10,11... | collective-permute-start | bytes 3538952 | tf_op jit(solution)/shard_map/ppermute | solution.py:62
  90.8 28.6 %collective-permute-start.12 = (bf16[128,3072]{1,0:T(8,128)(2,1)S(1)}, bf16[128,3072]{1,0:T(8,128)(2,1)S(1)}, u32[]{:S(2)}, u32[]{:S(2)}) collective-permute-start(bf16[128,3072]{1,0:T(8,128)(2,1)S(1)} %collective-permute-done.10.refs_7_.refs_10_), channel_id=1, source_target_pairs={{0,1},{1,0},{2,3},{3,2},{4,5},{5,4},{6,7},{7,6},{8,9},{9,8},{10,11... | collective-permute-start | bytes 2359304 | tf_op jit(solution)/shard_map/ppermute | solution.py:62
  109.4 10.0 %collective-permute-start.13 = (bf16[128,3072]{1,0:T(8,128)(2,1)S(1)}, bf16[128,3072]{1,0:T(8,128)(2,1)}, u32[]{:S(2)}, u32[]{:S(2)}) collective-permute-start(bf16[128,3072]{1,0:T(8,128)(2,1)S(1)} %collective-permute-done.11.refs_8_.refs_11_), channel_id=1, source_target_pairs={{0,1},{1,0},{2,3},{3,2},{4,5},{5,4},{6,7},{7,6},{8,9},{9,8},{10,11... | collective-permute-start | bytes 2359304 | tf_op jit(solution)/shard_map/ppermute | solution.py:62
  109.4 10.0 %collective-permute-start.25 = (bf16[128,1024]{1,0:T(8,128)(2,1)}, bf16[128,1024]{1,0:T(8,128)(2,1)}, u32[]{:S(2)}, u32[]{:S(2)}) collective-permute-start(bf16[128,1024]{1,0:T(8,128)(2,1)} %copy-done.15), channel_id=1, source_target_pairs={{0,1},{1,0},{2,3},{3,2},{4,5},{5,4},{6,7},{7,6},{8,9},{9,8},{10,11... | collective-permute-start | bytes 786440 | tf_op jit(solution)/shard_map/ppermute | solution.py:62
  110.0 9.4 %collective-permute-start.26 = (bf16[128,1024]{1,0:T(8,128)(2,1)}, bf16[128,1024]{1,0:T(8,128)(2,1)}, u32[]{:S(2)}, u32[]{:S(2)}) collective-permute-start(bf16[128,1024]{1,0:T(8,128)(2,1)} %copy-done.16), channel_id=1, source_target_pairs={{0,1},{1,0},{2,3},{3,2},{4,5},{5,4},{6,7},{7,6},{8,9},{9,8},{10,11... | collective-permute-start | bytes 786440 | tf_op jit(solution)/shard_map/ppermute | solution.py:62
  129.1 13.7 %collective-permute-start.49 = (bf16[128,1024]{1,0:T(8,128)(2,1)}, bf16[128,1024]{1,0:T(8,128)(2,1)S(1)}, u32[]{:S(2)}, u32[]{:S(2)}) collective-permute-start(bf16[128,1024]{1,0:T(8,128)(2,1)} %get-tuple-element.41.refs_3_), channel_id=1, source_target_pairs={{0,2},{1,3},{2,4},{3,5},{4,6},{5,7},{8,10},{9,11},{10,12},{11,13},... | collective-permute-start | bytes 786440 | tf_op jit(solution)/shard_map/ppermute | solution.py:66
  130.4 13.1 %collective-permute-start.50 = (bf16[128,1024]{1,0:T(8,128)(2,1)}, bf16[128,1024]{1,0:T(8,128)(2,1)S(1)}, u32[]{:S(2)}, u32[]{:S(2)}) collective-permute-start(bf16[128,1024]{1,0:T(8,128)(2,1)} %get-tuple-element.41.refs_3_), channel_id=1, source_target_pairs={{2,0},{3,1},{4,2},{5,3},{6,4},{7,5},{10,8},{11,9},{12,10},{13,11},... | collective-permute-start | bytes 786440 | tf_op jit(solution)/shard_map/ppermute | solution.py:66
  136.9 10.7 %collective-permute-start.29 = (bf16[128,1024]{1,0:T(8,128)(2,1)}, bf16[128,1024]{1,0:T(8,128)(2,1)S(1)}, u32[]{:S(2)}, u32[]{:S(2)}) collective-permute-start(bf16[128,1024]{1,0:T(8,128)(2,1)} %get-tuple-element.31.refs_4_), channel_id=1, source_target_pairs={{0,2},{1,3},{2,4},{3,5},{4,6},{5,7},{8,10},{9,11},{10,12},{11,13},... | collective-permute-start | bytes 786440 | tf_op jit(solution)/shard_map/ppermute | solution.py:66
  141.5 11.3 %collective-permute-start.30 = (bf16[128,1024]{1,0:T(8,128)(2,1)}, bf16[128,1024]{1,0:T(8,128)(2,1)S(1)}, u32[]{:S(2)}, u32[]{:S(2)}) collective-permute-start(bf16[128,1024]{1,0:T(8,128)(2,1)} %get-tuple-element.31.refs_4_), channel_id=1, source_target_pairs={{2,0},{3,1},{4,2},{5,3},{6,4},{7,5},{10,8},{11,9},{12,10},{13,11},... | collective-permute-start | bytes 786440 | tf_op jit(solution)/shard_map/ppermute | solution.py:66
  142.8 11.3 %collective-permute-start.55 = (bf16[128,1024]{1,0:T(8,128)(2,1)S(1)}, bf16[128,1024]{1,0:T(8,128)(2,1)S(1)}, u32[]{:S(2)}, u32[]{:S(2)}) collective-permute-start(bf16[128,1024]{1,0:T(8,128)(2,1)S(1)} %copy-done.36), channel_id=1, source_target_pairs={{0,1},{1,0},{2,3},{3,2},{4,5},{5,4},{6,7},{7,6},{8,9},{9,8},{10,11... | collective-permute-start | bytes 786440 | tf_op jit(solution)/shard_map/ppermute | solution.py:62
  142.9 11.3 %collective-permute-start.51 = (bf16[128,1024]{1,0:T(8,128)(2,1)S(1)}, bf16[128,1024]{1,0:T(8,128)(2,1)S(1)}, u32[]{:S(2)}, u32[]{:S(2)}) collective-permute-start(bf16[128,1024]{1,0:T(8,128)(2,1)S(1)} %collective-permute-done.49.refs_4_), channel_id=1, source_target_pairs={{2,4},{3,5},{4,6},{5,7},{10,12},{11,13},{12,14},{13,15},{18,20},{1... | collective-permute-start | bytes 786440 | tf_op jit(solution)/shard_map/ppermute | solution.py:66
  143.6 14.8 %collective-permute-start.52 = (bf16[128,1024]{1,0:T(8,128)(2,1)S(1)}, bf16[128,1024]{1,0:T(8,128)(2,1)S(1)}, u32[]{:S(2)}, u32[]{:S(2)}) collective-permute-start(bf16[128,1024]{1,0:T(8,128)(2,1)S(1)} %collective-permute-done.50.refs_5_), channel_id=1, source_target_pairs={{2,0},{3,1},{4,2},{5,3},{10,8},{11,9},{12,10},{13,11},{18,16},{19,... | collective-permute-start | bytes 786440 | tf_op jit(solution)/shard_map/ppermute | solution.py:66
  147.6 12.0 %collective-permute-start.31 = (bf16[128,1024]{1,0:T(8,128)(2,1)S(1)}, bf16[128,1024]{1,0:T(8,128)(2,1)S(1)}, u32[]{:S(2)}, u32[]{:S(2)}) collective-permute-start(bf16[128,1024]{1,0:T(8,128)(2,1)S(1)} %collective-permute-done.29.refs_5_), channel_id=1, source_target_pairs={{2,4},{3,5},{4,6},{5,7},{10,12},{11,13},{12,14},{13,15},{18,20},{1... | collective-permute-start | bytes 786440 | tf_op jit(solution)/shard_map/ppermute | solution.py:66
  152.8 11.2 %collective-permute-start.32 = (bf16[128,1024]{1,0:T(8,128)(2,1)S(1)}, bf16[128,1024]{1,0:T(8,128)(2,1)S(1)}, u32[]{:S(2)}, u32[]{:S(2)}) collective-permute-start(bf16[128,1024]{1,0:T(8,128)(2,1)S(1)} %collective-permute-done.30.refs_6_), channel_id=1, source_target_pairs={{2,0},{3,1},{4,2},{5,3},{10,8},{11,9},{12,10},{13,11},{18,16},{19,... | collective-permute-start | bytes 786440 | tf_op jit(solution)/shard_map/ppermute | solution.py:66
  154.1 9.9 %collective-permute-start.56 = (bf16[128,1024]{1,0:T(8,128)(2,1)S(1)}, bf16[128,1024]{1,0:T(8,128)(2,1)S(1)}, u32[]{:S(2)}, u32[]{:S(2)}) collective-permute-start(bf16[128,1024]{1,0:T(8,128)(2,1)S(1)} %collective-permute-done.49.refs_4_), channel_id=1, source_target_pairs={{0,1},{1,0},{2,3},{3,2},{4,5},{5,4},{6,7},{7,6},{8,9},{9,8},{10,11... | collective-permute-start | bytes 786440 | tf_op jit(solution)/shard_map/ppermute | solution.py:62
  154.2 10.3 %collective-permute-start.53 = (bf16[128,1024]{1,0:T(8,128)(2,1)S(1)}, bf16[128,1024]{1,0:T(8,128)(2,1)S(1)}, u32[]{:S(2)}, u32[]{:S(2)}) collective-permute-start(bf16[128,1024]{1,0:T(8,128)(2,1)S(1)} %collective-permute-done.51.refs_6_), channel_id=1, source_target_pairs={{4,6},{5,7},{12,14},{13,15},{20,22},{21,23},{28,30},{29,31}} | collective-permute-start | bytes 786440 | tf_op jit(solution)/shard_map/ppermute | solution.py:66
  158.4 10.1 %collective-permute-start.54 = (bf16[128,1024]{1,0:T(8,128)(2,1)S(1)}, bf16[128,1024]{1,0:T(8,128)(2,1)S(1)}, u32[]{:S(2)}, u32[]{:S(2)}) collective-permute-start(bf16[128,1024]{1,0:T(8,128)(2,1)S(1)} %collective-permute-done.52.refs_7_), channel_id=1, source_target_pairs={{2,0},{3,1},{10,8},{11,9},{18,16},{19,17},{26,24},{27,25}} | collective-permute-start | bytes 786440 | tf_op jit(solution)/shard_map/ppermute | solution.py:66
  159.7 8.8 %collective-permute-start.57 = (bf16[128,1024]{1,0:T(8,128)(2,1)S(1)}, bf16[128,1024]{1,0:T(8,128)(2,1)S(1)}, u32[]{:S(2)}, u32[]{:S(2)}) collective-permute-start(bf16[128,1024]{1,0:T(8,128)(2,1)S(1)} %collective-permute-done.50.refs_5_), channel_id=1, source_target_pairs={{0,1},{1,0},{2,3},{3,2},{4,5},{5,4},{6,7},{7,6},{8,9},{9,8},{10,11... | collective-permute-start | bytes 786440 | tf_op jit(solution)/shard_map/ppermute | solution.py:62
  164.0 5.0 %collective-permute-start.58 = (bf16[128,1024]{1,0:T(8,128)(2,1)S(1)}, bf16[128,1024]{1,0:T(8,128)(2,1)S(1)}, u32[]{:S(2)}, u32[]{:S(2)}) collective-permute-start(bf16[128,1024]{1,0:T(8,128)(2,1)S(1)} %collective-permute-done.51.refs_6_), channel_id=1, source_target_pairs={{0,1},{1,0},{2,3},{3,2},{4,5},{5,4},{6,7},{7,6},{8,9},{9,8},{10,11... | collective-permute-start | bytes 786440 | tf_op jit(solution)/shard_map/ppermute | solution.py:62
  164.0 5.1 %collective-permute-start.59 = (bf16[128,1024]{1,0:T(8,128)(2,1)S(1)}, bf16[128,1024]{1,0:T(8,128)(2,1)S(1)}, u32[]{:S(2)}, u32[]{:S(2)}) collective-permute-start(bf16[128,1024]{1,0:T(8,128)(2,1)S(1)} %collective-permute-done.52.refs_7_), channel_id=1, source_target_pairs={{0,1},{1,0},{2,3},{3,2},{4,5},{5,4},{6,7},{7,6},{8,9},{9,8},{10,11... | collective-permute-start | bytes 786440 | tf_op jit(solution)/shard_map/ppermute | solution.py:62
  164.5 5.0 %collective-permute-start.60 = (bf16[128,1024]{1,0:T(8,128)(2,1)S(1)}, bf16[128,1024]{1,0:T(8,128)(2,1)S(1)}, u32[]{:S(2)}, u32[]{:S(2)}) collective-permute-start(bf16[128,1024]{1,0:T(8,128)(2,1)S(1)} %collective-permute-done.53.refs_8_), channel_id=1, source_target_pairs={{0,1},{1,0},{2,3},{3,2},{4,5},{5,4},{6,7},{7,6},{8,9},{9,8},{10,11... | collective-permute-start | bytes 786440 | tf_op jit(solution)/shard_map/ppermute | solution.py:62
  168.5 19.8 %collective-permute-start.35 = (bf16[128,1024]{1,0:T(8,128)(2,1)}, bf16[128,1024]{1,0:T(8,128)(2,1)S(1)}, u32[]{:S(2)}, u32[]{:S(2)}) collective-permute-start(bf16[128,1024]{1,0:T(8,128)(2,1)} %get-tuple-element.31.refs_4_), channel_id=1, source_target_pairs={{0,1},{1,0},{2,3},{3,2},{4,5},{5,4},{6,7},{7,6},{8,9},{9,8},{10,11... | collective-permute-start | bytes 786440 | tf_op jit(solution)/shard_map/ppermute | solution.py:62
  169.0 19.5 %collective-permute-start.36 = (bf16[128,1024]{1,0:T(8,128)(2,1)S(1)}, bf16[128,1024]{1,0:T(8,128)(2,1)S(1)}, u32[]{:S(2)}, u32[]{:S(2)}) collective-permute-start(bf16[128,1024]{1,0:T(8,128)(2,1)S(1)} %collective-permute-done.29.refs_5_), channel_id=1, source_target_pairs={{0,1},{1,0},{2,3},{3,2},{4,5},{5,4},{6,7},{7,6},{8,9},{9,8},{10,11... | collective-permute-start | bytes 786440 | tf_op jit(solution)/shard_map/ppermute | solution.py:62
  169.1 19.9 %collective-permute-start.37 = (bf16[128,1024]{1,0:T(8,128)(2,1)S(1)}, bf16[128,1024]{1,0:T(8,128)(2,1)S(1)}, u32[]{:S(2)}, u32[]{:S(2)}) collective-permute-start(bf16[128,1024]{1,0:T(8,128)(2,1)S(1)} %collective-permute-done.30.refs_6_), channel_id=1, source_target_pairs={{0,1},{1,0},{2,3},{3,2},{4,5},{5,4},{6,7},{7,6},{8,9},{9,8},{10,11... | collective-permute-start | bytes 786440 | tf_op jit(solution)/shard_map/ppermute | solution.py:62
  169.5 19.6 %collective-permute-start.33 = (bf16[128,1024]{1,0:T(8,128)(2,1)S(1)}, bf16[128,1024]{1,0:T(8,128)(2,1)S(1)}, u32[]{:S(2)}, u32[]{:S(2)}) collective-permute-start(bf16[128,1024]{1,0:T(8,128)(2,1)S(1)} %collective-permute-done.31.refs_7_), channel_id=1, source_target_pairs={{4,6},{5,7},{12,14},{13,15},{20,22},{21,23},{28,30},{29,31}} | collective-permute-start | bytes 786440 | tf_op jit(solution)/shard_map/ppermute | solution.py:66
  170.2 19.4 %collective-permute-start.34 = (bf16[128,1024]{1,0:T(8,128)(2,1)S(1)}, bf16[128,1024]{1,0:T(8,128)(2,1)S(1)}, u32[]{:S(2)}, u32[]{:S(2)}) collective-permute-start(bf16[128,1024]{1,0:T(8,128)(2,1)S(1)} %collective-permute-done.32.refs_8_), channel_id=1, source_target_pairs={{2,0},{3,1},{10,8},{11,9},{18,16},{19,17},{26,24},{27,25}} | collective-permute-start | bytes 786440 | tf_op jit(solution)/shard_map/ppermute | solution.py:66
  188.4 14.2 %collective-permute-start.62 = (bf16[4,128,1024]{2,1,0:T(8,128)(2,1)}, bf16[4,128,1024]{2,1,0:T(8,128)(2,1)S(1)}, u32[]{:S(2)}, u32[]{:S(2)}) collective-permute-start(bf16[4,128,1024]{2,1,0:T(8,128)(2,1)} %get-tuple-element.43), channel_id=1, source_target_pairs={{0,1},{1,0},{2,3},{3,2},{4,5},{5,4},{6,7},{7,6},{8,9},{9,8},{10,11... | collective-permute-start | bytes 3145736 | tf_op jit(solution)/shard_map/ppermute | solution.py:62
  188.5 3.1 %collective-permute-start.38 = (bf16[128,1024]{1,0:T(8,128)(2,1)S(1)}, bf16[128,1024]{1,0:T(8,128)(2,1)S(1)}, u32[]{:S(2)}, u32[]{:S(2)}) collective-permute-start(bf16[128,1024]{1,0:T(8,128)(2,1)S(1)} %collective-permute-done.31.refs_7_), channel_id=1, source_target_pairs={{0,1},{1,0},{2,3},{3,2},{4,5},{5,4},{6,7},{7,6},{8,9},{9,8},{10,11... | collective-permute-start | bytes 786440 | tf_op jit(solution)/shard_map/ppermute | solution.py:62
  189.0 3.0 %collective-permute-start.39 = (bf16[128,1024]{1,0:T(8,128)(2,1)S(1)}, bf16[128,1024]{1,0:T(8,128)(2,1)S(1)}, u32[]{:S(2)}, u32[]{:S(2)}) collective-permute-start(bf16[128,1024]{1,0:T(8,128)(2,1)S(1)} %collective-permute-done.32.refs_8_), channel_id=1, source_target_pairs={{0,1},{1,0},{2,3},{3,2},{4,5},{5,4},{6,7},{7,6},{8,9},{9,8},{10,11... | collective-permute-start | bytes 786440 | tf_op jit(solution)/shard_map/ppermute | solution.py:62
  189.2 3.3 %collective-permute-start.40 = (bf16[128,1024]{1,0:T(8,128)(2,1)S(1)}, bf16[128,1024]{1,0:T(8,128)(2,1)S(1)}, u32[]{:S(2)}, u32[]{:S(2)}) collective-permute-start(bf16[128,1024]{1,0:T(8,128)(2,1)S(1)} %collective-permute-done.33.refs_9_), channel_id=1, source_target_pairs={{0,1},{1,0},{2,3},{3,2},{4,5},{5,4},{6,7},{7,6},{8,9},{9,8},{10,11... | collective-permute-start | bytes 786440 | tf_op jit(solution)/shard_map/ppermute | solution.py:62
  189.6 3.2 %collective-permute-start.41 = (bf16[128,1024]{1,0:T(8,128)(2,1)S(1)}, bf16[128,1024]{1,0:T(8,128)(2,1)S(1)}, u32[]{:S(2)}, u32[]{:S(2)}) collective-permute-start(bf16[128,1024]{1,0:T(8,128)(2,1)S(1)} %collective-permute-done.34.refs_10_), channel_id=1, source_target_pairs={{0,1},{1,0},{2,3},{3,2},{4,5},{5,4},{6,7},{7,6},{8,9},{9,8},{10,11... | collective-permute-start | bytes 786440 | tf_op jit(solution)/shard_map/ppermute | solution.py:62
  202.4 5.5 %collective-permute-start.42 = (bf16[4,128,1024]{2,1,0:T(8,128)(2,1)}, bf16[4,128,1024]{2,1,0:T(8,128)(2,1)S(1)}, u32[]{:S(2)}, u32[]{:S(2)}) collective-permute-start(bf16[4,128,1024]{2,1,0:T(8,128)(2,1)} %get-tuple-element.33), channel_id=1, source_target_pairs={{0,1},{1,0},{2,3},{3,2},{4,5},{5,4},{6,7},{7,6},{8,9},{9,8},{10,11... | collective-permute-start | bytes 3145736 | tf_op jit(solution)/shard_map/ppermute | solution.py:62
  204.0 51.1 %all-to-all-start.1 = ((bf16[4,128,1024]{2,1,0:T(8,128)(2,1)}), bf16[4,128,1024]{2,1,0:T(8,128)(2,1)S(1)}, u32[]{:S(2)}, u32[]{:S(2)}) async-start(bf16[4,128,1024]{2,1,0:T(8,128)(2,1)} %add.48), calls=%async_computation.1 | async-start | bytes 2097152 | tf_op jit(solution)/shard_map/all_to_all | solution.py:101
  211.6 19.6 %collective-permute-start.43 = (bf16[128,1024]{1,0:T(8,128)(2,1)}, bf16[128,1024]{1,0:T(8,128)(2,1)S(1)}, u32[]{:S(2)}, u32[]{:S(2)}) collective-permute-start(bf16[128,1024]{1,0:T(8,128)(2,1)} %get-tuple-element.37), channel_id=1, source_target_pairs={{0,2},{1,3},{8,10},{9,11},{16,18},{17,19},{24,26},{25,27}} | collective-permute-start | bytes 786440 | tf_op jit(solution)/shard_map/ppermute | solution.py:66
  215.9 15.3 %collective-permute-start.46 = (bf16[128,1024]{1,0:T(8,128)(2,1)}, bf16[128,1024]{1,0:T(8,128)(2,1)S(1)}, u32[]{:S(2)}, u32[]{:S(2)}) collective-permute-start(bf16[128,1024]{1,0:T(8,128)(2,1)} %get-tuple-element.35), channel_id=1, source_target_pairs={{6,4},{7,5},{14,12},{15,13},{22,20},{23,21},{30,28},{31,29}} | collective-permute-start | bytes 786440 | tf_op jit(solution)/shard_map/ppermute | solution.py:66
  232.2 5.6 %collective-permute-start.47 = (bf16[128,1024]{1,0:T(8,128)(2,1)S(1)}, bf16[128,1024]{1,0:T(8,128)(2,1)S(1)}, u32[]{:S(2)}, u32[]{:S(2)}) collective-permute-start(bf16[128,1024]{1,0:T(8,128)(2,1)S(1)} %get-tuple-element.47), channel_id=1, source_target_pairs={{4,2},{5,3},{6,4},{7,5},{12,10},{13,11},{14,12},{15,13},{20,18},{2... | collective-permute-start | bytes 786440 | tf_op jit(solution)/shard_map/ppermute | solution.py:66
  232.9 10.1 %collective-permute-start.44 = (bf16[128,1024]{1,0:T(8,128)(2,1)S(1)}, bf16[128,1024]{1,0:T(8,128)(2,1)S(1)}, u32[]{:S(2)}, u32[]{:S(2)}) collective-permute-start(bf16[128,1024]{1,0:T(8,128)(2,1)S(1)} %get-tuple-element.46), channel_id=1, source_target_pairs={{0,2},{1,3},{2,4},{3,5},{8,10},{9,11},{10,12},{11,13},{16,18},{17,... | collective-permute-start | bytes 786440 | tf_op jit(solution)/shard_map/ppermute | solution.py:66
  238.9 14.1 %collective-permute-start.48 = (bf16[128,1024]{1,0:T(8,128)(2,1)S(1)}, bf16[128,1024]{1,0:T(8,128)(2,1)S(1)}, u32[]{:S(2)}, u32[]{:S(2)}) collective-permute-start(bf16[128,1024]{1,0:T(8,128)(2,1)S(1)} %add.46), channel_id=1, source_target_pairs={{2,0},{3,1},{4,2},{5,3},{6,4},{7,5},{10,8},{11,9},{12,10},{13,11},... | collective-permute-start | bytes 786440 | tf_op jit(solution)/shard_map/ppermute | solution.py:66
  243.1 11.1 %collective-permute-start.45 = (bf16[128,1024]{1,0:T(8,128)(2,1)S(1)}, bf16[128,1024]{1,0:T(8,128)(2,1)S(1)}, u32[]{:S(2)}, u32[]{:S(2)}) collective-permute-start(bf16[128,1024]{1,0:T(8,128)(2,1)S(1)} %add.43), channel_id=1, source_target_pairs={{0,2},{1,3},{2,4},{3,5},{4,6},{5,7},{8,10},{9,11},{10,12},{11,13},... | collective-permute-start | bytes 786440 | tf_op jit(solution)/shard_map/ppermute | solution.py:66
  (54 other events, 930.2 us)

commit v5 on v4

--- a/solution.py
+++ b/solution.py
@@ -39,10 +39,10 @@
     return jnp.mean(values, axis=-1, keepdims=True)
 
 
-def passed_along(value, axis, steps):
-    count = lax.axis_size(axis)
+def passed_along(value, steps):
+    count = lax.axis_size("section")
     pairs = [(source, (source + steps) % count) for source in range(count)]
-    return lax.ppermute(value, axis, pairs)
+    return lax.ppermute(value, "section", pairs)
 
 
 def line_length():
@@ -162,13 +162,6 @@
 
 def wait_copies(*args):
     each_copy(*args, lambda copy: copy.wait())
-
-
-def wait_chip(ref, target, sems, rows, chip):
-    for owner in range(CORES * chip, CORES * (chip + 1)):
-        pltpu.make_async_copy(
-            ref, target.at[owner * rows : (owner + 1) * rows, :], sems.at[owner]
-        ).wait()
 
 
 def head_parts(proj_ref, head):
@@ -433,15 +426,11 @@
     place, x_ref, mixed_ref, grad_ref, gain_a = refs[:5]
     mix_refs = refs[5 : 5 + count]
     result_ref = refs[5 + count]
-    mix_w, normed, mix_sems = refs[6 + count :]
+    mix_w, mix_sems = refs[6 + count :]
     chip, core = place[0], place[1]
     start_copies(mix_refs, mix_w, mix_sems, depth, chip, core)
-    block = CORES * depth
-    for origin in range(mix_w.shape[0] // block):
-        wait_chip(mix_refs[0], mix_w, mix_sems, depth, origin)
-        span = slice(origin * block, (origin + 1) * block)
-        normed[:, span] = dot(mixed_ref[...], mix_w[span, :], NT)
-    grad_normed = normed[...]
+    wait_copies(mix_refs, mix_w, mix_sems, depth, chip, core)
+    grad_normed = dot(mixed_ref[...], mix_w[...], NT)
     x = x_ref[...].astype(F32)
     rms_one = lax.rsqrt(mean_last(x * x) + EPS)
     normal_one = x * rms_one
@@ -520,8 +509,8 @@
 
     mixers = with_partner(relayed(w_qkv[0]))
     outers = with_partner(relayed(w_out[0]))
-    arriving = passed_along(handoff_forward, "section", 1)
-    cotangent = passed_along(relay_cotangents, "section", -1)
+    arriving = passed_along(handoff_forward, 1)
+    cotangent = passed_along(relay_cotangents, -1)
     gates = gate_columns(routes, gate_logits, expert_count)
     cot_block = jnp.concatenate([cotangent, gates], axis=1)
     cots = spread(jnp.broadcast_to(cot_block[None], (length,) + cot_block.shape))
@@ -634,7 +623,6 @@
         VMEM,
         [
             pltpu.VMEM((width, columns), BF16),
-            pltpu.VMEM((tokens, width), F32),
             dma(expert_count),
         ],
         [place, stashed_input, grad_mixed, grad_hidden, attention_gain] + mixers,

time: 274 us -> 273 us (level)
  no operation moved by 1% of the time
where the time goes in v5:
time: 273 us; the launch traced here: 272 us
  waiting for transfers between devices  114 us (42%)
  starting transfers between devices  77.8 us (28%)
  Pallas kernels  65 us (24%)
  other arithmetic  6.39 us (2%)
  local copies, waits for them, and re-layouts  5.98 us (2%)
    ppermute x30, waiting for transfers between devices, hop(): return lax.ppermute(value, 'expert', chip_pairs(sources, move))  105 us
    pallas_call x9, Pallas kernels, call(): pl.pallas_call(kernel, out_shape=outs, in_specs=specs, out_specs=out_spec...  65 us
    ppermute x30, starting transfers between devices, hop(): return lax.ppermute(value, 'expert', chip_pairs(sources, move))  57 us
    all_to_all x2, starting transfers between devices, across(): lax.all_to_all(blocks, 'expert', split_axis=0, concat_axis=0, axis_index_...  11.5 us
    ppermute x31, starting transfers between devices, swapped(): return lax.ppermute(value, 'expert', [(i, i ^ 1) for i in range(count)])  6.7 us
  transfers between devices with their start and end apart: 65, of which 21 were waited for; matrix products, arithmetic and copies ran while one was open for 3% of the time, Pallas kernels for 18%

profile of v5, /device:TPU:0, one launch (start us, length us, event | category | flops | bytes accessed | tf_op | source)
XLA Modules:
  0.0 271.7 jit_solution(2520721969789373058)
XLA Ops:
  0.6 5.9 %collective-permute-start.1 = (bf16[128,3072]{1,0:T(8,128)(2,1)}, bf16[128,3072]{1,0:T(8,128)(2,1)}, u32[]{:S(2)}, u32[]{:S(2)}) collective-permute-start(bf16[128,3072]{1,0:T(8,128)(2,1)} %bitcast.32), channel_id=1, source_target_pairs={{0,2},{1,3},{2,4},{3,5},{4,6},{5,7},{8,10},{9,11},{10,12},{11,13},... | collective-permute-start | bytes 2359304 | tf_op jit(solution)/shard_map/ppermute | solution.py:66
  6.5 1.3 collective-permute-start.2
  7.8 2.5 collective-permute-start.27
  10.3 4.6 %collective-permute-start.14 = (bf16[128,1024]{1,0:T(8,128)(2,1)}, bf16[128,1024]{1,0:T(8,128)(2,1)S(1)}, u32[]{:S(2)}, u32[]{:S(2)}) collective-permute-start(bf16[128,1024]{1,0:T(8,128)(2,1)} %bitcast.37), channel_id=1, source_target_pairs={{0,2},{1,3},{2,4},{3,5},{4,6},{5,7},{8,10},{9,11},{10,12},{11,13},... | collective-permute-start | bytes 786440 | tf_op jit(solution)/shard_map/ppermute | solution.py:66
  14.9 0.7 add_divide_fusion
  15.6 0.7 select_reduce_fusion
  16.4 0.9 collective-permute-done.27.refs_1_
  17.3 1.3 collective-permute-start.15
  18.6 3.8 %collective-permute-done.refs_1_ = bf16[128,1024]{1,0:T(8,128)(2,1)S(1)} collective-permute-done((bf16[128,1024]{1,0:T(8,128)(2,1)}, bf16[128,1024]{1,0:T(8,128)(2,1)S(1)}, u32[]{:S(2)}, u32[]{:S(2)}) %collective-permute-start) | collective-permute-done | bytes 262176 | tf_op jit(solution)/shard_map/ppermute | solution.py:45
  22.4 5.9 %collective-permute-done.14.refs_12_.refs_6_.refs_8_ = bf16[128,1024]{1,0:T(8,128)(2,1)S(1)} collective-permute-done((bf16[128,1024]{1,0:T(8,128)(2,1)}, bf16[128,1024]{1,0:T(8,128)(2,1)S(1)}, u32[]{:S(2)}, u32[]{:S(2)}) %collective-permute-start.14) | collective-permute-done | bytes 262176 | tf_op jit(solution)/shard_map/ppermute | solution.py:66
  29.0 1.1 broadcast_in_dim.16
  30.1 7.6 %all-to-all-start = ((bf16[4,128,1152]{2,1,0:T(8,128)(2,1)}), bf16[4,128,1152]{2,1,0:T(8,128)(2,1)S(1)}, u32[]{:S(2)}, u32[]{:S(2)}) async-start(bf16[4,128,1152]{2,1,0:T(8,128)(2,1)} %broadcast_in_dim.16), calls=%async_computation | async-start | bytes 2359296 | tf_op jit(solution)/shard_map/all_to_all | solution.py:101
  37.7 1.3 collective-permute-start.17
  39.7 1.5 collective-permute-start.3
  41.2 1.3 collective-permute-start.4
  42.5 22.2 %collective-permute-done.17.refs_15_.refs_9_.refs_11_ = bf16[128,1024]{1,0:T(8,128)(2,1)S(1)} collective-permute-done((bf16[128,1024]{1,0:T(8,128)(2,1)S(1)}, bf16[128,1024]{1,0:T(8,128)(2,1)S(1)}, u32[]{:S(2)}, u32[]{:S(2)}) %collective-permute-start.17) | collective-permute-done | bytes 262176 | tf_op jit(solution)/shard_map/ppermute | solution.py:66
  65.4 1.3 collective-permute-start.19
  67.5 18.5 %collective-permute-done.19.refs_17_.refs_11_.refs_13_ = bf16[128,1024]{1,0:T(8,128)(2,1)S(1)} collective-permute-done((bf16[128,1024]{1,0:T(8,128)(2,1)S(1)}, bf16[128,1024]{1,0:T(8,128)(2,1)S(1)}, u32[]{:S(2)}, u32[]{:S(2)}) %collective-permute-start.19) | collective-permute-done | bytes 262176 | tf_op jit(solution)/shard_map/ppermute | solution.py:66
  86.7 0.7 collective-permute-start.10
  87.5 1.3 collective-permute-start.11
  91.2 18.2 %collective-permute-done.11.refs_8_.refs_11_ = bf16[128,3072]{1,0:T(8,128)(2,1)S(1)} collective-permute-done((bf16[128,3072]{1,0:T(8,128)(2,1)}, bf16[128,3072]{1,0:T(8,128)(2,1)S(1)}, u32[]{:S(2)}, u32[]{:S(2)}) %collective-permute-start.11) | collective-permute-done | bytes 786464 | tf_op jit(solution)/shard_map/ppermute | solution.py:66
  110.7 1.1 fusion.refs_4_
  111.7 7.6 %shard_map.131 = (f32[128,3072]{1,0:T(8,128)}, f32[128,3072]{1,0:T(8,128)}, bf16[256,1024]{1,0:T(8,128)(2,1)}, f32[2,128,128]{2,1,0:T(8,128)}) custom-call(s32[2]{0:T(128)} %pad_add_fusion.refs_0_.place, bf16[128,1024]{1,0:T(8,128)(2,1)} %copy-done.19, bf16[128,1024]{1,0:T(8,128)(2,1)} %refs_1_.1, f32[1,1024]{1,0:T(1,128)} %refs_4_.5, ...), custom_call_target="tpu_custom_call" | custom-call | tf_op jit(solution)/shard_map/pallas_call | solution.py:451
  119.4 0.9 copy-done.4
  120.3 8.8 %shard_map.132 = (f32[128,3072]{1,0:T(8,128)}, f32[128,3072]{1,0:T(8,128)}, f32[128,1024]{1,0:T(8,128)}, bf16[128,1024]{1,0:T(8,128)(2,1)}) custom-call(s32[2]{0:T(128)} %pad_add_fusion.refs_0_.place, f32[128,3072]{1,0:T(8,128)} %get-tuple-element.24.refs_1_, f32[128,3072]{1,0:T(8,128)} %get-tuple-element.25.refs_2_, ...), custom_call_target="tpu_custom_call" | custom-call | tf_op jit(solution)/shard_map/pallas_call | solution.py:451
  129.1 1.3 collective-permute-start.49
  130.4 1.3 collective-permute-start.50
  131.8 5.1 %shard_map.133 = (f32[128,1024]{1,0:T(8,128)}, bf16[128,1024]{1,0:T(8,128)(2,1)}) custom-call(s32[2]{0:T(128)} %pad_add_fusion.refs_0_.place, bf16[128,1024]{1,0:T(8,128)(2,1)} %copy-done.19, f32[128,3072]{1,0:T(8,128)} %get-tuple-element.28.refs_2_, f32[1,1024]{1,0:T(1,128)} %refs_4_.4, f32[2,128,128]{2,1,0:T(8,128)} %get-tuple-element.27.refs_6_.refs_4_.refs_5_, ...), custom_call_target="tpu_custom_call" | custom-call | tf_op jit(solution)/shard_map/pallas_call | solution.py:451
  136.9 4.6 %collective-permute-start.29 = (bf16[128,1024]{1,0:T(8,128)(2,1)}, bf16[128,1024]{1,0:T(8,128)(2,1)S(1)}, u32[]{:S(2)}, u32[]{:S(2)}) collective-permute-start(bf16[128,1024]{1,0:T(8,128)(2,1)} %get-tuple-element.31.refs_4_), channel_id=1, source_target_pairs={{0,2},{1,3},{2,4},{3,5},{4,6},{5,7},{8,10},{9,11},{10,12},{11,13},... | collective-permute-start | bytes 786440 | tf_op jit(solution)/shard_map/ppermute | solution.py:66
  141.5 1.3 collective-permute-start.30
  142.9 0.7 collective-permute-start.51
  143.6 1.3 collective-permute-start.52
  144.9 2.7 %collective-permute-done.29.refs_5_ = bf16[128,1024]{1,0:T(8,128)(2,1)S(1)} collective-permute-done((bf16[128,1024]{1,0:T(8,128)(2,1)}, bf16[128,1024]{1,0:T(8,128)(2,1)S(1)}, u32[]{:S(2)}, u32[]{:S(2)}) %collective-permute-start.29) | collective-permute-done | bytes 262176 | tf_op jit(solution)/shard_map/ppermute | solution.py:66
  148.3 4.5 %collective-permute-done.30.refs_6_ = bf16[128,1024]{1,0:T(8,128)(2,1)S(1)} collective-permute-done((bf16[128,1024]{1,0:T(8,128)(2,1)}, bf16[128,1024]{1,0:T(8,128)(2,1)S(1)}, u32[]{:S(2)}, u32[]{:S(2)}) %collective-permute-start.30) | collective-permute-done | bytes 262176 | tf_op jit(solution)/shard_map/ppermute | solution.py:66
  152.8 1.3 collective-permute-start.32
  154.9 3.5 %collective-permute-done.52.refs_7_ = bf16[128,1024]{1,0:T(8,128)(2,1)S(1)} collective-permute-done((bf16[128,1024]{1,0:T(8,128)(2,1)S(1)}, bf16[128,1024]{1,0:T(8,128)(2,1)S(1)}, u32[]{:S(2)}, u32[]{:S(2)}) %collective-permute-start.52) | collective-permute-done | bytes 262176 | tf_op jit(solution)/shard_map/ppermute | solution.py:66
  158.4 1.3 collective-permute-start.54
  159.8 4.2 %collective-permute-done.32.refs_8_ = bf16[128,1024]{1,0:T(8,128)(2,1)S(1)} collective-permute-done((bf16[128,1024]{1,0:T(8,128)(2,1)S(1)}, bf16[128,1024]{1,0:T(8,128)(2,1)S(1)}, u32[]{:S(2)}, u32[]{:S(2)}) %collective-permute-start.32) | collective-permute-done | bytes 262176 | tf_op jit(solution)/shard_map/ppermute | solution.py:66
  164.6 3.9 %collective-permute-done.54.refs_9_ = bf16[128,1024]{1,0:T(8,128)(2,1)S(1)} collective-permute-done((bf16[128,1024]{1,0:T(8,128)(2,1)S(1)}, bf16[128,1024]{1,0:T(8,128)(2,1)S(1)}, u32[]{:S(2)}, u32[]{:S(2)}) %collective-permute-start.54) | collective-permute-done | bytes 262176 | tf_op jit(solution)/shard_map/ppermute | solution.py:66
  170.2 1.5 collective-permute-start.34
  171.7 6.6 %shard_map.134 = (f32[1024,704]{1,0:T(8,128)}, f32[1024,128]{1,0:T(8,128)}) custom-call(s32[2]{0:T(128)} %pad_add_fusion.refs_0_.place, bf16[704,1024]{1,0:T(8,128)(2,1)} %bitcast.30, bf16[4,128,1152]{2,1,0:T(8,128)(2,1)} %copy-done, bf16[4,128,1152]{2,1,0:T(8,128)(2,1)} %collective-permute-done.28.refs_3_), custom_call_target="tpu_custom_call" | custom-call | tf_op jit(solution)/shard_map/pallas_call | solution.py:451
  178.5 9.8 %shard_map.137 = (bf16[4,128,1024]{2,1,0:T(8,128)(2,1)}, bf16[4,128,1024]{2,1,0:T(8,128)(2,1)}) custom-call(s32[2]{0:T(128)} %pad_add_fusion.refs_0_.place, bf16[704,1024]{1,0:T(8,128)(2,1)} %bitcast.28, f32[1024,704]{1,0:T(8,128)} %get-tuple-element.40.refs_2_, bf16[128,1024]{1,0:T(8,128)(2,1)} %get-tuple-element.41.refs_3_, bf16[128,1024]{1,0:T(8,128)(2,1)} %copy-done.37, ...), custom_call_target="tpu_custom_call" | custom-call | tf_op jit(solution)/shard_map/pallas_call | solution.py:451
  189.7 2.0 collective-permute-done.38.refs_14_
  193.5 8.8 %shard_map.135 = (bf16[4,128,1024]{2,1,0:T(8,128)(2,1)}, bf16[4,128,1024]{2,1,0:T(8,128)(2,1)}) custom-call(s32[2]{0:T(128)} %pad_add_fusion.refs_0_.place, bf16[704,1024]{1,0:T(8,128)(2,1)} %bitcast.29, bf16[704,1024]{1,0:T(8,128)(2,1)} %bitcast.31, f32[1024,128]{1,0:T(8,128)} %get-tuple-element.30.refs_3_, bf16[128,1024]{1,0:T(8,128)(2,1)} %get-tuple-element.31.refs_4_, ...), custom_call_target="tpu_custom_call" | custom-call | tf_op jit(solution)/shard_map/pallas_call | solution.py:451
  202.6 1.4 add.48
  204.0 3.9 %all-to-all-start.1 = ((bf16[4,128,1024]{2,1,0:T(8,128)(2,1)}), bf16[4,128,1024]{2,1,0:T(8,128)(2,1)S(1)}, u32[]{:S(2)}, u32[]{:S(2)}) async-start(bf16[4,128,1024]{2,1,0:T(8,128)(2,1)} %add.48), calls=%async_computation.1 | async-start | bytes 2097152 | tf_op jit(solution)/shard_map/all_to_all | solution.py:101
  207.9 1.0 copy-done.20
  208.9 2.7 shard_map.136
  211.6 4.3 %collective-permute-start.43 = (bf16[128,1024]{1,0:T(8,128)(2,1)}, bf16[128,1024]{1,0:T(8,128)(2,1)S(1)}, u32[]{:S(2)}, u32[]{:S(2)}) collective-permute-start(bf16[128,1024]{1,0:T(8,128)(2,1)} %get-tuple-element.37), channel_id=1, source_target_pairs={{0,2},{1,3},{8,10},{9,11},{16,18},{17,19},{24,26},{25,27}} | collective-permute-start | bytes 786440 | tf_op jit(solution)/shard_map/ppermute | solution.py:66
  215.9 0.7 collective-permute-start.46
  216.6 14.6 %collective-permute-done.43 = bf16[128,1024]{1,0:T(8,128)(2,1)S(1)} collective-permute-done((bf16[128,1024]{1,0:T(8,128)(2,1)}, bf16[128,1024]{1,0:T(8,128)(2,1)S(1)}, u32[]{:S(2)}, u32[]{:S(2)}) %collective-permute-start.43) | collective-permute-done | bytes 262176 | tf_op jit(solution)/shard_map/ppermute | solution.py:66
  231.2 1.0 fusion.20
  232.2 0.7 collective-permute-start.47
  232.9 4.9 %collective-permute-start.44 = (bf16[128,1024]{1,0:T(8,128)(2,1)S(1)}, bf16[128,1024]{1,0:T(8,128)(2,1)S(1)}, u32[]{:S(2)}, u32[]{:S(2)}) collective-permute-start(bf16[128,1024]{1,0:T(8,128)(2,1)S(1)} %get-tuple-element.46), channel_id=1, source_target_pairs={{0,2},{1,3},{2,4},{3,5},{8,10},{9,11},{10,12},{11,13},{16,18},{17,... | collective-permute-start | bytes 786440 | tf_op jit(solution)/shard_map/ppermute | solution.py:66
  237.8 1.0 add.46
  238.9 1.3 collective-permute-start.48
  240.2 2.9 %collective-permute-done.44 = bf16[128,1024]{1,0:T(8,128)(2,1)S(1)} collective-permute-done((bf16[128,1024]{1,0:T(8,128)(2,1)S(1)}, bf16[128,1024]{1,0:T(8,128)(2,1)S(1)}, u32[]{:S(2)}, u32[]{:S(2)}) %collective-permute-start.44) | collective-permute-done | bytes 262176 | tf_op jit(solution)/shard_map/ppermute | solution.py:66
  243.1 7.0 %collective-permute-start.45 = (bf16[128,1024]{1,0:T(8,128)(2,1)S(1)}, bf16[128,1024]{1,0:T(8,128)(2,1)S(1)}, u32[]{:S(2)}, u32[]{:S(2)}) collective-permute-start(bf16[128,1024]{1,0:T(8,128)(2,1)S(1)} %add.43), channel_id=1, source_target_pairs={{0,2},{1,3},{2,4},{3,5},{4,6},{5,7},{8,10},{9,11},{10,12},{11,13},... | collective-permute-start | bytes 786440 | tf_op jit(solution)/shard_map/ppermute | solution.py:66
  250.1 2.9 %collective-permute-done.48 = bf16[128,1024]{1,0:T(8,128)(2,1)S(1)} collective-permute-done((bf16[128,1024]{1,0:T(8,128)(2,1)S(1)}, bf16[128,1024]{1,0:T(8,128)(2,1)S(1)}, u32[]{:S(2)}, u32[]{:S(2)}) %collective-permute-start.48) | collective-permute-done | bytes 262176 | tf_op jit(solution)/shard_map/ppermute | solution.py:66
  252.9 1.3 collective-permute-done.45
  254.2 0.8 add_convert_fusion
  255.1 1.0 copy-done.1
  256.1 8.1 %shard_map.138 = (bf16[128,3072]{1,0:T(8,128)(2,1)}, f32[128,1024]{1,0:T(8,128)}) custom-call(s32[2]{0:T(128)} %pad_add_fusion.refs_0_.place, bf16[128,1024]{1,0:T(8,128)(2,1)} %copy-done.21, f32[128,1024]{1,0:T(8,128)} %get-tuple-element.38.refs_2_, f32[128,3072]{1,0:T(8,128)} %get-tuple-element.39.refs_3_, f32[1,1024]{1,0:T(1,128)} %refs_4_.4, ...), custom_call_target="tpu_custom_call" | custom-call | tf_op jit(solution)/shard_map/pallas_call | solution.py:451
  264.2 7.3 %shard_map.139 = bf16[128,1024]{1,0:T(8,128)(2,1)} custom-call(s32[2]{0:T(128)} %pad_add_fusion.refs_0_.place, bf16[128,1024]{1,0:T(8,128)(2,1)} %refs_1_.1, bf16[128,3072]{1,0:T(8,128)(2,1)} %get-tuple-element.44.refs_2_, f32[128,1024]{1,0:T(8,128)} %get-tuple-element.45.refs_3_, f32[1,1024]{1,0:T(1,128)} %refs_4_.5, bf16[128,3072]{1,0:T(8,128)(2,1)} %bitcast.35, ...), custom_call_target="tpu_custom_call" | custom-call | tf_op jit(solution)/shard_map/pallas_call | solution.py:451
  (198 shorter events, 14.6 us)
Async XLA Ops:
  0.6 39.0 %collective-permute-start.1 = (bf16[128,3072]{1,0:T(8,128)(2,1)}, bf16[128,3072]{1,0:T(8,128)(2,1)}, u32[]{:S(2)}, u32[]{:S(2)}) collective-permute-start(bf16[128,3072]{1,0:T(8,128)(2,1)} %bitcast.32), channel_id=1, source_target_pairs={{0,2},{1,3},{2,4},{3,5},{4,6},{5,7},{8,10},{9,11},{10,12},{11,13},... | collective-permute-start | bytes 2359304 | tf_op jit(solution)/shard_map/ppermute | solution.py:66
  6.5 34.7 %collective-permute-start.2 = (bf16[128,3072]{1,0:T(8,128)(2,1)}, bf16[128,3072]{1,0:T(8,128)(2,1)}, u32[]{:S(2)}, u32[]{:S(2)}) collective-permute-start(bf16[128,3072]{1,0:T(8,128)(2,1)} %bitcast.33), channel_id=1, source_target_pairs={{2,0},{3,1},{4,2},{5,3},{6,4},{7,5},{10,8},{11,9},{12,10},{13,11},... | collective-permute-start | bytes 2359304 | tf_op jit(solution)/shard_map/ppermute | solution.py:66
  7.8 9.5 %collective-permute-start.27 = (bf16[128,1024]{1,0:T(8,128)(2,1)}, bf16[128,1024]{1,0:T(8,128)(2,1)S(1)}, u32[]{:S(2)}, u32[]{:S(2)}) collective-permute-start(bf16[128,1024]{1,0:T(8,128)(2,1)} %param.14), channel_id=1, source_target_pairs={{0,24},{8,0},{16,8},{24,16},{1,25},{9,1},{17,9},{25,17},{2,26},{10... | collective-permute-start | bytes 786440 | tf_op jit(solution)/shard_map/ppermute | solution.py:45
  10.3 12.1 %collective-permute-start = (bf16[128,1024]{1,0:T(8,128)(2,1)}, bf16[128,1024]{1,0:T(8,128)(2,1)S(1)}, u32[]{:S(2)}, u32[]{:S(2)}) collective-permute-start(bf16[128,1024]{1,0:T(8,128)(2,1)} %param.12), channel_id=1, source_target_pairs={{0,8},{8,16},{16,24},{24,0},{1,9},{9,17},{17,25},{25,1},{2,10},{10... | collective-permute-start | bytes 786440 | tf_op jit(solution)/shard_map/ppermute | solution.py:45
  10.3 18.0 %collective-permute-start.14 = (bf16[128,1024]{1,0:T(8,128)(2,1)}, bf16[128,1024]{1,0:T(8,128)(2,1)S(1)}, u32[]{:S(2)}, u32[]{:S(2)}) collective-permute-start(bf16[128,1024]{1,0:T(8,128)(2,1)} %bitcast.37), channel_id=1, source_target_pairs={{0,2},{1,3},{2,4},{3,5},{4,6},{5,7},{8,10},{9,11},{10,12},{11,13},... | collective-permute-start | bytes 786440 | tf_op jit(solution)/shard_map/ppermute | solution.py:66
  17.3 20.4 %collective-permute-start.15 = (bf16[128,1024]{1,0:T(8,128)(2,1)}, bf16[128,1024]{1,0:T(8,128)(2,1)S(1)}, u32[]{:S(2)}, u32[]{:S(2)}) collective-permute-start(bf16[128,1024]{1,0:T(8,128)(2,1)} %bitcast.38), channel_id=1, source_target_pairs={{2,0},{3,1},{4,2},{5,3},{6,4},{7,5},{10,8},{11,9},{12,10},{13,11},... | collective-permute-start | bytes 786440 | tf_op jit(solution)/shard_map/ppermute | solution.py:66
  22.4 16.6 %collective-permute-start.20 = (bf16[128,1024]{1,0:T(8,128)(2,1)}, bf16[128,1024]{1,0:T(8,128)(2,1)S(1)}, u32[]{:S(2)}, u32[]{:S(2)}) collective-permute-start(bf16[128,1024]{1,0:T(8,128)(2,1)} %bitcast.39), channel_id=1, source_target_pairs={{0,1},{1,0},{2,3},{3,2},{4,5},{5,4},{6,7},{7,6},{8,9},{9,8},{10,11... | collective-permute-start | bytes 786440 | tf_op jit(solution)/shard_map/ppermute | solution.py:62
  28.3 10.8 %collective-permute-start.16 = (bf16[128,1024]{1,0:T(8,128)(2,1)S(1)}, bf16[128,1024]{1,0:T(8,128)(2,1)S(1)}, u32[]{:S(2)}, u32[]{:S(2)}) collective-permute-start(bf16[128,1024]{1,0:T(8,128)(2,1)S(1)} %collective-permute-done.14.refs_12_.refs_6_.refs_8_), channel_id=1, source_target_pairs={{2,4},{3,5},{4,6},{5,7},{10,12},{11,13},{12,14},{13,15},{18,20},{1... | collective-permute-start | bytes 786440 | tf_op jit(solution)/shard_map/ppermute | solution.py:66
  30.1 60.5 %all-to-all-start = ((bf16[4,128,1152]{2,1,0:T(8,128)(2,1)}), bf16[4,128,1152]{2,1,0:T(8,128)(2,1)S(1)}, u32[]{:S(2)}, u32[]{:S(2)}) async-start(bf16[4,128,1152]{2,1,0:T(8,128)(2,1)} %broadcast_in_dim.16), calls=%async_computation | async-start | bytes 2359296 | tf_op jit(solution)/shard_map/all_to_all | solution.py:101
  37.7 26.9 %collective-permute-start.17 = (bf16[128,1024]{1,0:T(8,128)(2,1)S(1)}, bf16[128,1024]{1,0:T(8,128)(2,1)S(1)}, u32[]{:S(2)}, u32[]{:S(2)}) collective-permute-start(bf16[128,1024]{1,0:T(8,128)(2,1)S(1)} %collective-permute-done.15.refs_13_.refs_7_.refs_9_), channel_id=1, source_target_pairs={{2,0},{3,1},{4,2},{5,3},{10,8},{11,9},{12,10},{13,11},{18,16},{19,... | collective-permute-start | bytes 786440 | tf_op jit(solution)/shard_map/ppermute | solution.py:66
  39.1 26.3 %collective-permute-start.21 = (bf16[128,1024]{1,0:T(8,128)(2,1)S(1)}, bf16[128,1024]{1,0:T(8,128)(2,1)S(1)}, u32[]{:S(2)}, u32[]{:S(2)}) collective-permute-start(bf16[128,1024]{1,0:T(8,128)(2,1)S(1)} %collective-permute-done.14.refs_12_.refs_6_.refs_8_), channel_id=1, source_target_pairs={{0,1},{1,0},{2,3},{3,2},{4,5},{5,4},{6,7},{7,6},{8,9},{9,8},{10,11... | collective-permute-start | bytes 786440 | tf_op jit(solution)/shard_map/ppermute | solution.py:62
  39.2 27.5 %collective-permute-start.22 = (bf16[128,1024]{1,0:T(8,128)(2,1)S(1)}, bf16[128,1024]{1,0:T(8,128)(2,1)S(1)}, u32[]{:S(2)}, u32[]{:S(2)}) collective-permute-start(bf16[128,1024]{1,0:T(8,128)(2,1)S(1)} %collective-permute-done.15.refs_13_.refs_7_.refs_9_), channel_id=1, source_target_pairs={{0,1},{1,0},{2,3},{3,2},{4,5},{5,4},{6,7},{7,6},{8,9},{9,8},{10,11... | collective-permute-start | bytes 786440 | tf_op jit(solution)/shard_map/ppermute | solution.py:62
  39.7 47.1 %collective-permute-start.3 = (bf16[128,3072]{1,0:T(8,128)(2,1)}, bf16[128,3072]{1,0:T(8,128)(2,1)}, u32[]{:S(2)}, u32[]{:S(2)}) collective-permute-start(bf16[128,3072]{1,0:T(8,128)(2,1)} %collective-permute-done.1.refs_6_), channel_id=1, source_target_pairs={{2,4},{3,5},{4,6},{5,7},{10,12},{11,13},{12,14},{13,15},{18,20},{1... | collective-permute-start | bytes 2359304 | tf_op jit(solution)/shard_map/ppermute | solution.py:66
  41.2 46.3 %collective-permute-start.4 = (bf16[128,3072]{1,0:T(8,128)(2,1)}, bf16[128,3072]{1,0:T(8,128)(2,1)}, u32[]{:S(2)}, u32[]{:S(2)}) collective-permute-start(bf16[128,3072]{1,0:T(8,128)(2,1)} %collective-permute-done.2.refs_7_), channel_id=1, source_target_pairs={{2,0},{3,1},{4,2},{5,3},{10,8},{11,9},{12,10},{13,11},{18,16},{19,... | collective-permute-start | bytes 2359304 | tf_op jit(solution)/shard_map/ppermute | solution.py:66
  64.7 2.1 collective-permute-start.18
  65.4 20.6 %collective-permute-start.19 = (bf16[128,1024]{1,0:T(8,128)(2,1)S(1)}, bf16[128,1024]{1,0:T(8,128)(2,1)S(1)}, u32[]{:S(2)}, u32[]{:S(2)}) collective-permute-start(bf16[128,1024]{1,0:T(8,128)(2,1)S(1)} %collective-permute-done.17.refs_15_.refs_9_.refs_11_), channel_id=1, source_target_pairs={{2,0},{3,1},{10,8},{11,9},{18,16},{19,17},{26,24},{27,25}} | collective-permute-start | bytes 786440 | tf_op jit(solution)/shard_map/ppermute | solution.py:66
  66.7 19.3 %collective-permute-start.23 = (bf16[128,1024]{1,0:T(8,128)(2,1)S(1)}, bf16[128,1024]{1,0:T(8,128)(2,1)}, u32[]{:S(2)}, u32[]{:S(2)}) collective-permute-start(bf16[128,1024]{1,0:T(8,128)(2,1)S(1)} %collective-permute-done.16.refs_14_.refs_8_.refs_10_), channel_id=1, source_target_pairs={{0,1},{1,0},{2,3},{3,2},{4,5},{5,4},{6,7},{7,6},{8,9},{9,8},{10,11... | collective-permute-start | bytes 786440 | tf_op jit(solution)/shard_map/ppermute | solution.py:62
  66.8 19.7 %collective-permute-start.24 = (bf16[128,1024]{1,0:T(8,128)(2,1)S(1)}, bf16[128,1024]{1,0:T(8,128)(2,1)S(1)}, u32[]{:S(2)}, u32[]{:S(2)}) collective-permute-start(bf16[128,1024]{1,0:T(8,128)(2,1)S(1)} %collective-permute-done.17.refs_15_.refs_9_.refs_11_), channel_id=1, source_target_pairs={{0,1},{1,0},{2,3},{3,2},{4,5},{5,4},{6,7},{7,6},{8,9},{9,8},{10,11... | collective-permute-start | bytes 786440 | tf_op jit(solution)/shard_map/ppermute | solution.py:62
  86.0 2.8 %collective-permute-start.5 = (bf16[128,3072]{1,0:T(8,128)(2,1)S(1)}, bf16[128,3072]{1,0:T(8,128)(2,1)S(1)}, u32[]{:S(2)}, u32[]{:S(2)}) collective-permute-start(bf16[128,3072]{1,0:T(8,128)(2,1)S(1)} %bitcast.36), channel_id=1, source_target_pairs={{0,1},{1,0},{2,3},{3,2},{4,5},{5,4},{6,7},{7,6},{8,9},{9,8},{10,11... | collective-permute-start | bytes 2359304 | tf_op jit(solution)/shard_map/ppermute | solution.py:62
  86.0 3.4 %collective-permute-start.6 = (bf16[128,3072]{1,0:T(8,128)(2,1)}, bf16[128,3072]{1,0:T(8,128)(2,1)S(1)}, u32[]{:S(2)}, u32[]{:S(2)}) collective-permute-start(bf16[128,3072]{1,0:T(8,128)(2,1)} %collective-permute-done.1.refs_6_), channel_id=1, source_target_pairs={{0,1},{1,0},{2,3},{3,2},{4,5},{5,4},{6,7},{7,6},{8,9},{9,8},{10,11... | collective-permute-start | bytes 2359304 | tf_op jit(solution)/shard_map/ppermute | solution.py:62
  86.5 4.1 %collective-permute-start.7 = (bf16[128,3072]{1,0:T(8,128)(2,1)}, bf16[128,3072]{1,0:T(8,128)(2,1)}, u32[]{:S(2)}, u32[]{:S(2)}) collective-permute-start(bf16[128,3072]{1,0:T(8,128)(2,1)} %collective-permute-done.2.refs_7_), channel_id=1, source_target_pairs={{0,1},{1,0},{2,3},{3,2},{4,5},{5,4},{6,7},{7,6},{8,9},{9,8},{10,11... | collective-permute-start | bytes 2359304 | tf_op jit(solution)/shard_map/ppermute | solution.py:62
  86.7 4.1 %collective-permute-start.10 = (bf16[128,3072]{1,0:T(8,128)(2,1)}, bf16[128,3072]{1,0:T(8,128)(2,1)S(1)}, u32[]{:S(2)}, u32[]{:S(2)}) collective-permute-start(bf16[128,3072]{1,0:T(8,128)(2,1)} %collective-permute-done.3.refs_8_), channel_id=1, source_target_pairs={{4,6},{5,7},{12,14},{13,15},{20,22},{21,23},{28,30},{29,31}} | collective-permute-start | bytes 2359304 | tf_op jit(solution)/shard_map/ppermute | solution.py:66
  87.5 21.9 %collective-permute-start.11 = (bf16[128,3072]{1,0:T(8,128)(2,1)}, bf16[128,3072]{1,0:T(8,128)(2,1)S(1)}, u32[]{:S(2)}, u32[]{:S(2)}) collective-permute-start(bf16[128,3072]{1,0:T(8,128)(2,1)} %collective-permute-done.4.refs_9_), channel_id=1, source_target_pairs={{2,0},{3,1},{10,8},{11,9},{18,16},{19,17},{26,24},{27,25}} | collective-permute-start | bytes 2359304 | tf_op jit(solution)/shard_map/ppermute | solution.py:66
  88.8 20.6 %collective-permute-start.8 = (bf16[128,3072]{1,0:T(8,128)(2,1)}, bf16[128,3072]{1,0:T(8,128)(2,1)}, u32[]{:S(2)}, u32[]{:S(2)}) collective-permute-start(bf16[128,3072]{1,0:T(8,128)(2,1)} %collective-permute-done.3.refs_8_), channel_id=1, source_target_pairs={{0,1},{1,0},{2,3},{3,2},{4,5},{5,4},{6,7},{7,6},{8,9},{9,8},{10,11... | collective-permute-start | bytes 2359304 | tf_op jit(solution)/shard_map/ppermute | solution.py:62
  89.4 20.5 %collective-permute-start.9 = (bf16[128,3072]{1,0:T(8,128)(2,1)}, bf16[128,3072]{1,0:T(8,128)(2,1)}, u32[]{:S(2)}, u32[]{:S(2)}) collective-permute-start(bf16[128,3072]{1,0:T(8,128)(2,1)} %collective-permute-done.4.refs_9_), channel_id=1, source_target_pairs={{0,1},{1,0},{2,3},{3,2},{4,5},{5,4},{6,7},{7,6},{8,9},{9,8},{10,11... | collective-permute-start | bytes 2359304 | tf_op jit(solution)/shard_map/ppermute | solution.py:62
  90.7 52.1 %collective-permute-start.28 = (bf16[4,128,1152]{2,1,0:T(8,128)(2,1)S(1)}, bf16[4,128,1152]{2,1,0:T(8,128)(2,1)}, u32[]{:S(2)}, u32[]{:S(2)}) collective-permute-start(bf16[4,128,1152]{2,1,0:T(8,128)(2,1)S(1)} %all-to-all-done.refs_2_), channel_id=1, source_target_pairs={{0,1},{1,0},{2,3},{3,2},{4,5},{5,4},{6,7},{7,6},{8,9},{9,8},{10,11... | collective-permute-start | bytes 3538952 | tf_op jit(solution)/shard_map/ppermute | solution.py:62
  90.8 28.6 %collective-permute-start.12 = (bf16[128,3072]{1,0:T(8,128)(2,1)S(1)}, bf16[128,3072]{1,0:T(8,128)(2,1)S(1)}, u32[]{:S(2)}, u32[]{:S(2)}) collective-permute-start(bf16[128,3072]{1,0:T(8,128)(2,1)S(1)} %collective-permute-done.10.refs_7_.refs_10_), channel_id=1, source_target_pairs={{0,1},{1,0},{2,3},{3,2},{4,5},{5,4},{6,7},{7,6},{8,9},{9,8},{10,11... | collective-permute-start | bytes 2359304 | tf_op jit(solution)/shard_map/ppermute | solution.py:62
  109.4 10.0 %collective-permute-start.13 = (bf16[128,3072]{1,0:T(8,128)(2,1)S(1)}, bf16[128,3072]{1,0:T(8,128)(2,1)}, u32[]{:S(2)}, u32[]{:S(2)}) collective-permute-start(bf16[128,3072]{1,0:T(8,128)(2,1)S(1)} %collective-permute-done.11.refs_8_.refs_11_), channel_id=1, source_target_pairs={{0,1},{1,0},{2,3},{3,2},{4,5},{5,4},{6,7},{7,6},{8,9},{9,8},{10,11... | collective-permute-start | bytes 2359304 | tf_op jit(solution)/shard_map/ppermute | solution.py:62
  109.4 10.0 %collective-permute-start.25 = (bf16[128,1024]{1,0:T(8,128)(2,1)}, bf16[128,1024]{1,0:T(8,128)(2,1)}, u32[]{:S(2)}, u32[]{:S(2)}) collective-permute-start(bf16[128,1024]{1,0:T(8,128)(2,1)} %copy-done.15), channel_id=1, source_target_pairs={{0,1},{1,0},{2,3},{3,2},{4,5},{5,4},{6,7},{7,6},{8,9},{9,8},{10,11... | collective-permute-start | bytes 786440 | tf_op jit(solution)/shard_map/ppermute | solution.py:62
  110.0 9.4 %collective-permute-start.26 = (bf16[128,1024]{1,0:T(8,128)(2,1)}, bf16[128,1024]{1,0:T(8,128)(2,1)}, u32[]{:S(2)}, u32[]{:S(2)}) collective-permute-start(bf16[128,1024]{1,0:T(8,128)(2,1)} %copy-done.16), channel_id=1, source_target_pairs={{0,1},{1,0},{2,3},{3,2},{4,5},{5,4},{6,7},{7,6},{8,9},{9,8},{10,11... | collective-permute-start | bytes 786440 | tf_op jit(solution)/shard_map/ppermute | solution.py:62
  129.1 13.7 %collective-permute-start.49 = (bf16[128,1024]{1,0:T(8,128)(2,1)}, bf16[128,1024]{1,0:T(8,128)(2,1)S(1)}, u32[]{:S(2)}, u32[]{:S(2)}) collective-permute-start(bf16[128,1024]{1,0:T(8,128)(2,1)} %get-tuple-element.41.refs_3_), channel_id=1, source_target_pairs={{0,2},{1,3},{2,4},{3,5},{4,6},{5,7},{8,10},{9,11},{10,12},{11,13},... | collective-permute-start | bytes 786440 | tf_op jit(solution)/shard_map/ppermute | solution.py:66
  130.4 13.1 %collective-permute-start.50 = (bf16[128,1024]{1,0:T(8,128)(2,1)}, bf16[128,1024]{1,0:T(8,128)(2,1)S(1)}, u32[]{:S(2)}, u32[]{:S(2)}) collective-permute-start(bf16[128,1024]{1,0:T(8,128)(2,1)} %get-tuple-element.41.refs_3_), channel_id=1, source_target_pairs={{2,0},{3,1},{4,2},{5,3},{6,4},{7,5},{10,8},{11,9},{12,10},{13,11},... | collective-permute-start | bytes 786440 | tf_op jit(solution)/shard_map/ppermute | solution.py:66
  136.9 10.7 %collective-permute-start.29 = (bf16[128,1024]{1,0:T(8,128)(2,1)}, bf16[128,1024]{1,0:T(8,128)(2,1)S(1)}, u32[]{:S(2)}, u32[]{:S(2)}) collective-permute-start(bf16[128,1024]{1,0:T(8,128)(2,1)} %get-tuple-element.31.refs_4_), channel_id=1, source_target_pairs={{0,2},{1,3},{2,4},{3,5},{4,6},{5,7},{8,10},{9,11},{10,12},{11,13},... | collective-permute-start | bytes 786440 | tf_op jit(solution)/shard_map/ppermute | solution.py:66
  141.5 11.3 %collective-permute-start.30 = (bf16[128,1024]{1,0:T(8,128)(2,1)}, bf16[128,1024]{1,0:T(8,128)(2,1)S(1)}, u32[]{:S(2)}, u32[]{:S(2)}) collective-permute-start(bf16[128,1024]{1,0:T(8,128)(2,1)} %get-tuple-element.31.refs_4_), channel_id=1, source_target_pairs={{2,0},{3,1},{4,2},{5,3},{6,4},{7,5},{10,8},{11,9},{12,10},{13,11},... | collective-permute-start | bytes 786440 | tf_op jit(solution)/shard_map/ppermute | solution.py:66
  142.8 11.3 %collective-permute-start.55 = (bf16[128,1024]{1,0:T(8,128)(2,1)S(1)}, bf16[128,1024]{1,0:T(8,128)(2,1)S(1)}, u32[]{:S(2)}, u32[]{:S(2)}) collective-permute-start(bf16[128,1024]{1,0:T(8,128)(2,1)S(1)} %copy-done.36), channel_id=1, source_target_pairs={{0,1},{1,0},{2,3},{3,2},{4,5},{5,4},{6,7},{7,6},{8,9},{9,8},{10,11... | collective-permute-start | bytes 786440 | tf_op jit(solution)/shard_map/ppermute | solution.py:62
  142.9 11.3 %collective-permute-start.51 = (bf16[128,1024]{1,0:T(8,128)(2,1)S(1)}, bf16[128,1024]{1,0:T(8,128)(2,1)S(1)}, u32[]{:S(2)}, u32[]{:S(2)}) collective-permute-start(bf16[128,1024]{1,0:T(8,128)(2,1)S(1)} %collective-permute-done.49.refs_4_), channel_id=1, source_target_pairs={{2,4},{3,5},{4,6},{5,7},{10,12},{11,13},{12,14},{13,15},{18,20},{1... | collective-permute-start | bytes 786440 | tf_op jit(solution)/shard_map/ppermute | solution.py:66
  143.6 14.8 %collective-permute-start.52 = (bf16[128,1024]{1,0:T(8,128)(2,1)S(1)}, bf16[128,1024]{1,0:T(8,128)(2,1)S(1)}, u32[]{:S(2)}, u32[]{:S(2)}) collective-permute-start(bf16[128,1024]{1,0:T(8,128)(2,1)S(1)} %collective-permute-done.50.refs_5_), channel_id=1, source_target_pairs={{2,0},{3,1},{4,2},{5,3},{10,8},{11,9},{12,10},{13,11},{18,16},{19,... | collective-permute-start | bytes 786440 | tf_op jit(solution)/shard_map/ppermute | solution.py:66
  147.6 12.0 %collective-permute-start.31 = (bf16[128,1024]{1,0:T(8,128)(2,1)S(1)}, bf16[128,1024]{1,0:T(8,128)(2,1)S(1)}, u32[]{:S(2)}, u32[]{:S(2)}) collective-permute-start(bf16[128,1024]{1,0:T(8,128)(2,1)S(1)} %collective-permute-done.29.refs_5_), channel_id=1, source_target_pairs={{2,4},{3,5},{4,6},{5,7},{10,12},{11,13},{12,14},{13,15},{18,20},{1... | collective-permute-start | bytes 786440 | tf_op jit(solution)/shard_map/ppermute | solution.py:66
  152.8 11.2 %collective-permute-start.32 = (bf16[128,1024]{1,0:T(8,128)(2,1)S(1)}, bf16[128,1024]{1,0:T(8,128)(2,1)S(1)}, u32[]{:S(2)}, u32[]{:S(2)}) collective-permute-start(bf16[128,1024]{1,0:T(8,128)(2,1)S(1)} %collective-permute-done.30.refs_6_), channel_id=1, source_target_pairs={{2,0},{3,1},{4,2},{5,3},{10,8},{11,9},{12,10},{13,11},{18,16},{19,... | collective-permute-start | bytes 786440 | tf_op jit(solution)/shard_map/ppermute | solution.py:66
  154.1 9.9 %collective-permute-start.56 = (bf16[128,1024]{1,0:T(8,128)(2,1)S(1)}, bf16[128,1024]{1,0:T(8,128)(2,1)S(1)}, u32[]{:S(2)}, u32[]{:S(2)}) collective-permute-start(bf16[128,1024]{1,0:T(8,128)(2,1)S(1)} %collective-permute-done.49.refs_4_), channel_id=1, source_target_pairs={{0,1},{1,0},{2,3},{3,2},{4,5},{5,4},{6,7},{7,6},{8,9},{9,8},{10,11... | collective-permute-start | bytes 786440 | tf_op jit(solution)/shard_map/ppermute | solution.py:62
  154.2 10.3 %collective-permute-start.53 = (bf16[128,1024]{1,0:T(8,128)(2,1)S(1)}, bf16[128,1024]{1,0:T(8,128)(2,1)S(1)}, u32[]{:S(2)}, u32[]{:S(2)}) collective-permute-start(bf16[128,1024]{1,0:T(8,128)(2,1)S(1)} %collective-permute-done.51.refs_6_), channel_id=1, source_target_pairs={{4,6},{5,7},{12,14},{13,15},{20,22},{21,23},{28,30},{29,31}} | collective-permute-start | bytes 786440 | tf_op jit(solution)/shard_map/ppermute | solution.py:66
  158.4 10.1 %collective-permute-start.54 = (bf16[128,1024]{1,0:T(8,128)(2,1)S(1)}, bf16[128,1024]{1,0:T(8,128)(2,1)S(1)}, u32[]{:S(2)}, u32[]{:S(2)}) collective-permute-start(bf16[128,1024]{1,0:T(8,128)(2,1)S(1)} %collective-permute-done.52.refs_7_), channel_id=1, source_target_pairs={{2,0},{3,1},{10,8},{11,9},{18,16},{19,17},{26,24},{27,25}} | collective-permute-start | bytes 786440 | tf_op jit(solution)/shard_map/ppermute | solution.py:66
  159.7 8.8 %collective-permute-start.57 = (bf16[128,1024]{1,0:T(8,128)(2,1)S(1)}, bf16[128,1024]{1,0:T(8,128)(2,1)S(1)}, u32[]{:S(2)}, u32[]{:S(2)}) collective-permute-start(bf16[128,1024]{1,0:T(8,128)(2,1)S(1)} %collective-permute-done.50.refs_5_), channel_id=1, source_target_pairs={{0,1},{1,0},{2,3},{3,2},{4,5},{5,4},{6,7},{7,6},{8,9},{9,8},{10,11... | collective-permute-start | bytes 786440 | tf_op jit(solution)/shard_map/ppermute | solution.py:62
  164.0 5.0 %collective-permute-start.58 = (bf16[128,1024]{1,0:T(8,128)(2,1)S(1)}, bf16[128,1024]{1,0:T(8,128)(2,1)S(1)}, u32[]{:S(2)}, u32[]{:S(2)}) collective-permute-start(bf16[128,1024]{1,0:T(8,128)(2,1)S(1)} %collective-permute-done.51.refs_6_), channel_id=1, source_target_pairs={{0,1},{1,0},{2,3},{3,2},{4,5},{5,4},{6,7},{7,6},{8,9},{9,8},{10,11... | collective-permute-start | bytes 786440 | tf_op jit(solution)/shard_map/ppermute | solution.py:62
  164.0 5.1 %collective-permute-start.59 = (bf16[128,1024]{1,0:T(8,128)(2,1)S(1)}, bf16[128,1024]{1,0:T(8,128)(2,1)S(1)}, u32[]{:S(2)}, u32[]{:S(2)}) collective-permute-start(bf16[128,1024]{1,0:T(8,128)(2,1)S(1)} %collective-permute-done.52.refs_7_), channel_id=1, source_target_pairs={{0,1},{1,0},{2,3},{3,2},{4,5},{5,4},{6,7},{7,6},{8,9},{9,8},{10,11... | collective-permute-start | bytes 786440 | tf_op jit(solution)/shard_map/ppermute | solution.py:62
  164.5 5.0 %collective-permute-start.60 = (bf16[128,1024]{1,0:T(8,128)(2,1)S(1)}, bf16[128,1024]{1,0:T(8,128)(2,1)S(1)}, u32[]{:S(2)}, u32[]{:S(2)}) collective-permute-start(bf16[128,1024]{1,0:T(8,128)(2,1)S(1)} %collective-permute-done.53.refs_8_), channel_id=1, source_target_pairs={{0,1},{1,0},{2,3},{3,2},{4,5},{5,4},{6,7},{7,6},{8,9},{9,8},{10,11... | collective-permute-start | bytes 786440 | tf_op jit(solution)/shard_map/ppermute | solution.py:62
  168.5 19.8 %collective-permute-start.35 = (bf16[128,1024]{1,0:T(8,128)(2,1)}, bf16[128,1024]{1,0:T(8,128)(2,1)S(1)}, u32[]{:S(2)}, u32[]{:S(2)}) collective-permute-start(bf16[128,1024]{1,0:T(8,128)(2,1)} %get-tuple-element.31.refs_4_), channel_id=1, source_target_pairs={{0,1},{1,0},{2,3},{3,2},{4,5},{5,4},{6,7},{7,6},{8,9},{9,8},{10,11... | collective-permute-start | bytes 786440 | tf_op jit(solution)/shard_map/ppermute | solution.py:62
  169.0 19.5 %collective-permute-start.36 = (bf16[128,1024]{1,0:T(8,128)(2,1)S(1)}, bf16[128,1024]{1,0:T(8,128)(2,1)S(1)}, u32[]{:S(2)}, u32[]{:S(2)}) collective-permute-start(bf16[128,1024]{1,0:T(8,128)(2,1)S(1)} %collective-permute-done.29.refs_5_), channel_id=1, source_target_pairs={{0,1},{1,0},{2,3},{3,2},{4,5},{5,4},{6,7},{7,6},{8,9},{9,8},{10,11... | collective-permute-start | bytes 786440 | tf_op jit(solution)/shard_map/ppermute | solution.py:62
  169.1 19.9 %collective-permute-start.37 = (bf16[128,1024]{1,0:T(8,128)(2,1)S(1)}, bf16[128,1024]{1,0:T(8,128)(2,1)S(1)}, u32[]{:S(2)}, u32[]{:S(2)}) collective-permute-start(bf16[128,1024]{1,0:T(8,128)(2,1)S(1)} %collective-permute-done.30.refs_6_), channel_id=1, source_target_pairs={{0,1},{1,0},{2,3},{3,2},{4,5},{5,4},{6,7},{7,6},{8,9},{9,8},{10,11... | collective-permute-start | bytes 786440 | tf_op jit(solution)/shard_map/ppermute | solution.py:62
  169.5 19.6 %collective-permute-start.33 = (bf16[128,1024]{1,0:T(8,128)(2,1)S(1)}, bf16[128,1024]{1,0:T(8,128)(2,1)S(1)}, u32[]{:S(2)}, u32[]{:S(2)}) collective-permute-start(bf16[128,1024]{1,0:T(8,128)(2,1)S(1)} %collective-permute-done.31.refs_7_), channel_id=1, source_target_pairs={{4,6},{5,7},{12,14},{13,15},{20,22},{21,23},{28,30},{29,31}} | collective-permute-start | bytes 786440 | tf_op jit(solution)/shard_map/ppermute | solution.py:66
  170.2 19.4 %collective-permute-start.34 = (bf16[128,1024]{1,0:T(8,128)(2,1)S(1)}, bf16[128,1024]{1,0:T(8,128)(2,1)S(1)}, u32[]{:S(2)}, u32[]{:S(2)}) collective-permute-start(bf16[128,1024]{1,0:T(8,128)(2,1)S(1)} %collective-permute-done.32.refs_8_), channel_id=1, source_target_pairs={{2,0},{3,1},{10,8},{11,9},{18,16},{19,17},{26,24},{27,25}} | collective-permute-start | bytes 786440 | tf_op jit(solution)/shard_map/ppermute | solution.py:66
  188.4 14.2 %collective-permute-start.62 = (bf16[4,128,1024]{2,1,0:T(8,128)(2,1)}, bf16[4,128,1024]{2,1,0:T(8,128)(2,1)S(1)}, u32[]{:S(2)}, u32[]{:S(2)}) collective-permute-start(bf16[4,128,1024]{2,1,0:T(8,128)(2,1)} %get-tuple-element.43), channel_id=1, source_target_pairs={{0,1},{1,0},{2,3},{3,2},{4,5},{5,4},{6,7},{7,6},{8,9},{9,8},{10,11... | collective-permute-start | bytes 3145736 | tf_op jit(solution)/shard_map/ppermute | solution.py:62
  188.5 3.1 %collective-permute-start.38 = (bf16[128,1024]{1,0:T(8,128)(2,1)S(1)}, bf16[128,1024]{1,0:T(8,128)(2,1)S(1)}, u32[]{:S(2)}, u32[]{:S(2)}) collective-permute-start(bf16[128,1024]{1,0:T(8,128)(2,1)S(1)} %collective-permute-done.31.refs_7_), channel_id=1, source_target_pairs={{0,1},{1,0},{2,3},{3,2},{4,5},{5,4},{6,7},{7,6},{8,9},{9,8},{10,11... | collective-permute-start | bytes 786440 | tf_op jit(solution)/shard_map/ppermute | solution.py:62
  189.0 3.0 %collective-permute-start.39 = (bf16[128,1024]{1,0:T(8,128)(2,1)S(1)}, bf16[128,1024]{1,0:T(8,128)(2,1)S(1)}, u32[]{:S(2)}, u32[]{:S(2)}) collective-permute-start(bf16[128,1024]{1,0:T(8,128)(2,1)S(1)} %collective-permute-done.32.refs_8_), channel_id=1, source_target_pairs={{0,1},{1,0},{2,3},{3,2},{4,5},{5,4},{6,7},{7,6},{8,9},{9,8},{10,11... | collective-permute-start | bytes 786440 | tf_op jit(solution)/shard_map/ppermute | solution.py:62
  189.2 3.3 %collective-permute-start.40 = (bf16[128,1024]{1,0:T(8,128)(2,1)S(1)}, bf16[128,1024]{1,0:T(8,128)(2,1)S(1)}, u32[]{:S(2)}, u32[]{:S(2)}) collective-permute-start(bf16[128,1024]{1,0:T(8,128)(2,1)S(1)} %collective-permute-done.33.refs_9_), channel_id=1, source_target_pairs={{0,1},{1,0},{2,3},{3,2},{4,5},{5,4},{6,7},{7,6},{8,9},{9,8},{10,11... | collective-permute-start | bytes 786440 | tf_op jit(solution)/shard_map/ppermute | solution.py:62
  189.6 3.2 %collective-permute-start.41 = (bf16[128,1024]{1,0:T(8,128)(2,1)S(1)}, bf16[128,1024]{1,0:T(8,128)(2,1)S(1)}, u32[]{:S(2)}, u32[]{:S(2)}) collective-permute-start(bf16[128,1024]{1,0:T(8,128)(2,1)S(1)} %collective-permute-done.34.refs_10_), channel_id=1, source_target_pairs={{0,1},{1,0},{2,3},{3,2},{4,5},{5,4},{6,7},{7,6},{8,9},{9,8},{10,11... | collective-permute-start | bytes 786440 | tf_op jit(solution)/shard_map/ppermute | solution.py:62
  202.4 5.5 %collective-permute-start.42 = (bf16[4,128,1024]{2,1,0:T(8,128)(2,1)}, bf16[4,128,1024]{2,1,0:T(8,128)(2,1)S(1)}, u32[]{:S(2)}, u32[]{:S(2)}) collective-permute-start(bf16[4,128,1024]{2,1,0:T(8,128)(2,1)} %get-tuple-element.33), channel_id=1, source_target_pairs={{0,1},{1,0},{2,3},{3,2},{4,5},{5,4},{6,7},{7,6},{8,9},{9,8},{10,11... | collective-permute-start | bytes 3145736 | tf_op jit(solution)/shard_map/ppermute | solution.py:62
  204.0 51.1 %all-to-all-start.1 = ((bf16[4,128,1024]{2,1,0:T(8,128)(2,1)}), bf16[4,128,1024]{2,1,0:T(8,128)(2,1)S(1)}, u32[]{:S(2)}, u32[]{:S(2)}) async-start(bf16[4,128,1024]{2,1,0:T(8,128)(2,1)} %add.48), calls=%async_computation.1 | async-start | bytes 2097152 | tf_op jit(solution)/shard_map/all_to_all | solution.py:101
  211.6 19.6 %collective-permute-start.43 = (bf16[128,1024]{1,0:T(8,128)(2,1)}, bf16[128,1024]{1,0:T(8,128)(2,1)S(1)}, u32[]{:S(2)}, u32[]{:S(2)}) collective-permute-start(bf16[128,1024]{1,0:T(8,128)(2,1)} %get-tuple-element.37), channel_id=1, source_target_pairs={{0,2},{1,3},{8,10},{9,11},{16,18},{17,19},{24,26},{25,27}} | collective-permute-start | bytes 786440 | tf_op jit(solution)/shard_map/ppermute | solution.py:66
  215.9 15.3 %collective-permute-start.46 = (bf16[128,1024]{1,0:T(8,128)(2,1)}, bf16[128,1024]{1,0:T(8,128)(2,1)S(1)}, u32[]{:S(2)}, u32[]{:S(2)}) collective-permute-start(bf16[128,1024]{1,0:T(8,128)(2,1)} %get-tuple-element.35), channel_id=1, source_target_pairs={{6,4},{7,5},{14,12},{15,13},{22,20},{23,21},{30,28},{31,29}} | collective-permute-start | bytes 786440 | tf_op jit(solution)/shard_map/ppermute | solution.py:66
  232.2 5.6 %collective-permute-start.47 = (bf16[128,1024]{1,0:T(8,128)(2,1)S(1)}, bf16[128,1024]{1,0:T(8,128)(2,1)S(1)}, u32[]{:S(2)}, u32[]{:S(2)}) collective-permute-start(bf16[128,1024]{1,0:T(8,128)(2,1)S(1)} %get-tuple-element.47), channel_id=1, source_target_pairs={{4,2},{5,3},{6,4},{7,5},{12,10},{13,11},{14,12},{15,13},{20,18},{2... | collective-permute-start | bytes 786440 | tf_op jit(solution)/shard_map/ppermute | solution.py:66
  232.9 10.1 %collective-permute-start.44 = (bf16[128,1024]{1,0:T(8,128)(2,1)S(1)}, bf16[128,1024]{1,0:T(8,128)(2,1)S(1)}, u32[]{:S(2)}, u32[]{:S(2)}) collective-permute-start(bf16[128,1024]{1,0:T(8,128)(2,1)S(1)} %get-tuple-element.46), channel_id=1, source_target_pairs={{0,2},{1,3},{2,4},{3,5},{8,10},{9,11},{10,12},{11,13},{16,18},{17,... | collective-permute-start | bytes 786440 | tf_op jit(solution)/shard_map/ppermute | solution.py:66
  238.9 14.1 %collective-permute-start.48 = (bf16[128,1024]{1,0:T(8,128)(2,1)S(1)}, bf16[128,1024]{1,0:T(8,128)(2,1)S(1)}, u32[]{:S(2)}, u32[]{:S(2)}) collective-permute-start(bf16[128,1024]{1,0:T(8,128)(2,1)S(1)} %add.46), channel_id=1, source_target_pairs={{2,0},{3,1},{4,2},{5,3},{6,4},{7,5},{10,8},{11,9},{12,10},{13,11},... | collective-permute-start | bytes 786440 | tf_op jit(solution)/shard_map/ppermute | solution.py:66
  243.1 11.1 %collective-permute-start.45 = (bf16[128,1024]{1,0:T(8,128)(2,1)S(1)}, bf16[128,1024]{1,0:T(8,128)(2,1)S(1)}, u32[]{:S(2)}, u32[]{:S(2)}) collective-permute-start(bf16[128,1024]{1,0:T(8,128)(2,1)S(1)} %add.43), channel_id=1, source_target_pairs={{0,2},{1,3},{2,4},{3,5},{4,6},{5,7},{8,10},{9,11},{10,12},{11,13},... | collective-permute-start | bytes 786440 | tf_op jit(solution)/shard_map/ppermute | solution.py:66
  (54 other events, 930.2 us)

commit v6 on v5

--- a/solution.py
+++ b/solution.py
@@ -194,7 +194,7 @@
     hidden = x.astype(F32) + dot(heads, out_w)
     hidden_ref[...] = hidden
     rms = lax.rsqrt(mean_last(hidden * hidden) + EPS)
-    expert_ref[...] = (hidden * rms * gain_e).astype(BF16)
+    expert_ref[...] = jnp.broadcast_to((hidden * rms * gain_e).astype(BF16), expert_ref.shape)
 
 
 def early_kernel(count, depth, *refs):
@@ -330,13 +330,12 @@
             out_ref[owner] = result[pl.ds(start, rows), :]
 
 
-def expert_backward_kernel(count, rows, *refs):
+def expert_backward_kernel(rows, *refs):
     place, up_ref, act_ref = refs[:3]
-    row_refs = refs[3 : 3 + count]
-    mine_ref, other_ref, tokens, result, sems = refs[3 + count :]
-    chip, core = place[0], place[1]
-    start_copies(row_refs, tokens, sems, rows, chip, core)
-    wait_copies(row_refs, tokens, sems, rows, chip, core)
+    row_refs = refs[3:5]
+    mine_ref, other_ref, tokens, result, sems = refs[5:]
+    chip, core = place[0], place[1]
+    fetch_line(row_refs, tokens, sems, rows, chip, core)
     chunk = 2 * rows
 
     def step(index, carry):
@@ -355,13 +354,12 @@
     give_back(result, mine_ref, other_ref, rows, core)
 
 
-def expert_forward_kernel(count, rows, *refs):
+def expert_forward_kernel(rows, *refs):
     place, up_ref, down_ref, gate_ref = refs[:4]
-    row_refs = refs[4 : 4 + count]
-    mine_ref, other_ref, tokens, result, sems = refs[4 + count :]
-    chip, core = place[0], place[1]
-    start_copies(row_refs, tokens, sems, rows, chip, core)
-    wait_copies(row_refs, tokens, sems, rows, chip, core)
+    row_refs = refs[4:6]
+    mine_ref, other_ref, tokens, result, sems = refs[6:]
+    chip, core = place[0], place[1]
+    fetch_line(row_refs, tokens, sems, rows, chip, core)
     chunk = 2 * rows
 
     def step(index, carry):
@@ -539,7 +537,7 @@
             shaped((tokens, columns), F32),
             shaped((tokens, columns), F32),
             shaped((tokens, width), F32),
-            shaped((tokens, width), BF16),
+            shaped((length, tokens, width), BF16),
         ),
         [SMEM] + [VMEM] * 6 + [ANY] * (4 + count),
         (VMEM,) * 4,
@@ -552,17 +550,17 @@
         ],
         [place, sum_fwd, sum_bwd, normed, stashed_input, expert_gain, mask] + last_mix + outers,
     )
-    rows_bwd = with_partner(relayed(expert_bwd))
+    rows_bwd = spread(expert_bwd)
 
     hidden_fwd, expert_fwd = call(
         functools.partial(forward_kernel, count, depth),
-        (shaped((tokens, width), F32), shaped((tokens, width), BF16)),
+        (shaped((tokens, width), F32), shaped((length, tokens, width), BF16)),
         [SMEM] + [VMEM] * 4 + [ANY] * count,
         (VMEM,) * 2,
         [pltpu.VMEM((width, width), BF16), pltpu.VMEM((tokens, width), BF16), dma(expert_count)],
         [place, arriving, proj_fwd, expert_gain, mask] + outers,
     )
-    rows_fwd = with_partner(relayed(expert_fwd))
+    rows_fwd = spread(expert_fwd)
 
     grad_act, gate_fwd = call(
         functools.partial(cotangent_kernel, tokens, width, expert_count),
@@ -579,21 +577,21 @@
         return [pltpu.VMEM((total, width), BF16), pltpu.VMEM((total, width), BF16), dma(sems)]
 
     mine, other = call(
-        functools.partial(expert_backward_kernel, count, tokens),
+        functools.partial(expert_backward_kernel, tokens),
         pair,
-        [SMEM, VMEM, VMEM] + [ANY] * count,
+        [SMEM, VMEM, VMEM] + [ANY] * 2,
         (VMEM,) * 2,
-        expert_scratch(expert_count),
+        expert_scratch((CORES, length)),
         [place, up_weight, grad_act] + rows_bwd,
     )
     grad_parts = across(mine + swapped(other))
 
     mine, other = call(
-        functools.partial(expert_forward_kernel, count, tokens),
+        functools.partial(expert_forward_kernel, tokens),
         pair,
-        [SMEM, VMEM, VMEM, VMEM] + [ANY] * count,
+        [SMEM, VMEM, VMEM, VMEM] + [ANY] * 2,
         (VMEM,) * 2,
-        expert_scratch(expert_count),
+        expert_scratch((CORES, length)),
         [place, up_weight, down_weight, gate_fwd] + rows_fwd,
     )
     moe_parts = scattered(

time: 273 us -> 295 us (1.081)
  waiting for transfers between devices: 114 us -> 153 us
  starting transfers between devices: 77.8 us -> 60.6 us
    all_to_all x2 -> x4, waiting for transfers between devices: 0.01 us -> 45.5 us  [across(): lax.all_to_all(blocks, 'expert', split_axis=0, concat_axis=0, axis_index_...]
    ppermute x30 -> x18, starting transfers between devices: 57 us -> 37.9 us  [hop(): return lax.ppermute(value, 'expert', chip_pairs(sources, move))]
    ppermute x2, waiting for transfers between devices: 4.71 us -> 1.63 us  [passed_along(): return lax.ppermute(value, 'section', pairs)]
    all_to_all x2 -> x4, starting transfers between devices: 11.5 us -> 14.3 us  [across(): lax.all_to_all(blocks, 'expert', split_axis=0, concat_axis=0, axis_index_...]
    ppermute x31 -> x19, starting transfers between devices: 6.7 us -> 4.39 us  [swapped(): return lax.ppermute(value, 'expert', [(i, i ^ 1) for i in range(count)])]
    ppermute x30 -> x18, waiting for transfers between devices: 105 us -> 104 us  [hop(): return lax.ppermute(value, 'expert', chip_pairs(sources, move))]
  transfers between devices with their start and end apart: 65 -> 43, of which waited for: 21 -> 13; matrix products, arithmetic and copies ran while one was open for 3% -> 3% of each run, Pallas kernels for 18% -> 17%
where the time goes in v6:
time: 295 us; the launch traced here: 294 us
  waiting for transfers between devices  153 us (52%)
  Pallas kernels  65.8 us (22%)
  starting transfers between devices  60.6 us (21%)
  other arithmetic  7.31 us (2%)
  local copies, waits for them, and re-layouts  5.23 us (2%)
    ppermute x18, waiting for transfers between devices, hop(): return lax.ppermute(value, 'expert', chip_pairs(sources, move))  104 us
    pallas_call x9, Pallas kernels, call(): pl.pallas_call(kernel, out_shape=outs, in_specs=specs, out_specs=out_spec...  65.8 us
    all_to_all x4, waiting for transfers between devices, across(): lax.all_to_all(blocks, 'expert', split_axis=0, concat_axis=0, axis_index_...  45.5 us
    ppermute x18, starting transfers between devices, hop(): return lax.ppermute(value, 'expert', chip_pairs(sources, move))  37.9 us
    all_to_all x4, starting transfers between devices, across(): lax.all_to_all(blocks, 'expert', split_axis=0, concat_axis=0, axis_index_...  14.3 us
  transfers between devices with their start and end apart: 43, of which 13 were waited for; matrix products, arithmetic and copies ran while one was open for 3% of the time, Pallas kernels for 17%

profile of v6, /device:TPU:0, one launch (start us, length us, event | category | flops | bytes accessed | tf_op | source)
XLA Modules:
  0.0 294.2 jit_solution(12921755395182581814)
XLA Ops:
  0.6 5.0 %collective-permute-start.1 = (bf16[128,3072]{1,0:T(8,128)(2,1)}, bf16[128,3072]{1,0:T(8,128)(2,1)S(1)}, u32[]{:S(2)}, u32[]{:S(2)}) collective-permute-start(bf16[128,3072]{1,0:T(8,128)(2,1)} %bitcast.32), channel_id=1, source_target_pairs={{0,2},{1,3},{2,4},{3,5},{4,6},{5,7},{8,10},{9,11},{10,12},{11,13},... | collective-permute-start | bytes 2359304 | tf_op jit(solution)/shard_map/ppermute | solution.py:66
  5.6 1.3 collective-permute-start.2
  6.9 1.5 collective-permute-start
  8.5 4.6 %collective-permute-start.14 = (bf16[128,1024]{1,0:T(8,128)(2,1)}, bf16[128,1024]{1,0:T(8,128)(2,1)S(1)}, u32[]{:S(2)}, u32[]{:S(2)}) collective-permute-start(bf16[128,1024]{1,0:T(8,128)(2,1)} %bitcast.37), channel_id=1, source_target_pairs={{0,2},{1,3},{2,4},{3,5},{4,6},{5,7},{8,10},{9,11},{10,12},{11,13},... | collective-permute-start | bytes 786440 | tf_op jit(solution)/shard_map/ppermute | solution.py:66
  13.1 1.3 collective-permute-start.15
  14.4 1.6 collective-permute-done.refs_1_
  16.0 12.3 %collective-permute-done.14.refs_12_.refs_6_.refs_8_ = bf16[128,1024]{1,0:T(8,128)(2,1)S(1)} collective-permute-done((bf16[128,1024]{1,0:T(8,128)(2,1)}, bf16[128,1024]{1,0:T(8,128)(2,1)S(1)}, u32[]{:S(2)}, u32[]{:S(2)}) %collective-permute-start.14) | collective-permute-done | bytes 262176 | tf_op jit(solution)/shard_map/ppermute | solution.py:66
  28.3 2.4 collective-permute-start.27
  30.8 1.6 collective-permute-done.15.refs_13_.refs_7_.refs_9_
  32.4 1.4 collective-permute-start.16
  33.8 0.7 add_divide_fusion
  34.5 1.5 collective-permute-start.3
  36.0 1.3 collective-permute-start.4
  37.3 0.7 select_reduce_fusion
  38.1 1.3 collective-permute-start.17
  39.4 0.5 collective-permute-start.22
  40.1 25.0 %collective-permute-done.17.refs_15_.refs_9_.refs_11_ = bf16[128,1024]{1,0:T(8,128)(2,1)S(1)} collective-permute-done((bf16[128,1024]{1,0:T(8,128)(2,1)S(1)}, bf16[128,1024]{1,0:T(8,128)(2,1)S(1)}, u32[]{:S(2)}, u32[]{:S(2)}) %collective-permute-start.17) | collective-permute-done | bytes 262176 | tf_op jit(solution)/shard_map/ppermute | solution.py:66
  65.1 1.4 collective-permute-start.18
  66.5 0.5 collective-permute-start.6
  67.0 1.0 fusion.4
  67.9 1.2 broadcast_in_dim.16
  69.2 3.5 %all-to-all-start = ((bf16[4,128,1152]{2,1,0:T(8,128)(2,1)}), bf16[4,128,1152]{2,1,0:T(8,128)(2,1)S(1)}, u32[]{:S(2)}, u32[]{:S(2)}) async-start(bf16[4,128,1152]{2,1,0:T(8,128)(2,1)} %broadcast_in_dim.16), calls=%async_computation | async-start | bytes 2359296 | tf_op jit(solution)/shard_map/all_to_all | solution.py:101
  72.7 1.3 collective-permute-start.19
  74.0 0.7 collective-permute-start.10
  74.8 1.3 collective-permute-start.11
  76.1 19.7 %collective-permute-done.19.refs_17_.refs_11_.refs_13_ = bf16[128,1024]{1,0:T(8,128)(2,1)S(1)} collective-permute-done((bf16[128,1024]{1,0:T(8,128)(2,1)}, bf16[128,1024]{1,0:T(8,128)(2,1)S(1)}, u32[]{:S(2)}, u32[]{:S(2)}) %collective-permute-start.19) | collective-permute-done | bytes 262176 | tf_op jit(solution)/shard_map/ppermute | solution.py:66
  95.8 1.7 collective-permute-done.23.refs_21_.refs_15_.refs_17_
  98.5 18.5 %collective-permute-done.11.refs_8_.refs_11_ = bf16[128,3072]{1,0:T(8,128)(2,1)S(1)} collective-permute-done((bf16[128,3072]{1,0:T(8,128)(2,1)}, bf16[128,3072]{1,0:T(8,128)(2,1)S(1)}, u32[]{:S(2)}, u32[]{:S(2)}) %collective-permute-start.11) | collective-permute-done | bytes 786464 | tf_op jit(solution)/shard_map/ppermute | solution.py:66
  117.1 0.5 collective-permute-start.24
  118.2 0.6 pad_add_fusion.refs_0_.place
  118.7 1.1 fusion.refs_4_
  119.8 7.6 %shard_map.131 = (f32[128,3072]{1,0:T(8,128)}, f32[128,3072]{1,0:T(8,128)}, bf16[256,1024]{1,0:T(8,128)(2,1)}, f32[2,128,128]{2,1,0:T(8,128)}) custom-call(s32[2]{0:T(128)} %pad_add_fusion.refs_0_.place, bf16[128,1024]{1,0:T(8,128)(2,1)} %collective-permute-done.refs_1_, bf16[128,1024]{1,0:T(8,128)(2,1)} %refs_1_.1, f32[1,1024]{1,0:T(1,128)} %refs_4_.5, ...), custom_call_target="tpu_custom_call" | custom-call | tf_op jit(solution)/shard_map/pallas_call | solution.py:449
  127.5 0.9 copy-done.6
  128.4 9.1 %shard_map.132 = (f32[128,3072]{1,0:T(8,128)}, f32[128,3072]{1,0:T(8,128)}, f32[128,1024]{1,0:T(8,128)}, bf16[4,128,1024]{2,1,0:T(8,128)(2,1)}) custom-call(s32[2]{0:T(128)} %pad_add_fusion.refs_0_.place, f32[128,3072]{1,0:T(8,128)} %get-tuple-element.24.refs_1_, f32[128,3072]{1,0:T(8,128)} %get-tuple-element.25.refs_2_, ...), custom_call_target="tpu_custom_call" | custom-call | tf_op jit(solution)/shard_map/pallas_call | solution.py:449
  137.6 3.5 %all-to-all-start.2 = ((bf16[4,128,1024]{2,1,0:T(8,128)(2,1)}), bf16[4,128,1024]{2,1,0:T(8,128)(2,1)S(1)}, u32[]{:S(2)}, u32[]{:S(2)}) async-start(bf16[4,128,1024]{2,1,0:T(8,128)(2,1)} %get-tuple-element.41), calls=%async_computation.2 | async-start | bytes 2097152 | tf_op jit(solution)/shard_map/all_to_all | solution.py:101
  141.1 5.3 %shard_map.133 = (f32[128,1024]{1,0:T(8,128)}, bf16[4,128,1024]{2,1,0:T(8,128)(2,1)}) custom-call(s32[2]{0:T(128)} %pad_add_fusion.refs_0_.place, bf16[128,1024]{1,0:T(8,128)(2,1)} %collective-permute-done.refs_1_, f32[128,3072]{1,0:T(8,128)} %get-tuple-element.28.refs_2_, f32[1,1024]{1,0:T(1,128)} %refs_4_.4, ...), custom_call_target="tpu_custom_call" | custom-call | tf_op jit(solution)/shard_map/pallas_call | solution.py:449
  146.5 20.9 %all-to-all-done.2.refs_3_ = bf16[4,128,1024]{2,1,0:T(8,128)(2,1)S(1)} async-done(((bf16[4,128,1024]{2,1,0:T(8,128)(2,1)}), bf16[4,128,1024]{2,1,0:T(8,128)(2,1)S(1)}, u32[]{:S(2)}, u32[]{:S(2)}) %all-to-all-start.2) | async-done | bytes 1048608 | tf_op jit(solution)/shard_map/all_to_all | solution.py:101
  167.3 3.7 %all-to-all-start.1 = ((bf16[4,128,1024]{2,1,0:T(8,128)(2,1)}), bf16[4,128,1024]{2,1,0:T(8,128)(2,1)S(1)}, u32[]{:S(2)}, u32[]{:S(2)}) async-start(bf16[4,128,1024]{2,1,0:T(8,128)(2,1)} %get-tuple-element.31), calls=%async_computation.1 | async-start | bytes 2097152 | tf_op jit(solution)/shard_map/all_to_all | solution.py:101
  171.1 0.5 collective-permute-start.37
  171.6 24.6 %all-to-all-done.1.refs_4_ = bf16[4,128,1024]{2,1,0:T(8,128)(2,1)S(1)} async-done(((bf16[4,128,1024]{2,1,0:T(8,128)(2,1)}), bf16[4,128,1024]{2,1,0:T(8,128)(2,1)S(1)}, u32[]{:S(2)}, u32[]{:S(2)}) %all-to-all-start.1) | async-done | bytes 1048608 | tf_op jit(solution)/shard_map/all_to_all | solution.py:101
  196.2 6.9 %shard_map.134 = (f32[1024,704]{1,0:T(8,128)}, f32[1024,128]{1,0:T(8,128)}) custom-call(s32[2]{0:T(128)} %pad_add_fusion.refs_0_.place, bf16[704,1024]{1,0:T(8,128)(2,1)} %bitcast.30, bf16[4,128,1152]{2,1,0:T(8,128)(2,1)} %copy-done, bf16[4,128,1152]{2,1,0:T(8,128)(2,1)} %collective-permute-done.28.refs_3_), custom_call_target="tpu_custom_call" | custom-call | tf_op jit(solution)/shard_map/pallas_call | solution.py:449
  203.2 9.8 %shard_map.137 = (bf16[4,128,1024]{2,1,0:T(8,128)(2,1)}, bf16[4,128,1024]{2,1,0:T(8,128)(2,1)}) custom-call(s32[2]{0:T(128)} %pad_add_fusion.refs_0_.place, bf16[704,1024]{1,0:T(8,128)(2,1)} %bitcast.28, f32[1024,704]{1,0:T(8,128)} %get-tuple-element.40.refs_2_, bf16[4,128,1024]{2,1,0:T(8,128)(2,1)} %copy-done.2, ...), custom_call_target="tpu_custom_call" | custom-call | tf_op jit(solution)/shard_map/pallas_call | solution.py:449
  213.2 1.0 copy-done.19
  214.2 8.8 %shard_map.135 = (bf16[4,128,1024]{2,1,0:T(8,128)(2,1)}, bf16[4,128,1024]{2,1,0:T(8,128)(2,1)}) custom-call(s32[2]{0:T(128)} %pad_add_fusion.refs_0_.place, bf16[704,1024]{1,0:T(8,128)(2,1)} %bitcast.29, bf16[704,1024]{1,0:T(8,128)(2,1)} %bitcast.31, f32[1024,128]{1,0:T(8,128)} %get-tuple-element.30.refs_3_, bf16[4,128,1024]{2,1,0:T(8,128)(2,1)} %copy-done.3, ...), custom_call_target="tpu_custom_call" | custom-call | tf_op jit(solution)/shard_map/pallas_call | solution.py:449
  223.5 1.4 add.48
  224.9 3.5 %all-to-all-start.3 = ((bf16[4,128,1024]{2,1,0:T(8,128)(2,1)}), bf16[4,128,1024]{2,1,0:T(8,128)(2,1)S(1)}, u32[]{:S(2)}, u32[]{:S(2)}) async-start(bf16[4,128,1024]{2,1,0:T(8,128)(2,1)} %add.48), calls=%async_computation.3 | async-start | bytes 2097152 | tf_op jit(solution)/shard_map/all_to_all | solution.py:101
  228.5 1.0 copy-done.18
  229.4 2.7 shard_map.136
  232.1 4.0 %collective-permute-start.31 = (bf16[128,1024]{1,0:T(8,128)(2,1)}, bf16[128,1024]{1,0:T(8,128)(2,1)S(1)}, u32[]{:S(2)}, u32[]{:S(2)}) collective-permute-start(bf16[128,1024]{1,0:T(8,128)(2,1)} %get-tuple-element.37), channel_id=1, source_target_pairs={{0,2},{1,3},{8,10},{9,11},{16,18},{17,19},{24,26},{25,27}} | collective-permute-start | bytes 786440 | tf_op jit(solution)/shard_map/ppermute | solution.py:66
  236.2 0.7 collective-permute-start.34
  236.8 14.9 %collective-permute-done.31 = bf16[128,1024]{1,0:T(8,128)(2,1)S(1)} collective-permute-done((bf16[128,1024]{1,0:T(8,128)(2,1)}, bf16[128,1024]{1,0:T(8,128)(2,1)S(1)}, u32[]{:S(2)}, u32[]{:S(2)}) %collective-permute-start.31) | collective-permute-done | bytes 262176 | tf_op jit(solution)/shard_map/ppermute | solution.py:66
  251.8 1.0 fusion.20
  252.8 4.3 %collective-permute-start.32 = (bf16[128,1024]{1,0:T(8,128)(2,1)S(1)}, bf16[128,1024]{1,0:T(8,128)(2,1)S(1)}, u32[]{:S(2)}, u32[]{:S(2)}) collective-permute-start(bf16[128,1024]{1,0:T(8,128)(2,1)S(1)} %get-tuple-element.46), channel_id=1, source_target_pairs={{0,2},{1,3},{2,4},{3,5},{8,10},{9,11},{10,12},{11,13},{16,18},{17,... | collective-permute-start | bytes 786440 | tf_op jit(solution)/shard_map/ppermute | solution.py:66
  257.1 0.7 collective-permute-start.35
  257.8 4.6 %collective-permute-done.32 = bf16[128,1024]{1,0:T(8,128)(2,1)S(1)} collective-permute-done((bf16[128,1024]{1,0:T(8,128)(2,1)S(1)}, bf16[128,1024]{1,0:T(8,128)(2,1)S(1)}, u32[]{:S(2)}, u32[]{:S(2)}) %collective-permute-start.32) | collective-permute-done | bytes 262176 | tf_op jit(solution)/shard_map/ppermute | solution.py:66
  262.3 1.0 add.43
  263.4 4.4 %collective-permute-start.33 = (bf16[128,1024]{1,0:T(8,128)(2,1)S(1)}, bf16[128,1024]{1,0:T(8,128)(2,1)S(1)}, u32[]{:S(2)}, u32[]{:S(2)}) collective-permute-start(bf16[128,1024]{1,0:T(8,128)(2,1)S(1)} %add.43), channel_id=1, source_target_pairs={{0,2},{1,3},{2,4},{3,5},{4,6},{5,7},{8,10},{9,11},{10,12},{11,13},... | collective-permute-start | bytes 786440 | tf_op jit(solution)/shard_map/ppermute | solution.py:66
  267.9 1.5 collective-permute-start.36
  269.4 2.8 collective-permute-done.33
  272.1 4.6 %collective-permute-done.36 = bf16[128,1024]{1,0:T(8,128)(2,1)S(1)} collective-permute-done((bf16[128,1024]{1,0:T(8,128)(2,1)S(1)}, bf16[128,1024]{1,0:T(8,128)(2,1)S(1)}, u32[]{:S(2)}, u32[]{:S(2)}) %collective-permute-start.36) | collective-permute-done | bytes 262176 | tf_op jit(solution)/shard_map/ppermute | solution.py:66
  276.7 0.8 add_convert_fusion
  277.6 1.0 copy-done.1
  278.6 8.1 %shard_map.138 = (bf16[128,3072]{1,0:T(8,128)(2,1)}, f32[128,1024]{1,0:T(8,128)}) custom-call(s32[2]{0:T(128)} %pad_add_fusion.refs_0_.place, bf16[128,1024]{1,0:T(8,128)(2,1)} %collective-permute-done.27.refs_1_, f32[128,1024]{1,0:T(8,128)} %get-tuple-element.38.refs_2_, f32[128,3072]{1,0:T(8,128)} %get-tuple-element.39.refs_3_, f32[1,1024]{1,0:T(1,128)} %refs_4_.4, ...), custom_call_target="tpu_custom_call" | custom-call | tf_op jit(solution)/shard_map/pallas_call | solution.py:449
  286.7 7.3 %shard_map.139 = bf16[128,1024]{1,0:T(8,128)(2,1)} custom-call(s32[2]{0:T(128)} %pad_add_fusion.refs_0_.place, bf16[128,1024]{1,0:T(8,128)(2,1)} %refs_1_.1, bf16[128,3072]{1,0:T(8,128)(2,1)} %get-tuple-element.44.refs_2_, f32[128,1024]{1,0:T(8,128)} %get-tuple-element.45.refs_3_, f32[1,1024]{1,0:T(1,128)} %refs_4_.5, bf16[128,3072]{1,0:T(8,128)(2,1)} %bitcast.36, ...), custom_call_target="tpu_custom_call" | custom-call | tf_op jit(solution)/shard_map/pallas_call | solution.py:449
  (96 shorter events, 2.7 us)
Async XLA Ops:
  0.6 33.8 %collective-permute-start.1 = (bf16[128,3072]{1,0:T(8,128)(2,1)}, bf16[128,3072]{1,0:T(8,128)(2,1)S(1)}, u32[]{:S(2)}, u32[]{:S(2)}) collective-permute-start(bf16[128,3072]{1,0:T(8,128)(2,1)} %bitcast.32), channel_id=1, source_target_pairs={{0,2},{1,3},{2,4},{3,5},{4,6},{5,7},{8,10},{9,11},{10,12},{11,13},... | collective-permute-start | bytes 2359304 | tf_op jit(solution)/shard_map/ppermute | solution.py:66
  5.6 30.4 %collective-permute-start.2 = (bf16[128,3072]{1,0:T(8,128)(2,1)}, bf16[128,3072]{1,0:T(8,128)(2,1)S(1)}, u32[]{:S(2)}, u32[]{:S(2)}) collective-permute-start(bf16[128,3072]{1,0:T(8,128)(2,1)} %bitcast.33), channel_id=1, source_target_pairs={{2,0},{3,1},{4,2},{5,3},{6,4},{7,5},{10,8},{11,9},{12,10},{13,11},... | collective-permute-start | bytes 2359304 | tf_op jit(solution)/shard_map/ppermute | solution.py:66
  6.9 9.0 %collective-permute-start = (bf16[128,1024]{1,0:T(8,128)(2,1)}, bf16[128,1024]{1,0:T(8,128)(2,1)}, u32[]{:S(2)}, u32[]{:S(2)}) collective-permute-start(bf16[128,1024]{1,0:T(8,128)(2,1)} %param.12), channel_id=1, source_target_pairs={{0,8},{8,16},{16,24},{24,0},{1,9},{9,17},{17,25},{25,1},{2,10},{10... | collective-permute-start | bytes 786440 | tf_op jit(solution)/shard_map/ppermute | solution.py:45
  8.5 19.8 %collective-permute-start.14 = (bf16[128,1024]{1,0:T(8,128)(2,1)}, bf16[128,1024]{1,0:T(8,128)(2,1)S(1)}, u32[]{:S(2)}, u32[]{:S(2)}) collective-permute-start(bf16[128,1024]{1,0:T(8,128)(2,1)} %bitcast.37), channel_id=1, source_target_pairs={{0,2},{1,3},{2,4},{3,5},{4,6},{5,7},{8,10},{9,11},{10,12},{11,13},... | collective-permute-start | bytes 786440 | tf_op jit(solution)/shard_map/ppermute | solution.py:66
  13.1 19.3 %collective-permute-start.15 = (bf16[128,1024]{1,0:T(8,128)(2,1)}, bf16[128,1024]{1,0:T(8,128)(2,1)S(1)}, u32[]{:S(2)}, u32[]{:S(2)}) collective-permute-start(bf16[128,1024]{1,0:T(8,128)(2,1)} %bitcast.38), channel_id=1, source_target_pairs={{2,0},{3,1},{4,2},{5,3},{6,4},{7,5},{10,8},{11,9},{12,10},{13,11},... | collective-permute-start | bytes 786440 | tf_op jit(solution)/shard_map/ppermute | solution.py:66
  16.0 22.0 %collective-permute-start.20 = (bf16[128,1024]{1,0:T(8,128)(2,1)}, bf16[128,1024]{1,0:T(8,128)(2,1)S(1)}, u32[]{:S(2)}, u32[]{:S(2)}) collective-permute-start(bf16[128,1024]{1,0:T(8,128)(2,1)} %bitcast.39), channel_id=1, source_target_pairs={{0,1},{1,0},{2,3},{3,2},{4,5},{5,4},{6,7},{7,6},{8,9},{9,8},{10,11... | collective-permute-start | bytes 786440 | tf_op jit(solution)/shard_map/ppermute | solution.py:62
  28.3 40.8 %copy-start.9 = (bf16[128,1024]{1,0:T(8,128)(2,1)}, bf16[128,1024]{1,0:T(8,128)(2,1)S(1)}, u32[]{:S(2)}) copy-start(bf16[128,1024]{1,0:T(8,128)(2,1)S(1)} %collective-permute-done.14.refs_12_.refs_6_.refs_8_) | copy-start | bytes 786436
  28.3 9.8 %collective-permute-start.27 = (bf16[128,1024]{1,0:T(8,128)(2,1)}, bf16[128,1024]{1,0:T(8,128)(2,1)}, u32[]{:S(2)}, u32[]{:S(2)}) collective-permute-start(bf16[128,1024]{1,0:T(8,128)(2,1)} %param.14), channel_id=1, source_target_pairs={{0,24},{8,0},{16,8},{24,16},{1,25},{9,1},{17,9},{25,17},{2,26},{10... | collective-permute-start | bytes 786440 | tf_op jit(solution)/shard_map/ppermute | solution.py:45
  32.4 36.8 %copy-start.10 = (bf16[128,1024]{1,0:T(8,128)(2,1)}, bf16[128,1024]{1,0:T(8,128)(2,1)S(1)}, u32[]{:S(2)}) copy-start(bf16[128,1024]{1,0:T(8,128)(2,1)S(1)} %collective-permute-done.15.refs_13_.refs_7_.refs_9_) | copy-start | bytes 786436
  32.4 7.0 %collective-permute-start.16 = (bf16[128,1024]{1,0:T(8,128)(2,1)S(1)}, bf16[128,1024]{1,0:T(8,128)(2,1)}, u32[]{:S(2)}, u32[]{:S(2)}) collective-permute-start(bf16[128,1024]{1,0:T(8,128)(2,1)S(1)} %collective-permute-done.14.refs_12_.refs_6_.refs_8_), channel_id=1, source_target_pairs={{2,4},{3,5},{4,6},{5,7},{10,12},{11,13},{12,14},{13,15},{18,20},{1... | collective-permute-start | bytes 786440 | tf_op jit(solution)/shard_map/ppermute | solution.py:66
  34.4 34.7 %copy-start.7 = (bf16[128,3072]{1,0:T(8,128)(2,1)}, bf16[128,3072]{1,0:T(8,128)(2,1)S(1)}, u32[]{:S(2)}) copy-start(bf16[128,3072]{1,0:T(8,128)(2,1)S(1)} %collective-permute-done.1.refs_6_) | copy-start | bytes 2359300
  34.5 39.6 %collective-permute-start.3 = (bf16[128,3072]{1,0:T(8,128)(2,1)S(1)}, bf16[128,3072]{1,0:T(8,128)(2,1)}, u32[]{:S(2)}, u32[]{:S(2)}) collective-permute-start(bf16[128,3072]{1,0:T(8,128)(2,1)S(1)} %collective-permute-done.1.refs_6_), channel_id=1, source_target_pairs={{2,4},{3,5},{4,6},{5,7},{10,12},{11,13},{12,14},{13,15},{18,20},{1... | collective-permute-start | bytes 2359304 | tf_op jit(solution)/shard_map/ppermute | solution.py:66
  36.0 33.2 %copy-start.8 = (bf16[128,3072]{1,0:T(8,128)(2,1)}, bf16[128,3072]{1,0:T(8,128)(2,1)S(1)}, u32[]{:S(2)}) copy-start(bf16[128,3072]{1,0:T(8,128)(2,1)S(1)} %collective-permute-done.2.refs_7_) | copy-start | bytes 2359300
  36.0 38.8 %collective-permute-start.4 = (bf16[128,3072]{1,0:T(8,128)(2,1)S(1)}, bf16[128,3072]{1,0:T(8,128)(2,1)}, u32[]{:S(2)}, u32[]{:S(2)}) collective-permute-start(bf16[128,3072]{1,0:T(8,128)(2,1)S(1)} %collective-permute-done.2.refs_7_), channel_id=1, source_target_pairs={{2,0},{3,1},{4,2},{5,3},{10,8},{11,9},{12,10},{13,11},{18,16},{19,... | collective-permute-start | bytes 2359304 | tf_op jit(solution)/shard_map/ppermute | solution.py:66
  38.0 31.2 %copy-start.11 = (bf16[128,1024]{1,0:T(8,128)(2,1)}, bf16[128,1024]{1,0:T(8,128)(2,1)S(1)}, u32[]{:S(2)}) copy-start(bf16[128,1024]{1,0:T(8,128)(2,1)S(1)} %collective-permute-done.20.refs_18_.refs_12_.refs_14_) | copy-start | bytes 786436
  38.0 27.1 %collective-permute-start.21 = (bf16[128,1024]{1,0:T(8,128)(2,1)S(1)}, bf16[128,1024]{1,0:T(8,128)(2,1)S(1)}, u32[]{:S(2)}, u32[]{:S(2)}) collective-permute-start(bf16[128,1024]{1,0:T(8,128)(2,1)S(1)} %collective-permute-done.14.refs_12_.refs_6_.refs_8_), channel_id=1, source_target_pairs={{0,1},{1,0},{2,3},{3,2},{4,5},{5,4},{6,7},{7,6},{8,9},{9,8},{10,11... | collective-permute-start | bytes 786440 | tf_op jit(solution)/shard_map/ppermute | solution.py:62
  38.1 27.0 %collective-permute-start.17 = (bf16[128,1024]{1,0:T(8,128)(2,1)S(1)}, bf16[128,1024]{1,0:T(8,128)(2,1)S(1)}, u32[]{:S(2)}, u32[]{:S(2)}) collective-permute-start(bf16[128,1024]{1,0:T(8,128)(2,1)S(1)} %collective-permute-done.15.refs_13_.refs_7_.refs_9_), channel_id=1, source_target_pairs={{2,0},{3,1},{4,2},{5,3},{10,8},{11,9},{12,10},{13,11},{18,16},{19,... | collective-permute-start | bytes 786440 | tf_op jit(solution)/shard_map/ppermute | solution.py:66
  39.4 27.1 %collective-permute-start.22 = (bf16[128,1024]{1,0:T(8,128)(2,1)S(1)}, bf16[128,1024]{1,0:T(8,128)(2,1)S(1)}, u32[]{:S(2)}, u32[]{:S(2)}) collective-permute-start(bf16[128,1024]{1,0:T(8,128)(2,1)S(1)} %collective-permute-done.15.refs_13_.refs_7_.refs_9_), channel_id=1, source_target_pairs={{0,1},{1,0},{2,3},{3,2},{4,5},{5,4},{6,7},{7,6},{8,9},{9,8},{10,11... | collective-permute-start | bytes 786440 | tf_op jit(solution)/shard_map/ppermute | solution.py:62
  65.1 4.1 %copy-start.13 = (bf16[128,1024]{1,0:T(8,128)(2,1)}, bf16[128,1024]{1,0:T(8,128)(2,1)S(1)}, u32[]{:S(2)}) copy-start(bf16[128,1024]{1,0:T(8,128)(2,1)S(1)} %collective-permute-done.17.refs_15_.refs_9_.refs_11_) | copy-start | bytes 786436
  65.1 32.6 %collective-permute-start.5 = (bf16[128,3072]{1,0:T(8,128)(2,1)}, bf16[128,3072]{1,0:T(8,128)(2,1)}, u32[]{:S(2)}, u32[]{:S(2)}) collective-permute-start(bf16[128,3072]{1,0:T(8,128)(2,1)} %bitcast.34), channel_id=1, source_target_pairs={{0,1},{1,0},{2,3},{3,2},{4,5},{5,4},{6,7},{7,6},{8,9},{9,8},{10,11... | collective-permute-start | bytes 2359304 | tf_op jit(solution)/shard_map/ppermute | solution.py:62
  65.1 4.1 %copy-start.12 = (bf16[128,1024]{1,0:T(8,128)(2,1)}, bf16[128,1024]{1,0:T(8,128)(2,1)S(1)}, u32[]{:S(2)}) copy-start(bf16[128,1024]{1,0:T(8,128)(2,1)S(1)} %collective-permute-done.21.refs_19_.refs_13_.refs_15_) | copy-start | bytes 786436
  65.1 7.6 %collective-permute-start.18 = (bf16[128,1024]{1,0:T(8,128)(2,1)}, bf16[128,1024]{1,0:T(8,128)(2,1)}, u32[]{:S(2)}, u32[]{:S(2)}) collective-permute-start(bf16[128,1024]{1,0:T(8,128)(2,1)} %collective-permute-done.16.refs_14_.refs_8_.refs_10_), channel_id=1, source_target_pairs={{4,6},{5,7},{12,14},{13,15},{20,22},{21,23},{28,30},{29,31}} | collective-permute-start | bytes 786440 | tf_op jit(solution)/shard_map/ppermute | solution.py:66
  66.5 2.7 copy-start.14
  66.5 31.6 %collective-permute-start.6 = (bf16[128,3072]{1,0:T(8,128)(2,1)S(1)}, bf16[128,3072]{1,0:T(8,128)(2,1)}, u32[]{:S(2)}, u32[]{:S(2)}) collective-permute-start(bf16[128,3072]{1,0:T(8,128)(2,1)S(1)} %collective-permute-done.1.refs_6_), channel_id=1, source_target_pairs={{0,1},{1,0},{2,3},{3,2},{4,5},{5,4},{6,7},{7,6},{8,9},{9,8},{10,11... | collective-permute-start | bytes 2359304 | tf_op jit(solution)/shard_map/ppermute | solution.py:62
  69.1 49.6 %copy-start.23 = (s32[2,1,8,8]{3,2,1,0:T(8,128)S(1)}, s32[2,1,8,8]{3,2,1,0:T(8,128)}, u32[]{:S(2)}) copy-start(s32[2,1,8,8]{3,2,1,0:T(8,128)} %param.23) | copy-start | bytes 1540
  69.2 68.4 %all-to-all-start = ((bf16[4,128,1152]{2,1,0:T(8,128)(2,1)}), bf16[4,128,1152]{2,1,0:T(8,128)(2,1)S(1)}, u32[]{:S(2)}, u32[]{:S(2)}) async-start(bf16[4,128,1152]{2,1,0:T(8,128)(2,1)} %broadcast_in_dim.16), calls=%async_computation | async-start | bytes 2359296 | tf_op jit(solution)/shard_map/all_to_all | solution.py:101
  72.7 23.0 %collective-permute-start.19 = (bf16[128,1024]{1,0:T(8,128)(2,1)}, bf16[128,1024]{1,0:T(8,128)(2,1)S(1)}, u32[]{:S(2)}, u32[]{:S(2)}) collective-permute-start(bf16[128,1024]{1,0:T(8,128)(2,1)} %copy-done.13), channel_id=1, source_target_pairs={{2,0},{3,1},{10,8},{11,9},{18,16},{19,17},{26,24},{27,25}} | collective-permute-start | bytes 786440 | tf_op jit(solution)/shard_map/ppermute | solution.py:66
  74.0 24.1 %collective-permute-start.10 = (bf16[128,3072]{1,0:T(8,128)(2,1)}, bf16[128,3072]{1,0:T(8,128)(2,1)S(1)}, u32[]{:S(2)}, u32[]{:S(2)}) collective-permute-start(bf16[128,3072]{1,0:T(8,128)(2,1)} %collective-permute-done.3.refs_8_), channel_id=1, source_target_pairs={{4,6},{5,7},{12,14},{13,15},{20,22},{21,23},{28,30},{29,31}} | collective-permute-start | bytes 2359304 | tf_op jit(solution)/shard_map/ppermute | solution.py:66
  74.8 42.3 %collective-permute-start.11 = (bf16[128,3072]{1,0:T(8,128)(2,1)}, bf16[128,3072]{1,0:T(8,128)(2,1)S(1)}, u32[]{:S(2)}, u32[]{:S(2)}) collective-permute-start(bf16[128,3072]{1,0:T(8,128)(2,1)} %collective-permute-done.4.refs_9_), channel_id=1, source_target_pairs={{2,0},{3,1},{10,8},{11,9},{18,16},{19,17},{26,24},{27,25}} | collective-permute-start | bytes 2359304 | tf_op jit(solution)/shard_map/ppermute | solution.py:66
  95.8 21.3 %copy-start.15 = (bf16[128,1024]{1,0:T(8,128)(2,1)}, bf16[128,1024]{1,0:T(8,128)(2,1)S(1)}, u32[]{:S(2)}) copy-start(bf16[128,1024]{1,0:T(8,128)(2,1)S(1)} %collective-permute-done.19.refs_17_.refs_11_.refs_13_) | copy-start | bytes 786436
  95.8 1.7 collective-permute-start.23
  97.5 19.5 %copy-start.16 = (bf16[128,1024]{1,0:T(8,128)(2,1)}, bf16[128,1024]{1,0:T(8,128)(2,1)S(1)}, u32[]{:S(2)}) copy-start(bf16[128,1024]{1,0:T(8,128)(2,1)S(1)} %collective-permute-done.23.refs_21_.refs_15_.refs_17_) | copy-start | bytes 786436
  97.5 19.6 %collective-permute-start.7 = (bf16[128,3072]{1,0:T(8,128)(2,1)}, bf16[128,3072]{1,0:T(8,128)(2,1)}, u32[]{:S(2)}, u32[]{:S(2)}) collective-permute-start(bf16[128,3072]{1,0:T(8,128)(2,1)} %copy-done.8), channel_id=1, source_target_pairs={{0,1},{1,0},{2,3},{3,2},{4,5},{5,4},{6,7},{7,6},{8,9},{9,8},{10,11... | collective-permute-start | bytes 2359304 | tf_op jit(solution)/shard_map/ppermute | solution.py:62
  97.6 20.0 %collective-permute-start.8 = (bf16[128,3072]{1,0:T(8,128)(2,1)}, bf16[128,3072]{1,0:T(8,128)(2,1)}, u32[]{:S(2)}, u32[]{:S(2)}) collective-permute-start(bf16[128,3072]{1,0:T(8,128)(2,1)} %collective-permute-done.3.refs_8_), channel_id=1, source_target_pairs={{0,1},{1,0},{2,3},{3,2},{4,5},{5,4},{6,7},{7,6},{8,9},{9,8},{10,11... | collective-permute-start | bytes 2359304 | tf_op jit(solution)/shard_map/ppermute | solution.py:62
  98.0 19.7 %collective-permute-start.9 = (bf16[128,3072]{1,0:T(8,128)(2,1)}, bf16[128,3072]{1,0:T(8,128)(2,1)}, u32[]{:S(2)}, u32[]{:S(2)}) collective-permute-start(bf16[128,3072]{1,0:T(8,128)(2,1)} %collective-permute-done.4.refs_9_), channel_id=1, source_target_pairs={{0,1},{1,0},{2,3},{3,2},{4,5},{5,4},{6,7},{7,6},{8,9},{9,8},{10,11... | collective-permute-start | bytes 2359304 | tf_op jit(solution)/shard_map/ppermute | solution.py:62
  98.2 29.3 %copy-start.4 = (bf16[128,3072]{1,0:T(8,128)(2,1)}, bf16[128,3072]{1,0:T(8,128)(2,1)S(1)}, u32[]{:S(2)}) copy-start(bf16[128,3072]{1,0:T(8,128)(2,1)S(1)} %collective-permute-done.10.refs_7_.refs_10_) | copy-start | bytes 2359300
  98.2 29.3 %collective-permute-start.12 = (bf16[128,3072]{1,0:T(8,128)(2,1)S(1)}, bf16[128,3072]{1,0:T(8,128)(2,1)S(1)}, u32[]{:S(2)}, u32[]{:S(2)}) collective-permute-start(bf16[128,3072]{1,0:T(8,128)(2,1)S(1)} %collective-permute-done.10.refs_7_.refs_10_), channel_id=1, source_target_pairs={{0,1},{1,0},{2,3},{3,2},{4,5},{5,4},{6,7},{7,6},{8,9},{9,8},{10,11... | collective-permute-start | bytes 2359304 | tf_op jit(solution)/shard_map/ppermute | solution.py:62
  117.0 10.4 %copy-start.5 = (bf16[128,3072]{1,0:T(8,128)(2,1)}, bf16[128,3072]{1,0:T(8,128)(2,1)S(1)}, u32[]{:S(2)}) copy-start(bf16[128,3072]{1,0:T(8,128)(2,1)S(1)} %collective-permute-done.11.refs_8_.refs_11_) | copy-start | bytes 2359300
  117.0 10.5 %collective-permute-start.13 = (bf16[128,3072]{1,0:T(8,128)(2,1)S(1)}, bf16[128,3072]{1,0:T(8,128)(2,1)}, u32[]{:S(2)}, u32[]{:S(2)}) collective-permute-start(bf16[128,3072]{1,0:T(8,128)(2,1)S(1)} %collective-permute-done.11.refs_8_.refs_11_), channel_id=1, source_target_pairs={{0,1},{1,0},{2,3},{3,2},{4,5},{5,4},{6,7},{7,6},{8,9},{9,8},{10,11... | collective-permute-start | bytes 2359304 | tf_op jit(solution)/shard_map/ppermute | solution.py:62
  117.1 10.4 %collective-permute-start.24 = (bf16[128,1024]{1,0:T(8,128)(2,1)}, bf16[128,1024]{1,0:T(8,128)(2,1)}, u32[]{:S(2)}, u32[]{:S(2)}) collective-permute-start(bf16[128,1024]{1,0:T(8,128)(2,1)} %copy-done.13), channel_id=1, source_target_pairs={{0,1},{1,0},{2,3},{3,2},{4,5},{5,4},{6,7},{7,6},{8,9},{9,8},{10,11... | collective-permute-start | bytes 786440 | tf_op jit(solution)/shard_map/ppermute | solution.py:62
  117.6 9.8 %collective-permute-start.25 = (bf16[128,1024]{1,0:T(8,128)(2,1)}, bf16[128,1024]{1,0:T(8,128)(2,1)}, u32[]{:S(2)}, u32[]{:S(2)}) collective-permute-start(bf16[128,1024]{1,0:T(8,128)(2,1)} %collective-permute-done.18.refs_16_.refs_10_.refs_12_), channel_id=1, source_target_pairs={{0,1},{1,0},{2,3},{3,2},{4,5},{5,4},{6,7},{7,6},{8,9},{9,8},{10,11... | collective-permute-start | bytes 786440 | tf_op jit(solution)/shard_map/ppermute | solution.py:62
  117.7 9.8 %collective-permute-start.26 = (bf16[128,1024]{1,0:T(8,128)(2,1)}, bf16[128,1024]{1,0:T(8,128)(2,1)}, u32[]{:S(2)}, u32[]{:S(2)}) collective-permute-start(bf16[128,1024]{1,0:T(8,128)(2,1)} %copy-done.15), channel_id=1, source_target_pairs={{0,1},{1,0},{2,3},{3,2},{4,5},{5,4},{6,7},{7,6},{8,9},{9,8},{10,11... | collective-permute-start | bytes 786440 | tf_op jit(solution)/shard_map/ppermute | solution.py:62
  137.6 33.5 %copy-start = (bf16[4,128,1152]{2,1,0:T(8,128)(2,1)}, bf16[4,128,1152]{2,1,0:T(8,128)(2,1)S(1)}, u32[]{:S(2)}) copy-start(bf16[4,128,1152]{2,1,0:T(8,128)(2,1)S(1)} %all-to-all-done.refs_2_) | copy-start | bytes 3538948
  137.6 29.8 %all-to-all-start.2 = ((bf16[4,128,1024]{2,1,0:T(8,128)(2,1)}), bf16[4,128,1024]{2,1,0:T(8,128)(2,1)S(1)}, u32[]{:S(2)}, u32[]{:S(2)}) async-start(bf16[4,128,1024]{2,1,0:T(8,128)(2,1)} %get-tuple-element.41), calls=%async_computation.2 | async-start | bytes 2097152 | tf_op jit(solution)/shard_map/all_to_all | solution.py:101
  167.3 35.9 %copy-start.2 = (bf16[4,128,1024]{2,1,0:T(8,128)(2,1)}, bf16[4,128,1024]{2,1,0:T(8,128)(2,1)S(1)}, u32[]{:S(2)}) copy-start(bf16[4,128,1024]{2,1,0:T(8,128)(2,1)S(1)} %all-to-all-done.2.refs_3_) | copy-start | bytes 3145732
  167.3 28.9 %all-to-all-start.1 = ((bf16[4,128,1024]{2,1,0:T(8,128)(2,1)}), bf16[4,128,1024]{2,1,0:T(8,128)(2,1)S(1)}, u32[]{:S(2)}, u32[]{:S(2)}) async-start(bf16[4,128,1024]{2,1,0:T(8,128)(2,1)} %get-tuple-element.31), calls=%async_computation.1 | async-start | bytes 2097152 | tf_op jit(solution)/shard_map/all_to_all | solution.py:101
  171.0 25.2 %collective-permute-start.28 = (bf16[4,128,1152]{2,1,0:T(8,128)(2,1)S(1)}, bf16[4,128,1152]{2,1,0:T(8,128)(2,1)}, u32[]{:S(2)}, u32[]{:S(2)}) collective-permute-start(bf16[4,128,1152]{2,1,0:T(8,128)(2,1)S(1)} %all-to-all-done.refs_2_), channel_id=1, source_target_pairs={{0,1},{1,0},{2,3},{3,2},{4,5},{5,4},{6,7},{7,6},{8,9},{9,8},{10,11... | collective-permute-start | bytes 3538952 | tf_op jit(solution)/shard_map/ppermute | solution.py:62
  171.1 32.1 %collective-permute-start.37 = (bf16[4,128,1024]{2,1,0:T(8,128)(2,1)S(1)}, bf16[4,128,1024]{2,1,0:T(8,128)(2,1)}, u32[]{:S(2)}, u32[]{:S(2)}) collective-permute-start(bf16[4,128,1024]{2,1,0:T(8,128)(2,1)S(1)} %all-to-all-done.2.refs_3_), channel_id=1, source_target_pairs={{0,1},{1,0},{2,3},{3,2},{4,5},{5,4},{6,7},{7,6},{8,9},{9,8},{10,11... | collective-permute-start | bytes 3145736 | tf_op jit(solution)/shard_map/ppermute | solution.py:62
  196.2 7.0 %copy-start.3 = (bf16[4,128,1024]{2,1,0:T(8,128)(2,1)}, bf16[4,128,1024]{2,1,0:T(8,128)(2,1)S(1)}, u32[]{:S(2)}) copy-start(bf16[4,128,1024]{2,1,0:T(8,128)(2,1)S(1)} %all-to-all-done.1.refs_4_) | copy-start | bytes 3145732
  196.2 17.0 %collective-permute-start.29 = (bf16[4,128,1024]{2,1,0:T(8,128)(2,1)S(1)}, bf16[4,128,1024]{2,1,0:T(8,128)(2,1)S(1)}, u32[]{:S(2)}, u32[]{:S(2)}) collective-permute-start(bf16[4,128,1024]{2,1,0:T(8,128)(2,1)S(1)} %all-to-all-done.1.refs_4_), channel_id=1, source_target_pairs={{0,1},{1,0},{2,3},{3,2},{4,5},{5,4},{6,7},{7,6},{8,9},{9,8},{10,11... | collective-permute-start | bytes 3145736 | tf_op jit(solution)/shard_map/ppermute | solution.py:62
  213.0 10.5 %collective-permute-start.38 = (bf16[4,128,1024]{2,1,0:T(8,128)(2,1)}, bf16[4,128,1024]{2,1,0:T(8,128)(2,1)S(1)}, u32[]{:S(2)}, u32[]{:S(2)}) collective-permute-start(bf16[4,128,1024]{2,1,0:T(8,128)(2,1)} %get-tuple-element.43), channel_id=1, source_target_pairs={{0,1},{1,0},{2,3},{3,2},{4,5},{5,4},{6,7},{7,6},{8,9},{9,8},{10,11... | collective-permute-start | bytes 3145736 | tf_op jit(solution)/shard_map/ppermute | solution.py:62
  213.2 1.0 copy-start.19
  214.2 9.3 %copy-start.17 = (bf16[4,128,1024]{2,1,0:T(8,128)(2,1)S(1)}, bf16[4,128,1024]{2,1,0:T(8,128)(2,1)}, u32[]{:S(2)}) copy-start(bf16[4,128,1024]{2,1,0:T(8,128)(2,1)} %get-tuple-element.42) | copy-start | bytes 3145732
  223.1 5.4 %collective-permute-start.30 = (bf16[4,128,1024]{2,1,0:T(8,128)(2,1)}, bf16[4,128,1024]{2,1,0:T(8,128)(2,1)S(1)}, u32[]{:S(2)}, u32[]{:S(2)}) collective-permute-start(bf16[4,128,1024]{2,1,0:T(8,128)(2,1)} %get-tuple-element.33), channel_id=1, source_target_pairs={{0,1},{1,0},{2,3},{3,2},{4,5},{5,4},{6,7},{7,6},{8,9},{9,8},{10,11... | collective-permute-start | bytes 3145736 | tf_op jit(solution)/shard_map/ppermute | solution.py:62
  224.9 52.7 %all-to-all-start.3 = ((bf16[4,128,1024]{2,1,0:T(8,128)(2,1)}), bf16[4,128,1024]{2,1,0:T(8,128)(2,1)S(1)}, u32[]{:S(2)}, u32[]{:S(2)}) async-start(bf16[4,128,1024]{2,1,0:T(8,128)(2,1)} %add.48), calls=%async_computation.3 | async-start | bytes 2097152 | tf_op jit(solution)/shard_map/all_to_all | solution.py:101
  232.1 35.7 %copy-start.21 = (bf16[128,1024]{1,0:T(8,128)(2,1)S(1)}, bf16[128,1024]{1,0:T(8,128)(2,1)}, u32[]{:S(2)}) copy-start(bf16[128,1024]{1,0:T(8,128)(2,1)} %get-tuple-element.37) | copy-start | bytes 786436
  232.1 44.6 %copy-start.20 = (f32[128,1024]{1,0:T(8,128)S(1)}, f32[128,1024]{1,0:T(8,128)}, u32[]{:S(2)}) copy-start(f32[128,1024]{1,0:T(8,128)} %get-tuple-element.29) | copy-start | bytes 1572868
  232.1 44.6 %copy-start.22 = (bf16[128,1024]{1,0:T(8,128)(2,1)S(1)}, bf16[128,1024]{1,0:T(8,128)(2,1)}, u32[]{:S(2)}) copy-start(bf16[128,1024]{1,0:T(8,128)(2,1)} %get-tuple-element.34) | copy-start | bytes 786436
  232.1 19.7 %collective-permute-start.31 = (bf16[128,1024]{1,0:T(8,128)(2,1)}, bf16[128,1024]{1,0:T(8,128)(2,1)S(1)}, u32[]{:S(2)}, u32[]{:S(2)}) collective-permute-start(bf16[128,1024]{1,0:T(8,128)(2,1)} %get-tuple-element.37), channel_id=1, source_target_pairs={{0,2},{1,3},{8,10},{9,11},{16,18},{17,19},{24,26},{25,27}} | collective-permute-start | bytes 786440 | tf_op jit(solution)/shard_map/ppermute | solution.py:66
  236.2 15.6 %collective-permute-start.34 = (bf16[128,1024]{1,0:T(8,128)(2,1)}, bf16[128,1024]{1,0:T(8,128)(2,1)S(1)}, u32[]{:S(2)}, u32[]{:S(2)}) collective-permute-start(bf16[128,1024]{1,0:T(8,128)(2,1)} %get-tuple-element.35), channel_id=1, source_target_pairs={{6,4},{7,5},{14,12},{15,13},{22,20},{23,21},{30,28},{31,29}} | collective-permute-start | bytes 786440 | tf_op jit(solution)/shard_map/ppermute | solution.py:66
  252.8 9.5 %collective-permute-start.32 = (bf16[128,1024]{1,0:T(8,128)(2,1)S(1)}, bf16[128,1024]{1,0:T(8,128)(2,1)S(1)}, u32[]{:S(2)}, u32[]{:S(2)}) collective-permute-start(bf16[128,1024]{1,0:T(8,128)(2,1)S(1)} %get-tuple-element.46), channel_id=1, source_target_pairs={{0,2},{1,3},{2,4},{3,5},{8,10},{9,11},{10,12},{11,13},{16,18},{17,... | collective-permute-start | bytes 786440 | tf_op jit(solution)/shard_map/ppermute | solution.py:66
  257.1 10.7 %collective-permute-start.35 = (bf16[128,1024]{1,0:T(8,128)(2,1)S(1)}, bf16[128,1024]{1,0:T(8,128)(2,1)S(1)}, u32[]{:S(2)}, u32[]{:S(2)}) collective-permute-start(bf16[128,1024]{1,0:T(8,128)(2,1)S(1)} %get-tuple-element.47), channel_id=1, source_target_pairs={{4,2},{5,3},{6,4},{7,5},{12,10},{13,11},{14,12},{15,13},{20,18},{2... | collective-permute-start | bytes 786440 | tf_op jit(solution)/shard_map/ppermute | solution.py:66
  263.4 8.8 %collective-permute-start.33 = (bf16[128,1024]{1,0:T(8,128)(2,1)S(1)}, bf16[128,1024]{1,0:T(8,128)(2,1)S(1)}, u32[]{:S(2)}, u32[]{:S(2)}) collective-permute-start(bf16[128,1024]{1,0:T(8,128)(2,1)S(1)} %add.43), channel_id=1, source_target_pairs={{0,2},{1,3},{2,4},{3,5},{4,6},{5,7},{8,10},{9,11},{10,12},{11,13},... | collective-permute-start | bytes 786440 | tf_op jit(solution)/shard_map/ppermute | solution.py:66
  267.9 8.9 %collective-permute-start.36 = (bf16[128,1024]{1,0:T(8,128)(2,1)S(1)}, bf16[128,1024]{1,0:T(8,128)(2,1)S(1)}, u32[]{:S(2)}, u32[]{:S(2)}) collective-permute-start(bf16[128,1024]{1,0:T(8,128)(2,1)S(1)} %add.46), channel_id=1, source_target_pairs={{2,0},{3,1},{4,2},{5,3},{6,4},{7,5},{10,8},{11,9},{12,10},{13,11},... | collective-permute-start | bytes 786440 | tf_op jit(solution)/shard_map/ppermute | solution.py:66
  (3 other events, 2.9 us)

commit v7 on v6

--- a/solution.py
+++ b/solution.py
@@ -25,7 +25,7 @@
 BF16 = jnp.bfloat16
 NT = (((1,), (1,)), ((), ()))
 TN = (((0,), (0,)), ((), ()))
-ANY = pl.BlockSpec(memory_space=pl.ANY)
+ANY = pl.BlockSpec(memory_space=pltpu.HBM)
 SMEM = pl.BlockSpec(memory_space=pltpu.SMEM)
 VMEM = pl.BlockSpec(memory_space=pltpu.VMEM)
 PARAMS = pltpu.CompilerParams(vmem_limit_bytes=56 * 1024 * 1024)
@@ -79,20 +79,6 @@
 
 def with_partner(entries):
     return entries + [swapped(block) for block in entries]
-
-
-def scattered(blocks):
-    length = line_length()
-    up = down = None
-    for step in range(1, length):
-        far = length - step
-        send_up, send_down = blocks[far], blocks[length - far]
-        if up is not None:
-            send_up = send_up + up
-            send_down = send_down + down
-        up = hop(send_up, range(0, step), 1)
-        down = hop(send_down, range(length - step, length), -1)
-    return [blocks[0], up, down]
 
 
 def across(blocks):
@@ -200,8 +186,8 @@
 def early_kernel(count, depth, *refs):
     place, xf_ref, xb_ref, gain_a, mask_ref = refs[:5]
     mix_refs = refs[5 : 5 + count]
-    sumf_ref, sumb_ref, normed_ref, allowed_ref = refs[5 + count : 9 + count]
-    mix_w, mix_sems = refs[9 + count :]
+    sumf_ref, sumb_ref, normedf_ref, normedb_ref, allowed_ref = refs[5 + count : 10 + count]
+    mix_w, normed, mix_sems = refs[10 + count :]
     allowed_ref[...] = mask_ref[...]
     chip, core = place[0], place[1]
     mix_w[...] = jnp.zeros_like(mix_w)
@@ -210,12 +196,14 @@
     for index, x_ref in enumerate((xf_ref, xb_ref)):
         x = x_ref[...].astype(F32)
         rms = lax.rsqrt(mean_last(x * x) + EPS)
-        normed_ref[index * rows : (index + 1) * rows, :] = (x * rms * gain_a[...]).astype(BF16)
+        normed[index * rows : (index + 1) * rows, :] = (x * rms * gain_a[...]).astype(BF16)
+    normedf_ref[...] = normed[:rows, :]
+    normedb_ref[...] = normed[rows:, :]
     wait_copies(mix_refs, mix_w, mix_sems, depth, chip, core)
     columns = mix_w.shape[1]
     chunk = 512
     for begin in range(0, columns, chunk):
-        piece = dot(normed_ref[...], mix_w[:, begin : begin + chunk])
+        piece = dot(normed[...], mix_w[:, begin : begin + chunk])
         sumf_ref[:, begin : begin + chunk] = piece[:rows]
         sumb_ref[:, begin : begin + chunk] = piece[rows:]
 
@@ -236,20 +224,10 @@
                 )
 
 
-def project_kernel(count, depth, length, *refs):
-    place, sumf_ref, sumb_ref, normed_ref, xb_ref, gain_e, mask_ref = refs[:7]
-    mix_refs = refs[7:11]
-    out_refs = refs[11 : 11 + count]
-    projf_ref, projb_ref, hidden_ref, expert_ref = refs[11 + count : 15 + count]
-    mix_w, out_w, heads, mix_sems, out_sems = refs[15 + count :]
-    chip, core = place[0], place[1]
-    last_copies(mix_refs, mix_w, mix_sems, depth, length, chip, core, lambda copy: copy.start())
-    start_copies(out_refs, out_w, out_sems, depth, chip, core)
-    last_copies(mix_refs, mix_w, mix_sems, depth, length, chip, core, lambda copy: copy.wait())
-    rows = xb_ref.shape[0]
+def add_last(sum_ref, normed_ref, mix_w, proj_ref, chip, length):
     columns = mix_w.shape[1]
+    block = mix_w.shape[0]
     chunk = 512
-    block = CORES * depth
     for end in (0, length - 1):
 
         @pl.when(chip == end)
@@ -258,27 +236,25 @@
             for begin in range(0, columns, chunk):
                 span = slice(begin, begin + chunk)
                 piece = dot(normed_ref[:, far : far + block], mix_w[:, span])
-                projf_ref[:, span] = sumf_ref[:, span] + piece[:rows]
-                projb_ref[:, span] = sumb_ref[:, span] + piece[rows:]
+                proj_ref[:, span] = sum_ref[:, span] + piece
 
     @pl.when((chip > 0) & (chip < length - 1))
     def _():
-        projf_ref[...] = sumf_ref[...]
-        projb_ref[...] = sumb_ref[...]
-
-    attend_rows(projb_ref, mask_ref[1], heads)
-    wait_copies(out_refs, out_w, out_sems, depth, chip, core)
-    finish_rows(xb_ref[...], heads[...], out_w[...], gain_e[...], hidden_ref, expert_ref)
-
-
-def forward_kernel(count, depth, *refs):
-    place, x_ref, proj_ref, gain_e, mask_ref = refs[:5]
-    out_refs = refs[5 : 5 + count]
-    hidden_ref, expert_ref = refs[5 + count : 7 + count]
-    out_w, heads, out_sems = refs[7 + count :]
+        proj_ref[...] = sum_ref[...]
+
+
+def project_kernel(count, depth, length, micro, *refs):
+    place, x_ref, sum_ref, normed_ref, gain_e, mask_ref = refs[:6]
+    mix_refs = refs[6:10]
+    out_refs = refs[10 : 10 + count]
+    proj_ref, hidden_ref, expert_ref = refs[10 + count : 13 + count]
+    mix_w, out_w, heads, mix_sems, out_sems = refs[13 + count :]
     chip, core = place[0], place[1]
+    last_copies(mix_refs, mix_w, mix_sems, depth, length, chip, core, lambda copy: copy.start())
     start_copies(out_refs, out_w, out_sems, depth, chip, core)
-    attend_rows(proj_ref, mask_ref[0], heads)
+    last_copies(mix_refs, mix_w, mix_sems, depth, length, chip, core, lambda copy: copy.wait())
+    add_last(sum_ref, normed_ref, mix_w, proj_ref, chip, length)
+    attend_rows(proj_ref, mask_ref[micro], heads)
     wait_copies(out_refs, out_w, out_sems, depth, chip, core)
     finish_rows(x_ref[...], heads[...], out_w[...], gain_e[...], hidden_ref, expert_ref)
 
@@ -330,12 +306,13 @@
             out_ref[owner] = result[pl.ds(start, rows), :]
 
 
-def expert_backward_kernel(rows, *refs):
+def expert_backward_kernel(count, rows, *refs):
     place, up_ref, act_ref = refs[:3]
-    row_refs = refs[3:5]
-    mine_ref, other_ref, tokens, result, sems = refs[5:]
+    row_refs = refs[3 : 3 + count]
+    mine_ref, other_ref, tokens, result, sems = refs[3 + count :]
     chip, core = place[0], place[1]
-    fetch_line(row_refs, tokens, sems, rows, chip, core)
+    start_copies(row_refs, tokens, sems, rows, chip, core)
+    wait_copies(row_refs, tokens, sems, rows, chip, core)
     chunk = 2 * rows
 
     def step(index, carry):
@@ -374,12 +351,6 @@
 
     each_chunk(tokens.shape[0] // chunk, step)
     give_back(result, mine_ref, other_ref, rows, core)
-
-
-def add_apart_kernel(place, mine_ref, other_ref, *out_refs):
-    for j, out_ref in enumerate(out_refs):
-        owner = lax.rem(place[0] + j, len(out_refs))
-        out_ref[...] = (mine_ref[owner].astype(F32) + other_ref[owner].astype(F32)).astype(BF16)
 
 
 def heads_backward_kernel(count, depth, *refs):
@@ -518,48 +489,51 @@
     early_mix = mixers[: half - 2] + mixers[half : count - 2]
     last_mix = mixers[half - 2 : half] + mixers[count - 2 :]
     early = len(early_mix)
-    sum_fwd, sum_bwd, normed, mask = call(
+    sum_fwd, sum_bwd, normed_fwd, normed_bwd, mask = call(
         functools.partial(early_kernel, early, depth),
         (
             shaped((tokens, columns), F32),
             shaped((tokens, columns), F32),
-            shaped((2 * tokens, width), BF16),
+            shaped((tokens, width), BF16),
+            shaped((tokens, width), BF16),
             shaped(mask.shape, F32),
         ),
         [SMEM] + [VMEM] * 4 + [ANY] * early,
-        (VMEM,) * 4,
-        [pltpu.VMEM((width, columns), BF16), dma(expert_count)],
-        [place, arriving, stashed_input, attention_gain, mask] + early_mix,
-    )
-    proj_fwd, proj_bwd, hidden_bwd, expert_bwd = call(
-        functools.partial(project_kernel, count, depth, length),
-        (
-            shaped((tokens, columns), F32),
-            shaped((tokens, columns), F32),
-            shaped((tokens, width), F32),
-            shaped((length, tokens, width), BF16),
-        ),
-        [SMEM] + [VMEM] * 6 + [ANY] * (4 + count),
-        (VMEM,) * 4,
+        (VMEM,) * 5,
         [
-            pltpu.VMEM((CORES * depth, columns), BF16),
-            pltpu.VMEM((width, width), BF16),
-            pltpu.VMEM((tokens, width), BF16),
-            dma(4),
+            pltpu.VMEM((width, columns), BF16),
+            pltpu.VMEM((2 * tokens, width), BF16),
             dma(expert_count),
         ],
-        [place, sum_fwd, sum_bwd, normed, stashed_input, expert_gain, mask] + last_mix + outers,
-    )
-    rows_bwd = spread(expert_bwd)
-
-    hidden_fwd, expert_fwd = call(
-        functools.partial(forward_kernel, count, depth),
-        (shaped((tokens, width), F32), shaped((length, tokens, width), BF16)),
-        [SMEM] + [VMEM] * 4 + [ANY] * count,
-        (VMEM,) * 2,
-        [pltpu.VMEM((width, width), BF16), pltpu.VMEM((tokens, width), BF16), dma(expert_count)],
-        [place, arriving, proj_fwd, expert_gain, mask] + outers,
-    )
+        [place, arriving, stashed_input, attention_gain, mask] + early_mix,
+    )
+
+    def attended(micro, x, sums, normed, block):
+        return call(
+            functools.partial(project_kernel, count, depth, length, micro),
+            (
+                shaped((tokens, columns), F32),
+                shaped((tokens, width), F32),
+                shaped(block, BF16),
+            ),
+            [SMEM] + [VMEM] * 5 + [ANY] * (4 + count),
+            (VMEM,) * 3,
+            [
+                pltpu.VMEM((CORES * depth, columns), BF16),
+                pltpu.VMEM((width, width), BF16),
+                pltpu.VMEM((tokens, width), BF16),
+                dma(4),
+                dma(expert_count),
+            ],
+            [place, x, sums, normed, expert_gain, mask] + last_mix + outers,
+        )
+
+    proj_bwd, hidden_bwd, expert_bwd = attended(
+        1, stashed_input, sum_bwd, normed_bwd, (tokens, width)
+    )
+    rows_bwd = with_partner(relayed(expert_bwd))
+
+    _, hidden_fwd, expert_fwd = attended(0, arriving, sum_fwd, normed_fwd, (length, tokens, width))
     rows_fwd = spread(expert_fwd)
 
     grad_act, gate_fwd = call(
@@ -577,11 +551,11 @@
         return [pltpu.VMEM((total, width), BF16), pltpu.VMEM((total, width), BF16), dma(sems)]
 
     mine, other = call(
-        functools.partial(expert_backward_kernel, tokens),
+        functools.partial(expert_backward_kernel, count, tokens),
         pair,
-        [SMEM, VMEM, VMEM] + [ANY] * 2,
+        [SMEM, VMEM, VMEM] + [ANY] * count,
         (VMEM,) * 2,
-        expert_scratch((CORES, length)),
+        expert_scratch(expert_count),
         [place, up_weight, grad_act] + rows_bwd,
     )
     grad_parts = across(mine + swapped(other))
@@ -594,16 +568,7 @@
         expert_scratch((CORES, length)),
         [place, up_weight, down_weight, gate_fwd] + rows_fwd,
     )
-    moe_parts = scattered(
-        call(
-            add_apart_kernel,
-            (shaped((tokens, width), BF16),) * length,
-            [SMEM] + [VMEM] * 2,
-            (VMEM,) * length,
-            [],
-            [place, mine, swapped(other)],
-        ),
-    )
+    moe_parts = across(mine + swapped(other))
 
     grad_mixed, grad_hidden = call(
         functools.partial(heads_backward_kernel, count, depth),
@@ -626,9 +591,7 @@
         [place, stashed_input, grad_mixed, grad_hidden, attention_gain] + mixers,
     )
 
-    layer_output = hidden_fwd
-    for part in moe_parts:
-        layer_output = layer_output + part.astype(F32)
+    layer_output = hidden_fwd + jnp.sum(moe_parts.astype(F32), axis=0)
     return (layer_output.astype(BF16), derivative)
 
 

time: 295 us -> 266 us (0.902)
  waiting for transfers between devices: 153 us -> 125 us
    all_to_all x4, waiting for transfers between devices: 45.5 us -> 21.2 us  [across(): lax.all_to_all(blocks, 'expert', split_axis=0, concat_axis=0, axis_index_...]
    ppermute x18, waiting for transfers between devices: 104 us -> 89.7 us  [hop(): return lax.ppermute(value, 'expert', chip_pairs(sources, move))]
    ppermute x18, starting transfers between devices: 37.9 us -> 28.9 us  [hop(): return lax.ppermute(value, 'expert', chip_pairs(sources, move))]
    all_to_all x4, starting transfers between devices: 14.3 us -> 22.1 us  [across(): lax.all_to_all(blocks, 'expert', split_axis=0, concat_axis=0, axis_index_...]
    ppermute x2, waiting for transfers between devices: 1.63 us -> 7.6 us  [passed_along(): return lax.ppermute(value, 'section', pairs)]
    ppermute x19 -> x25, waiting for transfers between devices: 1.79 us -> 6.31 us  [swapped(): return lax.ppermute(value, 'expert', [(i, i ^ 1) for i in range(count)])]
    pallas_call x9 -> x8, Pallas kernels: 65.8 us -> 63.9 us  [call(): pl.pallas_call(kernel, out_shape=outs, in_specs=specs, out_specs=out_spec...]
    ppermute x19 -> x25, starting transfers between devices: 4.39 us -> 6.11 us  [swapped(): return lax.ppermute(value, 'expert', [(i, i ^ 1) for i in range(count)])]
  transfers between devices with their start and end apart: 43 -> 49, of which waited for: 13 -> 13; matrix products, arithmetic and copies ran while one was open for 3% -> 4% of each run, Pallas kernels for 17% -> 24%
where the time goes in v7:
time: 266 us; the launch traced here: 265 us
  waiting for transfers between devices  125 us (47%)
  Pallas kernels  63.9 us (24%)
  starting transfers between devices  61.1 us (23%)
  other arithmetic  8.21 us (3%)
  local copies, waits for them, and re-layouts  4.45 us (2%)
    ppermute x18, waiting for transfers between devices, hop(): return lax.ppermute(value, 'expert', chip_pairs(sources, move))  89.7 us
    pallas_call x8, Pallas kernels, call(): pl.pallas_call(kernel, out_shape=outs, in_specs=specs, out_specs=out_spec...  63.9 us
    ppermute x18, starting transfers between devices, hop(): return lax.ppermute(value, 'expert', chip_pairs(sources, move))  28.9 us
    all_to_all x4, starting transfers between devices, across(): lax.all_to_all(blocks, 'expert', split_axis=0, concat_axis=0, axis_index_...  22.1 us
    all_to_all x4, waiting for transfers between devices, across(): lax.all_to_all(blocks, 'expert', split_axis=0, concat_axis=0, axis_index_...  21.2 us
    ppermute x2, waiting for transfers between devices, passed_along(): return lax.ppermute(value, 'section', pairs)  7.6 us
    ppermute x25, waiting for transfers between devices, swapped(): return lax.ppermute(value, 'expert', [(i, i ^ 1) for i in range(count)])  6.31 us
    ppermute x25, starting transfers between devices, swapped(): return lax.ppermute(value, 'expert', [(i, i ^ 1) for i in range(count)])  6.11 us
  transfers between devices with their start and end apart: 49, of which 13 were waited for; matrix products, arithmetic and copies ran while one was open for 4% of the time, Pallas kernels for 24%

profile of v7, /device:TPU:0, one launch (start us, length us, event | category | flops | bytes accessed | tf_op | source)
XLA Modules:
  0.0 264.9 jit_solution(6967623431336281189)
XLA Ops:
  0.6 5.0 %collective-permute-start.1 = (bf16[128,3072]{1,0:T(8,128)(2,1)}, bf16[128,3072]{1,0:T(8,128)(2,1)S(1)}, u32[]{:S(2)}, u32[]{:S(2)}) collective-permute-start(bf16[128,3072]{1,0:T(8,128)(2,1)} %bitcast.32), channel_id=1, source_target_pairs={{0,2},{1,3},{2,4},{3,5},{4,6},{5,7},{8,10},{9,11},{10,12},{11,13},... | collective-permute-start | bytes 2359304 | tf_op jit(solution)/shard_map/ppermute | solution.py:66
  5.6 1.3 collective-permute-start.2
  6.9 4.6 %collective-permute-start.14 = (bf16[128,1024]{1,0:T(8,128)(2,1)}, bf16[128,1024]{1,0:T(8,128)(2,1)S(1)}, u32[]{:S(2)}, u32[]{:S(2)}) collective-permute-start(bf16[128,1024]{1,0:T(8,128)(2,1)} %bitcast.37), channel_id=1, source_target_pairs={{0,2},{1,3},{2,4},{3,5},{4,6},{5,7},{8,10},{9,11},{10,12},{11,13},... | collective-permute-start | bytes 786440 | tf_op jit(solution)/shard_map/ppermute | solution.py:66
  11.5 1.3 collective-permute-start.15
  12.8 1.5 collective-permute-start
  14.4 0.7 add_divide_fusion
  15.1 0.7 select_reduce_fusion
  15.7 5.5 %collective-permute-done.refs_1_ = bf16[128,1024]{1,0:T(8,128)(2,1)} collective-permute-done((bf16[128,1024]{1,0:T(8,128)(2,1)}, bf16[128,1024]{1,0:T(8,128)(2,1)}, u32[]{:S(2)}, u32[]{:S(2)}) %collective-permute-start) | collective-permute-done | bytes 262176 | tf_op jit(solution)/shard_map/ppermute | solution.py:45
  21.3 7.0 %collective-permute-done.14.refs_11_.refs_8_ = bf16[128,1024]{1,0:T(8,128)(2,1)S(1)} collective-permute-done((bf16[128,1024]{1,0:T(8,128)(2,1)}, bf16[128,1024]{1,0:T(8,128)(2,1)S(1)}, u32[]{:S(2)}, u32[]{:S(2)}) %collective-permute-start.14) | collective-permute-done | bytes 262176 | tf_op jit(solution)/shard_map/ppermute | solution.py:66
  28.3 2.4 collective-permute-start.27
  30.9 1.5 collective-permute-done.15.refs_12_.refs_9_
  32.4 1.4 collective-permute-start.16
  33.7 2.1 collective-permute-done.27.refs_1_
  35.8 1.3 collective-permute-start.17
  37.1 1.5 collective-permute-start.3
  38.6 1.3 collective-permute-start.4
  40.0 1.1 broadcast_in_dim.16
  41.1 11.2 %all-to-all-start = ((bf16[4,128,1152]{2,1,0:T(8,128)(2,1)}), bf16[4,128,1152]{2,1,0:T(8,128)(2,1)}, u32[]{:S(2)}, u32[]{:S(2)}) async-start(bf16[4,128,1152]{2,1,0:T(8,128)(2,1)} %broadcast_in_dim.16), calls=%async_computation | async-start | bytes 2359296 | tf_op jit(solution)/shard_map/all_to_all | solution.py:87
  52.4 1.4 collective-permute-start.18
  53.7 1.3 collective-permute-start.19
  55.1 0.5 collective-permute-start.5
  55.7 27.6 %collective-permute-done.19.refs_16_.refs_13_ = bf16[128,1024]{1,0:T(8,128)(2,1)S(1)} collective-permute-done((bf16[128,1024]{1,0:T(8,128)(2,1)}, bf16[128,1024]{1,0:T(8,128)(2,1)S(1)}, u32[]{:S(2)}, u32[]{:S(2)}) %collective-permute-start.19) | collective-permute-done | bytes 262176 | tf_op jit(solution)/shard_map/ppermute | solution.py:66
  83.3 0.7 collective-permute-start.10
  84.1 1.3 collective-permute-start.11
  85.4 0.6 collective-permute-start.24
  86.0 1.4 collective-permute-done.24.refs_21_.refs_18_
  88.4 20.0 %collective-permute-done.11.refs_7_.refs_11_ = bf16[128,3072]{1,0:T(8,128)(2,1)S(1)} collective-permute-done((bf16[128,3072]{1,0:T(8,128)(2,1)}, bf16[128,3072]{1,0:T(8,128)(2,1)S(1)}, u32[]{:S(2)}, u32[]{:S(2)}) %collective-permute-start.11) | collective-permute-done | bytes 786464 | tf_op jit(solution)/shard_map/ppermute | solution.py:66
  108.5 0.5 collective-permute-start.28
  109.2 0.4 collective-permute-start.26
  109.6 0.6 pad_add_fusion.refs_0_
  110.2 1.1 fusion.refs_4_
  111.3 7.5 %shard_map.131 = (f32[128,3072]{1,0:T(8,128)}, f32[128,3072]{1,0:T(8,128)}, bf16[128,1024]{1,0:T(8,128)(2,1)}, bf16[128,1024]{1,0:T(8,128)(2,1)}, f32[2,128,128]{2,1,0:T(8,128)}) custom-call(s32[2]{0:T(128)} %pad_add_fusion.refs_0_, bf16[128,1024]{1,0:T(8,128)(2,1)} %collective-permute-done.refs_1_, bf16[128,1024]{1,0:T(8,128)(2,1)} %refs_1_.3, ...), custom_call_target="tpu_custom_call" | custom-call | tf_op jit(solution)/shard_map/pallas_call | solution.py:420
  118.9 0.8 copy-done.2
  120.0 7.7 %shard_map.135 = (f32[128,3072]{1,0:T(8,128)}, f32[128,1024]{1,0:T(8,128)}, bf16[128,1024]{1,0:T(8,128)(2,1)}) custom-call(s32[2]{0:T(128)} %pad_add_fusion.refs_0_, bf16[128,1024]{1,0:T(8,128)(2,1)} %refs_1_.3, f32[128,3072]{1,0:T(8,128)} %get-tuple-element.28.refs_2_, bf16[128,1024]{1,0:T(8,128)(2,1)} %get-tuple-element.29.refs_3_, f32[1,1024]{1,0:T(1,128)} %refs_4_.6, ...), custom_call_target="tpu_custom_call" | custom-call | tf_op jit(solution)/shard_map/pallas_call | solution.py:420
  127.7 1.3 collective-permute-start.31
  129.0 1.3 collective-permute-start.32
  130.3 8.0 %shard_map.132 = (f32[128,3072]{1,0:T(8,128)}, f32[128,1024]{1,0:T(8,128)}, bf16[4,128,1024]{2,1,0:T(8,128)(2,1)}) custom-call(s32[2]{0:T(128)} %pad_add_fusion.refs_0_, bf16[128,1024]{1,0:T(8,128)(2,1)} %collective-permute-done.refs_1_, f32[128,3072]{1,0:T(8,128)} %get-tuple-element.20.refs_2_, bf16[128,1024]{1,0:T(8,128)(2,1)} %get-tuple-element.21.refs_3_, ...), custom_call_target="tpu_custom_call" | custom-call | tf_op jit(solution)/shard_map/pallas_call | solution.py:420
  138.3 3.7 %all-to-all-start.1 = ((bf16[4,128,1024]{2,1,0:T(8,128)(2,1)}), bf16[4,128,1024]{2,1,0:T(8,128)(2,1)S(1)}, u32[]{:S(2)}, u32[]{:S(2)}) async-start(bf16[4,128,1024]{2,1,0:T(8,128)(2,1)} %get-tuple-element.25), calls=%async_computation.1 | async-start | bytes 2097152 | tf_op jit(solution)/shard_map/all_to_all | solution.py:87
  142.0 0.7 collective-permute-start.33
  142.7 1.3 collective-permute-start.34
  144.6 0.7 collective-permute-start.35
  145.3 17.5 %collective-permute-done.34.refs_7_ = bf16[128,1024]{1,0:T(8,128)(2,1)S(1)} collective-permute-done((bf16[128,1024]{1,0:T(8,128)(2,1)S(1)}, bf16[128,1024]{1,0:T(8,128)(2,1)S(1)}, u32[]{:S(2)}, u32[]{:S(2)}) %collective-permute-start.34) | collective-permute-done | bytes 262176 | tf_op jit(solution)/shard_map/ppermute | solution.py:66
  162.8 1.5 collective-permute-start.36
  164.4 0.5 collective-permute-start.40
  164.9 0.4 collective-permute-start.42
  165.4 16.1 %collective-permute-done.36.refs_9_ = bf16[128,1024]{1,0:T(8,128)(2,1)S(1)} collective-permute-done((bf16[128,1024]{1,0:T(8,128)(2,1)S(1)}, bf16[128,1024]{1,0:T(8,128)(2,1)S(1)}, u32[]{:S(2)}, u32[]{:S(2)}) %collective-permute-start.36) | collective-permute-done | bytes 262176 | tf_op jit(solution)/shard_map/ppermute | solution.py:66
  181.4 6.7 %shard_map.133 = (f32[1024,704]{1,0:T(8,128)}, f32[1024,128]{1,0:T(8,128)}) custom-call(s32[2]{0:T(128)} %pad_add_fusion.refs_0_, bf16[704,1024]{1,0:T(8,128)(2,1)} %bitcast.30, bf16[4,128,1152]{2,1,0:T(8,128)(2,1)} %all-to-all-done.refs_2_, bf16[4,128,1152]{2,1,0:T(8,128)(2,1)} %collective-permute-done.28.refs_3_), custom_call_target="tpu_custom_call" | custom-call | tf_op jit(solution)/shard_map/pallas_call | solution.py:420
  188.3 0.6 copy-done.31
  189.3 9.9 %shard_map.136 = (bf16[4,128,1024]{2,1,0:T(8,128)(2,1)}, bf16[4,128,1024]{2,1,0:T(8,128)(2,1)}) custom-call(s32[2]{0:T(128)} %pad_add_fusion.refs_0_, bf16[704,1024]{1,0:T(8,128)(2,1)} %bitcast.28, f32[1024,704]{1,0:T(8,128)} %get-tuple-element.32.refs_2_, bf16[128,1024]{1,0:T(8,128)(2,1)} %get-tuple-element.33.refs_3_, bf16[128,1024]{1,0:T(8,128)(2,1)} %copy-done.23, ...), custom_call_target="tpu_custom_call" | custom-call | tf_op jit(solution)/shard_map/pallas_call | solution.py:420
  199.2 0.5 collective-permute-start.44
  199.8 2.4 collective-permute-done.44
  202.2 2.6 add.28
  204.8 3.5 %all-to-all-start.3 = ((bf16[4,128,1024]{2,1,0:T(8,128)(2,1)}), bf16[4,128,1024]{2,1,0:T(8,128)(2,1)S(1)}, u32[]{:S(2)}, u32[]{:S(2)}) async-start(bf16[4,128,1024]{2,1,0:T(8,128)(2,1)} %add.28), calls=%async_computation.3 | async-start | bytes 2097152 | tf_op jit(solution)/shard_map/all_to_all | solution.py:87
  208.3 1.0 copy-done.20
  209.3 8.8 %shard_map.134 = (bf16[4,128,1024]{2,1,0:T(8,128)(2,1)}, bf16[4,128,1024]{2,1,0:T(8,128)(2,1)}) custom-call(s32[2]{0:T(128)} %pad_add_fusion.refs_0_, bf16[704,1024]{1,0:T(8,128)(2,1)} %bitcast.29, bf16[704,1024]{1,0:T(8,128)(2,1)} %bitcast.31, f32[1024,128]{1,0:T(8,128)} %get-tuple-element.24.refs_3_, bf16[4,128,1024]{2,1,0:T(8,128)(2,1)} %copy-done.5, ...), custom_call_target="tpu_custom_call" | custom-call | tf_op jit(solution)/shard_map/pallas_call | solution.py:420
  218.1 0.4 collective-permute-start.30
  218.5 2.5 collective-permute-done.30
  221.0 2.6 add.26
  223.6 11.2 %all-to-all-done.3.refs_6_ = bf16[4,128,1024]{2,1,0:T(8,128)(2,1)S(1)} async-done(((bf16[4,128,1024]{2,1,0:T(8,128)(2,1)}), bf16[4,128,1024]{2,1,0:T(8,128)(2,1)S(1)}, u32[]{:S(2)}, u32[]{:S(2)}) %all-to-all-start.3) | async-done | bytes 1048608 | tf_op jit(solution)/shard_map/all_to_all | solution.py:87
  234.8 3.7 %all-to-all-start.2 = ((bf16[4,128,1024]{2,1,0:T(8,128)(2,1)}), bf16[4,128,1024]{2,1,0:T(8,128)(2,1)S(1)}, u32[]{:S(2)}, u32[]{:S(2)}) async-start(bf16[4,128,1024]{2,1,0:T(8,128)(2,1)} %add.26), calls=%async_computation.2 | async-start | bytes 2097152 | tf_op jit(solution)/shard_map/all_to_all | solution.py:87
  238.6 8.1 %shard_map.137 = (bf16[128,3072]{1,0:T(8,128)(2,1)}, f32[128,1024]{1,0:T(8,128)}) custom-call(s32[2]{0:T(128)} %pad_add_fusion.refs_0_, bf16[128,1024]{1,0:T(8,128)(2,1)} %copy-done.19, f32[128,1024]{1,0:T(8,128)} %get-tuple-element.30.refs_2_, f32[128,3072]{1,0:T(8,128)} %get-tuple-element.31.refs_3_, f32[1,1024]{1,0:T(1,128)} %refs_4_.6, ...), custom_call_target="tpu_custom_call" | custom-call | tf_op jit(solution)/shard_map/pallas_call | solution.py:420
  246.7 7.3 %shard_map.138 = bf16[128,1024]{1,0:T(8,128)(2,1)} custom-call(s32[2]{0:T(128)} %pad_add_fusion.refs_0_, bf16[128,1024]{1,0:T(8,128)(2,1)} %refs_1_.3, bf16[128,3072]{1,0:T(8,128)(2,1)} %get-tuple-element.36.refs_2_, f32[128,1024]{1,0:T(8,128)} %get-tuple-element.37.refs_3_, f32[1,1024]{1,0:T(1,128)} %refs_4_.7, bf16[128,3072]{1,0:T(8,128)(2,1)} %bitcast.35, ...), custom_call_target="tpu_custom_call" | custom-call | tf_op jit(solution)/shard_map/pallas_call | solution.py:420
  254.0 10.0 %all-to-all-done.2 = bf16[4,128,1024]{2,1,0:T(8,128)(2,1)S(1)} async-done(((bf16[4,128,1024]{2,1,0:T(8,128)(2,1)}), bf16[4,128,1024]{2,1,0:T(8,128)(2,1)S(1)}, u32[]{:S(2)}, u32[]{:S(2)}) %all-to-all-start.2) | async-done | bytes 1048608 | tf_op jit(solution)/shard_map/all_to_all | solution.py:87
  264.2 0.8 add_convert_fusion
  (132 shorter events, 3.5 us)
Async XLA Ops:
  0.6 36.5 %collective-permute-start.1 = (bf16[128,3072]{1,0:T(8,128)(2,1)}, bf16[128,3072]{1,0:T(8,128)(2,1)S(1)}, u32[]{:S(2)}, u32[]{:S(2)}) collective-permute-start(bf16[128,3072]{1,0:T(8,128)(2,1)} %bitcast.32), channel_id=1, source_target_pairs={{0,2},{1,3},{2,4},{3,5},{4,6},{5,7},{8,10},{9,11},{10,12},{11,13},... | collective-permute-start | bytes 2359304 | tf_op jit(solution)/shard_map/ppermute | solution.py:66
  5.6 33.0 %collective-permute-start.2 = (bf16[128,3072]{1,0:T(8,128)(2,1)}, bf16[128,3072]{1,0:T(8,128)(2,1)S(1)}, u32[]{:S(2)}, u32[]{:S(2)}) collective-permute-start(bf16[128,3072]{1,0:T(8,128)(2,1)} %bitcast.33), channel_id=1, source_target_pairs={{2,0},{3,1},{4,2},{5,3},{6,4},{7,5},{10,8},{11,9},{12,10},{13,11},... | collective-permute-start | bytes 2359304 | tf_op jit(solution)/shard_map/ppermute | solution.py:66
  6.9 21.4 %collective-permute-start.14 = (bf16[128,1024]{1,0:T(8,128)(2,1)}, bf16[128,1024]{1,0:T(8,128)(2,1)S(1)}, u32[]{:S(2)}, u32[]{:S(2)}) collective-permute-start(bf16[128,1024]{1,0:T(8,128)(2,1)} %bitcast.37), channel_id=1, source_target_pairs={{0,2},{1,3},{2,4},{3,5},{4,6},{5,7},{8,10},{9,11},{10,12},{11,13},... | collective-permute-start | bytes 786440 | tf_op jit(solution)/shard_map/ppermute | solution.py:66
  11.5 20.9 %collective-permute-start.15 = (bf16[128,1024]{1,0:T(8,128)(2,1)}, bf16[128,1024]{1,0:T(8,128)(2,1)S(1)}, u32[]{:S(2)}, u32[]{:S(2)}) collective-permute-start(bf16[128,1024]{1,0:T(8,128)(2,1)} %bitcast.38), channel_id=1, source_target_pairs={{2,0},{3,1},{4,2},{5,3},{6,4},{7,5},{10,8},{11,9},{12,10},{13,11},... | collective-permute-start | bytes 786440 | tf_op jit(solution)/shard_map/ppermute | solution.py:66
  12.8 8.5 %collective-permute-start = (bf16[128,1024]{1,0:T(8,128)(2,1)}, bf16[128,1024]{1,0:T(8,128)(2,1)}, u32[]{:S(2)}, u32[]{:S(2)}) collective-permute-start(bf16[128,1024]{1,0:T(8,128)(2,1)} %param.12), channel_id=1, source_target_pairs={{0,8},{8,16},{16,24},{24,0},{1,9},{9,17},{17,25},{25,1},{2,10},{10... | collective-permute-start | bytes 786440 | tf_op jit(solution)/shard_map/ppermute | solution.py:45
  21.3 12.4 %collective-permute-start.20 = (bf16[128,1024]{1,0:T(8,128)(2,1)}, bf16[128,1024]{1,0:T(8,128)(2,1)S(1)}, u32[]{:S(2)}, u32[]{:S(2)}) collective-permute-start(bf16[128,1024]{1,0:T(8,128)(2,1)} %bitcast.39), channel_id=1, source_target_pairs={{0,1},{1,0},{2,3},{3,2},{4,5},{5,4},{6,7},{7,6},{8,9},{9,8},{10,11... | collective-permute-start | bytes 786440 | tf_op jit(solution)/shard_map/ppermute | solution.py:62
  28.3 7.5 %collective-permute-start.27 = (bf16[128,1024]{1,0:T(8,128)(2,1)}, bf16[128,1024]{1,0:T(8,128)(2,1)S(1)}, u32[]{:S(2)}, u32[]{:S(2)}) collective-permute-start(bf16[128,1024]{1,0:T(8,128)(2,1)} %param.14), channel_id=1, source_target_pairs={{0,24},{8,0},{16,8},{24,16},{1,25},{9,1},{17,9},{25,17},{2,26},{10... | collective-permute-start | bytes 786440 | tf_op jit(solution)/shard_map/ppermute | solution.py:45
  32.4 19.9 %collective-permute-start.16 = (bf16[128,1024]{1,0:T(8,128)(2,1)S(1)}, bf16[128,1024]{1,0:T(8,128)(2,1)}, u32[]{:S(2)}, u32[]{:S(2)}) collective-permute-start(bf16[128,1024]{1,0:T(8,128)(2,1)S(1)} %collective-permute-done.14.refs_11_.refs_8_), channel_id=1, source_target_pairs={{2,4},{3,5},{4,6},{5,7},{10,12},{11,13},{12,14},{13,15},{18,20},{1... | collective-permute-start | bytes 786440 | tf_op jit(solution)/shard_map/ppermute | solution.py:66
  33.7 20.0 %collective-permute-start.21 = (bf16[128,1024]{1,0:T(8,128)(2,1)S(1)}, bf16[128,1024]{1,0:T(8,128)(2,1)S(1)}, u32[]{:S(2)}, u32[]{:S(2)}) collective-permute-start(bf16[128,1024]{1,0:T(8,128)(2,1)S(1)} %collective-permute-done.14.refs_11_.refs_8_), channel_id=1, source_target_pairs={{0,1},{1,0},{2,3},{3,2},{4,5},{5,4},{6,7},{7,6},{8,9},{9,8},{10,11... | collective-permute-start | bytes 786440 | tf_op jit(solution)/shard_map/ppermute | solution.py:62
  35.8 16.6 %collective-permute-start.17 = (bf16[128,1024]{1,0:T(8,128)(2,1)S(1)}, bf16[128,1024]{1,0:T(8,128)(2,1)}, u32[]{:S(2)}, u32[]{:S(2)}) collective-permute-start(bf16[128,1024]{1,0:T(8,128)(2,1)S(1)} %collective-permute-done.15.refs_12_.refs_9_), channel_id=1, source_target_pairs={{2,0},{3,1},{4,2},{5,3},{10,8},{11,9},{12,10},{13,11},{18,16},{19,... | collective-permute-start | bytes 786440 | tf_op jit(solution)/shard_map/ppermute | solution.py:66
  37.1 46.2 %collective-permute-start.3 = (bf16[128,3072]{1,0:T(8,128)(2,1)S(1)}, bf16[128,3072]{1,0:T(8,128)(2,1)}, u32[]{:S(2)}, u32[]{:S(2)}) collective-permute-start(bf16[128,3072]{1,0:T(8,128)(2,1)S(1)} %collective-permute-done.1.refs_6_), channel_id=1, source_target_pairs={{2,4},{3,5},{4,6},{5,7},{10,12},{11,13},{12,14},{13,15},{18,20},{1... | collective-permute-start | bytes 2359304 | tf_op jit(solution)/shard_map/ppermute | solution.py:66
  38.6 45.4 %collective-permute-start.4 = (bf16[128,3072]{1,0:T(8,128)(2,1)S(1)}, bf16[128,3072]{1,0:T(8,128)(2,1)}, u32[]{:S(2)}, u32[]{:S(2)}) collective-permute-start(bf16[128,3072]{1,0:T(8,128)(2,1)S(1)} %collective-permute-done.2.refs_7_), channel_id=1, source_target_pairs={{2,0},{3,1},{4,2},{5,3},{10,8},{11,9},{12,10},{13,11},{18,16},{19,... | collective-permute-start | bytes 2359304 | tf_op jit(solution)/shard_map/ppermute | solution.py:66
  41.1 69.1 %copy-start.36 = (s32[2,1,8,8]{3,2,1,0:T(8,128)S(1)}, s32[2,1,8,8]{3,2,1,0:T(8,128)}, u32[]{:S(2)}) copy-start(s32[2,1,8,8]{3,2,1,0:T(8,128)} %param.23) | copy-start | bytes 1540
  41.1 67.5 %all-to-all-start = ((bf16[4,128,1152]{2,1,0:T(8,128)(2,1)}), bf16[4,128,1152]{2,1,0:T(8,128)(2,1)}, u32[]{:S(2)}, u32[]{:S(2)}) async-start(bf16[4,128,1152]{2,1,0:T(8,128)(2,1)} %broadcast_in_dim.16), calls=%async_computation | async-start | bytes 2359296 | tf_op jit(solution)/shard_map/all_to_all | solution.py:87
  52.3 2.8 %collective-permute-start.22 = (bf16[128,1024]{1,0:T(8,128)(2,1)S(1)}, bf16[128,1024]{1,0:T(8,128)(2,1)S(1)}, u32[]{:S(2)}, u32[]{:S(2)}) collective-permute-start(bf16[128,1024]{1,0:T(8,128)(2,1)S(1)} %collective-permute-done.15.refs_12_.refs_9_), channel_id=1, source_target_pairs={{0,1},{1,0},{2,3},{3,2},{4,5},{5,4},{6,7},{7,6},{8,9},{9,8},{10,11... | collective-permute-start | bytes 786440 | tf_op jit(solution)/shard_map/ppermute | solution.py:62
  52.4 3.2 %collective-permute-start.18 = (bf16[128,1024]{1,0:T(8,128)(2,1)}, bf16[128,1024]{1,0:T(8,128)(2,1)}, u32[]{:S(2)}, u32[]{:S(2)}) collective-permute-start(bf16[128,1024]{1,0:T(8,128)(2,1)} %collective-permute-done.16.refs_13_.refs_10_), channel_id=1, source_target_pairs={{4,6},{5,7},{12,14},{13,15},{20,22},{21,23},{28,30},{29,31}} | collective-permute-start | bytes 786440 | tf_op jit(solution)/shard_map/ppermute | solution.py:66
  53.7 29.6 %copy-start.14 = (bf16[128,1024]{1,0:T(8,128)(2,1)}, bf16[128,1024]{1,0:T(8,128)(2,1)S(1)}, u32[]{:S(2)}) copy-start(bf16[128,1024]{1,0:T(8,128)(2,1)S(1)} %collective-permute-done.21.refs_18_.refs_15_) | copy-start | bytes 786436
  53.7 29.6 %collective-permute-start.19 = (bf16[128,1024]{1,0:T(8,128)(2,1)}, bf16[128,1024]{1,0:T(8,128)(2,1)S(1)}, u32[]{:S(2)}, u32[]{:S(2)}) collective-permute-start(bf16[128,1024]{1,0:T(8,128)(2,1)} %collective-permute-done.17.refs_14_.refs_11_), channel_id=1, source_target_pairs={{2,0},{3,1},{10,8},{11,9},{18,16},{19,17},{26,24},{27,25}} | collective-permute-start | bytes 786440 | tf_op jit(solution)/shard_map/ppermute | solution.py:66
  55.0 28.3 %copy-start.15 = (bf16[128,1024]{1,0:T(8,128)(2,1)}, bf16[128,1024]{1,0:T(8,128)(2,1)S(1)}, u32[]{:S(2)}) copy-start(bf16[128,1024]{1,0:T(8,128)(2,1)S(1)} %collective-permute-done.22.refs_19_.refs_16_) | copy-start | bytes 786436
  55.1 32.7 %collective-permute-start.5 = (bf16[128,3072]{1,0:T(8,128)(2,1)S(1)}, bf16[128,3072]{1,0:T(8,128)(2,1)S(1)}, u32[]{:S(2)}, u32[]{:S(2)}) collective-permute-start(bf16[128,3072]{1,0:T(8,128)(2,1)S(1)} %bitcast.36), channel_id=1, source_target_pairs={{0,1},{1,0},{2,3},{3,2},{4,5},{5,4},{6,7},{7,6},{8,9},{9,8},{10,11... | collective-permute-start | bytes 2359304 | tf_op jit(solution)/shard_map/ppermute | solution.py:62
  55.6 32.2 %collective-permute-start.6 = (bf16[128,3072]{1,0:T(8,128)(2,1)S(1)}, bf16[128,3072]{1,0:T(8,128)(2,1)S(1)}, u32[]{:S(2)}, u32[]{:S(2)}) collective-permute-start(bf16[128,3072]{1,0:T(8,128)(2,1)S(1)} %collective-permute-done.1.refs_6_), channel_id=1, source_target_pairs={{0,1},{1,0},{2,3},{3,2},{4,5},{5,4},{6,7},{7,6},{8,9},{9,8},{10,11... | collective-permute-start | bytes 2359304 | tf_op jit(solution)/shard_map/ppermute | solution.py:62
  83.3 35.6 %copy-start.16 = (bf16[128,1024]{1,0:T(8,128)(2,1)}, bf16[128,1024]{1,0:T(8,128)(2,1)S(1)}, u32[]{:S(2)}) copy-start(bf16[128,1024]{1,0:T(8,128)(2,1)S(1)} %collective-permute-done.19.refs_16_.refs_13_) | copy-start | bytes 786436
  83.3 2.1 collective-permute-start.23
  83.3 4.9 %collective-permute-start.10 = (bf16[128,3072]{1,0:T(8,128)(2,1)}, bf16[128,3072]{1,0:T(8,128)(2,1)S(1)}, u32[]{:S(2)}, u32[]{:S(2)}) collective-permute-start(bf16[128,3072]{1,0:T(8,128)(2,1)} %collective-permute-done.3.refs_8_), channel_id=1, source_target_pairs={{4,6},{5,7},{12,14},{13,15},{20,22},{21,23},{28,30},{29,31}} | collective-permute-start | bytes 2359304 | tf_op jit(solution)/shard_map/ppermute | solution.py:66
  84.1 24.3 %collective-permute-start.11 = (bf16[128,3072]{1,0:T(8,128)(2,1)}, bf16[128,3072]{1,0:T(8,128)(2,1)S(1)}, u32[]{:S(2)}, u32[]{:S(2)}) collective-permute-start(bf16[128,3072]{1,0:T(8,128)(2,1)} %collective-permute-done.4.refs_9_), channel_id=1, source_target_pairs={{2,0},{3,1},{10,8},{11,9},{18,16},{19,17},{26,24},{27,25}} | collective-permute-start | bytes 2359304 | tf_op jit(solution)/shard_map/ppermute | solution.py:66
  85.4 23.0 %copy-start.17 = (bf16[128,1024]{1,0:T(8,128)(2,1)}, bf16[128,1024]{1,0:T(8,128)(2,1)S(1)}, u32[]{:S(2)}) copy-start(bf16[128,1024]{1,0:T(8,128)(2,1)S(1)} %collective-permute-done.23.refs_20_.refs_17_) | copy-start | bytes 786436
  85.4 1.9 collective-permute-start.24
  87.3 21.0 %copy-start.18 = (bf16[128,1024]{1,0:T(8,128)(2,1)}, bf16[128,1024]{1,0:T(8,128)(2,1)S(1)}, u32[]{:S(2)}) copy-start(bf16[128,1024]{1,0:T(8,128)(2,1)S(1)} %collective-permute-done.24.refs_21_.refs_18_) | copy-start | bytes 786436
  87.3 21.2 %collective-permute-start.7 = (bf16[128,3072]{1,0:T(8,128)(2,1)}, bf16[128,3072]{1,0:T(8,128)(2,1)}, u32[]{:S(2)}, u32[]{:S(2)}) collective-permute-start(bf16[128,3072]{1,0:T(8,128)(2,1)} %copy-done.8), channel_id=1, source_target_pairs={{0,1},{1,0},{2,3},{3,2},{4,5},{5,4},{6,7},{7,6},{8,9},{9,8},{10,11... | collective-permute-start | bytes 2359304 | tf_op jit(solution)/shard_map/ppermute | solution.py:62
  87.7 20.7 %copy-start.9 = (bf16[128,3072]{1,0:T(8,128)(2,1)}, bf16[128,3072]{1,0:T(8,128)(2,1)S(1)}, u32[]{:S(2)}) copy-start(bf16[128,3072]{1,0:T(8,128)(2,1)S(1)} %collective-permute-done.5.refs_10_.refs_12_) | copy-start | bytes 2359300
  87.7 21.3 %collective-permute-start.8 = (bf16[128,3072]{1,0:T(8,128)(2,1)}, bf16[128,3072]{1,0:T(8,128)(2,1)}, u32[]{:S(2)}, u32[]{:S(2)}) collective-permute-start(bf16[128,3072]{1,0:T(8,128)(2,1)} %collective-permute-done.3.refs_8_), channel_id=1, source_target_pairs={{0,1},{1,0},{2,3},{3,2},{4,5},{5,4},{6,7},{7,6},{8,9},{9,8},{10,11... | collective-permute-start | bytes 2359304 | tf_op jit(solution)/shard_map/ppermute | solution.py:62
  87.9 21.3 %collective-permute-start.9 = (bf16[128,3072]{1,0:T(8,128)(2,1)}, bf16[128,3072]{1,0:T(8,128)(2,1)}, u32[]{:S(2)}, u32[]{:S(2)}) collective-permute-start(bf16[128,3072]{1,0:T(8,128)(2,1)} %collective-permute-done.4.refs_9_), channel_id=1, source_target_pairs={{0,1},{1,0},{2,3},{3,2},{4,5},{5,4},{6,7},{7,6},{8,9},{9,8},{10,11... | collective-permute-start | bytes 2359304 | tf_op jit(solution)/shard_map/ppermute | solution.py:62
  88.2 30.6 %copy-start = (bf16[128,3072]{1,0:T(8,128)(2,1)}, bf16[128,3072]{1,0:T(8,128)(2,1)S(1)}, u32[]{:S(2)}) copy-start(bf16[128,3072]{1,0:T(8,128)(2,1)S(1)} %collective-permute-done.10.refs_6_.refs_10_) | copy-start | bytes 2359300
  88.2 30.6 %collective-permute-start.12 = (bf16[128,3072]{1,0:T(8,128)(2,1)S(1)}, bf16[128,3072]{1,0:T(8,128)(2,1)S(1)}, u32[]{:S(2)}, u32[]{:S(2)}) collective-permute-start(bf16[128,3072]{1,0:T(8,128)(2,1)S(1)} %collective-permute-done.10.refs_6_.refs_10_), channel_id=1, source_target_pairs={{0,1},{1,0},{2,3},{3,2},{4,5},{5,4},{6,7},{7,6},{8,9},{9,8},{10,11... | collective-permute-start | bytes 2359304 | tf_op jit(solution)/shard_map/ppermute | solution.py:62
  108.4 10.5 %collective-permute-start.13 = (bf16[128,3072]{1,0:T(8,128)(2,1)S(1)}, bf16[128,3072]{1,0:T(8,128)(2,1)S(1)}, u32[]{:S(2)}, u32[]{:S(2)}) collective-permute-start(bf16[128,3072]{1,0:T(8,128)(2,1)S(1)} %collective-permute-done.11.refs_7_.refs_11_), channel_id=1, source_target_pairs={{0,1},{1,0},{2,3},{3,2},{4,5},{5,4},{6,7},{7,6},{8,9},{9,8},{10,11... | collective-permute-start | bytes 2359304 | tf_op jit(solution)/shard_map/ppermute | solution.py:62
  108.5 55.7 %collective-permute-start.28 = (bf16[4,128,1152]{2,1,0:T(8,128)(2,1)}, bf16[4,128,1152]{2,1,0:T(8,128)(2,1)}, u32[]{:S(2)}, u32[]{:S(2)}) collective-permute-start(bf16[4,128,1152]{2,1,0:T(8,128)(2,1)} %all-to-all-done.refs_2_), channel_id=1, source_target_pairs={{0,1},{1,0},{2,3},{3,2},{4,5},{5,4},{6,7},{7,6},{8,9},{9,8},{10,11... | collective-permute-start | bytes 3538952 | tf_op jit(solution)/shard_map/ppermute | solution.py:62
  109.1 9.8 %collective-permute-start.25 = (bf16[128,1024]{1,0:T(8,128)(2,1)}, bf16[128,1024]{1,0:T(8,128)(2,1)}, u32[]{:S(2)}, u32[]{:S(2)}) collective-permute-start(bf16[128,1024]{1,0:T(8,128)(2,1)} %collective-permute-done.18.refs_15_.refs_12_), channel_id=1, source_target_pairs={{0,1},{1,0},{2,3},{3,2},{4,5},{5,4},{6,7},{7,6},{8,9},{9,8},{10,11... | collective-permute-start | bytes 786440 | tf_op jit(solution)/shard_map/ppermute | solution.py:62
  109.2 9.7 %collective-permute-start.26 = (bf16[128,1024]{1,0:T(8,128)(2,1)S(1)}, bf16[128,1024]{1,0:T(8,128)(2,1)}, u32[]{:S(2)}, u32[]{:S(2)}) collective-permute-start(bf16[128,1024]{1,0:T(8,128)(2,1)S(1)} %collective-permute-done.19.refs_16_.refs_13_), channel_id=1, source_target_pairs={{0,1},{1,0},{2,3},{3,2},{4,5},{5,4},{6,7},{7,6},{8,9},{9,8},{10,11... | collective-permute-start | bytes 786440 | tf_op jit(solution)/shard_map/ppermute | solution.py:62
  127.7 14.3 %collective-permute-start.31 = (bf16[128,1024]{1,0:T(8,128)(2,1)}, bf16[128,1024]{1,0:T(8,128)(2,1)S(1)}, u32[]{:S(2)}, u32[]{:S(2)}) collective-permute-start(bf16[128,1024]{1,0:T(8,128)(2,1)} %get-tuple-element.33.refs_3_), channel_id=1, source_target_pairs={{0,2},{1,3},{2,4},{3,5},{4,6},{5,7},{8,10},{9,11},{10,12},{11,13},... | collective-permute-start | bytes 786440 | tf_op jit(solution)/shard_map/ppermute | solution.py:66
  129.0 13.7 %collective-permute-start.32 = (bf16[128,1024]{1,0:T(8,128)(2,1)}, bf16[128,1024]{1,0:T(8,128)(2,1)S(1)}, u32[]{:S(2)}, u32[]{:S(2)}) collective-permute-start(bf16[128,1024]{1,0:T(8,128)(2,1)} %get-tuple-element.33.refs_3_), channel_id=1, source_target_pairs={{2,0},{3,1},{4,2},{5,3},{6,4},{7,5},{10,8},{11,9},{12,10},{13,11},... | collective-permute-start | bytes 786440 | tf_op jit(solution)/shard_map/ppermute | solution.py:66
  138.3 61.3 %all-to-all-start.1 = ((bf16[4,128,1024]{2,1,0:T(8,128)(2,1)}), bf16[4,128,1024]{2,1,0:T(8,128)(2,1)S(1)}, u32[]{:S(2)}, u32[]{:S(2)}) async-start(bf16[4,128,1024]{2,1,0:T(8,128)(2,1)} %get-tuple-element.25), calls=%async_computation.1 | async-start | bytes 2097152 | tf_op jit(solution)/shard_map/all_to_all | solution.py:87
  142.0 46.1 %copy-start.23 = (bf16[128,1024]{1,0:T(8,128)(2,1)}, bf16[128,1024]{1,0:T(8,128)(2,1)S(1)}, u32[]{:S(2)}) copy-start(bf16[128,1024]{1,0:T(8,128)(2,1)S(1)} %collective-permute-done.31.refs_4_) | copy-start | bytes 786436
  142.0 2.6 collective-permute-start.33
  142.7 45.4 %copy-start.24 = (bf16[128,1024]{1,0:T(8,128)(2,1)}, bf16[128,1024]{1,0:T(8,128)(2,1)S(1)}, u32[]{:S(2)}) copy-start(bf16[128,1024]{1,0:T(8,128)(2,1)S(1)} %collective-permute-done.32.refs_5_) | copy-start | bytes 786436
  142.7 20.1 %collective-permute-start.34 = (bf16[128,1024]{1,0:T(8,128)(2,1)S(1)}, bf16[128,1024]{1,0:T(8,128)(2,1)S(1)}, u32[]{:S(2)}, u32[]{:S(2)}) collective-permute-start(bf16[128,1024]{1,0:T(8,128)(2,1)S(1)} %collective-permute-done.32.refs_5_), channel_id=1, source_target_pairs={{2,0},{3,1},{4,2},{5,3},{10,8},{11,9},{12,10},{13,11},{18,16},{19,... | collective-permute-start | bytes 786440 | tf_op jit(solution)/shard_map/ppermute | solution.py:66
  144.0 20.3 %collective-permute-start.37 = (bf16[128,1024]{1,0:T(8,128)(2,1)S(1)}, bf16[128,1024]{1,0:T(8,128)(2,1)S(1)}, u32[]{:S(2)}, u32[]{:S(2)}) collective-permute-start(bf16[128,1024]{1,0:T(8,128)(2,1)S(1)} %copy-done.22), channel_id=1, source_target_pairs={{0,1},{1,0},{2,3},{3,2},{4,5},{5,4},{6,7},{7,6},{8,9},{9,8},{10,11... | collective-permute-start | bytes 786440 | tf_op jit(solution)/shard_map/ppermute | solution.py:62
  144.2 20.6 %collective-permute-start.38 = (bf16[128,1024]{1,0:T(8,128)(2,1)S(1)}, bf16[128,1024]{1,0:T(8,128)(2,1)S(1)}, u32[]{:S(2)}, u32[]{:S(2)}) collective-permute-start(bf16[128,1024]{1,0:T(8,128)(2,1)S(1)} %collective-permute-done.31.refs_4_), channel_id=1, source_target_pairs={{0,1},{1,0},{2,3},{3,2},{4,5},{5,4},{6,7},{7,6},{8,9},{9,8},{10,11... | collective-permute-start | bytes 786440 | tf_op jit(solution)/shard_map/ppermute | solution.py:62
  144.6 43.5 %copy-start.25 = (bf16[128,1024]{1,0:T(8,128)(2,1)}, bf16[128,1024]{1,0:T(8,128)(2,1)S(1)}, u32[]{:S(2)}) copy-start(bf16[128,1024]{1,0:T(8,128)(2,1)S(1)} %collective-permute-done.33.refs_6_) | copy-start | bytes 786436
  144.6 20.3 %collective-permute-start.35 = (bf16[128,1024]{1,0:T(8,128)(2,1)S(1)}, bf16[128,1024]{1,0:T(8,128)(2,1)S(1)}, u32[]{:S(2)}, u32[]{:S(2)}) collective-permute-start(bf16[128,1024]{1,0:T(8,128)(2,1)S(1)} %collective-permute-done.33.refs_6_), channel_id=1, source_target_pairs={{4,6},{5,7},{12,14},{13,15},{20,22},{21,23},{28,30},{29,31}} | collective-permute-start | bytes 786440 | tf_op jit(solution)/shard_map/ppermute | solution.py:66
  162.8 25.4 %copy-start.26 = (bf16[128,1024]{1,0:T(8,128)(2,1)}, bf16[128,1024]{1,0:T(8,128)(2,1)S(1)}, u32[]{:S(2)}) copy-start(bf16[128,1024]{1,0:T(8,128)(2,1)S(1)} %collective-permute-done.34.refs_7_) | copy-start | bytes 786436
  162.8 18.7 %collective-permute-start.36 = (bf16[128,1024]{1,0:T(8,128)(2,1)S(1)}, bf16[128,1024]{1,0:T(8,128)(2,1)S(1)}, u32[]{:S(2)}, u32[]{:S(2)}) collective-permute-start(bf16[128,1024]{1,0:T(8,128)(2,1)S(1)} %collective-permute-done.34.refs_7_), channel_id=1, source_target_pairs={{2,0},{3,1},{10,8},{11,9},{18,16},{19,17},{26,24},{27,25}} | collective-permute-start | bytes 786440 | tf_op jit(solution)/shard_map/ppermute | solution.py:66
  164.3 23.9 %collective-permute-start.39 = (bf16[128,1024]{1,0:T(8,128)(2,1)S(1)}, bf16[128,1024]{1,0:T(8,128)(2,1)S(1)}, u32[]{:S(2)}, u32[]{:S(2)}) collective-permute-start(bf16[128,1024]{1,0:T(8,128)(2,1)S(1)} %collective-permute-done.32.refs_5_), channel_id=1, source_target_pairs={{0,1},{1,0},{2,3},{3,2},{4,5},{5,4},{6,7},{7,6},{8,9},{9,8},{10,11... | collective-permute-start | bytes 786440 | tf_op jit(solution)/shard_map/ppermute | solution.py:62
  164.3 23.8 %copy-start.27 = (bf16[128,1024]{1,0:T(8,128)(2,1)}, bf16[128,1024]{1,0:T(8,128)(2,1)S(1)}, u32[]{:S(2)}) copy-start(bf16[128,1024]{1,0:T(8,128)(2,1)S(1)} %collective-permute-done.37.refs_10_) | copy-start | bytes 786436
  164.4 23.9 %collective-permute-start.40 = (bf16[128,1024]{1,0:T(8,128)(2,1)S(1)}, bf16[128,1024]{1,0:T(8,128)(2,1)S(1)}, u32[]{:S(2)}, u32[]{:S(2)}) collective-permute-start(bf16[128,1024]{1,0:T(8,128)(2,1)S(1)} %collective-permute-done.33.refs_6_), channel_id=1, source_target_pairs={{0,1},{1,0},{2,3},{3,2},{4,5},{5,4},{6,7},{7,6},{8,9},{9,8},{10,11... | collective-permute-start | bytes 786440 | tf_op jit(solution)/shard_map/ppermute | solution.py:62
  164.8 23.3 %copy-start.28 = (bf16[128,1024]{1,0:T(8,128)(2,1)}, bf16[128,1024]{1,0:T(8,128)(2,1)S(1)}, u32[]{:S(2)}) copy-start(bf16[128,1024]{1,0:T(8,128)(2,1)S(1)} %collective-permute-done.38.refs_11_) | copy-start | bytes 786436
  164.8 23.4 %collective-permute-start.41 = (bf16[128,1024]{1,0:T(8,128)(2,1)S(1)}, bf16[128,1024]{1,0:T(8,128)(2,1)S(1)}, u32[]{:S(2)}, u32[]{:S(2)}) collective-permute-start(bf16[128,1024]{1,0:T(8,128)(2,1)S(1)} %collective-permute-done.34.refs_7_), channel_id=1, source_target_pairs={{0,1},{1,0},{2,3},{3,2},{4,5},{5,4},{6,7},{7,6},{8,9},{9,8},{10,11... | collective-permute-start | bytes 786440 | tf_op jit(solution)/shard_map/ppermute | solution.py:62
  164.9 23.2 %copy-start.29 = (bf16[128,1024]{1,0:T(8,128)(2,1)}, bf16[128,1024]{1,0:T(8,128)(2,1)S(1)}, u32[]{:S(2)}) copy-start(bf16[128,1024]{1,0:T(8,128)(2,1)S(1)} %collective-permute-done.35.refs_8_) | copy-start | bytes 786436
  164.9 23.3 %collective-permute-start.42 = (bf16[128,1024]{1,0:T(8,128)(2,1)S(1)}, bf16[128,1024]{1,0:T(8,128)(2,1)S(1)}, u32[]{:S(2)}, u32[]{:S(2)}) collective-permute-start(bf16[128,1024]{1,0:T(8,128)(2,1)S(1)} %collective-permute-done.35.refs_8_), channel_id=1, source_target_pairs={{0,1},{1,0},{2,3},{3,2},{4,5},{5,4},{6,7},{7,6},{8,9},{9,8},{10,11... | collective-permute-start | bytes 786440 | tf_op jit(solution)/shard_map/ppermute | solution.py:62
  181.4 6.8 %collective-permute-start.43 = (bf16[128,1024]{1,0:T(8,128)(2,1)S(1)}, bf16[128,1024]{1,0:T(8,128)(2,1)S(1)}, u32[]{:S(2)}, u32[]{:S(2)}) collective-permute-start(bf16[128,1024]{1,0:T(8,128)(2,1)S(1)} %collective-permute-done.36.refs_9_), channel_id=1, source_target_pairs={{0,1},{1,0},{2,3},{3,2},{4,5},{5,4},{6,7},{7,6},{8,9},{9,8},{10,11... | collective-permute-start | bytes 786440 | tf_op jit(solution)/shard_map/ppermute | solution.py:62
  199.2 3.0 %collective-permute-start.44 = (bf16[4,128,1024]{2,1,0:T(8,128)(2,1)}, bf16[4,128,1024]{2,1,0:T(8,128)(2,1)S(1)}, u32[]{:S(2)}, u32[]{:S(2)}) collective-permute-start(bf16[4,128,1024]{2,1,0:T(8,128)(2,1)} %get-tuple-element.35), channel_id=1, source_target_pairs={{0,1},{1,0},{2,3},{3,2},{4,5},{5,4},{6,7},{7,6},{8,9},{9,8},{10,11... | collective-permute-start | bytes 3145736 | tf_op jit(solution)/shard_map/ppermute | solution.py:62
  199.7 8.6 %collective-permute-start.29 = (bf16[4,128,1024]{2,1,0:T(8,128)(2,1)S(1)}, bf16[4,128,1024]{2,1,0:T(8,128)(2,1)S(1)}, u32[]{:S(2)}, u32[]{:S(2)}) collective-permute-start(bf16[4,128,1024]{2,1,0:T(8,128)(2,1)S(1)} %all-to-all-done.1.refs_4_), channel_id=1, source_target_pairs={{0,1},{1,0},{2,3},{3,2},{4,5},{5,4},{6,7},{7,6},{8,9},{9,8},{10,11... | collective-permute-start | bytes 3145736 | tf_op jit(solution)/shard_map/ppermute | solution.py:62
  204.8 30.0 %all-to-all-start.3 = ((bf16[4,128,1024]{2,1,0:T(8,128)(2,1)}), bf16[4,128,1024]{2,1,0:T(8,128)(2,1)S(1)}, u32[]{:S(2)}, u32[]{:S(2)}) async-start(bf16[4,128,1024]{2,1,0:T(8,128)(2,1)} %add.28), calls=%async_computation.3 | async-start | bytes 2097152 | tf_op jit(solution)/shard_map/all_to_all | solution.py:87
  218.1 2.9 %collective-permute-start.30 = (bf16[4,128,1024]{2,1,0:T(8,128)(2,1)}, bf16[4,128,1024]{2,1,0:T(8,128)(2,1)S(1)}, u32[]{:S(2)}, u32[]{:S(2)}) collective-permute-start(bf16[4,128,1024]{2,1,0:T(8,128)(2,1)} %get-tuple-element.27), channel_id=1, source_target_pairs={{0,1},{1,0},{2,3},{3,2},{4,5},{5,4},{6,7},{7,6},{8,9},{9,8},{10,11... | collective-permute-start | bytes 3145736 | tf_op jit(solution)/shard_map/ppermute | solution.py:62
  234.8 29.2 %all-to-all-start.2 = ((bf16[4,128,1024]{2,1,0:T(8,128)(2,1)}), bf16[4,128,1024]{2,1,0:T(8,128)(2,1)S(1)}, u32[]{:S(2)}, u32[]{:S(2)}) async-start(bf16[4,128,1024]{2,1,0:T(8,128)(2,1)} %add.26), calls=%async_computation.2 | async-start | bytes 2097152 | tf_op jit(solution)/shard_map/all_to_all | solution.py:87
  (22 other events, 150.0 us)

commit v8 on v7

--- a/solution.py
+++ b/solution.py
@@ -306,13 +306,12 @@
             out_ref[owner] = result[pl.ds(start, rows), :]
 
 
-def expert_backward_kernel(count, rows, *refs):
+def expert_backward_kernel(rows, *refs):
     place, up_ref, act_ref = refs[:3]
-    row_refs = refs[3 : 3 + count]
-    mine_ref, other_ref, tokens, result, sems = refs[3 + count :]
+    row_refs = refs[3:5]
+    mine_ref, other_ref, tokens, result, sems = refs[5:]
     chip, core = place[0], place[1]
-    start_copies(row_refs, tokens, sems, rows, chip, core)
-    wait_copies(row_refs, tokens, sems, rows, chip, core)
+    fetch_line(row_refs, tokens, sems, rows, chip, core)
     chunk = 2 * rows
 
     def step(index, carry):
@@ -508,13 +507,13 @@
         [place, arriving, stashed_input, attention_gain, mask] + early_mix,
     )
 
-    def attended(micro, x, sums, normed, block):
+    def attended(micro, x, sums, normed):
         return call(
             functools.partial(project_kernel, count, depth, length, micro),
             (
                 shaped((tokens, columns), F32),
                 shaped((tokens, width), F32),
-                shaped(block, BF16),
+                shaped((length, tokens, width), BF16),
             ),
             [SMEM] + [VMEM] * 5 + [ANY] * (4 + count),
             (VMEM,) * 3,
@@ -528,12 +527,10 @@
             [place, x, sums, normed, expert_gain, mask] + last_mix + outers,
         )
 
-    proj_bwd, hidden_bwd, expert_bwd = attended(
-        1, stashed_input, sum_bwd, normed_bwd, (tokens, width)
-    )
-    rows_bwd = with_partner(relayed(expert_bwd))
-
-    _, hidden_fwd, expert_fwd = attended(0, arriving, sum_fwd, normed_fwd, (length, tokens, width))
+    proj_bwd, hidden_bwd, expert_bwd = attended(1, stashed_input, sum_bwd, normed_bwd)
+    rows_bwd = spread(expert_bwd)
+
+    _, hidden_fwd, expert_fwd = attended(0, arriving, sum_fwd, normed_fwd)
     rows_fwd = spread(expert_fwd)
 
     grad_act, gate_fwd = call(
@@ -551,11 +548,11 @@
         return [pltpu.VMEM((total, width), BF16), pltpu.VMEM((total, width), BF16), dma(sems)]
 
     mine, other = call(
-        functools.partial(expert_backward_kernel, count, tokens),
+        functools.partial(expert_backward_kernel, tokens),
         pair,
-        [SMEM, VMEM, VMEM] + [ANY] * count,
+        [SMEM, VMEM, VMEM] + [ANY] * 2,
         (VMEM,) * 2,
-        expert_scratch(expert_count),
+        expert_scratch((CORES, length)),
         [place, up_weight, grad_act] + rows_bwd,
     )
     grad_parts = across(mine + swapped(other))

time: 266 us -> 275 us (1.034)
  waiting for transfers between devices: 125 us -> 146 us
  starting transfers between devices: 61.1 us -> 47.9 us
    all_to_all x4 -> x5, waiting for transfers between devices: 21.2 us -> 61.6 us  [across(): lax.all_to_all(blocks, 'expert', split_axis=0, concat_axis=0, axis_index_...]
    ppermute x18 -> x12, waiting for transfers between devices: 89.7 us -> 78.3 us  [hop(): return lax.ppermute(value, 'expert', chip_pairs(sources, move))]
    ppermute x18 -> x12, starting transfers between devices: 28.9 us -> 21 us  [hop(): return lax.ppermute(value, 'expert', chip_pairs(sources, move))]
    ppermute x2, waiting for transfers between devices: 7.6 us -> 1.52 us  [passed_along(): return lax.ppermute(value, 'section', pairs)]
    all_to_all x4 -> x5, starting transfers between devices: 22.1 us -> 18.8 us  [across(): lax.all_to_all(blocks, 'expert', split_axis=0, concat_axis=0, axis_index_...]
    ppermute x25 -> x19, waiting for transfers between devices: 6.31 us -> 4.31 us  [swapped(): return lax.ppermute(value, 'expert', [(i, i ^ 1) for i in range(count)])]
    ppermute x25 -> x19, starting transfers between devices: 6.11 us -> 4.16 us  [swapped(): return lax.ppermute(value, 'expert', [(i, i ^ 1) for i in range(count)])]
  transfers between devices with their start and end apart: 49 -> 38, of which waited for: 13 -> 12; matrix products, arithmetic and copies ran while one was open for 4% -> 4% of each run, Pallas kernels for 24% -> 18%
where the time goes in v8:
time: 275 us; the launch traced here: 274 us
  waiting for transfers between devices  146 us (53%)
  Pallas kernels  64 us (23%)
  starting transfers between devices  47.9 us (17%)
  other arithmetic  8.68 us (3%)
  local copies, waits for them, and re-layouts  5.51 us (2%)
    ppermute x12, waiting for transfers between devices, hop(): return lax.ppermute(value, 'expert', chip_pairs(sources, move))  78.3 us
    pallas_call x8, Pallas kernels, call(): pl.pallas_call(kernel, out_shape=outs, in_specs=specs, out_specs=out_spec...  64 us
    all_to_all x5, waiting for transfers between devices, across(): lax.all_to_all(blocks, 'expert', split_axis=0, concat_axis=0, axis_index_...  61.6 us
    ppermute x12, starting transfers between devices, hop(): return lax.ppermute(value, 'expert', chip_pairs(sources, move))  21 us
    all_to_all x5, starting transfers between devices, across(): lax.all_to_all(blocks, 'expert', split_axis=0, concat_axis=0, axis_index_...  18.8 us
  transfers between devices with their start and end apart: 38, of which 12 were waited for; matrix products, arithmetic and copies ran while one was open for 4% of the time, Pallas kernels for 18%

profile of v8, /device:TPU:0, one launch (start us, length us, event | category | flops | bytes accessed | tf_op | source)
XLA Modules:
  0.0 274.2 jit_solution(12703766684394100148)
XLA Ops:
  0.6 5.0 %collective-permute-start.1 = (bf16[128,3072]{1,0:T(8,128)(2,1)}, bf16[128,3072]{1,0:T(8,128)(2,1)S(1)}, u32[]{:S(2)}, u32[]{:S(2)}) collective-permute-start(bf16[128,3072]{1,0:T(8,128)(2,1)} %bitcast.32), channel_id=1, source_target_pairs={{0,2},{1,3},{2,4},{3,5},{4,6},{5,7},{8,10},{9,11},{10,12},{11,13},... | collective-permute-start | bytes 2359304 | tf_op jit(solution)/shard_map/ppermute | solution.py:66
  5.6 1.3 collective-permute-start.2
  6.9 1.5 collective-permute-start
  8.5 4.6 %collective-permute-start.14 = (bf16[128,1024]{1,0:T(8,128)(2,1)}, bf16[128,1024]{1,0:T(8,128)(2,1)S(1)}, u32[]{:S(2)}, u32[]{:S(2)}) collective-permute-start(bf16[128,1024]{1,0:T(8,128)(2,1)} %bitcast.37), channel_id=1, source_target_pairs={{0,2},{1,3},{2,4},{3,5},{4,6},{5,7},{8,10},{9,11},{10,12},{11,13},... | collective-permute-start | bytes 786440 | tf_op jit(solution)/shard_map/ppermute | solution.py:66
  13.1 1.3 collective-permute-start.15
  14.4 1.5 collective-permute-done.refs_1_
  15.9 12.4 %collective-permute-done.14.refs_11_.refs_8_ = bf16[128,1024]{1,0:T(8,128)(2,1)S(1)} collective-permute-done((bf16[128,1024]{1,0:T(8,128)(2,1)}, bf16[128,1024]{1,0:T(8,128)(2,1)S(1)}, u32[]{:S(2)}, u32[]{:S(2)}) %collective-permute-start.14) | collective-permute-done | bytes 262176 | tf_op jit(solution)/shard_map/ppermute | solution.py:66
  28.3 2.4 collective-permute-start.27
  30.8 1.6 collective-permute-done.15.refs_12_.refs_9_
  32.4 0.7 collective-permute-start.16
  33.1 0.7 add_divide_fusion
  33.8 1.6 collective-permute-start.3
  35.4 1.3 collective-permute-start.4
  36.7 0.7 select_reduce_fusion
  37.5 1.3 collective-permute-start.17
  38.8 0.5 collective-permute-start.22
  39.5 26.0 %collective-permute-done.17.refs_14_.refs_11_ = bf16[128,1024]{1,0:T(8,128)(2,1)} collective-permute-done((bf16[128,1024]{1,0:T(8,128)(2,1)S(1)}, bf16[128,1024]{1,0:T(8,128)(2,1)}, u32[]{:S(2)}, u32[]{:S(2)}) %collective-permute-start.17) | collective-permute-done | bytes 262176 | tf_op jit(solution)/shard_map/ppermute | solution.py:66
  65.5 0.7 collective-permute-start.18
  66.2 0.6 collective-permute-start.6
  66.7 1.1 broadcast_in_dim.16
  67.9 4.3 %all-to-all-start = ((bf16[4,128,1152]{2,1,0:T(8,128)(2,1)}), bf16[4,128,1152]{2,1,0:T(8,128)(2,1)}, u32[]{:S(2)}, u32[]{:S(2)}) async-start(bf16[4,128,1152]{2,1,0:T(8,128)(2,1)} %broadcast_in_dim.16), calls=%async_computation | async-start | bytes 2359296 | tf_op jit(solution)/shard_map/all_to_all | solution.py:87
  72.2 1.3 collective-permute-start.19
  73.5 0.7 collective-permute-start.10
  74.2 1.3 collective-permute-start.11
  75.5 19.7 %collective-permute-done.19.refs_16_.refs_13_ = bf16[128,1024]{1,0:T(8,128)(2,1)S(1)} collective-permute-done((bf16[128,1024]{1,0:T(8,128)(2,1)}, bf16[128,1024]{1,0:T(8,128)(2,1)S(1)}, u32[]{:S(2)}, u32[]{:S(2)}) %collective-permute-start.19) | collective-permute-done | bytes 262176 | tf_op jit(solution)/shard_map/ppermute | solution.py:66
  95.2 1.5 collective-permute-done.23.refs_20_.refs_17_
  96.9 0.4 collective-permute-start.8
  97.3 0.1 collective-permute-start.9
  97.4 0.4 collective-permute-start.12
  97.8 18.6 %collective-permute-done.11.refs_7_.refs_11_ = bf16[128,3072]{1,0:T(8,128)(2,1)S(1)} collective-permute-done((bf16[128,3072]{1,0:T(8,128)(2,1)}, bf16[128,3072]{1,0:T(8,128)(2,1)S(1)}, u32[]{:S(2)}, u32[]{:S(2)}) %collective-permute-start.11) | collective-permute-done | bytes 786464 | tf_op jit(solution)/shard_map/ppermute | solution.py:66
  116.5 0.5 collective-permute-start.24
  117.1 0.4 collective-permute-start.26
  117.5 0.7 pad_add_fusion.refs_0_
  118.2 1.1 fusion.refs_4_
  119.2 7.5 %shard_map.131 = (f32[128,3072]{1,0:T(8,128)}, f32[128,3072]{1,0:T(8,128)}, bf16[128,1024]{1,0:T(8,128)(2,1)}, bf16[128,1024]{1,0:T(8,128)(2,1)}, f32[2,128,128]{2,1,0:T(8,128)}) custom-call(s32[2]{0:T(128)} %pad_add_fusion.refs_0_, bf16[128,1024]{1,0:T(8,128)(2,1)} %copy-done.20, bf16[128,1024]{1,0:T(8,128)(2,1)} %refs_1_.3, f32[1,1024]{1,0:T(1,128)} %refs_4_.7, ...), custom_call_target="tpu_custom_call" | custom-call | tf_op jit(solution)/shard_map/pallas_call | solution.py:419
  126.9 0.6 copy-done.18
  127.5 0.3 copy-done.2
  127.8 0.3 copy-done.3
  128.0 7.9 %shard_map.132 = (f32[128,3072]{1,0:T(8,128)}, f32[128,1024]{1,0:T(8,128)}, bf16[4,128,1024]{2,1,0:T(8,128)(2,1)}) custom-call(s32[2]{0:T(128)} %pad_add_fusion.refs_0_, bf16[128,1024]{1,0:T(8,128)(2,1)} %copy-done.20, f32[128,3072]{1,0:T(8,128)} %get-tuple-element.20.refs_2_, bf16[128,1024]{1,0:T(8,128)(2,1)} %get-tuple-element.21.refs_3_, ...), custom_call_target="tpu_custom_call" | custom-call | tf_op jit(solution)/shard_map/pallas_call | solution.py:419
  136.0 3.5 %all-to-all-start.1 = ((bf16[4,128,1024]{2,1,0:T(8,128)(2,1)}), bf16[4,128,1024]{2,1,0:T(8,128)(2,1)S(1)}, u32[]{:S(2)}, u32[]{:S(2)}) async-start(bf16[4,128,1024]{2,1,0:T(8,128)(2,1)} %get-tuple-element.25), calls=%async_computation.1 | async-start | bytes 2097152 | tf_op jit(solution)/shard_map/all_to_all | solution.py:87
  139.5 0.1 collective-permute-start.28
  139.6 8.0 %shard_map.135 = (f32[128,3072]{1,0:T(8,128)}, f32[128,1024]{1,0:T(8,128)}, bf16[4,128,1024]{2,1,0:T(8,128)(2,1)}) custom-call(s32[2]{0:T(128)} %pad_add_fusion.refs_0_, bf16[128,1024]{1,0:T(8,128)(2,1)} %refs_1_.3, f32[128,3072]{1,0:T(8,128)} %get-tuple-element.28.refs_2_, bf16[128,1024]{1,0:T(8,128)(2,1)} %get-tuple-element.29.refs_3_, f32[1,1024]{1,0:T(1,128)} %refs_4_.6, ...), custom_call_target="tpu_custom_call" | custom-call | tf_op jit(solution)/shard_map/pallas_call | solution.py:419
  147.6 18.1 %all-to-all-done.1.refs_4_ = bf16[4,128,1024]{2,1,0:T(8,128)(2,1)S(1)} async-done(((bf16[4,128,1024]{2,1,0:T(8,128)(2,1)}), bf16[4,128,1024]{2,1,0:T(8,128)(2,1)S(1)}, u32[]{:S(2)}, u32[]{:S(2)}) %all-to-all-start.1) | async-done | bytes 1048608 | tf_op jit(solution)/shard_map/all_to_all | solution.py:87
  165.7 3.7 %all-to-all-start.3 = ((bf16[4,128,1024]{2,1,0:T(8,128)(2,1)}), bf16[4,128,1024]{2,1,0:T(8,128)(2,1)S(1)}, u32[]{:S(2)}, u32[]{:S(2)}) async-start(bf16[4,128,1024]{2,1,0:T(8,128)(2,1)} %get-tuple-element.33), calls=%async_computation.3 | async-start | bytes 2097152 | tf_op jit(solution)/shard_map/all_to_all | solution.py:87
  169.4 1.0 copy-done.19
  170.4 6.6 %shard_map.133 = (f32[1024,704]{1,0:T(8,128)}, f32[1024,128]{1,0:T(8,128)}) custom-call(s32[2]{0:T(128)} %pad_add_fusion.refs_0_, bf16[704,1024]{1,0:T(8,128)(2,1)} %bitcast.28, bf16[4,128,1152]{2,1,0:T(8,128)(2,1)} %all-to-all-done.refs_2_, bf16[4,128,1152]{2,1,0:T(8,128)(2,1)} %copy-done.19), custom_call_target="tpu_custom_call" | custom-call | tf_op jit(solution)/shard_map/pallas_call | solution.py:419
  177.0 8.8 %shard_map.134 = (bf16[4,128,1024]{2,1,0:T(8,128)(2,1)}, bf16[4,128,1024]{2,1,0:T(8,128)(2,1)}) custom-call(s32[2]{0:T(128)} %pad_add_fusion.refs_0_, bf16[704,1024]{1,0:T(8,128)(2,1)} %bitcast.30, bf16[704,1024]{1,0:T(8,128)(2,1)} %bitcast.29, f32[1024,128]{1,0:T(8,128)} %get-tuple-element.24.refs_3_, bf16[4,128,1024]{2,1,0:T(8,128)(2,1)} %copy-done.6, ...), custom_call_target="tpu_custom_call" | custom-call | tf_op jit(solution)/shard_map/pallas_call | solution.py:419
  185.8 0.6 collective-permute-start.30
  186.4 9.5 %all-to-all-done.3.refs_3_ = bf16[4,128,1024]{2,1,0:T(8,128)(2,1)S(1)} async-done(((bf16[4,128,1024]{2,1,0:T(8,128)(2,1)}), bf16[4,128,1024]{2,1,0:T(8,128)(2,1)S(1)}, u32[]{:S(2)}, u32[]{:S(2)}) %all-to-all-start.3) | async-done | bytes 1048608 | tf_op jit(solution)/shard_map/all_to_all | solution.py:87
  195.9 3.0 %add.26 = bf16[4,128,1024]{2,1,0:T(8,128)(2,1)} add(bf16[4,128,1024]{2,1,0:T(8,128)(2,1)} %get-tuple-element.26, bf16[4,128,1024]{2,1,0:T(8,128)(2,1)S(1)} %collective-permute-done.30) | non-fusion elementwise | flops 524288 | bytes 3145728 | tf_op jit(solution)/shard_map/add | solution.py:568
  198.9 3.5 %all-to-all-start.2 = ((bf16[4,128,1024]{2,1,0:T(8,128)(2,1)}), bf16[4,128,1024]{2,1,0:T(8,128)(2,1)S(1)}, u32[]{:S(2)}, u32[]{:S(2)}) async-start(bf16[4,128,1024]{2,1,0:T(8,128)(2,1)} %add.26), calls=%async_computation.2 | async-start | bytes 2097152 | tf_op jit(solution)/shard_map/all_to_all | solution.py:87
  202.4 1.0 copy-done.22
  203.4 9.8 %shard_map.136 = (bf16[4,128,1024]{2,1,0:T(8,128)(2,1)}, bf16[4,128,1024]{2,1,0:T(8,128)(2,1)}) custom-call(s32[2]{0:T(128)} %pad_add_fusion.refs_0_, bf16[704,1024]{1,0:T(8,128)(2,1)} %bitcast.31, f32[1024,704]{1,0:T(8,128)} %get-tuple-element.32.refs_2_, bf16[4,128,1024]{2,1,0:T(8,128)(2,1)} %copy-done.5, bf16[4,128,1024]{2,1,0:T(8,128)(2,1)} %copy-done.22), custom_call_target="tpu_custom_call" | custom-call | tf_op jit(solution)/shard_map/pallas_call | solution.py:419
  213.3 0.2 collective-permute-start.32
  213.5 2.7 collective-permute-done.32
  216.2 2.7 add.28
  218.9 9.8 %all-to-all-done.2 = bf16[4,128,1024]{2,1,0:T(8,128)(2,1)S(1)} async-done(((bf16[4,128,1024]{2,1,0:T(8,128)(2,1)}), bf16[4,128,1024]{2,1,0:T(8,128)(2,1)S(1)}, u32[]{:S(2)}, u32[]{:S(2)}) %all-to-all-start.2) | async-done | bytes 1048608 | tf_op jit(solution)/shard_map/all_to_all | solution.py:87
  228.7 3.7 %all-to-all-start.4 = ((bf16[4,128,1024]{2,1,0:T(8,128)(2,1)}), bf16[4,128,1024]{2,1,0:T(8,128)(2,1)S(1)}, u32[]{:S(2)}, u32[]{:S(2)}) async-start(bf16[4,128,1024]{2,1,0:T(8,128)(2,1)} %add.28), calls=%async_computation.4 | async-start | bytes 2097152 | tf_op jit(solution)/shard_map/all_to_all | solution.py:87
  232.4 0.2 convert_reduce_fusion
  232.6 0.8 add_convert_fusion
  233.4 24.2 %all-to-all-done.4.refs_6_ = bf16[4,128,1024]{2,1,0:T(8,128)(2,1)S(1)} async-done(((bf16[4,128,1024]{2,1,0:T(8,128)(2,1)}), bf16[4,128,1024]{2,1,0:T(8,128)(2,1)S(1)}, u32[]{:S(2)}, u32[]{:S(2)}) %all-to-all-start.4) | async-done | bytes 1048608 | tf_op jit(solution)/shard_map/all_to_all | solution.py:87
  257.6 1.0 copy-done.4
  258.6 8.1 %shard_map.137 = (bf16[128,3072]{1,0:T(8,128)(2,1)}, f32[128,1024]{1,0:T(8,128)}) custom-call(s32[2]{0:T(128)} %pad_add_fusion.refs_0_, bf16[128,1024]{1,0:T(8,128)(2,1)} %copy-done.21, f32[128,1024]{1,0:T(8,128)} %get-tuple-element.30.refs_2_, f32[128,3072]{1,0:T(8,128)} %get-tuple-element.31.refs_3_, f32[1,1024]{1,0:T(1,128)} %refs_4_.6, ...), custom_call_target="tpu_custom_call" | custom-call | tf_op jit(solution)/shard_map/pallas_call | solution.py:419
  266.8 7.3 %shard_map.138 = bf16[128,1024]{1,0:T(8,128)(2,1)} custom-call(s32[2]{0:T(128)} %pad_add_fusion.refs_0_, bf16[128,1024]{1,0:T(8,128)(2,1)} %refs_1_.3, bf16[128,3072]{1,0:T(8,128)(2,1)} %get-tuple-element.36.refs_2_, f32[128,1024]{1,0:T(8,128)} %get-tuple-element.37.refs_3_, f32[1,1024]{1,0:T(1,128)} %refs_4_.7, bf16[128,3072]{1,0:T(8,128)(2,1)} %bitcast.36, ...), custom_call_target="tpu_custom_call" | custom-call | tf_op jit(solution)/shard_map/pallas_call | solution.py:419
  (86 shorter events, 0.6 us)
Async XLA Ops:
  0.6 33.1 %collective-permute-start.1 = (bf16[128,3072]{1,0:T(8,128)(2,1)}, bf16[128,3072]{1,0:T(8,128)(2,1)S(1)}, u32[]{:S(2)}, u32[]{:S(2)}) collective-permute-start(bf16[128,3072]{1,0:T(8,128)(2,1)} %bitcast.32), channel_id=1, source_target_pairs={{0,2},{1,3},{2,4},{3,5},{4,6},{5,7},{8,10},{9,11},{10,12},{11,13},... | collective-permute-start | bytes 2359304 | tf_op jit(solution)/shard_map/ppermute | solution.py:66
  5.6 29.7 %collective-permute-start.2 = (bf16[128,3072]{1,0:T(8,128)(2,1)}, bf16[128,3072]{1,0:T(8,128)(2,1)}, u32[]{:S(2)}, u32[]{:S(2)}) collective-permute-start(bf16[128,3072]{1,0:T(8,128)(2,1)} %bitcast.33), channel_id=1, source_target_pairs={{2,0},{3,1},{4,2},{5,3},{6,4},{7,5},{10,8},{11,9},{12,10},{13,11},... | collective-permute-start | bytes 2359304 | tf_op jit(solution)/shard_map/ppermute | solution.py:66
  6.9 8.9 %collective-permute-start = (bf16[128,1024]{1,0:T(8,128)(2,1)}, bf16[128,1024]{1,0:T(8,128)(2,1)S(1)}, u32[]{:S(2)}, u32[]{:S(2)}) collective-permute-start(bf16[128,1024]{1,0:T(8,128)(2,1)} %param.12), channel_id=1, source_target_pairs={{0,8},{8,16},{16,24},{24,0},{1,9},{9,17},{17,25},{25,1},{2,10},{10... | collective-permute-start | bytes 786440 | tf_op jit(solution)/shard_map/ppermute | solution.py:45
  8.5 19.8 %collective-permute-start.14 = (bf16[128,1024]{1,0:T(8,128)(2,1)}, bf16[128,1024]{1,0:T(8,128)(2,1)S(1)}, u32[]{:S(2)}, u32[]{:S(2)}) collective-permute-start(bf16[128,1024]{1,0:T(8,128)(2,1)} %bitcast.37), channel_id=1, source_target_pairs={{0,2},{1,3},{2,4},{3,5},{4,6},{5,7},{8,10},{9,11},{10,12},{11,13},... | collective-permute-start | bytes 786440 | tf_op jit(solution)/shard_map/ppermute | solution.py:66
  13.1 19.3 %collective-permute-start.15 = (bf16[128,1024]{1,0:T(8,128)(2,1)}, bf16[128,1024]{1,0:T(8,128)(2,1)S(1)}, u32[]{:S(2)}, u32[]{:S(2)}) collective-permute-start(bf16[128,1024]{1,0:T(8,128)(2,1)} %bitcast.38), channel_id=1, source_target_pairs={{2,0},{3,1},{4,2},{5,3},{6,4},{7,5},{10,8},{11,9},{12,10},{13,11},... | collective-permute-start | bytes 786440 | tf_op jit(solution)/shard_map/ppermute | solution.py:66
  15.9 16.5 %copy-start.20 = (bf16[128,1024]{1,0:T(8,128)(2,1)}, bf16[128,1024]{1,0:T(8,128)(2,1)S(1)}, u32[]{:S(2)}) copy-start(bf16[128,1024]{1,0:T(8,128)(2,1)S(1)} %collective-permute-done.refs_1_) | copy-start | bytes 786436
  15.9 21.5 %collective-permute-start.20 = (bf16[128,1024]{1,0:T(8,128)(2,1)}, bf16[128,1024]{1,0:T(8,128)(2,1)S(1)}, u32[]{:S(2)}, u32[]{:S(2)}) collective-permute-start(bf16[128,1024]{1,0:T(8,128)(2,1)} %bitcast.39), channel_id=1, source_target_pairs={{0,1},{1,0},{2,3},{3,2},{4,5},{5,4},{6,7},{7,6},{8,9},{9,8},{10,11... | collective-permute-start | bytes 786440 | tf_op jit(solution)/shard_map/ppermute | solution.py:62
  28.3 39.5 %copy-start.9 = (bf16[128,1024]{1,0:T(8,128)(2,1)}, bf16[128,1024]{1,0:T(8,128)(2,1)S(1)}, u32[]{:S(2)}) copy-start(bf16[128,1024]{1,0:T(8,128)(2,1)S(1)} %collective-permute-done.14.refs_11_.refs_8_) | copy-start | bytes 786436
  28.3 9.1 %collective-permute-start.27 = (bf16[128,1024]{1,0:T(8,128)(2,1)}, bf16[128,1024]{1,0:T(8,128)(2,1)S(1)}, u32[]{:S(2)}, u32[]{:S(2)}) collective-permute-start(bf16[128,1024]{1,0:T(8,128)(2,1)} %param.14), channel_id=1, source_target_pairs={{0,24},{8,0},{16,8},{24,16},{1,25},{9,1},{17,9},{25,17},{2,26},{10... | collective-permute-start | bytes 786440 | tf_op jit(solution)/shard_map/ppermute | solution.py:45
  32.4 35.5 %copy-start.10 = (bf16[128,1024]{1,0:T(8,128)(2,1)}, bf16[128,1024]{1,0:T(8,128)(2,1)S(1)}, u32[]{:S(2)}) copy-start(bf16[128,1024]{1,0:T(8,128)(2,1)S(1)} %collective-permute-done.15.refs_12_.refs_9_) | copy-start | bytes 786436
  32.4 6.4 %collective-permute-start.16 = (bf16[128,1024]{1,0:T(8,128)(2,1)S(1)}, bf16[128,1024]{1,0:T(8,128)(2,1)S(1)}, u32[]{:S(2)}, u32[]{:S(2)}) collective-permute-start(bf16[128,1024]{1,0:T(8,128)(2,1)S(1)} %collective-permute-done.14.refs_11_.refs_8_), channel_id=1, source_target_pairs={{2,4},{3,5},{4,6},{5,7},{10,12},{11,13},{12,14},{13,15},{18,20},{1... | collective-permute-start | bytes 786440 | tf_op jit(solution)/shard_map/ppermute | solution.py:66
  33.7 34.1 %copy-start.7 = (bf16[128,3072]{1,0:T(8,128)(2,1)}, bf16[128,3072]{1,0:T(8,128)(2,1)S(1)}, u32[]{:S(2)}) copy-start(bf16[128,3072]{1,0:T(8,128)(2,1)S(1)} %collective-permute-done.1.refs_6_) | copy-start | bytes 2359300
  33.8 39.7 %collective-permute-start.3 = (bf16[128,3072]{1,0:T(8,128)(2,1)S(1)}, bf16[128,3072]{1,0:T(8,128)(2,1)}, u32[]{:S(2)}, u32[]{:S(2)}) collective-permute-start(bf16[128,3072]{1,0:T(8,128)(2,1)S(1)} %collective-permute-done.1.refs_6_), channel_id=1, source_target_pairs={{2,4},{3,5},{4,6},{5,7},{10,12},{11,13},{12,14},{13,15},{18,20},{1... | collective-permute-start | bytes 2359304 | tf_op jit(solution)/shard_map/ppermute | solution.py:66
  35.4 38.9 %collective-permute-start.4 = (bf16[128,3072]{1,0:T(8,128)(2,1)}, bf16[128,3072]{1,0:T(8,128)(2,1)}, u32[]{:S(2)}, u32[]{:S(2)}) collective-permute-start(bf16[128,3072]{1,0:T(8,128)(2,1)} %collective-permute-done.2.refs_7_), channel_id=1, source_target_pairs={{2,0},{3,1},{4,2},{5,3},{10,8},{11,9},{12,10},{13,11},{18,16},{19,... | collective-permute-start | bytes 2359304 | tf_op jit(solution)/shard_map/ppermute | solution.py:66
  37.4 2.1 copy-start.11
  37.4 28.1 %collective-permute-start.21 = (bf16[128,1024]{1,0:T(8,128)(2,1)S(1)}, bf16[128,1024]{1,0:T(8,128)(2,1)S(1)}, u32[]{:S(2)}, u32[]{:S(2)}) collective-permute-start(bf16[128,1024]{1,0:T(8,128)(2,1)S(1)} %collective-permute-done.14.refs_11_.refs_8_), channel_id=1, source_target_pairs={{0,1},{1,0},{2,3},{3,2},{4,5},{5,4},{6,7},{7,6},{8,9},{9,8},{10,11... | collective-permute-start | bytes 786440 | tf_op jit(solution)/shard_map/ppermute | solution.py:62
  37.4 30.4 %copy-start.21 = (bf16[128,1024]{1,0:T(8,128)(2,1)}, bf16[128,1024]{1,0:T(8,128)(2,1)S(1)}, u32[]{:S(2)}) copy-start(bf16[128,1024]{1,0:T(8,128)(2,1)S(1)} %collective-permute-done.27.refs_1_) | copy-start | bytes 786436
  37.5 28.0 %collective-permute-start.17 = (bf16[128,1024]{1,0:T(8,128)(2,1)S(1)}, bf16[128,1024]{1,0:T(8,128)(2,1)}, u32[]{:S(2)}, u32[]{:S(2)}) collective-permute-start(bf16[128,1024]{1,0:T(8,128)(2,1)S(1)} %collective-permute-done.15.refs_12_.refs_9_), channel_id=1, source_target_pairs={{2,0},{3,1},{4,2},{5,3},{10,8},{11,9},{12,10},{13,11},{18,16},{19,... | collective-permute-start | bytes 786440 | tf_op jit(solution)/shard_map/ppermute | solution.py:66
  38.8 56.4 %copy-start.12 = (bf16[128,1024]{1,0:T(8,128)(2,1)}, bf16[128,1024]{1,0:T(8,128)(2,1)S(1)}, u32[]{:S(2)}) copy-start(bf16[128,1024]{1,0:T(8,128)(2,1)S(1)} %collective-permute-done.16.refs_13_.refs_10_) | copy-start | bytes 786436
  38.8 27.4 %collective-permute-start.22 = (bf16[128,1024]{1,0:T(8,128)(2,1)S(1)}, bf16[128,1024]{1,0:T(8,128)(2,1)S(1)}, u32[]{:S(2)}, u32[]{:S(2)}) collective-permute-start(bf16[128,1024]{1,0:T(8,128)(2,1)S(1)} %collective-permute-done.15.refs_12_.refs_9_), channel_id=1, source_target_pairs={{0,1},{1,0},{2,3},{3,2},{4,5},{5,4},{6,7},{7,6},{8,9},{9,8},{10,11... | collective-permute-start | bytes 786440 | tf_op jit(solution)/shard_map/ppermute | solution.py:62
  65.4 31.4 %collective-permute-start.5 = (bf16[128,3072]{1,0:T(8,128)(2,1)}, bf16[128,3072]{1,0:T(8,128)(2,1)S(1)}, u32[]{:S(2)}, u32[]{:S(2)}) collective-permute-start(bf16[128,3072]{1,0:T(8,128)(2,1)} %bitcast.34), channel_id=1, source_target_pairs={{0,1},{1,0},{2,3},{3,2},{4,5},{5,4},{6,7},{7,6},{8,9},{9,8},{10,11... | collective-permute-start | bytes 2359304 | tf_op jit(solution)/shard_map/ppermute | solution.py:62
  65.5 2.4 copy-start.13
  65.5 6.7 %collective-permute-start.18 = (bf16[128,1024]{1,0:T(8,128)(2,1)S(1)}, bf16[128,1024]{1,0:T(8,128)(2,1)S(1)}, u32[]{:S(2)}, u32[]{:S(2)}) collective-permute-start(bf16[128,1024]{1,0:T(8,128)(2,1)S(1)} %collective-permute-done.16.refs_13_.refs_10_), channel_id=1, source_target_pairs={{4,6},{5,7},{12,14},{13,15},{20,22},{21,23},{28,30},{29,31}} | collective-permute-start | bytes 786440 | tf_op jit(solution)/shard_map/ppermute | solution.py:66
  66.2 1.7 copy-start.14
  66.2 31.1 %collective-permute-start.6 = (bf16[128,3072]{1,0:T(8,128)(2,1)S(1)}, bf16[128,3072]{1,0:T(8,128)(2,1)}, u32[]{:S(2)}, u32[]{:S(2)}) collective-permute-start(bf16[128,3072]{1,0:T(8,128)(2,1)S(1)} %collective-permute-done.1.refs_6_), channel_id=1, source_target_pairs={{0,1},{1,0},{2,3},{3,2},{4,5},{5,4},{6,7},{7,6},{8,9},{9,8},{10,11... | collective-permute-start | bytes 2359304 | tf_op jit(solution)/shard_map/ppermute | solution.py:62
  67.8 50.3 %copy-start.24 = (s32[2,1,8,8]{3,2,1,0:T(8,128)S(1)}, s32[2,1,8,8]{3,2,1,0:T(8,128)}, u32[]{:S(2)}) copy-start(s32[2,1,8,8]{3,2,1,0:T(8,128)} %param.23) | copy-start | bytes 1540
  67.9 68.1 %all-to-all-start = ((bf16[4,128,1152]{2,1,0:T(8,128)(2,1)}), bf16[4,128,1152]{2,1,0:T(8,128)(2,1)}, u32[]{:S(2)}, u32[]{:S(2)}) async-start(bf16[4,128,1152]{2,1,0:T(8,128)(2,1)} %broadcast_in_dim.16), calls=%async_computation | async-start | bytes 2359296 | tf_op jit(solution)/shard_map/all_to_all | solution.py:87
  72.2 1.3 copy-start.15
  72.2 23.0 %collective-permute-start.19 = (bf16[128,1024]{1,0:T(8,128)(2,1)}, bf16[128,1024]{1,0:T(8,128)(2,1)S(1)}, u32[]{:S(2)}, u32[]{:S(2)}) collective-permute-start(bf16[128,1024]{1,0:T(8,128)(2,1)} %collective-permute-done.17.refs_14_.refs_11_), channel_id=1, source_target_pairs={{2,0},{3,1},{10,8},{11,9},{18,16},{19,17},{26,24},{27,25}} | collective-permute-start | bytes 786440 | tf_op jit(solution)/shard_map/ppermute | solution.py:66
  73.5 23.9 %collective-permute-start.10 = (bf16[128,3072]{1,0:T(8,128)(2,1)}, bf16[128,3072]{1,0:T(8,128)(2,1)S(1)}, u32[]{:S(2)}, u32[]{:S(2)}) collective-permute-start(bf16[128,3072]{1,0:T(8,128)(2,1)} %collective-permute-done.3.refs_8_), channel_id=1, source_target_pairs={{4,6},{5,7},{12,14},{13,15},{20,22},{21,23},{28,30},{29,31}} | collective-permute-start | bytes 2359304 | tf_op jit(solution)/shard_map/ppermute | solution.py:66
  74.2 42.1 %collective-permute-start.11 = (bf16[128,3072]{1,0:T(8,128)(2,1)}, bf16[128,3072]{1,0:T(8,128)(2,1)S(1)}, u32[]{:S(2)}, u32[]{:S(2)}) collective-permute-start(bf16[128,3072]{1,0:T(8,128)(2,1)} %collective-permute-done.4.refs_9_), channel_id=1, source_target_pairs={{2,0},{3,1},{10,8},{11,9},{18,16},{19,17},{26,24},{27,25}} | collective-permute-start | bytes 2359304 | tf_op jit(solution)/shard_map/ppermute | solution.py:66
  95.2 21.2 %copy-start.16 = (bf16[128,1024]{1,0:T(8,128)(2,1)}, bf16[128,1024]{1,0:T(8,128)(2,1)S(1)}, u32[]{:S(2)}) copy-start(bf16[128,1024]{1,0:T(8,128)(2,1)S(1)} %collective-permute-done.19.refs_16_.refs_13_) | copy-start | bytes 786436
  95.2 1.5 collective-permute-start.23
  96.7 19.7 %copy-start.17 = (bf16[128,1024]{1,0:T(8,128)(2,1)}, bf16[128,1024]{1,0:T(8,128)(2,1)S(1)}, u32[]{:S(2)}) copy-start(bf16[128,1024]{1,0:T(8,128)(2,1)S(1)} %collective-permute-done.23.refs_20_.refs_17_) | copy-start | bytes 786436
  96.7 19.7 %collective-permute-start.7 = (bf16[128,3072]{1,0:T(8,128)(2,1)}, bf16[128,3072]{1,0:T(8,128)(2,1)}, u32[]{:S(2)}, u32[]{:S(2)}) collective-permute-start(bf16[128,3072]{1,0:T(8,128)(2,1)} %collective-permute-done.2.refs_7_), channel_id=1, source_target_pairs={{0,1},{1,0},{2,3},{3,2},{4,5},{5,4},{6,7},{7,6},{8,9},{9,8},{10,11... | collective-permute-start | bytes 2359304 | tf_op jit(solution)/shard_map/ppermute | solution.py:62
  96.9 0.9 copy-start.8
  96.9 20.1 %collective-permute-start.8 = (bf16[128,3072]{1,0:T(8,128)(2,1)}, bf16[128,3072]{1,0:T(8,128)(2,1)}, u32[]{:S(2)}, u32[]{:S(2)}) collective-permute-start(bf16[128,3072]{1,0:T(8,128)(2,1)} %collective-permute-done.3.refs_8_), channel_id=1, source_target_pairs={{0,1},{1,0},{2,3},{3,2},{4,5},{5,4},{6,7},{7,6},{8,9},{9,8},{10,11... | collective-permute-start | bytes 2359304 | tf_op jit(solution)/shard_map/ppermute | solution.py:62
  97.3 19.8 %collective-permute-start.9 = (bf16[128,3072]{1,0:T(8,128)(2,1)}, bf16[128,3072]{1,0:T(8,128)(2,1)}, u32[]{:S(2)}, u32[]{:S(2)}) collective-permute-start(bf16[128,3072]{1,0:T(8,128)(2,1)} %collective-permute-done.4.refs_9_), channel_id=1, source_target_pairs={{0,1},{1,0},{2,3},{3,2},{4,5},{5,4},{6,7},{7,6},{8,9},{9,8},{10,11... | collective-permute-start | bytes 2359304 | tf_op jit(solution)/shard_map/ppermute | solution.py:62
  97.4 29.4 %copy-start = (bf16[128,3072]{1,0:T(8,128)(2,1)}, bf16[128,3072]{1,0:T(8,128)(2,1)S(1)}, u32[]{:S(2)}) copy-start(bf16[128,3072]{1,0:T(8,128)(2,1)S(1)} %collective-permute-done.10.refs_6_.refs_10_) | copy-start | bytes 2359300
  97.4 29.4 %collective-permute-start.12 = (bf16[128,3072]{1,0:T(8,128)(2,1)S(1)}, bf16[128,3072]{1,0:T(8,128)(2,1)S(1)}, u32[]{:S(2)}, u32[]{:S(2)}) collective-permute-start(bf16[128,3072]{1,0:T(8,128)(2,1)S(1)} %collective-permute-done.10.refs_6_.refs_10_), channel_id=1, source_target_pairs={{0,1},{1,0},{2,3},{3,2},{4,5},{5,4},{6,7},{7,6},{8,9},{9,8},{10,11... | collective-permute-start | bytes 2359304 | tf_op jit(solution)/shard_map/ppermute | solution.py:62
  116.4 10.4 %copy-start.1 = (bf16[128,3072]{1,0:T(8,128)(2,1)}, bf16[128,3072]{1,0:T(8,128)(2,1)S(1)}, u32[]{:S(2)}) copy-start(bf16[128,3072]{1,0:T(8,128)(2,1)S(1)} %collective-permute-done.11.refs_7_.refs_11_) | copy-start | bytes 2359300
  116.4 10.5 %collective-permute-start.13 = (bf16[128,3072]{1,0:T(8,128)(2,1)S(1)}, bf16[128,3072]{1,0:T(8,128)(2,1)S(1)}, u32[]{:S(2)}, u32[]{:S(2)}) collective-permute-start(bf16[128,3072]{1,0:T(8,128)(2,1)S(1)} %collective-permute-done.11.refs_7_.refs_11_), channel_id=1, source_target_pairs={{0,1},{1,0},{2,3},{3,2},{4,5},{5,4},{6,7},{7,6},{8,9},{9,8},{10,11... | collective-permute-start | bytes 2359304 | tf_op jit(solution)/shard_map/ppermute | solution.py:62
  116.5 10.3 %collective-permute-start.24 = (bf16[128,1024]{1,0:T(8,128)(2,1)}, bf16[128,1024]{1,0:T(8,128)(2,1)S(1)}, u32[]{:S(2)}, u32[]{:S(2)}) collective-permute-start(bf16[128,1024]{1,0:T(8,128)(2,1)} %collective-permute-done.17.refs_14_.refs_11_), channel_id=1, source_target_pairs={{0,1},{1,0},{2,3},{3,2},{4,5},{5,4},{6,7},{7,6},{8,9},{9,8},{10,11... | collective-permute-start | bytes 786440 | tf_op jit(solution)/shard_map/ppermute | solution.py:62
  117.0 9.8 %collective-permute-start.25 = (bf16[128,1024]{1,0:T(8,128)(2,1)}, bf16[128,1024]{1,0:T(8,128)(2,1)}, u32[]{:S(2)}, u32[]{:S(2)}) collective-permute-start(bf16[128,1024]{1,0:T(8,128)(2,1)} %copy-done.15), channel_id=1, source_target_pairs={{0,1},{1,0},{2,3},{3,2},{4,5},{5,4},{6,7},{7,6},{8,9},{9,8},{10,11... | collective-permute-start | bytes 786440 | tf_op jit(solution)/shard_map/ppermute | solution.py:62
  117.1 9.7 %collective-permute-start.26 = (bf16[128,1024]{1,0:T(8,128)(2,1)}, bf16[128,1024]{1,0:T(8,128)(2,1)}, u32[]{:S(2)}, u32[]{:S(2)}) collective-permute-start(bf16[128,1024]{1,0:T(8,128)(2,1)} %copy-done.16), channel_id=1, source_target_pairs={{0,1},{1,0},{2,3},{3,2},{4,5},{5,4},{6,7},{7,6},{8,9},{9,8},{10,11... | collective-permute-start | bytes 786440 | tf_op jit(solution)/shard_map/ppermute | solution.py:62
  126.8 0.7 copy-start.18
  126.8 0.9 copy-start.2
  126.9 1.2 copy-start.3
  136.0 29.7 %all-to-all-start.1 = ((bf16[4,128,1024]{2,1,0:T(8,128)(2,1)}), bf16[4,128,1024]{2,1,0:T(8,128)(2,1)S(1)}, u32[]{:S(2)}, u32[]{:S(2)}) async-start(bf16[4,128,1024]{2,1,0:T(8,128)(2,1)} %get-tuple-element.25), calls=%async_computation.1 | async-start | bytes 2097152 | tf_op jit(solution)/shard_map/all_to_all | solution.py:87
  139.5 29.9 %collective-permute-start.28 = (bf16[4,128,1152]{2,1,0:T(8,128)(2,1)}, bf16[4,128,1152]{2,1,0:T(8,128)(2,1)S(1)}, u32[]{:S(2)}, u32[]{:S(2)}) collective-permute-start(bf16[4,128,1152]{2,1,0:T(8,128)(2,1)} %all-to-all-done.refs_2_), channel_id=1, source_target_pairs={{0,1},{1,0},{2,3},{3,2},{4,5},{5,4},{6,7},{7,6},{8,9},{9,8},{10,11... | collective-permute-start | bytes 3538952 | tf_op jit(solution)/shard_map/ppermute | solution.py:62
  165.7 11.3 %copy-start.6 = (bf16[4,128,1024]{2,1,0:T(8,128)(2,1)}, bf16[4,128,1024]{2,1,0:T(8,128)(2,1)S(1)}, u32[]{:S(2)}) copy-start(bf16[4,128,1024]{2,1,0:T(8,128)(2,1)S(1)} %all-to-all-done.1.refs_4_) | copy-start | bytes 3145732
  165.7 11.3 %collective-permute-start.29 = (bf16[4,128,1024]{2,1,0:T(8,128)(2,1)S(1)}, bf16[4,128,1024]{2,1,0:T(8,128)(2,1)}, u32[]{:S(2)}, u32[]{:S(2)}) collective-permute-start(bf16[4,128,1024]{2,1,0:T(8,128)(2,1)S(1)} %all-to-all-done.1.refs_4_), channel_id=1, source_target_pairs={{0,1},{1,0},{2,3},{3,2},{4,5},{5,4},{6,7},{7,6},{8,9},{9,8},{10,11... | collective-permute-start | bytes 3145736 | tf_op jit(solution)/shard_map/ppermute | solution.py:62
  165.7 30.2 %all-to-all-start.3 = ((bf16[4,128,1024]{2,1,0:T(8,128)(2,1)}), bf16[4,128,1024]{2,1,0:T(8,128)(2,1)S(1)}, u32[]{:S(2)}, u32[]{:S(2)}) async-start(bf16[4,128,1024]{2,1,0:T(8,128)(2,1)} %get-tuple-element.33), calls=%async_computation.3 | async-start | bytes 2097152 | tf_op jit(solution)/shard_map/all_to_all | solution.py:87
  169.4 1.0 copy-start.19
  185.8 10.1 %collective-permute-start.30 = (bf16[4,128,1024]{2,1,0:T(8,128)(2,1)}, bf16[4,128,1024]{2,1,0:T(8,128)(2,1)S(1)}, u32[]{:S(2)}, u32[]{:S(2)}) collective-permute-start(bf16[4,128,1024]{2,1,0:T(8,128)(2,1)} %get-tuple-element.27), channel_id=1, source_target_pairs={{0,1},{1,0},{2,3},{3,2},{4,5},{5,4},{6,7},{7,6},{8,9},{9,8},{10,11... | collective-permute-start | bytes 3145736 | tf_op jit(solution)/shard_map/ppermute | solution.py:62
  195.9 3.0 %copy-start.5 = (bf16[4,128,1024]{2,1,0:T(8,128)(2,1)}, bf16[4,128,1024]{2,1,0:T(8,128)(2,1)S(1)}, u32[]{:S(2)}) copy-start(bf16[4,128,1024]{2,1,0:T(8,128)(2,1)S(1)} %all-to-all-done.3.refs_3_) | copy-start | bytes 3145732
  195.9 6.5 %collective-permute-start.31 = (bf16[4,128,1024]{2,1,0:T(8,128)(2,1)S(1)}, bf16[4,128,1024]{2,1,0:T(8,128)(2,1)S(1)}, u32[]{:S(2)}, u32[]{:S(2)}) collective-permute-start(bf16[4,128,1024]{2,1,0:T(8,128)(2,1)S(1)} %all-to-all-done.3.refs_3_), channel_id=1, source_target_pairs={{0,1},{1,0},{2,3},{3,2},{4,5},{5,4},{6,7},{7,6},{8,9},{9,8},{10,11... | collective-permute-start | bytes 3145736 | tf_op jit(solution)/shard_map/ppermute | solution.py:62
  198.9 29.8 %all-to-all-start.2 = ((bf16[4,128,1024]{2,1,0:T(8,128)(2,1)}), bf16[4,128,1024]{2,1,0:T(8,128)(2,1)S(1)}, u32[]{:S(2)}, u32[]{:S(2)}) async-start(bf16[4,128,1024]{2,1,0:T(8,128)(2,1)} %add.26), calls=%async_computation.2 | async-start | bytes 2097152 | tf_op jit(solution)/shard_map/all_to_all | solution.py:87
  202.4 1.0 copy-start.22
  213.3 2.9 %collective-permute-start.32 = (bf16[4,128,1024]{2,1,0:T(8,128)(2,1)}, bf16[4,128,1024]{2,1,0:T(8,128)(2,1)S(1)}, u32[]{:S(2)}, u32[]{:S(2)}) collective-permute-start(bf16[4,128,1024]{2,1,0:T(8,128)(2,1)} %get-tuple-element.35), channel_id=1, source_target_pairs={{0,1},{1,0},{2,3},{3,2},{4,5},{5,4},{6,7},{7,6},{8,9},{9,8},{10,11... | collective-permute-start | bytes 3145736 | tf_op jit(solution)/shard_map/ppermute | solution.py:62
  218.9 13.8 %copy-start.23 = (f32[128,1024]{1,0:T(8,128)S(1)}, f32[128,1024]{1,0:T(8,128)}, u32[]{:S(2)}) copy-start(f32[128,1024]{1,0:T(8,128)} %get-tuple-element.23) | copy-start | bytes 1572868
  228.7 28.9 %all-to-all-start.4 = ((bf16[4,128,1024]{2,1,0:T(8,128)(2,1)}), bf16[4,128,1024]{2,1,0:T(8,128)(2,1)S(1)}, u32[]{:S(2)}, u32[]{:S(2)}) async-start(bf16[4,128,1024]{2,1,0:T(8,128)(2,1)} %add.28), calls=%async_computation.4 | async-start | bytes 2097152 | tf_op jit(solution)/shard_map/all_to_all | solution.py:87
  257.6 1.0 copy-start.4

commit v9 on v8

--- a/solution.py
+++ b/solution.py
@@ -266,18 +266,19 @@
     return jnp.sum(jnp.where(hit, gates, 0.0), axis=-1, keepdims=True)
 
 
-def cotangent_kernel(rows, width, expert_count, *refs):
-    place, down_ref, mine, other, act_ref, gate_ref, cot, sems = refs
+def cotangent_kernel(rows, expert_count, *refs):
+    place, down_ref = refs[:2]
+    act_ref, gate_ref, cot, columns, sems, gate_sems = refs[6:]
     chip, core = place[0], place[1]
     me = CORES * chip + core
-    fetch_line((mine, other), cot, sems, rows, chip, core)
+    fetch_line(refs[4:6], columns, gate_sems, rows, chip, core)
+    fetch_line(refs[2:4], cot, sems, rows, chip, core)
     chunk = 2 * rows
 
     def step(index, carry):
         start = chunk_start(index, chunk)
-        block = cot[pl.ds(start, chunk), :]
-        gates = block[:, width:].astype(F32)
-        grad_act = dot(block[:, :width], down_ref[...], NT)
+        gates = columns[pl.ds(start, chunk), :].astype(F32)
+        grad_act = dot(cot[pl.ds(start, chunk), :], down_ref[...], NT)
         act_ref[pl.ds(start, chunk), :] = grad_act * picked_gate(gates, me, expert_count, 1)
         gate_ref[pl.ds(start, chunk), :] = jnp.broadcast_to(
             picked_gate(gates, me, expert_count, 0), (chunk, LANES)
@@ -480,8 +481,8 @@
     arriving = passed_along(handoff_forward, 1)
     cotangent = passed_along(relay_cotangents, -1)
     gates = gate_columns(routes, gate_logits, expert_count)
-    cot_block = jnp.concatenate([cotangent, gates], axis=1)
-    cots = spread(jnp.broadcast_to(cot_block[None], (length,) + cot_block.shape))
+    cots = spread(jnp.broadcast_to(cotangent[None], (length,) + cotangent.shape))
+    gate_blocks = spread(jnp.broadcast_to(gates[None], (length,) + gates.shape))
     mask = allowed_of(block_mask[:, 0])
 
     half = count // 2
@@ -534,12 +535,17 @@
     rows_fwd = spread(expert_fwd)
 
     grad_act, gate_fwd = call(
-        functools.partial(cotangent_kernel, tokens, width, expert_count),
+        functools.partial(cotangent_kernel, tokens, expert_count),
         (shaped((total, hidden_units), F32), shaped((total, LANES), F32)),
-        [SMEM, VMEM] + [ANY] * 2,
+        [SMEM, VMEM] + [ANY] * 4,
         (VMEM,) * 2,
-        [pltpu.VMEM((total, width + LANES), BF16), dma((CORES, length))],
-        [place, down_weight] + cots,
+        [
+            pltpu.VMEM((total, width), BF16),
+            pltpu.VMEM((total, LANES), BF16),
+            dma((CORES, length)),
+            dma((CORES, length)),
+        ],
+        [place, down_weight] + cots + gate_blocks,
     )
 
     pair = (shaped((length, tokens, width), BF16),) * 2

time: 275 us -> 278 us (1.011)
  starting transfers between devices: 47.9 us -> 57.4 us
  waiting for transfers between devices: 146 us -> 138 us
    ppermute x12, waiting for transfers between devices: 78.3 us -> 64 us  [hop(): return lax.ppermute(value, 'expert', chip_pairs(sources, move))]
    all_to_all x5 -> x6, starting transfers between devices: 18.8 us -> 28.1 us  [across(): lax.all_to_all(blocks, 'expert', split_axis=0, concat_axis=0, axis_index_...]
    all_to_all x5 -> x6, waiting for transfers between devices: 61.6 us -> 67.1 us  [across(): lax.all_to_all(blocks, 'expert', split_axis=0, concat_axis=0, axis_index_...]
    ppermute x19 -> x20, waiting for transfers between devices: 4.31 us -> 5.87 us  [swapped(): return lax.ppermute(value, 'expert', [(i, i ^ 1) for i in range(count)])]
  transfers between devices with their start and end apart: 38 -> 40, of which waited for: 12 -> 12; matrix products, arithmetic and copies ran while one was open for 4% -> 3% of each run, Pallas kernels for 18% -> 18%
where the time goes in v9:
time: 278 us; the launch traced here: 277 us
  waiting for transfers between devices  138 us (50%)
  Pallas kernels  64.9 us (23%)
  starting transfers between devices  57.4 us (21%)
  other arithmetic  7.24 us (3%)
  local copies, waits for them, and re-layouts  6.21 us (2%)
    all_to_all x6, waiting for transfers between devices, across(): lax.all_to_all(blocks, 'expert', split_axis=0, concat_axis=0, axis_index_...  67.1 us
    pallas_call x8, Pallas kernels, call(): pl.pallas_call(kernel, out_shape=outs, in_specs=specs, out_specs=out_spec...  64.9 us
    ppermute x12, waiting for transfers between devices, hop(): return lax.ppermute(value, 'expert', chip_pairs(sources, move))  64 us
    all_to_all x6, starting transfers between devices, across(): lax.all_to_all(blocks, 'expert', split_axis=0, concat_axis=0, axis_index_...  28.1 us
    ppermute x12, starting transfers between devices, hop(): return lax.ppermute(value, 'expert', chip_pairs(sources, move))  21.1 us
    ppermute x20, waiting for transfers between devices, swapped(): return lax.ppermute(value, 'expert', [(i, i ^ 1) for i in range(count)])  5.87 us
  transfers between devices with their start and end apart: 40, of which 12 were waited for; matrix products, arithmetic and copies ran while one was open for 3% of the time, Pallas kernels for 18%

profile of v9, /device:TPU:0, one launch (start us, length us, event | category | flops | bytes accessed | tf_op | source)
XLA Modules:
  0.0 276.6 jit_solution(15837136026868182637)
XLA Ops:
  0.6 5.0 %collective-permute-start.1 = (bf16[128,3072]{1,0:T(8,128)(2,1)}, bf16[128,3072]{1,0:T(8,128)(2,1)S(1)}, u32[]{:S(2)}, u32[]{:S(2)}) collective-permute-start(bf16[128,3072]{1,0:T(8,128)(2,1)} %bitcast.32), channel_id=1, source_target_pairs={{0,2},{1,3},{2,4},{3,5},{4,6},{5,7},{8,10},{9,11},{10,12},{11,13},... | collective-permute-start | bytes 2359304 | tf_op jit(solution)/shard_map/ppermute | solution.py:66
  5.6 1.3 collective-permute-start.2
  6.9 1.5 collective-permute-start
  8.5 4.7 %collective-permute-start.14 = (bf16[128,1024]{1,0:T(8,128)(2,1)}, bf16[128,1024]{1,0:T(8,128)(2,1)S(1)}, u32[]{:S(2)}, u32[]{:S(2)}) collective-permute-start(bf16[128,1024]{1,0:T(8,128)(2,1)} %bitcast.37), channel_id=1, source_target_pairs={{0,2},{1,3},{2,4},{3,5},{4,6},{5,7},{8,10},{9,11},{10,12},{11,13},... | collective-permute-start | bytes 786440 | tf_op jit(solution)/shard_map/ppermute | solution.py:66
  13.2 1.3 collective-permute-start.15
  14.5 1.4 collective-permute-done.refs_1_
  15.9 12.4 %collective-permute-done.14.refs_11_.refs_8_ = bf16[128,1024]{1,0:T(8,128)(2,1)S(1)} collective-permute-done((bf16[128,1024]{1,0:T(8,128)(2,1)}, bf16[128,1024]{1,0:T(8,128)(2,1)S(1)}, u32[]{:S(2)}, u32[]{:S(2)}) %collective-permute-start.14) | collective-permute-done | bytes 262176 | tf_op jit(solution)/shard_map/ppermute | solution.py:66
  28.3 2.4 collective-permute-start.27
  30.8 1.6 collective-permute-done.15.refs_12_.refs_9_
  32.4 0.7 collective-permute-start.16
  33.1 1.6 collective-permute-start.3
  34.7 1.3 collective-permute-start.4
  36.0 1.3 collective-permute-start.17
  37.4 0.5 collective-permute-start.22
  37.9 26.9 %collective-permute-done.17.refs_14_.refs_11_ = bf16[128,1024]{1,0:T(8,128)(2,1)} collective-permute-done((bf16[128,1024]{1,0:T(8,128)(2,1)S(1)}, bf16[128,1024]{1,0:T(8,128)(2,1)}, u32[]{:S(2)}, u32[]{:S(2)}) %collective-permute-start.17) | collective-permute-done | bytes 262176 | tf_op jit(solution)/shard_map/ppermute | solution.py:66
  64.8 0.7 collective-permute-start.18
  65.6 0.5 collective-permute-start.6
  66.1 1.3 collective-permute-start.19
  67.4 0.7 collective-permute-start.10
  68.1 1.3 collective-permute-start.11
  69.4 1.1 broadcast_in_dim.16
  70.6 9.0 %all-to-all-start = ((bf16[4,128,1024]{2,1,0:T(8,128)(2,1)}), bf16[4,128,1024]{2,1,0:T(8,128)(2,1)}, u32[]{:S(2)}, u32[]{:S(2)}) async-start(bf16[4,128,1024]{2,1,0:T(8,128)(2,1)} %broadcast_in_dim.16), calls=%async_computation | async-start | bytes 2097152 | tf_op jit(solution)/shard_map/all_to_all | solution.py:87
  79.5 1.7 collective-permute-done.23.refs_20_.refs_17_
  81.4 0.4 collective-permute-start.8
  82.0 0.4 collective-permute-start.12
  82.3 23.1 %collective-permute-done.11.refs_7_.refs_11_ = bf16[128,3072]{1,0:T(8,128)(2,1)S(1)} collective-permute-done((bf16[128,3072]{1,0:T(8,128)(2,1)}, bf16[128,3072]{1,0:T(8,128)(2,1)S(1)}, u32[]{:S(2)}, u32[]{:S(2)}) %collective-permute-start.11) | collective-permute-done | bytes 786464 | tf_op jit(solution)/shard_map/ppermute | solution.py:66
  105.5 0.6 collective-permute-start.24
  106.1 0.4 collective-permute-start.26
  106.5 0.6 pad_add_fusion.refs_0_
  107.2 1.1 fusion.refs_4_
  108.2 7.5 %shard_map.131 = (f32[128,3072]{1,0:T(8,128)}, f32[128,3072]{1,0:T(8,128)}, bf16[128,1024]{1,0:T(8,128)(2,1)}, bf16[128,1024]{1,0:T(8,128)(2,1)}, f32[2,128,128]{2,1,0:T(8,128)}) custom-call(s32[2]{0:T(128)} %pad_add_fusion.refs_0_, bf16[128,1024]{1,0:T(8,128)(2,1)} %copy-done.19, bf16[128,1024]{1,0:T(8,128)(2,1)} %refs_1_.3, f32[1,1024]{1,0:T(1,128)} %refs_4_.7, ...), custom_call_target="tpu_custom_call" | custom-call | tf_op jit(solution)/shard_map/pallas_call | solution.py:420
  115.9 0.6 copy-done.17
  116.5 0.3 copy-done.2
  116.8 0.3 copy-done.3
  117.1 8.0 %shard_map.132 = (f32[128,3072]{1,0:T(8,128)}, f32[128,1024]{1,0:T(8,128)}, bf16[4,128,1024]{2,1,0:T(8,128)(2,1)}) custom-call(s32[2]{0:T(128)} %pad_add_fusion.refs_0_, bf16[128,1024]{1,0:T(8,128)(2,1)} %copy-done.19, f32[128,3072]{1,0:T(8,128)} %get-tuple-element.20.refs_2_, bf16[128,1024]{1,0:T(8,128)(2,1)} %get-tuple-element.21.refs_3_, ...), custom_call_target="tpu_custom_call" | custom-call | tf_op jit(solution)/shard_map/pallas_call | solution.py:420
  125.1 3.5 %all-to-all-start.2 = ((bf16[4,128,1024]{2,1,0:T(8,128)(2,1)}), bf16[4,128,1024]{2,1,0:T(8,128)(2,1)S(1)}, u32[]{:S(2)}, u32[]{:S(2)}) async-start(bf16[4,128,1024]{2,1,0:T(8,128)(2,1)} %get-tuple-element.25), calls=%async_computation.2 | async-start | bytes 2097152 | tf_op jit(solution)/shard_map/all_to_all | solution.py:87
  128.8 26.0 %all-to-all-done.2.refs_4_ = bf16[4,128,1024]{2,1,0:T(8,128)(2,1)S(1)} async-done(((bf16[4,128,1024]{2,1,0:T(8,128)(2,1)}), bf16[4,128,1024]{2,1,0:T(8,128)(2,1)S(1)}, u32[]{:S(2)}, u32[]{:S(2)}) %all-to-all-start.2) | async-done | bytes 1048608 | tf_op jit(solution)/shard_map/all_to_all | solution.py:87
  154.8 0.7 broadcast_in_dim.19
  155.6 3.3 %all-to-all-start.1 = ((bf16[4,128,128]{2,1,0:T(8,128)(2,1)}), bf16[4,128,128]{2,1,0:T(8,128)(2,1)S(1)}, u32[]{:S(2)}, u32[]{:S(2)}) async-start(bf16[4,128,128]{2,1,0:T(8,128)(2,1)} %broadcast_in_dim.19), calls=%async_computation.1 | async-start | bytes 262144 | tf_op jit(solution)/shard_map/all_to_all | solution.py:87
  159.0 7.9 %shard_map.135 = (f32[128,3072]{1,0:T(8,128)}, f32[128,1024]{1,0:T(8,128)}, bf16[4,128,1024]{2,1,0:T(8,128)(2,1)}) custom-call(s32[2]{0:T(128)} %pad_add_fusion.refs_0_, bf16[128,1024]{1,0:T(8,128)(2,1)} %refs_1_.3, f32[128,3072]{1,0:T(8,128)} %get-tuple-element.28.refs_2_, bf16[128,1024]{1,0:T(8,128)(2,1)} %get-tuple-element.29.refs_3_, f32[1,1024]{1,0:T(1,128)} %refs_4_.6, ...), custom_call_target="tpu_custom_call" | custom-call | tf_op jit(solution)/shard_map/pallas_call | solution.py:420
  166.9 0.5 collective-permute-start.30
  167.4 5.0 %all-to-all-start.4 = ((bf16[4,128,1024]{2,1,0:T(8,128)(2,1)}), bf16[4,128,1024]{2,1,0:T(8,128)(2,1)S(1)}, u32[]{:S(2)}, u32[]{:S(2)}) async-start(bf16[4,128,1024]{2,1,0:T(8,128)(2,1)} %get-tuple-element.33), calls=%async_computation.4 | async-start | bytes 2097152 | tf_op jit(solution)/shard_map/all_to_all | solution.py:87
  172.4 1.3 collective-permute-done.29.refs_5_
  173.7 0.6 copy-done.24
  174.4 0.4 copy-done.20
  174.8 7.4 %shard_map.133 = (f32[1024,704]{1,0:T(8,128)}, f32[1024,128]{1,0:T(8,128)}) custom-call(s32[2]{0:T(128)} %pad_add_fusion.refs_0_, bf16[704,1024]{1,0:T(8,128)(2,1)} %bitcast.28, bf16[4,128,1024]{2,1,0:T(8,128)(2,1)} %all-to-all-done.refs_2_, bf16[4,128,1024]{2,1,0:T(8,128)(2,1)} %copy-done.20, bf16[4,128,128]{2,1,0:T(8,128)(2,1)} %copy-done.22, ...), custom_call_target="tpu_custom_call" | custom-call | tf_op jit(solution)/shard_map/pallas_call | solution.py:420
  182.2 8.8 %shard_map.134 = (bf16[4,128,1024]{2,1,0:T(8,128)(2,1)}, bf16[4,128,1024]{2,1,0:T(8,128)(2,1)}) custom-call(s32[2]{0:T(128)} %pad_add_fusion.refs_0_, bf16[704,1024]{1,0:T(8,128)(2,1)} %bitcast.30, bf16[704,1024]{1,0:T(8,128)(2,1)} %bitcast.29, f32[1024,128]{1,0:T(8,128)} %get-tuple-element.24.refs_3_, bf16[4,128,1024]{2,1,0:T(8,128)(2,1)} %copy-done.5, ...), custom_call_target="tpu_custom_call" | custom-call | tf_op jit(solution)/shard_map/pallas_call | solution.py:420
  191.0 0.2 collective-permute-start.31
  191.2 7.1 %all-to-all-done.4.refs_3_ = bf16[4,128,1024]{2,1,0:T(8,128)(2,1)S(1)} async-done(((bf16[4,128,1024]{2,1,0:T(8,128)(2,1)}), bf16[4,128,1024]{2,1,0:T(8,128)(2,1)S(1)}, u32[]{:S(2)}, u32[]{:S(2)}) %all-to-all-start.4) | async-done | bytes 1048608 | tf_op jit(solution)/shard_map/all_to_all | solution.py:87
  198.3 3.0 %add.26 = bf16[4,128,1024]{2,1,0:T(8,128)(2,1)} add(bf16[4,128,1024]{2,1,0:T(8,128)(2,1)} %get-tuple-element.26, bf16[4,128,1024]{2,1,0:T(8,128)(2,1)S(1)} %collective-permute-done.31) | non-fusion elementwise | flops 524288 | bytes 3145728 | tf_op jit(solution)/shard_map/add | solution.py:574
  201.3 3.5 %all-to-all-start.3 = ((bf16[4,128,1024]{2,1,0:T(8,128)(2,1)}), bf16[4,128,1024]{2,1,0:T(8,128)(2,1)S(1)}, u32[]{:S(2)}, u32[]{:S(2)}) async-start(bf16[4,128,1024]{2,1,0:T(8,128)(2,1)} %add.26), calls=%async_computation.3 | async-start | bytes 2097152 | tf_op jit(solution)/shard_map/all_to_all | solution.py:87
  204.9 1.0 copy-done.21
  205.9 9.9 %shard_map.136 = (bf16[4,128,1024]{2,1,0:T(8,128)(2,1)}, bf16[4,128,1024]{2,1,0:T(8,128)(2,1)}) custom-call(s32[2]{0:T(128)} %pad_add_fusion.refs_0_, bf16[704,1024]{1,0:T(8,128)(2,1)} %bitcast.31, f32[1024,704]{1,0:T(8,128)} %get-tuple-element.32.refs_2_, bf16[4,128,1024]{2,1,0:T(8,128)(2,1)} %copy-done.6, bf16[4,128,1024]{2,1,0:T(8,128)(2,1)} %copy-done.21), custom_call_target="tpu_custom_call" | custom-call | tf_op jit(solution)/shard_map/pallas_call | solution.py:420
  215.7 0.2 collective-permute-start.33
  215.9 2.7 collective-permute-done.33
  218.7 2.6 add.28
  221.3 9.8 %all-to-all-done.3 = bf16[4,128,1024]{2,1,0:T(8,128)(2,1)S(1)} async-done(((bf16[4,128,1024]{2,1,0:T(8,128)(2,1)}), bf16[4,128,1024]{2,1,0:T(8,128)(2,1)S(1)}, u32[]{:S(2)}, u32[]{:S(2)}) %all-to-all-start.3) | async-done | bytes 1048608 | tf_op jit(solution)/shard_map/all_to_all | solution.py:87
  231.1 3.7 %all-to-all-start.5 = ((bf16[4,128,1024]{2,1,0:T(8,128)(2,1)}), bf16[4,128,1024]{2,1,0:T(8,128)(2,1)S(1)}, u32[]{:S(2)}, u32[]{:S(2)}) async-start(bf16[4,128,1024]{2,1,0:T(8,128)(2,1)} %add.28), calls=%async_computation.5 | async-start | bytes 2097152 | tf_op jit(solution)/shard_map/all_to_all | solution.py:87
  234.9 0.2 convert_reduce_fusion
  235.1 0.8 add_convert_fusion
  235.8 24.2 %all-to-all-done.5.refs_6_ = bf16[4,128,1024]{2,1,0:T(8,128)(2,1)S(1)} async-done(((bf16[4,128,1024]{2,1,0:T(8,128)(2,1)}), bf16[4,128,1024]{2,1,0:T(8,128)(2,1)S(1)}, u32[]{:S(2)}, u32[]{:S(2)}) %all-to-all-start.5) | async-done | bytes 1048608 | tf_op jit(solution)/shard_map/all_to_all | solution.py:87
  260.1 1.0 copy-done.4
  261.1 8.1 %shard_map.137 = (bf16[128,3072]{1,0:T(8,128)(2,1)}, f32[128,1024]{1,0:T(8,128)}) custom-call(s32[2]{0:T(128)} %pad_add_fusion.refs_0_, bf16[128,1024]{1,0:T(8,128)(2,1)} %copy-done.18, f32[128,1024]{1,0:T(8,128)} %get-tuple-element.30.refs_2_, f32[128,3072]{1,0:T(8,128)} %get-tuple-element.31.refs_3_, f32[1,1024]{1,0:T(1,128)} %refs_4_.6, ...), custom_call_target="tpu_custom_call" | custom-call | tf_op jit(solution)/shard_map/pallas_call | solution.py:420
  269.2 7.3 %shard_map.138 = bf16[128,1024]{1,0:T(8,128)(2,1)} custom-call(s32[2]{0:T(128)} %pad_add_fusion.refs_0_, bf16[128,1024]{1,0:T(8,128)(2,1)} %refs_1_.3, bf16[128,3072]{1,0:T(8,128)(2,1)} %get-tuple-element.36.refs_2_, f32[128,1024]{1,0:T(8,128)} %get-tuple-element.37.refs_3_, f32[1,1024]{1,0:T(1,128)} %refs_4_.7, bf16[128,3072]{1,0:T(8,128)(2,1)} %bitcast.36, ...), custom_call_target="tpu_custom_call" | custom-call | tf_op jit(solution)/shard_map/pallas_call | solution.py:420
  (97 shorter events, 0.9 us)
Async XLA Ops:
  0.6 32.4 %collective-permute-start.1 = (bf16[128,3072]{1,0:T(8,128)(2,1)}, bf16[128,3072]{1,0:T(8,128)(2,1)S(1)}, u32[]{:S(2)}, u32[]{:S(2)}) collective-permute-start(bf16[128,3072]{1,0:T(8,128)(2,1)} %bitcast.32), channel_id=1, source_target_pairs={{0,2},{1,3},{2,4},{3,5},{4,6},{5,7},{8,10},{9,11},{10,12},{11,13},... | collective-permute-start | bytes 2359304 | tf_op jit(solution)/shard_map/ppermute | solution.py:66
  5.6 29.0 %collective-permute-start.2 = (bf16[128,3072]{1,0:T(8,128)(2,1)}, bf16[128,3072]{1,0:T(8,128)(2,1)}, u32[]{:S(2)}, u32[]{:S(2)}) collective-permute-start(bf16[128,3072]{1,0:T(8,128)(2,1)} %bitcast.33), channel_id=1, source_target_pairs={{2,0},{3,1},{4,2},{5,3},{6,4},{7,5},{10,8},{11,9},{12,10},{13,11},... | collective-permute-start | bytes 2359304 | tf_op jit(solution)/shard_map/ppermute | solution.py:66
  6.9 8.9 %collective-permute-start = (bf16[128,1024]{1,0:T(8,128)(2,1)}, bf16[128,1024]{1,0:T(8,128)(2,1)S(1)}, u32[]{:S(2)}, u32[]{:S(2)}) collective-permute-start(bf16[128,1024]{1,0:T(8,128)(2,1)} %param.12), channel_id=1, source_target_pairs={{0,8},{8,16},{16,24},{24,0},{1,9},{9,17},{17,25},{25,1},{2,10},{10... | collective-permute-start | bytes 786440 | tf_op jit(solution)/shard_map/ppermute | solution.py:45
  8.5 98.7 %copy-start.25 = (s32[2,1,8,8]{3,2,1,0:T(8,128)S(1)}, s32[2,1,8,8]{3,2,1,0:T(8,128)}, u32[]{:S(2)}) copy-start(s32[2,1,8,8]{3,2,1,0:T(8,128)} %param.23) | copy-start | bytes 1540
  8.5 19.8 %collective-permute-start.14 = (bf16[128,1024]{1,0:T(8,128)(2,1)}, bf16[128,1024]{1,0:T(8,128)(2,1)S(1)}, u32[]{:S(2)}, u32[]{:S(2)}) collective-permute-start(bf16[128,1024]{1,0:T(8,128)(2,1)} %bitcast.37), channel_id=1, source_target_pairs={{0,2},{1,3},{2,4},{3,5},{4,6},{5,7},{8,10},{9,11},{10,12},{11,13},... | collective-permute-start | bytes 786440 | tf_op jit(solution)/shard_map/ppermute | solution.py:66
  13.2 19.2 %collective-permute-start.15 = (bf16[128,1024]{1,0:T(8,128)(2,1)}, bf16[128,1024]{1,0:T(8,128)(2,1)S(1)}, u32[]{:S(2)}, u32[]{:S(2)}) collective-permute-start(bf16[128,1024]{1,0:T(8,128)(2,1)} %bitcast.38), channel_id=1, source_target_pairs={{2,0},{3,1},{4,2},{5,3},{6,4},{7,5},{10,8},{11,9},{12,10},{13,11},... | collective-permute-start | bytes 786440 | tf_op jit(solution)/shard_map/ppermute | solution.py:66
  15.9 14.9 %copy-start.19 = (bf16[128,1024]{1,0:T(8,128)(2,1)}, bf16[128,1024]{1,0:T(8,128)(2,1)S(1)}, u32[]{:S(2)}) copy-start(bf16[128,1024]{1,0:T(8,128)(2,1)S(1)} %collective-permute-done.refs_1_) | copy-start | bytes 786436
  15.9 20.1 %collective-permute-start.20 = (bf16[128,1024]{1,0:T(8,128)(2,1)}, bf16[128,1024]{1,0:T(8,128)(2,1)S(1)}, u32[]{:S(2)}, u32[]{:S(2)}) collective-permute-start(bf16[128,1024]{1,0:T(8,128)(2,1)} %bitcast.39), channel_id=1, source_target_pairs={{0,1},{1,0},{2,3},{3,2},{4,5},{5,4},{6,7},{7,6},{8,9},{9,8},{10,11... | collective-permute-start | bytes 786440 | tf_op jit(solution)/shard_map/ppermute | solution.py:62
  28.3 42.3 %copy-start.9 = (bf16[128,1024]{1,0:T(8,128)(2,1)}, bf16[128,1024]{1,0:T(8,128)(2,1)S(1)}, u32[]{:S(2)}) copy-start(bf16[128,1024]{1,0:T(8,128)(2,1)S(1)} %collective-permute-done.14.refs_11_.refs_8_) | copy-start | bytes 786436
  28.3 9.0 %collective-permute-start.27 = (bf16[128,1024]{1,0:T(8,128)(2,1)}, bf16[128,1024]{1,0:T(8,128)(2,1)S(1)}, u32[]{:S(2)}, u32[]{:S(2)}) collective-permute-start(bf16[128,1024]{1,0:T(8,128)(2,1)} %param.14), channel_id=1, source_target_pairs={{0,24},{8,0},{16,8},{24,16},{1,25},{9,1},{17,9},{25,17},{2,26},{10... | collective-permute-start | bytes 786440 | tf_op jit(solution)/shard_map/ppermute | solution.py:45
  32.4 35.7 %copy-start.10 = (bf16[128,1024]{1,0:T(8,128)(2,1)}, bf16[128,1024]{1,0:T(8,128)(2,1)S(1)}, u32[]{:S(2)}) copy-start(bf16[128,1024]{1,0:T(8,128)(2,1)S(1)} %collective-permute-done.15.refs_12_.refs_9_) | copy-start | bytes 786436
  32.4 5.0 %collective-permute-start.16 = (bf16[128,1024]{1,0:T(8,128)(2,1)S(1)}, bf16[128,1024]{1,0:T(8,128)(2,1)S(1)}, u32[]{:S(2)}, u32[]{:S(2)}) collective-permute-start(bf16[128,1024]{1,0:T(8,128)(2,1)S(1)} %collective-permute-done.14.refs_11_.refs_8_), channel_id=1, source_target_pairs={{2,4},{3,5},{4,6},{5,7},{10,12},{11,13},{12,14},{13,15},{18,20},{1... | collective-permute-start | bytes 786440 | tf_op jit(solution)/shard_map/ppermute | solution.py:66
  33.1 37.5 %copy-start.7 = (bf16[128,3072]{1,0:T(8,128)(2,1)}, bf16[128,3072]{1,0:T(8,128)(2,1)S(1)}, u32[]{:S(2)}) copy-start(bf16[128,3072]{1,0:T(8,128)(2,1)S(1)} %collective-permute-done.1.refs_6_) | copy-start | bytes 2359300
  33.1 34.3 %collective-permute-start.3 = (bf16[128,3072]{1,0:T(8,128)(2,1)S(1)}, bf16[128,3072]{1,0:T(8,128)(2,1)}, u32[]{:S(2)}, u32[]{:S(2)}) collective-permute-start(bf16[128,3072]{1,0:T(8,128)(2,1)S(1)} %collective-permute-done.1.refs_6_), channel_id=1, source_target_pairs={{2,4},{3,5},{4,6},{5,7},{10,12},{11,13},{12,14},{13,15},{18,20},{1... | collective-permute-start | bytes 2359304 | tf_op jit(solution)/shard_map/ppermute | solution.py:66
  34.7 33.4 %collective-permute-start.4 = (bf16[128,3072]{1,0:T(8,128)(2,1)}, bf16[128,3072]{1,0:T(8,128)(2,1)}, u32[]{:S(2)}, u32[]{:S(2)}) collective-permute-start(bf16[128,3072]{1,0:T(8,128)(2,1)} %collective-permute-done.2.refs_7_), channel_id=1, source_target_pairs={{2,0},{3,1},{4,2},{5,3},{10,8},{11,9},{12,10},{13,11},{18,16},{19,... | collective-permute-start | bytes 2359304 | tf_op jit(solution)/shard_map/ppermute | solution.py:66
  36.0 29.5 %copy-start.11 = (bf16[128,1024]{1,0:T(8,128)(2,1)}, bf16[128,1024]{1,0:T(8,128)(2,1)S(1)}, u32[]{:S(2)}) copy-start(bf16[128,1024]{1,0:T(8,128)(2,1)S(1)} %collective-permute-done.20.refs_17_.refs_14_) | copy-start | bytes 786436
  36.0 28.8 %collective-permute-start.17 = (bf16[128,1024]{1,0:T(8,128)(2,1)S(1)}, bf16[128,1024]{1,0:T(8,128)(2,1)}, u32[]{:S(2)}, u32[]{:S(2)}) collective-permute-start(bf16[128,1024]{1,0:T(8,128)(2,1)S(1)} %collective-permute-done.15.refs_12_.refs_9_), channel_id=1, source_target_pairs={{2,0},{3,1},{4,2},{5,3},{10,8},{11,9},{12,10},{13,11},{18,16},{19,... | collective-permute-start | bytes 786440 | tf_op jit(solution)/shard_map/ppermute | solution.py:66
  37.3 32.1 %copy-start.18 = (bf16[128,1024]{1,0:T(8,128)(2,1)}, bf16[128,1024]{1,0:T(8,128)(2,1)S(1)}, u32[]{:S(2)}) copy-start(bf16[128,1024]{1,0:T(8,128)(2,1)S(1)} %collective-permute-done.27.refs_1_) | copy-start | bytes 786436
  37.3 28.1 %collective-permute-start.21 = (bf16[128,1024]{1,0:T(8,128)(2,1)S(1)}, bf16[128,1024]{1,0:T(8,128)(2,1)S(1)}, u32[]{:S(2)}, u32[]{:S(2)}) collective-permute-start(bf16[128,1024]{1,0:T(8,128)(2,1)S(1)} %collective-permute-done.14.refs_11_.refs_8_), channel_id=1, source_target_pairs={{0,1},{1,0},{2,3},{3,2},{4,5},{5,4},{6,7},{7,6},{8,9},{9,8},{10,11... | collective-permute-start | bytes 786440 | tf_op jit(solution)/shard_map/ppermute | solution.py:62
  37.4 30.7 %copy-start.12 = (bf16[128,1024]{1,0:T(8,128)(2,1)}, bf16[128,1024]{1,0:T(8,128)(2,1)S(1)}, u32[]{:S(2)}) copy-start(bf16[128,1024]{1,0:T(8,128)(2,1)S(1)} %collective-permute-done.16.refs_13_.refs_10_) | copy-start | bytes 786436
  37.4 28.1 %collective-permute-start.22 = (bf16[128,1024]{1,0:T(8,128)(2,1)S(1)}, bf16[128,1024]{1,0:T(8,128)(2,1)S(1)}, u32[]{:S(2)}, u32[]{:S(2)}) collective-permute-start(bf16[128,1024]{1,0:T(8,128)(2,1)S(1)} %collective-permute-done.15.refs_12_.refs_9_), channel_id=1, source_target_pairs={{0,1},{1,0},{2,3},{3,2},{4,5},{5,4},{6,7},{7,6},{8,9},{9,8},{10,11... | collective-permute-start | bytes 786440 | tf_op jit(solution)/shard_map/ppermute | solution.py:62
  64.8 1.3 collective-permute-start.18
  65.5 2.6 copy-start.13
  65.5 16.0 %collective-permute-start.5 = (bf16[128,3072]{1,0:T(8,128)(2,1)}, bf16[128,3072]{1,0:T(8,128)(2,1)S(1)}, u32[]{:S(2)}, u32[]{:S(2)}) collective-permute-start(bf16[128,3072]{1,0:T(8,128)(2,1)} %bitcast.34), channel_id=1, source_target_pairs={{0,1},{1,0},{2,3},{3,2},{4,5},{5,4},{6,7},{7,6},{8,9},{9,8},{10,11... | collective-permute-start | bytes 2359304 | tf_op jit(solution)/shard_map/ppermute | solution.py:62
  65.6 2.6 copy-start.14
  65.6 16.2 %collective-permute-start.6 = (bf16[128,3072]{1,0:T(8,128)(2,1)S(1)}, bf16[128,3072]{1,0:T(8,128)(2,1)}, u32[]{:S(2)}, u32[]{:S(2)}) collective-permute-start(bf16[128,3072]{1,0:T(8,128)(2,1)S(1)} %collective-permute-done.1.refs_6_), channel_id=1, source_target_pairs={{0,1},{1,0},{2,3},{3,2},{4,5},{5,4},{6,7},{7,6},{8,9},{9,8},{10,11... | collective-permute-start | bytes 2359304 | tf_op jit(solution)/shard_map/ppermute | solution.py:62
  66.1 2.1 copy-start.15
  66.1 13.5 %collective-permute-start.19 = (bf16[128,1024]{1,0:T(8,128)(2,1)}, bf16[128,1024]{1,0:T(8,128)(2,1)}, u32[]{:S(2)}, u32[]{:S(2)}) collective-permute-start(bf16[128,1024]{1,0:T(8,128)(2,1)} %collective-permute-done.17.refs_14_.refs_11_), channel_id=1, source_target_pairs={{2,0},{3,1},{10,8},{11,9},{18,16},{19,17},{26,24},{27,25}} | collective-permute-start | bytes 786440 | tf_op jit(solution)/shard_map/ppermute | solution.py:66
  67.4 14.6 %collective-permute-start.10 = (bf16[128,3072]{1,0:T(8,128)(2,1)}, bf16[128,3072]{1,0:T(8,128)(2,1)S(1)}, u32[]{:S(2)}, u32[]{:S(2)}) collective-permute-start(bf16[128,3072]{1,0:T(8,128)(2,1)} %collective-permute-done.3.refs_8_), channel_id=1, source_target_pairs={{4,6},{5,7},{12,14},{13,15},{20,22},{21,23},{28,30},{29,31}} | collective-permute-start | bytes 2359304 | tf_op jit(solution)/shard_map/ppermute | solution.py:66
  68.1 37.3 %collective-permute-start.11 = (bf16[128,3072]{1,0:T(8,128)(2,1)}, bf16[128,3072]{1,0:T(8,128)(2,1)S(1)}, u32[]{:S(2)}, u32[]{:S(2)}) collective-permute-start(bf16[128,3072]{1,0:T(8,128)(2,1)} %collective-permute-done.4.refs_9_), channel_id=1, source_target_pairs={{2,0},{3,1},{10,8},{11,9},{18,16},{19,17},{26,24},{27,25}} | collective-permute-start | bytes 2359304 | tf_op jit(solution)/shard_map/ppermute | solution.py:66
  70.6 54.5 %all-to-all-start = ((bf16[4,128,1024]{2,1,0:T(8,128)(2,1)}), bf16[4,128,1024]{2,1,0:T(8,128)(2,1)}, u32[]{:S(2)}, u32[]{:S(2)}) async-start(bf16[4,128,1024]{2,1,0:T(8,128)(2,1)} %broadcast_in_dim.16), calls=%async_computation | async-start | bytes 2097152 | tf_op jit(solution)/shard_map/all_to_all | solution.py:87
  79.5 1.7 collective-permute-start.23
  81.3 1.0 copy-start.16
  81.3 24.2 %collective-permute-start.7 = (bf16[128,3072]{1,0:T(8,128)(2,1)}, bf16[128,3072]{1,0:T(8,128)(2,1)}, u32[]{:S(2)}, u32[]{:S(2)}) collective-permute-start(bf16[128,3072]{1,0:T(8,128)(2,1)} %collective-permute-done.2.refs_7_), channel_id=1, source_target_pairs={{0,1},{1,0},{2,3},{3,2},{4,5},{5,4},{6,7},{7,6},{8,9},{9,8},{10,11... | collective-permute-start | bytes 2359304 | tf_op jit(solution)/shard_map/ppermute | solution.py:62
  81.4 24.6 %collective-permute-start.8 = (bf16[128,3072]{1,0:T(8,128)(2,1)}, bf16[128,3072]{1,0:T(8,128)(2,1)}, u32[]{:S(2)}, u32[]{:S(2)}) collective-permute-start(bf16[128,3072]{1,0:T(8,128)(2,1)} %collective-permute-done.3.refs_8_), channel_id=1, source_target_pairs={{0,1},{1,0},{2,3},{3,2},{4,5},{5,4},{6,7},{7,6},{8,9},{9,8},{10,11... | collective-permute-start | bytes 2359304 | tf_op jit(solution)/shard_map/ppermute | solution.py:62
  81.8 24.3 %collective-permute-start.9 = (bf16[128,3072]{1,0:T(8,128)(2,1)}, bf16[128,3072]{1,0:T(8,128)(2,1)}, u32[]{:S(2)}, u32[]{:S(2)}) collective-permute-start(bf16[128,3072]{1,0:T(8,128)(2,1)} %collective-permute-done.4.refs_9_), channel_id=1, source_target_pairs={{0,1},{1,0},{2,3},{3,2},{4,5},{5,4},{6,7},{7,6},{8,9},{9,8},{10,11... | collective-permute-start | bytes 2359304 | tf_op jit(solution)/shard_map/ppermute | solution.py:62
  81.9 33.8 %copy-start = (bf16[128,3072]{1,0:T(8,128)(2,1)}, bf16[128,3072]{1,0:T(8,128)(2,1)S(1)}, u32[]{:S(2)}) copy-start(bf16[128,3072]{1,0:T(8,128)(2,1)S(1)} %collective-permute-done.10.refs_6_.refs_10_) | copy-start | bytes 2359300
  82.0 33.9 %collective-permute-start.12 = (bf16[128,3072]{1,0:T(8,128)(2,1)S(1)}, bf16[128,3072]{1,0:T(8,128)(2,1)S(1)}, u32[]{:S(2)}, u32[]{:S(2)}) collective-permute-start(bf16[128,3072]{1,0:T(8,128)(2,1)S(1)} %collective-permute-done.10.refs_6_.refs_10_), channel_id=1, source_target_pairs={{0,1},{1,0},{2,3},{3,2},{4,5},{5,4},{6,7},{7,6},{8,9},{9,8},{10,11... | collective-permute-start | bytes 2359304 | tf_op jit(solution)/shard_map/ppermute | solution.py:62
  105.4 10.4 %copy-start.1 = (bf16[128,3072]{1,0:T(8,128)(2,1)}, bf16[128,3072]{1,0:T(8,128)(2,1)S(1)}, u32[]{:S(2)}) copy-start(bf16[128,3072]{1,0:T(8,128)(2,1)S(1)} %collective-permute-done.11.refs_7_.refs_11_) | copy-start | bytes 2359300
  105.4 10.4 %collective-permute-start.13 = (bf16[128,3072]{1,0:T(8,128)(2,1)S(1)}, bf16[128,3072]{1,0:T(8,128)(2,1)S(1)}, u32[]{:S(2)}, u32[]{:S(2)}) collective-permute-start(bf16[128,3072]{1,0:T(8,128)(2,1)S(1)} %collective-permute-done.11.refs_7_.refs_11_), channel_id=1, source_target_pairs={{0,1},{1,0},{2,3},{3,2},{4,5},{5,4},{6,7},{7,6},{8,9},{9,8},{10,11... | collective-permute-start | bytes 2359304 | tf_op jit(solution)/shard_map/ppermute | solution.py:62
  105.5 10.4 %collective-permute-start.24 = (bf16[128,1024]{1,0:T(8,128)(2,1)}, bf16[128,1024]{1,0:T(8,128)(2,1)S(1)}, u32[]{:S(2)}, u32[]{:S(2)}) collective-permute-start(bf16[128,1024]{1,0:T(8,128)(2,1)} %collective-permute-done.17.refs_14_.refs_11_), channel_id=1, source_target_pairs={{0,1},{1,0},{2,3},{3,2},{4,5},{5,4},{6,7},{7,6},{8,9},{9,8},{10,11... | collective-permute-start | bytes 786440 | tf_op jit(solution)/shard_map/ppermute | solution.py:62
  106.0 9.8 %collective-permute-start.25 = (bf16[128,1024]{1,0:T(8,128)(2,1)}, bf16[128,1024]{1,0:T(8,128)(2,1)}, u32[]{:S(2)}, u32[]{:S(2)}) collective-permute-start(bf16[128,1024]{1,0:T(8,128)(2,1)} %copy-done.15), channel_id=1, source_target_pairs={{0,1},{1,0},{2,3},{3,2},{4,5},{5,4},{6,7},{7,6},{8,9},{9,8},{10,11... | collective-permute-start | bytes 786440 | tf_op jit(solution)/shard_map/ppermute | solution.py:62
  106.1 9.7 %collective-permute-start.26 = (bf16[128,1024]{1,0:T(8,128)(2,1)}, bf16[128,1024]{1,0:T(8,128)(2,1)}, u32[]{:S(2)}, u32[]{:S(2)}) collective-permute-start(bf16[128,1024]{1,0:T(8,128)(2,1)} %collective-permute-done.19.refs_16_.refs_13_), channel_id=1, source_target_pairs={{0,1},{1,0},{2,3},{3,2},{4,5},{5,4},{6,7},{7,6},{8,9},{9,8},{10,11... | collective-permute-start | bytes 786440 | tf_op jit(solution)/shard_map/ppermute | solution.py:62
  115.9 1.2 copy-start.3
  125.0 3.6 %copy-start.26 = (f32[2,128,2]{1,2,0:T(2,128)S(1)}, f32[2,128,2]{1,2,0:T(2,128)}, u32[]{:S(2)}) copy-start(f32[2,128,2]{1,2,0:T(2,128)} %param.22) | copy-start | bytes 6148
  125.1 3.6 %copy-start.27 = (s32[2,128,2]{1,2,0:T(2,128)S(1)}, s32[2,128,2]{1,2,0:T(2,128)}, u32[]{:S(2)}) copy-start(s32[2,128,2]{1,2,0:T(2,128)} %param.21) | copy-start | bytes 6148
  125.1 29.8 %all-to-all-start.2 = ((bf16[4,128,1024]{2,1,0:T(8,128)(2,1)}), bf16[4,128,1024]{2,1,0:T(8,128)(2,1)S(1)}, u32[]{:S(2)}, u32[]{:S(2)}) async-start(bf16[4,128,1024]{2,1,0:T(8,128)(2,1)} %get-tuple-element.25), calls=%async_computation.2 | async-start | bytes 2097152 | tf_op jit(solution)/shard_map/all_to_all | solution.py:87
  154.8 12.0 %copy-start.5 = (bf16[4,128,1024]{2,1,0:T(8,128)(2,1)}, bf16[4,128,1024]{2,1,0:T(8,128)(2,1)S(1)}, u32[]{:S(2)}) copy-start(bf16[4,128,1024]{2,1,0:T(8,128)(2,1)S(1)} %all-to-all-done.2.refs_4_) | copy-start | bytes 3145732
  155.6 11.8 %all-to-all-start.1 = ((bf16[4,128,128]{2,1,0:T(8,128)(2,1)}), bf16[4,128,128]{2,1,0:T(8,128)(2,1)S(1)}, u32[]{:S(2)}, u32[]{:S(2)}) async-start(bf16[4,128,128]{2,1,0:T(8,128)(2,1)} %broadcast_in_dim.19), calls=%async_computation.1 | async-start | bytes 262144 | tf_op jit(solution)/shard_map/all_to_all | solution.py:87
  158.9 14.9 %collective-permute-start.28 = (bf16[4,128,1024]{2,1,0:T(8,128)(2,1)}, bf16[4,128,1024]{2,1,0:T(8,128)(2,1)S(1)}, u32[]{:S(2)}, u32[]{:S(2)}) collective-permute-start(bf16[4,128,1024]{2,1,0:T(8,128)(2,1)} %all-to-all-done.refs_2_), channel_id=1, source_target_pairs={{0,1},{1,0},{2,3},{3,2},{4,5},{5,4},{6,7},{7,6},{8,9},{9,8},{10,11... | collective-permute-start | bytes 3145736 | tf_op jit(solution)/shard_map/ppermute | solution.py:62
  166.9 15.3 %collective-permute-start.30 = (bf16[4,128,1024]{2,1,0:T(8,128)(2,1)S(1)}, bf16[4,128,1024]{2,1,0:T(8,128)(2,1)}, u32[]{:S(2)}, u32[]{:S(2)}) collective-permute-start(bf16[4,128,1024]{2,1,0:T(8,128)(2,1)S(1)} %all-to-all-done.2.refs_4_), channel_id=1, source_target_pairs={{0,1},{1,0},{2,3},{3,2},{4,5},{5,4},{6,7},{7,6},{8,9},{9,8},{10,11... | collective-permute-start | bytes 3145736 | tf_op jit(solution)/shard_map/ppermute | solution.py:62
  167.4 6.4 %copy-start.22 = (bf16[4,128,128]{2,1,0:T(8,128)(2,1)}, bf16[4,128,128]{2,1,0:T(8,128)(2,1)S(1)}, u32[]{:S(2)}) copy-start(bf16[4,128,128]{2,1,0:T(8,128)(2,1)S(1)} %all-to-all-done.1.refs_4_) | copy-start | bytes 393220
  167.4 30.9 %all-to-all-start.4 = ((bf16[4,128,1024]{2,1,0:T(8,128)(2,1)}), bf16[4,128,1024]{2,1,0:T(8,128)(2,1)S(1)}, u32[]{:S(2)}, u32[]{:S(2)}) async-start(bf16[4,128,1024]{2,1,0:T(8,128)(2,1)} %get-tuple-element.33), calls=%async_computation.4 | async-start | bytes 2097152 | tf_op jit(solution)/shard_map/all_to_all | solution.py:87
  172.4 1.3 collective-permute-start.29
  173.7 1.0 copy-start.20
  191.0 7.3 %collective-permute-start.31 = (bf16[4,128,1024]{2,1,0:T(8,128)(2,1)}, bf16[4,128,1024]{2,1,0:T(8,128)(2,1)S(1)}, u32[]{:S(2)}, u32[]{:S(2)}) collective-permute-start(bf16[4,128,1024]{2,1,0:T(8,128)(2,1)} %get-tuple-element.27), channel_id=1, source_target_pairs={{0,1},{1,0},{2,3},{3,2},{4,5},{5,4},{6,7},{7,6},{8,9},{9,8},{10,11... | collective-permute-start | bytes 3145736 | tf_op jit(solution)/shard_map/ppermute | solution.py:62
  198.3 3.0 %copy-start.6 = (bf16[4,128,1024]{2,1,0:T(8,128)(2,1)}, bf16[4,128,1024]{2,1,0:T(8,128)(2,1)S(1)}, u32[]{:S(2)}) copy-start(bf16[4,128,1024]{2,1,0:T(8,128)(2,1)S(1)} %all-to-all-done.4.refs_3_) | copy-start | bytes 3145732
  198.3 6.5 %collective-permute-start.32 = (bf16[4,128,1024]{2,1,0:T(8,128)(2,1)S(1)}, bf16[4,128,1024]{2,1,0:T(8,128)(2,1)S(1)}, u32[]{:S(2)}, u32[]{:S(2)}) collective-permute-start(bf16[4,128,1024]{2,1,0:T(8,128)(2,1)S(1)} %all-to-all-done.4.refs_3_), channel_id=1, source_target_pairs={{0,1},{1,0},{2,3},{3,2},{4,5},{5,4},{6,7},{7,6},{8,9},{9,8},{10,11... | collective-permute-start | bytes 3145736 | tf_op jit(solution)/shard_map/ppermute | solution.py:62
  201.3 29.8 %all-to-all-start.3 = ((bf16[4,128,1024]{2,1,0:T(8,128)(2,1)}), bf16[4,128,1024]{2,1,0:T(8,128)(2,1)S(1)}, u32[]{:S(2)}, u32[]{:S(2)}) async-start(bf16[4,128,1024]{2,1,0:T(8,128)(2,1)} %add.26), calls=%async_computation.3 | async-start | bytes 2097152 | tf_op jit(solution)/shard_map/all_to_all | solution.py:87
  204.9 1.0 copy-start.21
  215.7 2.9 %collective-permute-start.33 = (bf16[4,128,1024]{2,1,0:T(8,128)(2,1)}, bf16[4,128,1024]{2,1,0:T(8,128)(2,1)S(1)}, u32[]{:S(2)}, u32[]{:S(2)}) collective-permute-start(bf16[4,128,1024]{2,1,0:T(8,128)(2,1)} %get-tuple-element.35), channel_id=1, source_target_pairs={{0,1},{1,0},{2,3},{3,2},{4,5},{5,4},{6,7},{7,6},{8,9},{9,8},{10,11... | collective-permute-start | bytes 3145736 | tf_op jit(solution)/shard_map/ppermute | solution.py:62
  221.3 13.8 %copy-start.23 = (f32[128,1024]{1,0:T(8,128)S(1)}, f32[128,1024]{1,0:T(8,128)}, u32[]{:S(2)}) copy-start(f32[128,1024]{1,0:T(8,128)} %get-tuple-element.23) | copy-start | bytes 1572868
  231.1 28.9 %all-to-all-start.5 = ((bf16[4,128,1024]{2,1,0:T(8,128)(2,1)}), bf16[4,128,1024]{2,1,0:T(8,128)(2,1)S(1)}, u32[]{:S(2)}, u32[]{:S(2)}) async-start(bf16[4,128,1024]{2,1,0:T(8,128)(2,1)} %add.28), calls=%async_computation.5 | async-start | bytes 2097152 | tf_op jit(solution)/shard_map/all_to_all | solution.py:87
  260.0 1.0 copy-start.4
  (4 other events, 3.2 us)
